TPU v7x, 256 devices: a whole 4x4x8 slice. The times are simulated.
256 devices in a mesh: geo: 8 (over x, core), spec: 32 (over z, y).
Axes of the slice: x: 4, y: 4, z: 8, core: 2. Of those that a mesh axis runs over, the one named last changes fastest.
Arguments:
- spectrum: float32 [32, 36, 256, 512], P('spec', None, 'geo'), may hold values from 0.01 to 50, as said below
- land_sea: int32 [256, 512], P('geo'), may hold values from 0 to 1, as said below
- sea_index: int32 [8, 12288], P('geo'), may hold values from 0 to 16383, as said below
- sea_count: int32 [8], P('geo'), may hold values from 4096 to 12288, as said below
- wind_speed: float32 [256, 512], P('geo'), may hold values from 4 to 24
- wind_dir: float32 [256, 512], P('geo'), may hold values from -3.140625 to 3.140625
- slope_x: float32 [256, 512], P('geo'), may hold values from -0.5 to 0.5
- slope_y: float32 [256, 512], P('geo'), may hold values from -0.5 to 0.5
Outputs:
- next_spectrum: float32 [32, 36, 256, 512], P('spec', None, 'geo')
Inputs may be any that keep to these rules, and one draw needn't show every extreme that they name: `spectrum`: A positive energy density. `land_sea`: land comes in aligned 8 x 8 blocks of cells. `sea_index`: row t lists the sea cells of tile t in increasing position, then its land cells in increasing position, all distinct; its first sea_count[t] entries are exactly the tile's sea cells. `sea_count`: the number of sea cells of each tile; at least one tile has exactly 12288.
All inputs are finite; a program needn't handle non-finite values.
Results may differ from a plain program's by a relative error of at most 0.0003.
Values sent between devices are 32-bit elements; how exact they have to be, the bound alone decides.
A program may use at most 64 MiB of HBM per device.

v0:
```python
import math

import jax
import jax.numpy as jnp
from jax import lax
from jax.sharding import PartitionSpec as P

GRAVITY = 9.81
BASE_FREQ = 0.035
GROWTH = 1.1
COURANT_TOP = 0.9
TURN_TOP = 1.2
SPACING = 0.1
USTAR_RATIO = 0.035
WIND_COEF = 0.0375
WHITECAP = 0.36
STEEP_REF = 1.6
EPSILON = 1e-06
QUAD_COEF = 100.0


def extended(cells, sides, width):
    for axis, dim in sides:
        count = lax.axis_size(axis)
        ends = count - 1
        head = lax.slice_in_dim(cells, 0, width, axis=dim)
        tail = lax.slice_in_dim(cells, cells.shape[dim] - width, cells.shape[dim], axis=dim)
        cells = jnp.concatenate(
            [
                lax.ppermute(tail, axis, [(i, (i + 1) % count) for i in range(ends)]),
                cells,
                lax.ppermute(head, axis, [((i + 1) % count, i) for i in range(ends)]),
            ],
            axis=dim,
        )
    return cells


def band_table(band_ids):
    growth_factor = jnp.power(GROWTH, band_ids)
    radian_freq = 2.0 * math.pi * BASE_FREQ * growth_factor
    wavenum = radian_freq * radian_freq / GRAVITY
    return (
        radian_freq,
        wavenum,
        COURANT_TOP / growth_factor,
        TURN_TOP / growth_factor,
        SPACING * radian_freq,
    )


def quick_flux(far_left, near_left, near_right, far_right, courant):
    forward = courant >= 0
    upwind = jnp.where(forward, far_left, far_right)
    center = jnp.where(forward, near_left, near_right)
    downwind = jnp.where(forward, near_right, near_left)
    face_value = (
        0.5 * (center + downwind)
        - 0.5 * jnp.abs(courant) * (downwind - center)
        - (1.0 - courant * courant) / 6.0 * (downwind - 2.0 * center + upwind)
    )
    return courant * face_value


def advect(padded, courant, along):
    face_count = padded.shape[along] - 4
    shifted = [
        lax.slice_in_dim(padded, offset, offset + face_count + 1, axis=along) for offset in range(4)
    ]
    face_flux = quick_flux(shifted[0], shifted[1], shifted[2], shifted[3], courant)
    centre_cells = lax.slice_in_dim(padded, 2, 2 + face_count, axis=along)
    upper_flux = lax.slice_in_dim(face_flux, 1, face_count + 1, axis=along)
    lower_flux = lax.slice_in_dim(face_flux, 0, face_count, axis=along)
    return centre_cells - (upper_flux - lower_flux)


def quad_delta(center, above, below, energy, dir_axis):
    plus = jnp.roll(above, -1, axis=dir_axis)
    minus = jnp.roll(below, 3, axis=dir_axis)
    return (
        QUAD_COEF
        * (center * center * (plus + minus) - 2.0 * center * plus * minus)
        / (energy * energy)
    )


def quad_term(delta, delta_above, delta_below, dir_axis):
    return (
        -2.0 * delta
        + jnp.roll(delta_below, 1, axis=dir_axis)
        + jnp.roll(delta_above, -3, axis=dir_axis)
    )


def band_neighbours(values):
    empty = jnp.zeros((1,) + values.shape[1:], jnp.float32)
    return (
        jnp.concatenate([values[1:], empty], axis=0),
        jnp.concatenate([empty, values[:-1]], axis=0),
    )


def sources(density, energy_sum, first_sum, root_sum, radian_freq, wavenum, cosine, wind_speed):
    energy = energy_sum + EPSILON
    mean_sigma = energy / (first_sum + EPSILON)
    ratio_k = energy / (root_sum + EPSILON)
    mean_k = ratio_k * ratio_k
    steepness = energy * mean_k * mean_k / STEEP_REF
    decay_rate = WHITECAP * mean_sigma * (wavenum / mean_k) * steepness * steepness
    growth_rate = (
        WIND_COEF
        * radian_freq
        * jnp.maximum(28.0 * USTAR_RATIO * wind_speed * radian_freq / GRAVITY * cosine - 1.0, 0.0)
    )
    return density * (1.0 + growth_rate) / (1.0 + decay_rate)


def local_sources(point_block, wind_block, wind_angle, angles, dtheta):
    band_total = point_block.shape[0]
    band_ids = jnp.arange(band_total).astype(jnp.float32)
    radian_freq, wavenum, courant, turn_rate, band_spread = band_table(band_ids)
    scaled = point_block * (band_spread * dtheta)[:, None, None]
    energy_sum = jnp.sum(scaled, axis=(0, 1))
    first_sum = jnp.sum(scaled / radian_freq[:, None, None], axis=(0, 1))
    root_sum = jnp.sum(scaled / jnp.sqrt(wavenum)[:, None, None], axis=(0, 1))
    energy = energy_sum + EPSILON
    above, below = band_neighbours(point_block)
    delta = quad_delta(point_block, above, below, energy, 1)
    delta_above, delta_below = band_neighbours(delta)
    extra = quad_term(delta, delta_above, delta_below, 1)
    cosine = jnp.cos(angles[:, None] - wind_angle[None, :])
    return (
        sources(
            point_block,
            energy_sum,
            first_sum,
            root_sum,
            radian_freq[:, None, None],
            wavenum[:, None, None],
            cosine,
            wind_block,
        )
        + extra
    )


def shards(spectrum, land_sea, sea_index, sea_count, wind_speed, wind_dir, slope_x, slope_y):
    local_bands, dir_count, row_count, col_count = spectrum.shape
    spec_count = lax.axis_size("spec")
    spec_pos = lax.axis_index("spec")
    band_total = local_bands * spec_count
    tile_cells = row_count * col_count
    dtheta = 2.0 * math.pi / dir_count
    angles = (jnp.arange(dir_count).astype(jnp.float32) + 0.5) * dtheta
    face_angles = jnp.arange(dir_count + 1).astype(jnp.float32) * dtheta
    band_ids = (spec_pos * local_bands + jnp.arange(local_bands)).astype(jnp.float32)
    radian_freq, wavenum, courant, turn_rate, band_spread = band_table(band_ids)
    wet_mask = land_sea.astype(jnp.float32)
    density = spectrum * wet_mask
    padded = extended(density, (("geo", 2),), 2)
    density = (
        advect(padded, (courant[:, None] * jnp.cos(angles)[None, :])[:, :, None, None], 2)
        * wet_mask
    )
    padded = jnp.pad(density, ((0, 0), (0, 0), (0, 0), (2, 2)))
    density = (
        advect(padded, (courant[:, None] * jnp.sin(angles)[None, :])[:, :, None, None], 3)
        * wet_mask
    )
    turning = turn_rate[:, None, None, None] * (
        jnp.sin(face_angles)[None, :, None, None] * slope_x
        - jnp.cos(face_angles)[None, :, None, None] * slope_y
    )
    padded = jnp.concatenate([density[:, -2:], density, density[:, :2]], axis=1)
    floored = jnp.maximum(advect(padded, turning, 1), 0.0)
    per_device = tile_cells // spec_count
    point_block = lax.all_to_all(floored, "spec", split_axis=2, concat_axis=0, tiled=True).reshape(
        band_total, dir_count, per_device
    )
    wind_block = lax.dynamic_slice_in_dim(
        wind_speed.reshape(tile_cells), spec_pos * per_device, per_device
    )
    wind_angle = lax.dynamic_slice_in_dim(
        wind_dir.reshape(tile_cells), spec_pos * per_device, per_device
    )
    wet_block = lax.dynamic_slice_in_dim(
        wet_mask.reshape(tile_cells), spec_pos * per_device, per_device
    )
    updated = local_sources(point_block, wind_block, wind_angle, angles, dtheta) * wet_block
    returned = lax.all_to_all(
        updated.reshape(band_total, dir_count, 1, per_device),
        "spec",
        split_axis=0,
        concat_axis=2,
        tiled=True,
    )
    return returned


def solution(mesh):
    placed = (
        P("spec", None, "geo", None),
        P("geo", None),
        P("geo", None),
        P("geo"),
        P("geo", None),
        P("geo", None),
        P("geo", None),
        P("geo", None),
    )
    return jax.shard_map(
        shards, mesh=mesh, in_specs=placed, out_specs=P("spec", None, "geo", None), check_vma=False
    )
```

profile of v0, /device:TPU:2, one launch (start us, length us, event | category | flops | bytes accessed | tf_op | source)
XLA Modules:
  0.0 170.7 jit_solution(6317280934112765547)
XLA Ops:
  0.0 0.8 convert_bitcast_fusion
  0.9 2.0 %broadcast_multiply_fusion = f32[1,36,32,512]{3,2,1,0:T(8,128)S(1)} fusion(f32[1,36,32,512]{3,2,1,0:T(8,128)} %param.8, f32[32,512]{1,0:T(8,128)S(1)} %get-tuple-element.23), kind=kLoop, calls=%fused_computation.85 | loop fusion | flops 589824 | bytes 4784128 | tf_op jit(solution)/shard_map/mul | solution.py:159
  2.9 0.1 fusion.60
  3.0 1.9 %collective-permute-start = (f32[1,36,2,512]{3,2,1,0:T(2,128)S(1)}, f32[1,36,2,512]{3,2,1,0:T(2,128)S(1)}, u32[]{:S(2)}, u32[]{:S(2)}) collective-permute-start(f32[1,36,2,512]{3,2,1,0:T(2,128)S(1)} %get-tuple-element.20), channel_id=1, source_target_pairs={{0,32},{32,64},{64,96},{96,128},{128,160},{160,192},{192,224},{1,3... | collective-permute-start | bytes 442376 | tf_op jit(solution)/shard_map/ppermute | solution.py:30
  4.9 3.6 %collective-permute-start.1 = (f32[1,36,2,512]{3,2,1,0:T(2,128)S(1)}, f32[1,36,2,512]{3,2,1,0:T(2,128)S(1)}, u32[]{:S(2)}, u32[]{:S(2)}) collective-permute-start(f32[1,36,2,512]{3,2,1,0:T(2,128)S(1)} %get-tuple-element.21), channel_id=1, source_target_pairs={{32,0},{64,32},{96,64},{128,96},{160,128},{192,160},{224,192},{33,... | collective-permute-start | bytes 442376 | tf_op jit(solution)/shard_map/ppermute | solution.py:32
  8.9 0.6 collective-permute-done
  9.5 1.8 %collective-permute-done.1 = f32[1,36,2,512]{3,2,1,0:T(2,128)S(1)} collective-permute-done((f32[1,36,2,512]{3,2,1,0:T(2,128)S(1)}, f32[1,36,2,512]{3,2,1,0:T(2,128)S(1)}, u32[]{:S(2)}, u32[]{:S(2)}) %collective-permute-start.1) | collective-permute-done | bytes 147488 | tf_op jit(solution)/shard_map/ppermute | solution.py:32
  11.2 0.0 copy-start
  11.2 2.5 %fusion.9 = f32[1,36,33,512]{3,2,1,0:T(8,128)S(1)} fusion(f32[1,36,2,512]{3,2,1,0:T(2,128)S(1)} %collective-permute-done.1, f32[1,36,32,512]{3,2,1,0:T(8,128)S(1)} %broadcast_multiply_fusion, f32[1,36,2,512]{3,2,1,0:T(2,128)S(1)} %collective-permute-done, f32[36]{0:T(128)S(1)} %get-tuple-element.31, f32[36]{0:T(128)S(1)} %get-tuple-element.32, ...), kind=kLoop, calls=%fused_computation.14 | loop fusion | flops 10948608 | bytes 5087700 | tf_op jit(solution)/shard_map/mul | solution.py:62
  13.8 0.0 copy-done
  13.8 0.7 fusion.22
  14.5 2.8 %fusion.4 = f32[1,36,32,513]{3,2,1,0:T(8,128)S(1)} fusion(f32[1,36,32,512]{3,2,1,0:T(8,128)S(1)} %fusion.22, f32[36]{0:T(128)S(1)} %get-tuple-element.28, f32[36]{0:T(128)S(1)} %get-tuple-element.29, f32[36]{0:T(128)S(1)} %get-tuple-element.30, pred[36]{0:T(512)(128)(4,1)S(1)} %get-tuple-element.34), kind=kLoop, calls=%fused_computation.8 | loop fusion | flops 8273664 | bytes 4723668 | tf_op jit(solution)/shard_map/mul | solution.py:62
  17.3 0.0 copy-start.1
  17.3 0.0 copy-start.2
  17.3 0.7 fusion.20
  18.1 0.1 copy-done.1
  18.1 0.0 copy-done.2
  18.2 3.1 %fusion.16 = f32[1,37,32,512]{3,2,1,0:T(8,128)S(1)} fusion(f32[1,2,32,512]{3,2,1,0:T(8,128)S(1)} %get-tuple-element.19, f32[1,36,32,512]{3,2,1,0:T(8,128)S(1)} %fusion.20, f32[1,2,32,512]{3,2,1,0:T(8,128)S(1)} %get-tuple-element.18, f32[32,512]{1,0:T(8,128)S(1)} %copy-done.1, f32[37]{0:T(128)S(1)} %get-tuple-element.36, f32[32,512]{1,0:T(8,128)S(1)} %copy-done.2, ...), kind=kLoop, calls=%fused_computation.29 | loop fusion | flops 16973824 | bytes 5177644 | tf_op jit(solution)/shard_map/mul | solution.py:62
  21.3 0.6 fusion.18
  21.9 3.8 %copy.20 = f32[1,36,32,512]{3,0,1,2:T(1,128)} copy(f32[1,36,32,512]{3,2,1,0:T(8,128)S(1)} %fusion.18) | data formatting | bytes 4718592 | tf_op jit(solution)/shard_map/max | solution.py:175
  25.7 0.0 copy-start.3
  25.7 0.0 copy-start.4
  25.7 11.8 %all-to-all-start = ((f32[1,36,32,512]{3,0,1,2:T(1,128)}), f32[1,36,32,512]{3,0,1,2:T(1,128)S(1)}, u32[]{:S(2)}, u32[]{:S(2)}) async-start(f32[1,36,32,512]{3,0,1,2:T(1,128)} %copy.20), calls=%async_computation | async-start | bytes 4718592 | tf_op jit(solution)/shard_map/all_to_all | solution.py:177
  37.5 0.0 copy-done.3
  37.5 0.0 copy-done.4
  37.6 0.1 dynamic_slice.10
  37.7 0.1 dynamic_slice.11
  37.8 0.1 dynamic-slice_multiply_fusion
  37.9 0.1 multiply_multiply_fusion
  38.0 0.3 subtract_cosine_fusion
  38.3 53.9 %all-to-all-done = f32[1,36,32,512]{3,0,1,2:T(1,128)S(1)} async-done(((f32[1,36,32,512]{3,0,1,2:T(1,128)}), f32[1,36,32,512]{3,0,1,2:T(1,128)S(1)}, u32[]{:S(2)}, u32[]{:S(2)}) %all-to-all-start) | async-done | bytes 2359328 | tf_op jit(solution)/shard_map/all_to_all | solution.py:177
  92.3 0.8 copy.36
  93.0 0.6 slice_bitcast_fusion.1
  93.8 0.3 fusion.56
  94.1 0.6 fusion.57
  94.7 0.8 divide_reduce_fusion.1
  95.5 1.0 fusion.29
  96.5 0.6 fusion.58
  97.2 0.4 slice_bitcast_fusion.2
  97.7 0.4 fusion.40
  98.0 0.1 fusion.45
  98.1 2.1 %fusion.25 = f32[32,36,1,512]{3,0,1,2:T(8,128)S(1)} fusion(f32[32,35,1,512]{3,0,1,2:T(8,128)S(1)} %slice_bitcast_fusion.2, f32[32,1,1,512]{3,0,1,2:T(8,128)S(1)} %fusion.46, f32[32,3,1,512]{3,0,1,2:T(8,128)S(1)} %fusion.42, f32[32,33,1,512]{3,0,1,2:T(8,128)S(1)} %fusion.40, f32[32,33,1,512]{3,0,1,2:T(8,128)S(1)} %get-tuple-element.12, ...), kind=kLoop, calls=%fused_computation.50 | loop fusion | flops 14745600 | bytes 14364800 | tf_op jit(solution)/shard_map/mul | solution.py:189
  100.2 2.4 %copy.23 = f32[32,36,1,512]{3,2,1,0:T(1,128)S(1)} copy(f32[32,36,1,512]{3,0,1,2:T(8,128)S(1)} %fusion.25) | data formatting | bytes 4718592 | tf_op jit(solution)/shard_map/mul | solution.py:189
  102.7 65.9 %all_to_all.33 = f32[32,36,1,512]{3,2,1,0:T(1,128)S(1)} all-to-all(f32[32,36,1,512]{3,2,1,0:T(1,128)S(1)} %copy.23), channel_id=1, replica_groups=mesh['geo'=8,'spec'=32] {'spec'}, dimensions={0} | all-to-all | bytes 4718592 | tf_op jit(solution)/shard_map/all_to_all | solution.py:190
  168.6 2.1 %copy.35 = f32[32,36,1,512]{3,0,1,2:T(8,128)} copy(f32[32,36,1,512]{3,2,1,0:T(1,128)S(1)} %all_to_all.33) | data formatting | bytes 4718592 | tf_op jit(solution)/shard_map/all_to_all | solution.py:190
  (20 shorter events, 0.4 us)
Async XLA Ops:
  3.0 6.5 %collective-permute-start = (f32[1,36,2,512]{3,2,1,0:T(2,128)S(1)}, f32[1,36,2,512]{3,2,1,0:T(2,128)S(1)}, u32[]{:S(2)}, u32[]{:S(2)}) collective-permute-start(f32[1,36,2,512]{3,2,1,0:T(2,128)S(1)} %get-tuple-element.20), channel_id=1, source_target_pairs={{0,32},{32,64},{64,96},{96,128},{128,160},{160,192},{192,224},{1,3... | collective-permute-start | bytes 442376 | tf_op jit(solution)/shard_map/ppermute | solution.py:30
  4.9 6.3 %collective-permute-start.1 = (f32[1,36,2,512]{3,2,1,0:T(2,128)S(1)}, f32[1,36,2,512]{3,2,1,0:T(2,128)S(1)}, u32[]{:S(2)}, u32[]{:S(2)}) collective-permute-start(f32[1,36,2,512]{3,2,1,0:T(2,128)S(1)} %get-tuple-element.21), channel_id=1, source_target_pairs={{32,0},{64,32},{96,64},{128,96},{160,128},{192,160},{224,192},{33,... | collective-permute-start | bytes 442376 | tf_op jit(solution)/shard_map/ppermute | solution.py:32
  11.2 2.5 %copy-start = (f32[1,36,32,512]{3,2,1,0:T(8,128)S(1)}, f32[1,36,32,512]{3,2,1,0:T(8,128)}, u32[]{:S(2)}) copy-start(f32[1,36,32,512]{3,2,1,0:T(8,128)} %param.8) | copy-start | bytes 7077892
  17.3 0.8 copy-start.1
  17.3 0.9 copy-start.2
  25.7 11.8 %copy-start.3 = (f32[32,512]{1,0:T(8,128)S(1)}, f32[32,512]{1,0:T(8,128)}, u32[]{:S(2)}) copy-start(f32[32,512]{1,0:T(8,128)} %param.10) | copy-start | bytes 196612
  25.7 11.9 %copy-start.4 = (f32[32,512]{1,0:T(8,128)S(1)}, f32[32,512]{1,0:T(8,128)}, u32[]{:S(2)}) copy-start(f32[32,512]{1,0:T(8,128)} %param.11) | copy-start | bytes 196612
  25.7 66.6 %all-to-all-start = ((f32[1,36,32,512]{3,0,1,2:T(1,128)}), f32[1,36,32,512]{3,0,1,2:T(1,128)S(1)}, u32[]{:S(2)}, u32[]{:S(2)}) async-start(f32[1,36,32,512]{3,0,1,2:T(1,128)} %copy.20), calls=%async_computation | async-start | bytes 4718592 | tf_op jit(solution)/shard_map/all_to_all | solution.py:177
where the time goes:
time: 172 us; the launch traced here: 171 us
  blocking collectives  65.9 us (38%)
  waiting for transfers between devices  56.3 us (33%)
  other arithmetic  18 us (10%)
  starting transfers between devices  17.4 us (10%)
  local copies, waits for them, and re-layouts  12.7 us (7%)
    all_to_all x1, blocking collectives, shards(): lax.all_to_all(updated.reshape(band_total, dir_count, 1, per_device), 'sp...  65.9 us
    all_to_all x1, waiting for transfers between devices, shards(): lax.all_to_all(floored, 'spec', split_axis=2, concat_axis=0, tiled=True)  53.9 us
    all_to_all x1, starting transfers between devices, shards(): lax.all_to_all(floored, 'spec', split_axis=2, concat_axis=0, tiled=True)  11.8 us
    mul x3, other arithmetic, quick_flux(): return courant * face_value  8.41 us
    max x1, local copies, waits for them, and re-layouts, shards(): floored = jnp.maximum(advect(padded, turning, 1), 0.0)  3.83 us
    ppermute x1, starting transfers between devices, extended(): lax.ppermute(head, axis, [((i + 1) % count, i) for i in range(ends)])  3.64 us
  transfers between devices with their start and end apart: 3, of which 3 were waited for; matrix products, arithmetic and copies ran while one was open for 1% of the time, Pallas kernels for 0%

commit v1 on v0

--- a/solution.py
+++ b/solution.py
@@ -144,12 +144,16 @@
     )
 
 
+Y_GROUP = 4
+
+
 def shards(spectrum, land_sea, sea_index, sea_count, wind_speed, wind_dir, slope_x, slope_y):
     local_bands, dir_count, row_count, col_count = spectrum.shape
-    spec_count = lax.axis_size("spec")
-    spec_pos = lax.axis_index("spec")
-    band_total = local_bands * spec_count
-    tile_cells = row_count * col_count
+    z_count = lax.axis_size("z")
+    y_count = lax.axis_size("y")
+    z_pos = lax.axis_index("z")
+    y_pos = lax.axis_index("y")
+    spec_pos = z_pos * y_count + y_pos
     dtheta = 2.0 * math.pi / dir_count
     angles = (jnp.arange(dir_count).astype(jnp.float32) + 0.5) * dtheta
     face_angles = jnp.arange(dir_count + 1).astype(jnp.float32) * dtheta
@@ -173,33 +177,61 @@
     )
     padded = jnp.concatenate([density[:, -2:], density, density[:, :2]], axis=1)
     floored = jnp.maximum(advect(padded, turning, 1), 0.0)
-    per_device = tile_cells // spec_count
-    point_block = lax.all_to_all(floored, "spec", split_axis=2, concat_axis=0, tiled=True).reshape(
-        band_total, dir_count, per_device
-    )
-    wind_block = lax.dynamic_slice_in_dim(
-        wind_speed.reshape(tile_cells), spec_pos * per_device, per_device
-    )
-    wind_angle = lax.dynamic_slice_in_dim(
-        wind_dir.reshape(tile_cells), spec_pos * per_device, per_device
-    )
-    wet_block = lax.dynamic_slice_in_dim(
-        wet_mask.reshape(tile_cells), spec_pos * per_device, per_device
-    )
-    updated = local_sources(point_block, wind_block, wind_angle, angles, dtheta) * wet_block
-    returned = lax.all_to_all(
-        updated.reshape(band_total, dir_count, 1, per_device),
-        "spec",
-        split_axis=0,
-        concat_axis=2,
-        tiled=True,
-    )
-    return returned
+    point = lax.all_to_all(floored, "y", split_axis=2, concat_axis=0, tiled=True)
+    group = point.shape[0]
+    part_rows = point.shape[2]
+    lower = lax.ppermute(point[group - 2 :], "z", [(i, i + 1) for i in range(z_count - 1)])
+    upper = lax.ppermute(point[:2], "z", [(i + 1, i) for i in range(z_count - 1)])
+    group_ids = (z_pos * group + jnp.arange(group)).astype(jnp.float32)
+    radian_freq, wavenum, courant, turn_rate, band_spread = band_table(group_ids)
+    scaled = point * (band_spread * dtheta)[:, None, None, None]
+    sums = jnp.stack(
+        [
+            jnp.sum(scaled, axis=(0, 1)),
+            jnp.sum(scaled / radian_freq[:, None, None, None], axis=(0, 1)),
+            jnp.sum(scaled / jnp.sqrt(wavenum)[:, None, None, None], axis=(0, 1)),
+        ]
+    )
+    sums = lax.psum(sums, "z")
+    energy_sum, first_sum, root_sum = sums[0], sums[1], sums[2]
+    energy = energy_sum + EPSILON
+    ext = jnp.concatenate([lower, point, upper], axis=0)
+    delta = quad_delta(ext[1:-1], ext[2:], ext[:-2], energy, 1)
+    extra = (
+        -2.0 * delta[1:-1]
+        + jnp.roll(delta[:-2], 1, axis=1)
+        + jnp.roll(delta[2:], -3, axis=1)
+    )
+    row_start = y_pos * part_rows
+    wind_block = lax.dynamic_slice_in_dim(wind_speed, row_start, part_rows, axis=0)
+    wind_angle = lax.dynamic_slice_in_dim(wind_dir, row_start, part_rows, axis=0)
+    wet_block = lax.dynamic_slice_in_dim(wet_mask, row_start, part_rows, axis=0)
+    cosine = jnp.cos(angles[:, None, None] - wind_angle[None])
+    updated = (
+        sources(
+            point,
+            energy_sum,
+            first_sum,
+            root_sum,
+            radian_freq[:, None, None, None],
+            wavenum[:, None, None, None],
+            cosine,
+            wind_block,
+        )
+        + extra
+    ) * wet_block
+    return lax.all_to_all(updated, "y", split_axis=0, concat_axis=2, tiled=True)
 
 
 def solution(mesh):
+    geo_count = mesh.shape["geo"]
+    spec_count = mesh.shape["spec"]
+    local = jax.sharding.Mesh(
+        mesh.devices.reshape(geo_count, spec_count // Y_GROUP, Y_GROUP), ("geo", "z", "y")
+    )
+    spec = ("z", "y")
     placed = (
-        P("spec", None, "geo", None),
+        P(spec, None, "geo", None),
         P("geo", None),
         P("geo", None),
         P("geo"),
@@ -209,5 +241,5 @@
         P("geo", None),
     )
     return jax.shard_map(
-        shards, mesh=mesh, in_specs=placed, out_specs=P("spec", None, "geo", None), check_vma=False
-    )
+        shards, mesh=local, in_specs=placed, out_specs=P(spec, None, "geo", None), check_vma=False
+    )

time: 172 us -> 161 us (0.936)
  waiting for transfers between devices: 56.3 us -> 29.6 us
  other arithmetic: 18 us -> 31.6 us
  blocking collectives: 65.9 us -> 76.5 us
  local copies, waits for them, and re-layouts: 12.7 us -> 6.14 us
    psum x0 -> x1, blocking collectives: none -> 50.8 us  [shards(): sums = lax.psum(sums, 'z')]
    all_to_all x1, blocking collectives: 65.9 us -> 25.7 us  [shards(): return lax.all_to_all(updated, 'y', split_axis=0, concat_axis=2, tiled=True)]
    all_to_all x1, waiting for transfers between devices: 53.9 us -> 27.1 us  [shards(): lax.all_to_all(floored, 'y', split_axis=2, concat_axis=0, tiled=True)]
    all_to_all x1, starting transfers between devices: 11.8 us -> 4.46 us  [shards(): lax.all_to_all(floored, 'y', split_axis=2, concat_axis=0, tiled=True)]
    ppermute x0 -> x2, starting transfers between devices: none -> 6.11 us  [the longest x1 4.83 us: shards(): lax.ppermute(point[group - 2:], 'z', [(i, i + 1) for i in range(z_count -...]
    max x1 -> x0, local copies, waits for them, and re-layouts: 3.83 us -> none  [shards(): floored = jnp.maximum(advect(padded, turning, 1), 0.0)]
    cos x1, other arithmetic: 0.34 us -> 2.77 us  [shards(): cosine = jnp.cos(angles[:, None, None] - wind_angle[None])]
    mul x1 -> x0, local copies, waits for them, and re-layouts: 2.43 us -> none  [shards(): local_sources(point_block, wind_block, wind_angle, angles, dtheta)]
  transfers between devices with their start and end apart: 3 -> 5, of which waited for: 3 -> 3; matrix products, arithmetic and copies ran while one was open for 1% -> 7% of each run, Pallas kernels for 0% -> 0%
where the time goes in v1:
time: 161 us; the launch traced here: 160 us
  blocking collectives  76.5 us (48%)
  other arithmetic  31.6 us (20%)
  waiting for transfers between devices  29.6 us (18%)
  starting transfers between devices  16.1 us (10%)
  local copies, waits for them, and re-layouts  6.14 us (4%)
    psum x1, blocking collectives, shards(): sums = lax.psum(sums, 'z')  50.8 us
    all_to_all x1, waiting for transfers between devices, shards(): lax.all_to_all(floored, 'y', split_axis=2, concat_axis=0, tiled=True)  27.1 us
    all_to_all x1, blocking collectives, shards(): return lax.all_to_all(updated, 'y', split_axis=0, concat_axis=2, tiled=True)  25.7 us
    mul x3, other arithmetic, quick_flux(): return courant * face_value  7.44 us
    ppermute x1, starting transfers between devices, shards(): lax.ppermute(point[group - 2:], 'z', [(i, i + 1) for i in range(z_count -...  4.83 us
    all_to_all x1, starting transfers between devices, shards(): lax.all_to_all(floored, 'y', split_axis=2, concat_axis=0, tiled=True)  4.46 us
    ppermute x1, starting transfers between devices, extended(): lax.ppermute(head, axis, [((i + 1) % count, i) for i in range(ends)])  3.64 us
  transfers between devices with their start and end apart: 5, of which 3 were waited for; matrix products, arithmetic and copies ran while one was open for 7% of the time, Pallas kernels for 0%

profile of v1, /device:TPU:2, one launch (start us, length us, event | category | flops | bytes accessed | tf_op | source)
XLA Modules:
  0.0 160.3 jit_solution(7413247275264117152)
XLA Ops:
  0.0 0.8 convert_element_type.84
  0.8 3.0 %copy_multiply_fusion = f32[1,36,32,512]{3,1,2,0:T(8,128)S(1)} fusion(f32[1,36,32,512]{3,2,1,0:T(8,128)} %param.8, f32[32,512]{1,0:T(8,128)S(1)} %convert_element_type.84), kind=kLoop, calls=%fused_computation.52 | loop fusion | flops 589824 | bytes 4784128 | tf_op jit(solution)/shard_map/mul | solution.py:163
  3.9 1.9 %collective-permute-start = (f32[1,36,2,512]{3,1,2,0:T(8,128)S(1)}, f32[1,36,2,512]{3,1,2,0:T(8,128)S(1)}, u32[]{:S(2)}, u32[]{:S(2)}) collective-permute-start(f32[1,36,2,512]{3,1,2,0:T(8,128)S(1)} %get-tuple-element.13), channel_id=1, source_target_pairs={{0,32},{32,64},{64,96},{96,128},{128,160},{160,192},{192,224},{1,3... | collective-permute-start | bytes 442376 | tf_op jit(solution)/shard_map/ppermute | solution.py:30
  5.9 3.6 %collective-permute-start.1 = (f32[1,36,2,512]{3,1,2,0:T(8,128)S(1)}, f32[1,36,2,512]{3,1,2,0:T(8,128)S(1)}, u32[]{:S(2)}, u32[]{:S(2)}) collective-permute-start(f32[1,36,2,512]{3,1,2,0:T(8,128)S(1)} %get-tuple-element.14), channel_id=1, source_target_pairs={{32,0},{64,32},{96,64},{128,96},{160,128},{192,160},{224,192},{33,... | collective-permute-start | bytes 442376 | tf_op jit(solution)/shard_map/ppermute | solution.py:32
  9.8 0.8 collective-permute-done
  10.6 1.8 %collective-permute-done.1 = f32[1,36,2,512]{3,1,2,0:T(8,128)S(1)} collective-permute-done((f32[1,36,2,512]{3,1,2,0:T(8,128)S(1)}, f32[1,36,2,512]{3,1,2,0:T(8,128)S(1)}, u32[]{:S(2)}, u32[]{:S(2)}) %collective-permute-start.1) | collective-permute-done | bytes 147488 | tf_op jit(solution)/shard_map/ppermute | solution.py:32
  12.3 1.6 %fusion.14 = f32[1,36,33,512]{3,1,2,0:T(8,128)S(1)} fusion(f32[1,36,2,512]{3,1,2,0:T(8,128)S(1)} %collective-permute-done.1, f32[1,36,32,512]{3,1,2,0:T(8,128)S(1)} %copy_multiply_fusion, f32[1,36,2,512]{3,1,2,0:T(8,128)S(1)} %collective-permute-done, f32[36]{0:T(128)S(1)} %get-tuple-element.26, f32[36]{0:T(128)S(1)} %get-tuple-element.27, ...), kind=kLoop, calls=%fused_computation.31 | loop fusion | flops 10948608 | bytes 5087700 | tf_op jit(solution)/shard_map/mul | solution.py:62
  13.9 0.1 copy-done.1
  14.0 1.7 %fusion.26 = f32[1,36,32,512]{3,1,2,0:T(8,128)S(1)} fusion(f32[1,36,33,512]{3,1,2,0:T(8,128)S(1)} %fusion.14, f32[32,512]{1,0:T(8,128)S(1)} %convert_element_type.84, f32[1,36,32,512]{3,2,1,0:T(8,128)S(1)} %copy-done.1), kind=kLoop, calls=%fused_computation.51 | loop fusion | flops 2359296 | bytes 9502720 | tf_op jit(solution)/shard_map/mul | solution.py:166
  15.7 2.8 %fusion.7 = f32[1,36,32,513]{3,1,2,0:T(8,128)S(1)} fusion(f32[1,36,32,512]{3,1,2,0:T(8,128)S(1)} %fusion.26, f32[36]{0:T(128)S(1)} %get-tuple-element.23, f32[36]{0:T(128)S(1)} %get-tuple-element.24, f32[36]{0:T(128)S(1)} %get-tuple-element.25, pred[36]{0:T(512)(128)(4,1)S(1)} %get-tuple-element.29), kind=kLoop, calls=%fused_computation.19 | loop fusion | flops 8273664 | bytes 4723668 | tf_op jit(solution)/shard_map/mul | solution.py:62
  18.5 0.0 copy-start.4
  18.5 0.0 copy-start.5
  18.5 0.8 fusion.24
  19.3 0.1 fusion.47
  19.4 0.0 copy-done.4
  19.4 0.0 copy-done.5
  19.4 3.0 %fusion.22 = f32[1,37,32,512]{3,1,2,0:T(8,128)S(1)} fusion(f32[1,2,32,512]{3,1,2,0:T(2,128)S(1)} %get-tuple-element.12, f32[1,36,32,512]{3,1,2,0:T(8,128)S(1)} %fusion.24, f32[1,2,32,512]{3,1,2,0:T(2,128)S(1)} %get-tuple-element.11, f32[32,512]{1,0:T(8,128)S(1)} %copy-done.4, f32[37]{0:T(128)S(1)} %get-tuple-element.31, f32[32,512]{1,0:T(8,128)S(1)} %copy-done.5, ...), kind=kLoop, calls=%fused_computation.42 | loop fusion | flops 16973824 | bytes 5177644 | tf_op jit(solution)/shard_map/mul | solution.py:62
  22.5 2.2 %fusion.17 = f32[1,36,32,512]{3,1,0,2:T(8,128)} fusion(f32[1,36,32,512]{3,1,2,0:T(8,128)S(1)} %fusion.24, f32[1,37,32,512]{3,1,2,0:T(8,128)S(1)} %fusion.22), kind=kLoop, calls=%fused_computation.36 | loop fusion | flops 1769472 | bytes 9437184 | tf_op jit(solution)/shard_map/max | solution.py:179
  24.7 4.5 %all-to-all-start = ((f32[1,36,32,512]{3,1,0,2:T(8,128)}), f32[1,36,32,512]{3,1,0,2:T(8,128)S(1)}, u32[]{:S(2)}, u32[]{:S(2)}) async-start(f32[1,36,32,512]{3,1,0,2:T(8,128)} %fusion.17), calls=%async_computation | async-start | bytes 5242880 | tf_op jit(solution)/shard_map/all_to_all | solution.py:180
  29.2 0.6 multiply_multiply_fusion.2
  29.7 0.5 broadcast_multiply_fusion.2
  30.2 0.5 broadcast_multiply_fusion
  30.8 0.7 dynamic-slice_multiply_fusion
  31.5 0.7 multiply_multiply_fusion
  32.2 2.8 %subtract_cosine_fusion = f32[36,8,512]{2,1,0:T(8,128)} fusion(f32[8,512]{1,0:T(8,128)S(1)} %get-tuple-element.34, f32[36]{0:T(128)S(1)} %add_multiply_fusion), kind=kLoop, calls=%fused_computation.67 | loop fusion | flops 147456 | bytes 606352 | tf_op jit(solution)/shard_map/cos | solution.py:209
  35.0 27.1 %all-to-all-done = f32[1,36,32,512]{3,1,0,2:T(8,128)S(1)} async-done(((f32[1,36,32,512]{3,1,0,2:T(8,128)}), f32[1,36,32,512]{3,1,0,2:T(8,128)S(1)}, u32[]{:S(2)}, u32[]{:S(2)}) %all-to-all-start) | async-done | bytes 2359328 | tf_op jit(solution)/shard_map/all_to_all | solution.py:180
  62.1 1.4 copy.22
  63.5 1.6 %slice_bitcast_fusion.1 = (f32[2,36,8,512]{3,2,1,0:T(8,128)}, f32[2,36,8,512]{3,2,1,0:T(8,128)}) fusion(f32[4,1,36,8,512]{4,3,2,0,1:T(8,128)S(1)} %bitcast.50), kind=kLoop, calls=%fused_computation.66 | loop fusion | bytes 4718592 | tf_op jit(solution)/shard_map/slice | solution.py:183
  65.1 4.8 %collective-permute-start.2 = (f32[2,36,8,512]{3,2,1,0:T(8,128)}, f32[2,36,8,512]{3,2,1,0:T(8,128)}, u32[]{:S(2)}, u32[]{:S(2)}) collective-permute-start(f32[2,36,8,512]{3,2,1,0:T(8,128)} %get-tuple-element.15), channel_id=1, source_target_pairs={{0,4},{4,8},{8,12},{12,16},{16,20},{20,24},{24,28},{1,5},{5,9},{9,... | collective-permute-start | bytes 3538952 | tf_op jit(solution)/shard_map/ppermute | solution.py:183
  69.9 1.3 collective-permute-start.3
  71.2 0.0 copy-done.9
  71.2 0.0 copy-done.10
  71.2 0.0 copy-done.7
  71.2 3.2 %multiply_reduce_fusion = (f32[8,512]{1,0:T(8,128)S(1)}, f32[8,512]{1,0:T(8,128)S(1)}, f32[8,512]{1,0:T(8,128)S(1)}, f32[4,36,8,512]{3,2,1,0:T(8,128)S(1)}) fusion(f32[4]{0:T(128)S(1)} %copy-done.9, f32[4]{0:T(128)S(1)} %copy-done.7, f32[4]{0:T(128)S(1)} %copy-done.10, f32[1,36,4,8,512]{4,1,3,2,0:T(8,128)} %bitcast.49), kind=kLoop, calls=%fused_computation.64 | loop fusion | flops 3526656 | bytes 4767792 | tf_op jit(solution)/shard_map/reduce_sum | solution.py:190
  74.4 0.6 pad_maximum_fusion.9
  75.0 50.8 %psum.7 = f32[3,8,512]{2,1,0:T(8,128)} all-reduce(f32[3,8,512]{2,1,0:T(8,128)} %pad_maximum_fusion.9), channel_id=1, replica_groups=mesh['geo'=8,'z'=8,'y'=4] {'z'}, use_global_device_ids=true, to_apply=%region_3.4 | all-reduce | flops 12288 | bytes 98304 | tf_op jit(solution)/shard_map/psum | solution.py:195
  125.8 0.8 fusion.40
  126.6 0.7 fusion.33
  127.3 0.0 collective-permute-done.3
  127.3 0.3 fusion.2
  127.6 0.0 collective-permute-done.2
  127.7 2.5 %multiply_divide_fusion = f32[6,36,8,512]{3,2,1,0:T(8,128)S(1)} fusion(f32[2,36,8,512]{3,2,1,0:T(8,128)S(1)} %collective-permute-done.3, f32[4,36,8,512]{3,2,1,0:T(8,128)S(1)} %get-tuple-element.10, f32[6,35,8,512]{3,2,1,0:T(8,128)S(1)} %fusion.2, f32[2,36,8,512]{3,2,1,0:T(8,128)} %collective-permute-done.2, f32[8,512]{1,0:T(8,128)S(1)} %get-tuple-element.18), kind=kLoop, calls=%fused_computation.13 | loop fusion | flops 14155776 | bytes 11714560 | tf_op jit(solution)/shard_map/div | solution.py:81
  130.2 0.2 slice.213
  130.5 0.2 slice.212
  130.7 0.8 copy-done.2
  131.5 1.4 fusion.30
  132.9 25.7 %all_to_all.36 = f32[4,36,8,512]{3,2,1,0:T(8,128)S(1)} all-to-all(f32[4,36,8,512]{3,2,1,0:T(8,128)S(1)} %fusion.30), channel_id=1, replica_groups=mesh['geo'=8,'z'=8,'y'=4] {'y'}, dimensions={0} | all-to-all | bytes 4718592 | tf_op jit(solution)/shard_map/all_to_all | solution.py:223
  158.6 1.7 %copy.21 = f32[4,36,8,512]{3,2,0,1:T(8,128)} copy(f32[4,36,8,512]{3,2,1,0:T(8,128)S(1)} %all_to_all.36) | data formatting | bytes 4718592 | tf_op jit(solution)/shard_map/all_to_all | solution.py:223
  (24 shorter events, 0.3 us)
Async XLA Ops:
  3.9 6.6 %collective-permute-start = (f32[1,36,2,512]{3,1,2,0:T(8,128)S(1)}, f32[1,36,2,512]{3,1,2,0:T(8,128)S(1)}, u32[]{:S(2)}, u32[]{:S(2)}) collective-permute-start(f32[1,36,2,512]{3,1,2,0:T(8,128)S(1)} %get-tuple-element.13), channel_id=1, source_target_pairs={{0,32},{32,64},{64,96},{96,128},{128,160},{160,192},{192,224},{1,3... | collective-permute-start | bytes 442376 | tf_op jit(solution)/shard_map/ppermute | solution.py:30
  5.9 6.5 %collective-permute-start.1 = (f32[1,36,2,512]{3,1,2,0:T(8,128)S(1)}, f32[1,36,2,512]{3,1,2,0:T(8,128)S(1)}, u32[]{:S(2)}, u32[]{:S(2)}) collective-permute-start(f32[1,36,2,512]{3,1,2,0:T(8,128)S(1)} %get-tuple-element.14), channel_id=1, source_target_pairs={{32,0},{64,32},{96,64},{128,96},{160,128},{192,160},{224,192},{33,... | collective-permute-start | bytes 442376 | tf_op jit(solution)/shard_map/ppermute | solution.py:32
  12.3 1.7 %copy-start.1 = (f32[1,36,32,512]{3,2,1,0:T(8,128)S(1)}, f32[1,36,32,512]{3,2,1,0:T(8,128)}, u32[]{:S(2)}) copy-start(f32[1,36,32,512]{3,2,1,0:T(8,128)} %param.8) | copy-start | bytes 7077892
  18.5 0.9 copy-start.4
  18.5 0.9 copy-start.5
  24.7 37.4 %all-to-all-start = ((f32[1,36,32,512]{3,1,0,2:T(8,128)}), f32[1,36,32,512]{3,1,0,2:T(8,128)S(1)}, u32[]{:S(2)}, u32[]{:S(2)}) async-start(f32[1,36,32,512]{3,1,0,2:T(8,128)} %fusion.17), calls=%async_computation | async-start | bytes 5242880 | tf_op jit(solution)/shard_map/all_to_all | solution.py:180
  29.1 34.3 %copy-start.6 = (f32[4]{0:T(128)}, f32[4]{0:T(128)S(1)}, u32[]{:S(2)}) copy-start(f32[4]{0:T(128)S(1)} %broadcast_multiply_fusion.1) | copy-start | bytes 52
  62.0 3.0 %copy-start = (f32[1,36,32,512]{3,1,0,2:T(8,128)}, f32[1,36,32,512]{3,1,0,2:T(8,128)S(1)}, u32[]{:S(2)}) copy-start(f32[1,36,32,512]{3,1,0,2:T(8,128)S(1)} %all-to-all-done) | copy-start | bytes 7077892
  63.4 7.8 %copy-start.9 = (f32[4]{0:T(128)S(1)}, f32[4]{0:T(128)}, u32[]{:S(2)}) copy-start(f32[4]{0:T(128)} %get-tuple-element.21) | copy-start | bytes 52
  63.4 7.8 %copy-start.10 = (f32[4]{0:T(128)S(1)}, f32[4]{0:T(128)}, u32[]{:S(2)}) copy-start(f32[4]{0:T(128)} %get-tuple-element.22) | copy-start | bytes 52
  63.5 7.8 %copy-start.7 = (f32[4]{0:T(128)S(1)}, f32[4]{0:T(128)}, u32[]{:S(2)}) copy-start(f32[4]{0:T(128)} %copy-done.6) | copy-start | bytes 52
  65.1 62.6 %collective-permute-start.2 = (f32[2,36,8,512]{3,2,1,0:T(8,128)}, f32[2,36,8,512]{3,2,1,0:T(8,128)}, u32[]{:S(2)}, u32[]{:S(2)}) collective-permute-start(f32[2,36,8,512]{3,2,1,0:T(8,128)} %get-tuple-element.15), channel_id=1, source_target_pairs={{0,4},{4,8},{8,12},{12,16},{16,20},{20,24},{24,28},{1,5},{5,9},{9,... | collective-permute-start | bytes 3538952 | tf_op jit(solution)/shard_map/ppermute | solution.py:183
  69.9 57.4 %collective-permute-start.3 = (f32[2,36,8,512]{3,2,1,0:T(8,128)}, f32[2,36,8,512]{3,2,1,0:T(8,128)S(1)}, u32[]{:S(2)}, u32[]{:S(2)}) collective-permute-start(f32[2,36,8,512]{3,2,1,0:T(8,128)} %get-tuple-element.16), channel_id=1, source_target_pairs={{4,0},{8,4},{12,8},{16,12},{20,16},{24,20},{28,24},{5,1},{9,5},{13... | collective-permute-start | bytes 3538952 | tf_op jit(solution)/shard_map/ppermute | solution.py:184
  130.4 1.1 copy-start.2
  130.4 1.1 copy-start.3
  130.5 1.1 copy-start.8

commit v2 on v1

--- a/solution.py
+++ b/solution.py
@@ -192,16 +192,15 @@
             jnp.sum(scaled / jnp.sqrt(wavenum)[:, None, None, None], axis=(0, 1)),
         ]
     )
-    sums = lax.psum(sums, "z")
+    sums = jnp.sum(lax.all_gather(sums, "z"), axis=0)
     energy_sum, first_sum, root_sum = sums[0], sums[1], sums[2]
     energy = energy_sum + EPSILON
     ext = jnp.concatenate([lower, point, upper], axis=0)
-    delta = quad_delta(ext[1:-1], ext[2:], ext[:-2], energy, 1)
+    center, plus, minus = ext[1:-1], jnp.roll(ext[2:], -1, axis=1), jnp.roll(ext[:-2], 3, axis=1)
+    cubic = center * center * (plus + minus) - 2.0 * center * plus * minus
     extra = (
-        -2.0 * delta[1:-1]
-        + jnp.roll(delta[:-2], 1, axis=1)
-        + jnp.roll(delta[2:], -3, axis=1)
-    )
+        -2.0 * cubic[1:-1] + jnp.roll(cubic[:-2], 1, axis=1) + jnp.roll(cubic[2:], -3, axis=1)
+    ) * (QUAD_COEF / (energy * energy))
     row_start = y_pos * part_rows
     wind_block = lax.dynamic_slice_in_dim(wind_speed, row_start, part_rows, axis=0)
     wind_angle = lax.dynamic_slice_in_dim(wind_dir, row_start, part_rows, axis=0)

time: 161 us -> 157 us (0.975)
  other arithmetic: 31.6 us -> 28 us
  waiting for transfers between devices: 29.6 us -> 32.6 us
  blocking collectives: 76.5 us -> 73.7 us
    psum x1 -> x0, blocking collectives: 50.8 us -> none  [shards(): sums = lax.psum(sums, 'z')]
    all_gather x0 -> x1, blocking collectives: none -> 47.5 us  [shards(): sums = jnp.sum(lax.all_gather(sums, 'z'), axis=0)]
    all_to_all x1, waiting for transfers between devices: 27.1 us -> 30.1 us  [shards(): lax.all_to_all(floored, 'y', split_axis=2, concat_axis=0, tiled=True)]
    sub x0 -> x1, other arithmetic: none -> 2.58 us  [shards(): cubic = center * center * (plus + minus) - 2.0 * center * plus * minus]
    div x1 -> x0, other arithmetic: 2.51 us -> none  [quad_delta(): QUAD_COEF * (center * center * (plus + minus) - 2.0 * center * plus * minus)]
  transfers between devices with their start and end apart: 5 -> 5, of which waited for: 3 -> 3; matrix products, arithmetic and copies ran while one was open for 7% -> 5% of each run, Pallas kernels for 0% -> 0%
where the time goes in v2:
time: 157 us; the launch traced here: 156 us
  blocking collectives  73.7 us (47%)
  waiting for transfers between devices  32.6 us (21%)
  other arithmetic  28 us (18%)
  starting transfers between devices  16.2 us (10%)
  local copies, waits for them, and re-layouts  5.31 us (3%)
    all_gather x1, blocking collectives, shards(): sums = jnp.sum(lax.all_gather(sums, 'z'), axis=0)  47.5 us
    all_to_all x1, waiting for transfers between devices, shards(): lax.all_to_all(floored, 'y', split_axis=2, concat_axis=0, tiled=True)  30.1 us
    all_to_all x1, blocking collectives, shards(): return lax.all_to_all(updated, 'y', split_axis=0, concat_axis=2, tiled=True)  26.2 us
    mul x3, other arithmetic, quick_flux(): return courant * face_value  7.44 us
    ppermute x1, starting transfers between devices, shards(): lax.ppermute(point[group - 2:], 'z', [(i, i + 1) for i in range(z_count -...  4.87 us
    all_to_all x1, starting transfers between devices, shards(): lax.all_to_all(floored, 'y', split_axis=2, concat_axis=0, tiled=True)  4.46 us
    ppermute x1, starting transfers between devices, extended(): lax.ppermute(head, axis, [((i + 1) % count, i) for i in range(ends)])  3.64 us
    reduce_sum x1, other arithmetic, shards(): jnp.sum(scaled, axis=(0, 1))  3.15 us
  transfers between devices with their start and end apart: 5, of which 3 were waited for; matrix products, arithmetic and copies ran while one was open for 5% of the time, Pallas kernels for 0%

profile of v2, /device:TPU:2, one launch (start us, length us, event | category | flops | bytes accessed | tf_op | source)
XLA Modules:
  0.0 156.1 jit_solution(4902433601523823258)
XLA Ops:
  0.0 0.0 copy-start
  0.0 0.9 convert_element_type.84
  0.9 3.0 %copy_multiply_fusion = f32[1,36,32,512]{3,1,2,0:T(8,128)S(1)} fusion(f32[1,36,32,512]{3,2,1,0:T(8,128)} %param.8, f32[32,512]{1,0:T(8,128)S(1)} %convert_element_type.84), kind=kLoop, calls=%fused_computation.52 | loop fusion | flops 589824 | bytes 4784128 | tf_op jit(solution)/shard_map/mul | solution.py:163
  4.0 1.9 %collective-permute-start = (f32[1,36,2,512]{3,1,2,0:T(8,128)S(1)}, f32[1,36,2,512]{3,1,2,0:T(8,128)S(1)}, u32[]{:S(2)}, u32[]{:S(2)}) collective-permute-start(f32[1,36,2,512]{3,1,2,0:T(8,128)S(1)} %get-tuple-element.13), channel_id=1, source_target_pairs={{0,32},{32,64},{64,96},{96,128},{128,160},{160,192},{192,224},{1,3... | collective-permute-start | bytes 442376 | tf_op jit(solution)/shard_map/ppermute | solution.py:30
  5.9 3.6 %collective-permute-start.1 = (f32[1,36,2,512]{3,1,2,0:T(8,128)S(1)}, f32[1,36,2,512]{3,1,2,0:T(8,128)S(1)}, u32[]{:S(2)}, u32[]{:S(2)}) collective-permute-start(f32[1,36,2,512]{3,1,2,0:T(8,128)S(1)} %get-tuple-element.14), channel_id=1, source_target_pairs={{32,0},{64,32},{96,64},{128,96},{160,128},{192,160},{224,192},{33,... | collective-permute-start | bytes 442376 | tf_op jit(solution)/shard_map/ppermute | solution.py:32
  9.8 0.8 collective-permute-done
  10.6 1.8 %collective-permute-done.1 = f32[1,36,2,512]{3,1,2,0:T(8,128)S(1)} collective-permute-done((f32[1,36,2,512]{3,1,2,0:T(8,128)S(1)}, f32[1,36,2,512]{3,1,2,0:T(8,128)S(1)}, u32[]{:S(2)}, u32[]{:S(2)}) %collective-permute-start.1) | collective-permute-done | bytes 147488 | tf_op jit(solution)/shard_map/ppermute | solution.py:32
  12.4 0.0 copy-start.2
  12.4 1.6 %fusion.14 = f32[1,36,33,512]{3,1,2,0:T(8,128)S(1)} fusion(f32[1,36,2,512]{3,1,2,0:T(8,128)S(1)} %collective-permute-done.1, f32[1,36,32,512]{3,1,2,0:T(8,128)S(1)} %copy_multiply_fusion, f32[1,36,2,512]{3,1,2,0:T(8,128)S(1)} %collective-permute-done, f32[36]{0:T(128)S(1)} %get-tuple-element.28, f32[36]{0:T(128)S(1)} %get-tuple-element.29, ...), kind=kLoop, calls=%fused_computation.31 | loop fusion | flops 10948608 | bytes 5087700 | tf_op jit(solution)/shard_map/mul | solution.py:62
  14.0 0.1 copy-done.2
  14.0 1.7 %fusion.26 = f32[1,36,32,512]{3,1,2,0:T(8,128)S(1)} fusion(f32[1,36,33,512]{3,1,2,0:T(8,128)S(1)} %fusion.14, f32[32,512]{1,0:T(8,128)S(1)} %convert_element_type.84, f32[1,36,32,512]{3,2,1,0:T(8,128)S(1)} %copy-done.2), kind=kLoop, calls=%fused_computation.51 | loop fusion | flops 2359296 | bytes 9502720 | tf_op jit(solution)/shard_map/mul | solution.py:166
  15.8 2.8 %fusion.7 = f32[1,36,32,513]{3,1,2,0:T(8,128)S(1)} fusion(f32[1,36,32,512]{3,1,2,0:T(8,128)S(1)} %fusion.26, f32[36]{0:T(128)S(1)} %get-tuple-element.25, f32[36]{0:T(128)S(1)} %get-tuple-element.26, f32[36]{0:T(128)S(1)} %get-tuple-element.27, pred[36]{0:T(512)(128)(4,1)S(1)} %get-tuple-element.31), kind=kLoop, calls=%fused_computation.19 | loop fusion | flops 8273664 | bytes 4723668 | tf_op jit(solution)/shard_map/mul | solution.py:62
  18.5 0.0 copy-start.3
  18.6 0.0 copy-start.4
  18.6 0.8 fusion.24
  19.3 0.1 fusion.47
  19.5 0.0 copy-done.3
  19.5 0.0 copy-done.4
  19.5 3.0 %fusion.22 = f32[1,37,32,512]{3,1,2,0:T(8,128)S(1)} fusion(f32[1,2,32,512]{3,1,2,0:T(2,128)S(1)} %get-tuple-element.12, f32[1,36,32,512]{3,1,2,0:T(8,128)S(1)} %fusion.24, f32[1,2,32,512]{3,1,2,0:T(2,128)S(1)} %get-tuple-element.11, f32[32,512]{1,0:T(8,128)S(1)} %copy-done.3, f32[37]{0:T(128)S(1)} %get-tuple-element.33, f32[32,512]{1,0:T(8,128)S(1)} %copy-done.4, ...), kind=kLoop, calls=%fused_computation.42 | loop fusion | flops 16973824 | bytes 5177644 | tf_op jit(solution)/shard_map/mul | solution.py:62
  22.5 2.2 %fusion.17 = f32[1,36,32,512]{3,1,0,2:T(8,128)} fusion(f32[1,36,32,512]{3,1,2,0:T(8,128)S(1)} %fusion.24, f32[1,37,32,512]{3,1,2,0:T(8,128)S(1)} %fusion.22), kind=kLoop, calls=%fused_computation.36 | loop fusion | flops 1769472 | bytes 9437184 | tf_op jit(solution)/shard_map/max | solution.py:179
  24.7 4.5 %all-to-all-start = ((f32[1,36,32,512]{3,1,0,2:T(8,128)}), f32[1,36,32,512]{3,1,0,2:T(8,128)S(1)}, u32[]{:S(2)}, u32[]{:S(2)}) async-start(f32[1,36,32,512]{3,1,0,2:T(8,128)} %fusion.17), calls=%async_computation | async-start | bytes 5242880 | tf_op jit(solution)/shard_map/all_to_all | solution.py:180
  29.2 0.0 copy-done
  29.3 0.7 dynamic-slice_multiply_fusion
  30.0 0.1 multiply_multiply_fusion
  30.1 1.9 %subtract_cosine_fusion = f32[36,8,512]{2,1,0:T(8,128)S(1)} fusion(f32[8,512]{1,0:T(8,128)S(1)} %constant_dynamic-slice_fusion.1, f32[36]{0:T(128)S(1)} %add_multiply_fusion), kind=kLoop, calls=%fused_computation.68 | loop fusion | flops 147456 | bytes 606352 | tf_op jit(solution)/shard_map/cos | solution.py:208
  32.0 30.1 %all-to-all-done = f32[1,36,32,512]{3,1,0,2:T(8,128)S(1)} async-done(((f32[1,36,32,512]{3,1,0,2:T(8,128)}), f32[1,36,32,512]{3,1,0,2:T(8,128)S(1)}, u32[]{:S(2)}, u32[]{:S(2)}) %all-to-all-start) | async-done | bytes 2359328 | tf_op jit(solution)/shard_map/all_to_all | solution.py:180
  62.1 0.0 copy-start.1
  62.1 1.4 copy.22
  63.5 1.6 %slice_bitcast_fusion.1 = (f32[2,36,8,512]{3,2,1,0:T(8,128)}, f32[2,36,8,512]{3,2,1,0:T(8,128)}) fusion(f32[4,1,36,8,512]{4,3,2,0,1:T(8,128)S(1)} %bitcast.51), kind=kLoop, calls=%fused_computation.67 | loop fusion | bytes 4718592 | tf_op jit(solution)/shard_map/slice | solution.py:183
  65.1 0.0 copy-done.1
  65.1 4.9 %collective-permute-start.2 = (f32[2,36,8,512]{3,2,1,0:T(8,128)}, f32[2,36,8,512]{3,2,1,0:T(8,128)}, u32[]{:S(2)}, u32[]{:S(2)}) collective-permute-start(f32[2,36,8,512]{3,2,1,0:T(8,128)} %get-tuple-element.15), channel_id=1, source_target_pairs={{0,4},{4,8},{8,12},{12,16},{16,20},{20,24},{24,28},{1,5},{5,9},{9,... | collective-permute-start | bytes 3538952 | tf_op jit(solution)/shard_map/ppermute | solution.py:183
  70.0 1.3 collective-permute-start.3
  71.2 3.2 %multiply_reduce_fusion = (f32[8,512]{1,0:T(8,128)S(1)}, f32[8,512]{1,0:T(8,128)S(1)}, f32[8,512]{1,0:T(8,128)S(1)}, f32[4,36,8,512]{3,2,1,0:T(8,128)S(1)}) fusion(f32[4]{0:T(128)S(1)} %get-tuple-element.23, f32[4]{0:T(128)S(1)} %get-tuple-element.22, f32[4]{0:T(128)S(1)} %get-tuple-element.24, f32[1,36,4,8,512]{4,1,3,2,0:T(8,128)} %bitcast.50), kind=kLoop, calls=%fused_computation.65 | loop fusion | flops 3526656 | bytes 4767792 | tf_op jit(solution)/shard_map/reduce_sum | solution.py:190
  74.4 47.5 %all-gather = f32[24,8,512]{2,1,0:T(8,128)S(1)} all-gather(f32[3,8,512]{2,1,0:T(8,128)S(1)} %pad_maximum_fusion.9), channel_id=2, replica_groups=mesh['geo'=8,'z'=8,'y'=4] {'z'}, dimensions={0}, use_global_device_ids=true | all-gather | bytes 442368 | tf_op jit(solution)/shard_map/all_gather | solution.py:195
  122.0 0.1 fusion.34
  122.0 0.0 collective-permute-done.3
  122.1 1.6 %fusion.2 = f32[6,35,8,512]{3,2,1,0:T(8,128)S(1)} fusion(f32[4,36,8,512]{3,2,1,0:T(8,128)S(1)} %get-tuple-element.10, f32[2,36,8,512]{3,2,1,0:T(8,128)} %collective-permute-done.3), kind=kLoop, calls=%fused_computation.14 | loop fusion | flops 860160 | bytes 6979584 | tf_op jit(solution)/shard_map/concatenate | solution.py:198
  123.7 0.0 collective-permute-done.2
  123.7 2.6 %multiply_subtract_fusion = f32[6,36,8,512]{3,2,1,0:T(8,128)S(1)} fusion(f32[2,36,8,512]{3,2,1,0:T(8,128)} %collective-permute-done.3, f32[4,36,8,512]{3,2,1,0:T(8,128)S(1)} %get-tuple-element.10, f32[6,35,8,512]{3,2,1,0:T(8,128)S(1)} %fusion.2, f32[2,36,8,512]{3,2,1,0:T(8,128)} %collective-permute-done.2), kind=kLoop, calls=%fused_computation.13 | loop fusion | flops 12386304 | bytes 11698176 | tf_op jit(solution)/shard_map/sub | solution.py:200
  126.3 0.2 slice.213
  126.5 0.2 slice.212
  126.8 1.4 fusion.31
  128.2 26.2 %all_to_all.36 = f32[4,36,8,512]{3,2,1,0:T(8,128)S(1)} all-to-all(f32[4,36,8,512]{3,2,1,0:T(8,128)S(1)} %fusion.31), channel_id=1, replica_groups=mesh['geo'=8,'z'=8,'y'=4] {'y'}, dimensions={0} | all-to-all | bytes 4718592 | tf_op jit(solution)/shard_map/all_to_all | solution.py:222
  154.4 1.7 %copy.21 = f32[4,36,8,512]{3,2,0,1:T(8,128)} copy(f32[4,36,8,512]{3,2,1,0:T(8,128)S(1)} %all_to_all.36) | data formatting | bytes 4718592 | tf_op jit(solution)/shard_map/all_to_all | solution.py:222
  (16 shorter events, 0.4 us)
Async XLA Ops:
  0.0 29.2 %copy-start = (f32[32,512]{1,0:T(8,128)S(1)}, f32[32,512]{1,0:T(8,128)}, u32[]{:S(2)}) copy-start(f32[32,512]{1,0:T(8,128)} %param.11) | copy-start | bytes 196612
  4.0 6.6 %collective-permute-start = (f32[1,36,2,512]{3,1,2,0:T(8,128)S(1)}, f32[1,36,2,512]{3,1,2,0:T(8,128)S(1)}, u32[]{:S(2)}, u32[]{:S(2)}) collective-permute-start(f32[1,36,2,512]{3,1,2,0:T(8,128)S(1)} %get-tuple-element.13), channel_id=1, source_target_pairs={{0,32},{32,64},{64,96},{96,128},{128,160},{160,192},{192,224},{1,3... | collective-permute-start | bytes 442376 | tf_op jit(solution)/shard_map/ppermute | solution.py:30
  5.9 6.5 %collective-permute-start.1 = (f32[1,36,2,512]{3,1,2,0:T(8,128)S(1)}, f32[1,36,2,512]{3,1,2,0:T(8,128)S(1)}, u32[]{:S(2)}, u32[]{:S(2)}) collective-permute-start(f32[1,36,2,512]{3,1,2,0:T(8,128)S(1)} %get-tuple-element.14), channel_id=1, source_target_pairs={{32,0},{64,32},{96,64},{128,96},{160,128},{192,160},{224,192},{33,... | collective-permute-start | bytes 442376 | tf_op jit(solution)/shard_map/ppermute | solution.py:32
  12.4 1.7 %copy-start.2 = (f32[1,36,32,512]{3,2,1,0:T(8,128)S(1)}, f32[1,36,32,512]{3,2,1,0:T(8,128)}, u32[]{:S(2)}) copy-start(f32[1,36,32,512]{3,2,1,0:T(8,128)} %param.8) | copy-start | bytes 7077892
  18.5 0.9 copy-start.3
  18.6 0.9 copy-start.4
  24.7 37.4 %all-to-all-start = ((f32[1,36,32,512]{3,1,0,2:T(8,128)}), f32[1,36,32,512]{3,1,0,2:T(8,128)S(1)}, u32[]{:S(2)}, u32[]{:S(2)}) async-start(f32[1,36,32,512]{3,1,0,2:T(8,128)} %fusion.17), calls=%async_computation | async-start | bytes 5242880 | tf_op jit(solution)/shard_map/all_to_all | solution.py:180
  62.1 3.0 %copy-start.1 = (f32[1,36,32,512]{3,1,0,2:T(8,128)}, f32[1,36,32,512]{3,1,0,2:T(8,128)S(1)}, u32[]{:S(2)}) copy-start(f32[1,36,32,512]{3,1,0,2:T(8,128)S(1)} %all-to-all-done) | copy-start | bytes 7077892
  65.1 58.6 %collective-permute-start.2 = (f32[2,36,8,512]{3,2,1,0:T(8,128)}, f32[2,36,8,512]{3,2,1,0:T(8,128)}, u32[]{:S(2)}, u32[]{:S(2)}) collective-permute-start(f32[2,36,8,512]{3,2,1,0:T(8,128)} %get-tuple-element.15), channel_id=1, source_target_pairs={{0,4},{4,8},{8,12},{12,16},{16,20},{20,24},{24,28},{1,5},{5,9},{9,... | collective-permute-start | bytes 3538952 | tf_op jit(solution)/shard_map/ppermute | solution.py:183
  70.0 52.1 %collective-permute-start.3 = (f32[2,36,8,512]{3,2,1,0:T(8,128)}, f32[2,36,8,512]{3,2,1,0:T(8,128)}, u32[]{:S(2)}, u32[]{:S(2)}) collective-permute-start(f32[2,36,8,512]{3,2,1,0:T(8,128)} %get-tuple-element.16), channel_id=1, source_target_pairs={{4,0},{8,4},{12,8},{16,12},{20,16},{24,20},{28,24},{5,1},{9,5},{13... | collective-permute-start | bytes 3538952 | tf_op jit(solution)/shard_map/ppermute | solution.py:184

commit v3 on v2

--- a/solution.py
+++ b/solution.py
@@ -192,7 +192,10 @@
             jnp.sum(scaled / jnp.sqrt(wavenum)[:, None, None, None], axis=(0, 1)),
         ]
     )
-    sums = jnp.sum(lax.all_gather(sums, "z"), axis=0)
+    step = 1
+    while step < z_count:
+        sums = sums + lax.ppermute(sums, "z", [(i, i ^ step) for i in range(z_count)])
+        step *= 2
     energy_sum, first_sum, root_sum = sums[0], sums[1], sums[2]
     energy = energy_sum + EPSILON
     ext = jnp.concatenate([lower, point, upper], axis=0)

time: 157 us -> 145 us (0.924)
  blocking collectives: 73.7 us -> 30.4 us
  waiting for transfers between devices: 32.6 us -> 58.4 us
  starting transfers between devices: 16.2 us -> 27.1 us
  other arithmetic: 28 us -> 23.9 us
    all_gather x1 -> x0, blocking collectives: 47.5 us -> none  [shards(): sums = jnp.sum(lax.all_gather(sums, 'z'), axis=0)]
    ppermute x0 -> x3, waiting for transfers between devices: none -> 25.8 us  [shards(): lax.ppermute(sums, 'z', [(i, i ^ step) for i in range(z_count)])]
    ppermute x0 -> x3, starting transfers between devices: none -> 11.2 us  [shards(): lax.ppermute(sums, 'z', [(i, i ^ step) for i in range(z_count)])]
    all_to_all x1, blocking collectives: 26.2 us -> 30.4 us  [shards(): return lax.all_to_all(updated, 'y', split_axis=0, concat_axis=2, tiled=True)]
    reduce_sum x1, other arithmetic: 3.15 us -> 1.41 us  [shards(): jnp.sum(scaled, axis=(0, 1))]
  transfers between devices with their start and end apart: 5 -> 8, of which waited for: 3 -> 5; matrix products, arithmetic and copies ran while one was open for 5% -> 3% of each run, Pallas kernels for 0% -> 0%
where the time goes in v3:
time: 145 us; the launch traced here: 144 us
  waiting for transfers between devices  58.4 us (40%)
  blocking collectives  30.4 us (21%)
  starting transfers between devices  27.1 us (19%)
  other arithmetic  23.9 us (16%)
  local copies, waits for them, and re-layouts  3.91 us (3%)
    all_to_all x1, blocking collectives, shards(): return lax.all_to_all(updated, 'y', split_axis=0, concat_axis=2, tiled=True)  30.4 us
    all_to_all x1, waiting for transfers between devices, shards(): lax.all_to_all(floored, 'y', split_axis=2, concat_axis=0, tiled=True)  30.1 us
    ppermute x3, waiting for transfers between devices, shards(): lax.ppermute(sums, 'z', [(i, i ^ step) for i in range(z_count)])  25.8 us
    ppermute x3, starting transfers between devices, shards(): lax.ppermute(sums, 'z', [(i, i ^ step) for i in range(z_count)])  11.2 us
    mul x3, other arithmetic, quick_flux(): return courant * face_value  7.44 us
    ppermute x1, starting transfers between devices, shards(): lax.ppermute(point[group - 2:], 'z', [(i, i + 1) for i in range(z_count -...  4.62 us
    all_to_all x1, starting transfers between devices, shards(): lax.all_to_all(floored, 'y', split_axis=2, concat_axis=0, tiled=True)  4.46 us
    ppermute x1, starting transfers between devices, extended(): lax.ppermute(head, axis, [((i + 1) % count, i) for i in range(ends)])  3.64 us
  transfers between devices with their start and end apart: 8, of which 5 were waited for; matrix products, arithmetic and copies ran while one was open for 3% of the time, Pallas kernels for 0%

profile of v3, /device:TPU:2, one launch (start us, length us, event | category | flops | bytes accessed | tf_op | source)
XLA Modules:
  0.0 144.1 jit_solution(14841275391848862202)
XLA Ops:
  0.0 0.8 convert_element_type.84
  0.8 3.0 %copy_multiply_fusion = f32[1,36,32,512]{3,1,2,0:T(8,128)S(1)} fusion(f32[1,36,32,512]{3,2,1,0:T(8,128)} %param.8, f32[32,512]{1,0:T(8,128)S(1)} %convert_element_type.84), kind=kLoop, calls=%fused_computation.52 | loop fusion | flops 589824 | bytes 4784128 | tf_op jit(solution)/shard_map/mul | solution.py:163
  3.9 1.9 %collective-permute-start = (f32[1,36,2,512]{3,1,2,0:T(8,128)S(1)}, f32[1,36,2,512]{3,1,2,0:T(8,128)S(1)}, u32[]{:S(2)}, u32[]{:S(2)}) collective-permute-start(f32[1,36,2,512]{3,1,2,0:T(8,128)S(1)} %get-tuple-element.13), channel_id=1, source_target_pairs={{0,32},{32,64},{64,96},{96,128},{128,160},{160,192},{192,224},{1,3... | collective-permute-start | bytes 442376 | tf_op jit(solution)/shard_map/ppermute | solution.py:30
  5.9 3.6 %collective-permute-start.1 = (f32[1,36,2,512]{3,1,2,0:T(8,128)S(1)}, f32[1,36,2,512]{3,1,2,0:T(8,128)S(1)}, u32[]{:S(2)}, u32[]{:S(2)}) collective-permute-start(f32[1,36,2,512]{3,1,2,0:T(8,128)S(1)} %get-tuple-element.14), channel_id=1, source_target_pairs={{32,0},{64,32},{96,64},{128,96},{160,128},{192,160},{224,192},{33,... | collective-permute-start | bytes 442376 | tf_op jit(solution)/shard_map/ppermute | solution.py:32
  9.8 0.8 collective-permute-done
  10.6 1.8 %collective-permute-done.1 = f32[1,36,2,512]{3,1,2,0:T(8,128)S(1)} collective-permute-done((f32[1,36,2,512]{3,1,2,0:T(8,128)S(1)}, f32[1,36,2,512]{3,1,2,0:T(8,128)S(1)}, u32[]{:S(2)}, u32[]{:S(2)}) %collective-permute-start.1) | collective-permute-done | bytes 147488 | tf_op jit(solution)/shard_map/ppermute | solution.py:32
  12.3 0.0 copy-start
  12.3 1.6 %fusion.14 = f32[1,36,33,512]{3,1,2,0:T(8,128)S(1)} fusion(f32[1,36,2,512]{3,1,2,0:T(8,128)S(1)} %collective-permute-done.1, f32[1,36,32,512]{3,1,2,0:T(8,128)S(1)} %copy_multiply_fusion, f32[1,36,2,512]{3,1,2,0:T(8,128)S(1)} %collective-permute-done, f32[36]{0:T(128)S(1)} %get-tuple-element.26, f32[36]{0:T(128)S(1)} %get-tuple-element.27, ...), kind=kLoop, calls=%fused_computation.31 | loop fusion | flops 10948608 | bytes 5087700 | tf_op jit(solution)/shard_map/mul | solution.py:62
  13.9 0.1 copy-done
  14.0 1.7 %fusion.26 = f32[1,36,32,512]{3,1,2,0:T(8,128)S(1)} fusion(f32[1,36,33,512]{3,1,2,0:T(8,128)S(1)} %fusion.14, f32[32,512]{1,0:T(8,128)S(1)} %convert_element_type.84, f32[1,36,32,512]{3,2,1,0:T(8,128)S(1)} %copy-done), kind=kLoop, calls=%fused_computation.51 | loop fusion | flops 2359296 | bytes 9502720 | tf_op jit(solution)/shard_map/mul | solution.py:166
  15.7 2.8 %fusion.7 = f32[1,36,32,513]{3,1,2,0:T(8,128)S(1)} fusion(f32[1,36,32,512]{3,1,2,0:T(8,128)S(1)} %fusion.26, f32[36]{0:T(128)S(1)} %get-tuple-element.23, f32[36]{0:T(128)S(1)} %get-tuple-element.24, f32[36]{0:T(128)S(1)} %get-tuple-element.25, pred[36]{0:T(512)(128)(4,1)S(1)} %get-tuple-element.29), kind=kLoop, calls=%fused_computation.19 | loop fusion | flops 8273664 | bytes 4723668 | tf_op jit(solution)/shard_map/mul | solution.py:62
  18.5 0.0 copy-start.1
  18.5 0.0 copy-start.2
  18.5 0.8 fusion.24
  19.3 0.1 fusion.48
  19.4 0.0 copy-done.1
  19.4 0.0 copy-done.2
  19.4 3.0 %fusion.22 = f32[1,37,32,512]{3,1,2,0:T(8,128)S(1)} fusion(f32[1,2,32,512]{3,1,2,0:T(2,128)S(1)} %get-tuple-element.12, f32[1,36,32,512]{3,1,2,0:T(8,128)S(1)} %fusion.24, f32[1,2,32,512]{3,1,2,0:T(2,128)S(1)} %get-tuple-element.11, f32[32,512]{1,0:T(8,128)S(1)} %copy-done.1, f32[37]{0:T(128)S(1)} %get-tuple-element.31, f32[32,512]{1,0:T(8,128)S(1)} %copy-done.2, ...), kind=kLoop, calls=%fused_computation.42 | loop fusion | flops 16973824 | bytes 5177644 | tf_op jit(solution)/shard_map/mul | solution.py:62
  22.5 2.2 %fusion.17 = f32[1,36,32,512]{3,1,0,2:T(8,128)} fusion(f32[1,36,32,512]{3,1,2,0:T(8,128)S(1)} %fusion.24, f32[1,37,32,512]{3,1,2,0:T(8,128)S(1)} %fusion.22), kind=kLoop, calls=%fused_computation.36 | loop fusion | flops 1769472 | bytes 9437184 | tf_op jit(solution)/shard_map/max | solution.py:179
  24.7 4.5 %all-to-all-start = ((f32[1,36,32,512]{3,1,0,2:T(8,128)}), f32[1,36,32,512]{3,1,0,2:T(8,128)S(1)}, u32[]{:S(2)}, u32[]{:S(2)}) async-start(f32[1,36,32,512]{3,1,0,2:T(8,128)} %fusion.17), calls=%async_computation | async-start | bytes 5242880 | tf_op jit(solution)/shard_map/all_to_all | solution.py:180
  29.2 0.7 dynamic-slice_multiply_fusion
  29.9 0.1 multiply_multiply_fusion
  30.0 1.9 %subtract_cosine_fusion = f32[36,8,512]{2,1,0:T(8,128)S(1)} fusion(f32[8,512]{1,0:T(8,128)S(1)} %get-tuple-element.34, f32[36]{0:T(128)S(1)} %add_multiply_fusion), kind=kLoop, calls=%fused_computation.68 | loop fusion | flops 147456 | bytes 606352 | tf_op jit(solution)/shard_map/cos | solution.py:211
  32.0 30.1 %all-to-all-done = f32[1,36,32,512]{3,1,0,2:T(8,128)S(1)} async-done(((f32[1,36,32,512]{3,1,0,2:T(8,128)}), f32[1,36,32,512]{3,1,0,2:T(8,128)S(1)}, u32[]{:S(2)}, u32[]{:S(2)}) %all-to-all-start) | async-done | bytes 2359328 | tf_op jit(solution)/shard_map/all_to_all | solution.py:180
  62.0 1.4 copy.22
  63.4 0.2 slice_bitcast_fusion.1
  63.6 1.4 multiply_reduce_fusion
  65.1 2.0 %collective-permute-start.2 = (f32[3,8,512]{2,1,0:T(8,128)S(1)}, f32[3,8,512]{2,1,0:T(8,128)S(1)}, u32[]{:S(2)}, u32[]{:S(2)}) collective-permute-start(f32[3,8,512]{2,1,0:T(8,128)S(1)} %pad_maximum_fusion.9), channel_id=1, source_target_pairs={{0,4},{4,0},{8,12},{12,8},{16,20},{20,16},{24,28},{28,24},{1,5},{5... | collective-permute-start | bytes 147464 | tf_op jit(solution)/shard_map/ppermute | solution.py:197
  67.1 1.3 collective-permute-start.6
  68.4 4.6 %collective-permute-start.5 = (f32[2,36,8,512]{3,2,1,0:T(8,128)S(1)}, f32[2,36,8,512]{3,2,1,0:T(8,128)S(1)}, u32[]{:S(2)}, u32[]{:S(2)}) collective-permute-start(f32[2,36,8,512]{3,2,1,0:T(8,128)S(1)} %get-tuple-element.15), channel_id=1, source_target_pairs={{0,4},{4,8},{8,12},{12,16},{16,20},{20,24},{24,28},{1,5},{5,9},{9,... | collective-permute-start | bytes 3538952 | tf_op jit(solution)/shard_map/ppermute | solution.py:183
  73.0 0.0 collective-permute-done.2
  73.0 3.3 %collective-permute-start.3 = (f32[3,8,512]{2,1,0:T(8,128)S(1)}, f32[3,8,512]{2,1,0:T(8,128)S(1)}, u32[]{:S(2)}, u32[]{:S(2)}) collective-permute-start(f32[3,8,512]{2,1,0:T(8,128)S(1)} %fusion.46), channel_id=1, source_target_pairs={{0,8},{4,12},{8,0},{12,4},{16,24},{20,28},{24,16},{28,20},{1,9},{5... | collective-permute-start | bytes 147464 | tf_op jit(solution)/shard_map/ppermute | solution.py:197
  76.3 23.6 %collective-permute-done.3 = f32[3,8,512]{2,1,0:T(8,128)S(1)} collective-permute-done((f32[3,8,512]{2,1,0:T(8,128)S(1)}, f32[3,8,512]{2,1,0:T(8,128)S(1)}, u32[]{:S(2)}, u32[]{:S(2)}) %collective-permute-start.3) | collective-permute-done | bytes 49184 | tf_op jit(solution)/shard_map/ppermute | solution.py:197
  99.9 5.9 %collective-permute-start.4 = (f32[3,8,512]{2,1,0:T(8,128)S(1)}, f32[3,8,512]{2,1,0:T(8,128)S(1)}, u32[]{:S(2)}, u32[]{:S(2)}) collective-permute-start(f32[3,8,512]{2,1,0:T(8,128)S(1)} %fusion.50), channel_id=1, source_target_pairs={{0,16},{4,20},{8,24},{12,28},{16,0},{20,4},{24,8},{28,12},{1,17},{... | collective-permute-start | bytes 147464 | tf_op jit(solution)/shard_map/ppermute | solution.py:197
  105.8 2.2 %collective-permute-done.4 = f32[3,8,512]{2,1,0:T(8,128)S(1)} collective-permute-done((f32[3,8,512]{2,1,0:T(8,128)S(1)}, f32[3,8,512]{2,1,0:T(8,128)S(1)}, u32[]{:S(2)}, u32[]{:S(2)}) %collective-permute-start.4) | collective-permute-done | bytes 49184 | tf_op jit(solution)/shard_map/ppermute | solution.py:197
  108.1 0.1 fusion.34
  108.2 0.0 collective-permute-done.6
  108.2 0.5 fusion.2
  108.7 0.0 collective-permute-done.5
  108.7 1.4 multiply_subtract_fusion
  110.2 0.2 slice.213
  110.4 0.2 slice.212
  110.6 1.4 fusion.31
  112.1 30.4 %all_to_all.36 = f32[4,36,8,512]{3,2,1,0:T(8,128)S(1)} all-to-all(f32[4,36,8,512]{3,2,1,0:T(8,128)S(1)} %fusion.31), channel_id=1, replica_groups=mesh['geo'=8,'z'=8,'y'=4] {'y'}, dimensions={0} | all-to-all | bytes 4718592 | tf_op jit(solution)/shard_map/all_to_all | solution.py:225
  142.4 1.7 %copy.21 = f32[4,36,8,512]{3,2,0,1:T(8,128)} copy(f32[4,36,8,512]{3,2,1,0:T(8,128)S(1)} %all_to_all.36) | data formatting | bytes 4718592 | tf_op jit(solution)/shard_map/all_to_all | solution.py:225
  (19 shorter events, 0.4 us)
Async XLA Ops:
  3.9 6.6 %collective-permute-start = (f32[1,36,2,512]{3,1,2,0:T(8,128)S(1)}, f32[1,36,2,512]{3,1,2,0:T(8,128)S(1)}, u32[]{:S(2)}, u32[]{:S(2)}) collective-permute-start(f32[1,36,2,512]{3,1,2,0:T(8,128)S(1)} %get-tuple-element.13), channel_id=1, source_target_pairs={{0,32},{32,64},{64,96},{96,128},{128,160},{160,192},{192,224},{1,3... | collective-permute-start | bytes 442376 | tf_op jit(solution)/shard_map/ppermute | solution.py:30
  5.9 6.5 %collective-permute-start.1 = (f32[1,36,2,512]{3,1,2,0:T(8,128)S(1)}, f32[1,36,2,512]{3,1,2,0:T(8,128)S(1)}, u32[]{:S(2)}, u32[]{:S(2)}) collective-permute-start(f32[1,36,2,512]{3,1,2,0:T(8,128)S(1)} %get-tuple-element.14), channel_id=1, source_target_pairs={{32,0},{64,32},{96,64},{128,96},{160,128},{192,160},{224,192},{33,... | collective-permute-start | bytes 442376 | tf_op jit(solution)/shard_map/ppermute | solution.py:32
  12.3 1.7 %copy-start = (f32[1,36,32,512]{3,2,1,0:T(8,128)S(1)}, f32[1,36,32,512]{3,2,1,0:T(8,128)}, u32[]{:S(2)}) copy-start(f32[1,36,32,512]{3,2,1,0:T(8,128)} %param.8) | copy-start | bytes 7077892
  18.5 0.9 copy-start.1
  18.5 0.9 copy-start.2
  24.7 37.4 %all-to-all-start = ((f32[1,36,32,512]{3,1,0,2:T(8,128)}), f32[1,36,32,512]{3,1,0,2:T(8,128)S(1)}, u32[]{:S(2)}, u32[]{:S(2)}) async-start(f32[1,36,32,512]{3,1,0,2:T(8,128)} %fusion.17), calls=%async_computation | async-start | bytes 5242880 | tf_op jit(solution)/shard_map/all_to_all | solution.py:180
  65.1 7.9 %collective-permute-start.2 = (f32[3,8,512]{2,1,0:T(8,128)S(1)}, f32[3,8,512]{2,1,0:T(8,128)S(1)}, u32[]{:S(2)}, u32[]{:S(2)}) collective-permute-start(f32[3,8,512]{2,1,0:T(8,128)S(1)} %pad_maximum_fusion.9), channel_id=1, source_target_pairs={{0,4},{4,0},{8,12},{12,8},{16,20},{20,16},{24,28},{28,24},{1,5},{5... | collective-permute-start | bytes 147464 | tf_op jit(solution)/shard_map/ppermute | solution.py:197
  67.1 41.1 %collective-permute-start.6 = (f32[2,36,8,512]{3,2,1,0:T(8,128)S(1)}, f32[2,36,8,512]{3,2,1,0:T(8,128)S(1)}, u32[]{:S(2)}, u32[]{:S(2)}) collective-permute-start(f32[2,36,8,512]{3,2,1,0:T(8,128)S(1)} %get-tuple-element.16), channel_id=1, source_target_pairs={{4,0},{8,4},{12,8},{16,12},{20,16},{24,20},{28,24},{5,1},{9,5},{13... | collective-permute-start | bytes 3538952 | tf_op jit(solution)/shard_map/ppermute | solution.py:184
  68.4 40.3 %collective-permute-start.5 = (f32[2,36,8,512]{3,2,1,0:T(8,128)S(1)}, f32[2,36,8,512]{3,2,1,0:T(8,128)S(1)}, u32[]{:S(2)}, u32[]{:S(2)}) collective-permute-start(f32[2,36,8,512]{3,2,1,0:T(8,128)S(1)} %get-tuple-element.15), channel_id=1, source_target_pairs={{0,4},{4,8},{8,12},{12,16},{16,20},{20,24},{24,28},{1,5},{5,9},{9,... | collective-permute-start | bytes 3538952 | tf_op jit(solution)/shard_map/ppermute | solution.py:183
  73.0 26.9 %collective-permute-start.3 = (f32[3,8,512]{2,1,0:T(8,128)S(1)}, f32[3,8,512]{2,1,0:T(8,128)S(1)}, u32[]{:S(2)}, u32[]{:S(2)}) collective-permute-start(f32[3,8,512]{2,1,0:T(8,128)S(1)} %fusion.46), channel_id=1, source_target_pairs={{0,8},{4,12},{8,0},{12,4},{16,24},{20,28},{24,16},{28,20},{1,9},{5... | collective-permute-start | bytes 147464 | tf_op jit(solution)/shard_map/ppermute | solution.py:197
  99.9 8.1 %collective-permute-start.4 = (f32[3,8,512]{2,1,0:T(8,128)S(1)}, f32[3,8,512]{2,1,0:T(8,128)S(1)}, u32[]{:S(2)}, u32[]{:S(2)}) collective-permute-start(f32[3,8,512]{2,1,0:T(8,128)S(1)} %fusion.50), channel_id=1, source_target_pairs={{0,16},{4,20},{8,24},{12,28},{16,0},{20,4},{24,8},{28,12},{1,17},{... | collective-permute-start | bytes 147464 | tf_op jit(solution)/shard_map/ppermute | solution.py:197

commit v4 on v3

--- a/solution.py
+++ b/solution.py
@@ -145,6 +145,7 @@
 
 
 Y_GROUP = 4
+COLUMN_CHUNKS = 2
 
 
 def shards(spectrum, land_sea, sea_index, sea_count, wind_speed, wind_dir, slope_x, slope_y):
@@ -177,6 +178,27 @@
     )
     padded = jnp.concatenate([density[:, -2:], density, density[:, :2]], axis=1)
     floored = jnp.maximum(advect(padded, turning, 1), 0.0)
+    chunk_width = col_count // COLUMN_CHUNKS
+    pieces = []
+    for chunk in range(COLUMN_CHUNKS):
+        columns = slice(chunk * chunk_width, (chunk + 1) * chunk_width)
+        pieces.append(
+            source_chunk(
+                floored[..., columns],
+                wind_speed[:, columns],
+                wind_dir[:, columns],
+                wet_mask[:, columns],
+                angles,
+                dtheta,
+            )
+        )
+    return jnp.concatenate(pieces, axis=3)
+
+
+def source_chunk(floored, wind_speed, wind_dir, wet_mask, angles, dtheta):
+    z_count = lax.axis_size("z")
+    z_pos = lax.axis_index("z")
+    y_pos = lax.axis_index("y")
     point = lax.all_to_all(floored, "y", split_axis=2, concat_axis=0, tiled=True)
     group = point.shape[0]
     part_rows = point.shape[2]

time: 145 us -> 152 us (1.048)
  the two profiles are of different devices: /device:TPU:2 before, /device:TPU:32 now
where the time goes in v4:
time: 152 us; the launch traced here: 151 us
  waiting for transfers between devices  69.7 us (46%)
  starting transfers between devices  46.7 us (31%)
  other arithmetic  25.2 us (17%)
  local copies, waits for them, and re-layouts  8.89 us (6%)
    all_to_all x2, waiting for transfers between devices, source_chunk(): return lax.all_to_all(updated, 'y', split_axis=0, concat_axis=2, tiled=True)  26.6 us
    all_to_all x2, waiting for transfers between devices, source_chunk(): lax.all_to_all(floored, 'y', split_axis=2, concat_axis=0, tiled=True)  23.2 us
    ppermute x2, waiting for transfers between devices, source_chunk(): lax.ppermute(point[:2], 'z', [(i + 1, i) for i in range(z_count - 1)])  15 us
    ppermute x6, starting transfers between devices, source_chunk(): lax.ppermute(sums, 'z', [(i, i ^ step) for i in range(z_count)])  12.9 us
    all_to_all x2, starting transfers between devices, source_chunk(): lax.all_to_all(floored, 'y', split_axis=2, concat_axis=0, tiled=True)  8.89 us
    all_to_all x2, starting transfers between devices, source_chunk(): return lax.all_to_all(updated, 'y', split_axis=0, concat_axis=2, tiled=True)  8.56 us
    ppermute x2, starting transfers between devices, source_chunk(): lax.ppermute(point[group - 2:], 'z', [(i, i + 1) for i in range(z_count -...  8.32 us
    mul x3, other arithmetic, quick_flux(): return courant * face_value  7.44 us
  transfers between devices with their start and end apart: 16, of which 8 were waited for; matrix products, arithmetic and copies ran while one was open for 10% of the time, Pallas kernels for 0%

profile of v4, /device:TPU:32, one launch (start us, length us, event | category | flops | bytes accessed | tf_op | source)
XLA Modules:
  0.0 150.9 jit_solution(12413567954914049698)
XLA Ops:
  0.0 0.8 convert_element_type.86
  0.8 3.0 %copy_multiply_fusion = f32[1,36,32,512]{3,1,2,0:T(8,128)S(1)} fusion(f32[1,36,32,512]{3,2,1,0:T(8,128)} %param.8, f32[32,512]{1,0:T(8,128)S(1)} %convert_element_type.86), kind=kLoop, calls=%fused_computation.40 | loop fusion | flops 589824 | bytes 4784128 | tf_op jit(solution)/shard_map/mul | solution.py:164
  3.9 1.7 %collective-permute-start = (f32[1,36,2,512]{3,1,2,0:T(8,128)S(1)}, f32[1,36,2,512]{3,1,2,0:T(8,128)S(1)}, u32[]{:S(2)}, u32[]{:S(2)}) collective-permute-start(f32[1,36,2,512]{3,1,2,0:T(8,128)S(1)} %get-tuple-element.24), channel_id=1, source_target_pairs={{0,32},{32,64},{64,96},{96,128},{128,160},{160,192},{192,224},{1,3... | collective-permute-start | bytes 442376 | tf_op jit(solution)/shard_map/ppermute | solution.py:30
  5.7 1.3 collective-permute-start.1
  7.4 2.9 %collective-permute-done.1 = f32[1,36,2,512]{3,1,2,0:T(8,128)S(1)} collective-permute-done((f32[1,36,2,512]{3,1,2,0:T(8,128)S(1)}, f32[1,36,2,512]{3,1,2,0:T(8,128)S(1)}, u32[]{:S(2)}, u32[]{:S(2)}) %collective-permute-start.1) | collective-permute-done | bytes 147488 | tf_op jit(solution)/shard_map/ppermute | solution.py:32
  10.2 1.6 %fusion.11 = f32[1,36,33,512]{3,1,2,0:T(8,128)S(1)} fusion(f32[1,36,2,512]{3,1,2,0:T(8,128)S(1)} %collective-permute-done.1, f32[1,36,32,512]{3,1,2,0:T(8,128)S(1)} %copy_multiply_fusion, f32[1,36,2,512]{3,1,2,0:T(8,128)S(1)} %collective-permute-done, f32[36]{0:T(128)S(1)} %get-tuple-element.55, f32[36]{0:T(128)S(1)} %get-tuple-element.56, ...), kind=kLoop, calls=%fused_computation.20 | loop fusion | flops 10948608 | bytes 5087700 | tf_op jit(solution)/shard_map/mul | solution.py:62
  11.9 1.7 %fusion.22 = f32[1,36,32,512]{3,1,2,0:T(8,128)S(1)} fusion(f32[1,36,33,512]{3,1,2,0:T(8,128)S(1)} %fusion.11, f32[32,512]{1,0:T(8,128)S(1)} %convert_element_type.86, f32[1,36,32,512]{3,2,1,0:T(8,128)S(1)} %copy-done), kind=kLoop, calls=%fused_computation.39 | loop fusion | flops 2359296 | bytes 9502720 | tf_op jit(solution)/shard_map/mul | solution.py:167
  13.6 2.8 %fusion.4 = f32[1,36,32,513]{3,1,2,0:T(8,128)S(1)} fusion(f32[1,36,32,512]{3,1,2,0:T(8,128)S(1)} %fusion.22, f32[36]{0:T(128)S(1)} %get-tuple-element.52, f32[36]{0:T(128)S(1)} %get-tuple-element.53, f32[36]{0:T(128)S(1)} %get-tuple-element.54, pred[36]{0:T(512)(128)(4,1)S(1)} %get-tuple-element.58), kind=kLoop, calls=%fused_computation.8 | loop fusion | flops 8273664 | bytes 4723668 | tf_op jit(solution)/shard_map/mul | solution.py:62
  16.5 0.8 fusion.20
  17.4 3.0 %fusion.18 = f32[1,37,32,512]{3,1,2,0:T(8,128)S(1)} fusion(f32[1,2,32,512]{3,1,2,0:T(2,128)S(1)} %get-tuple-element.23, f32[1,36,32,512]{3,1,2,0:T(8,128)S(1)} %fusion.20, f32[1,2,32,512]{3,1,2,0:T(2,128)S(1)} %get-tuple-element.22, f32[32,512]{1,0:T(8,128)S(1)} %copy-done.2, f32[37]{0:T(128)S(1)} %get-tuple-element.60, f32[32,512]{1,0:T(8,128)S(1)} %copy-done.3, ...), kind=kLoop, calls=%fused_computation.30 | loop fusion | flops 16973824 | bytes 5177644 | tf_op jit(solution)/shard_map/mul | solution.py:62
  20.4 0.7 fusion.13
  21.1 1.7 %slice_bitcast_fusion.1 = (f32[1,36,32,256]{3,1,0,2:T(8,128)}, f32[1,36,32,256]{3,1,0,2:T(8,128)}) fusion(f32[1,36,32,512]{3,1,2,0:T(8,128)S(1)} %fusion.13), kind=kLoop, calls=%fused_computation.66 | loop fusion | bytes 4718592 | tf_op jit(solution)/shard_map/slice | solution.py:187
  22.8 4.6 %all-to-all-start.2 = ((f32[1,36,32,256]{3,1,0,2:T(8,128)}), f32[1,36,32,256]{3,1,0,2:T(8,128)S(1)}, u32[]{:S(2)}, u32[]{:S(2)}) async-start(f32[1,36,32,256]{3,1,0,2:T(8,128)} %get-tuple-element.21), calls=%async_computation.2 | async-start | bytes 2621440 | tf_op jit(solution)/shard_map/all_to_all | solution.py:202
  27.5 16.6 %all-to-all-done.2 = f32[1,36,32,256]{3,1,0,2:T(8,128)S(1)} async-done(((f32[1,36,32,256]{3,1,0,2:T(8,128)}), f32[1,36,32,256]{3,1,0,2:T(8,128)S(1)}, u32[]{:S(2)}, u32[]{:S(2)}) %all-to-all-start.2) | async-done | bytes 1179680 | tf_op jit(solution)/shard_map/all_to_all | solution.py:202
  44.1 4.3 %all-to-all-start = ((f32[1,36,32,256]{3,1,0,2:T(8,128)}), f32[1,36,32,256]{3,1,0,2:T(8,128)}, u32[]{:S(2)}, u32[]{:S(2)}) async-start(f32[1,36,32,256]{3,1,0,2:T(8,128)} %get-tuple-element.20), calls=%async_computation | async-start | bytes 2621440 | tf_op jit(solution)/shard_map/all_to_all | solution.py:202
  48.5 2.7 %subtract_cosine_fusion.1 = (f32[36,8,256]{2,1,0:T(8,128)}, f32[36,8,256]{2,1,0:T(8,128)S(1)}) fusion(f32[8,256]{1,0:T(8,128)S(1)} %get-tuple-element.65, f32[36]{0:T(128)S(1)} %add_multiply_fusion, f32[8,256]{1,0:T(8,128)S(1)} %get-tuple-element.64), kind=kLoop, calls=%fused_computation.96 | loop fusion | flops 147456 | bytes 606352 | tf_op jit(solution)/shard_map/cos | solution.py:233
  51.2 0.4 copy.33
  51.6 1.1 slice_bitcast_fusion.3
  52.7 3.8 %collective-permute-start.10 = (f32[2,36,8,256]{3,2,0,1:T(8,128)}, f32[2,36,8,256]{3,2,0,1:T(8,128)}, u32[]{:S(2)}, u32[]{:S(2)}) collective-permute-start(f32[2,36,8,256]{3,2,0,1:T(8,128)} %get-tuple-element.28), channel_id=1, source_target_pairs={{0,4},{4,8},{8,12},{12,16},{16,20},{20,24},{24,28},{1,5},{5,9},{9,... | collective-permute-start | bytes 1769480 | tf_op jit(solution)/shard_map/ppermute | solution.py:205
  56.5 3.0 %collective-permute-start.11 = (f32[2,36,8,256]{3,2,0,1:T(8,128)}, f32[2,36,8,256]{3,2,0,1:T(8,128)S(1)}, u32[]{:S(2)}, u32[]{:S(2)}) collective-permute-start(f32[2,36,8,256]{3,2,0,1:T(8,128)} %get-tuple-element.29), channel_id=1, source_target_pairs={{4,0},{8,4},{12,8},{16,12},{20,16},{24,20},{28,24},{5,1},{9,5},{13... | collective-permute-start | bytes 1769480 | tf_op jit(solution)/shard_map/ppermute | solution.py:206
  59.5 6.7 %all-to-all-done = f32[1,36,32,256]{3,1,0,2:T(8,128)} async-done(((f32[1,36,32,256]{3,1,0,2:T(8,128)}), f32[1,36,32,256]{3,1,0,2:T(8,128)}, u32[]{:S(2)}, u32[]{:S(2)}) %all-to-all-start) | async-done | bytes 1179680 | tf_op jit(solution)/shard_map/all_to_all | solution.py:202
  66.2 2.1 %multiply_reduce_fusion = (f32[8,256]{1,0:T(8,128)S(1)}, f32[8,256]{1,0:T(8,128)S(1)}, f32[8,256]{1,0:T(8,128)S(1)}, f32[8,256]{1,0:T(8,128)S(1)}, f32[8,256]{1,...) fusion(f32[4]{0:T(128)S(1)} %get-tuple-element.50, ...), kind=kLoop, calls=%fused_computation.89 | loop fusion | flops 3526656 | bytes 4767792 | tf_op jit(solution)/shard_map/reduce_sum | solution.py:212
  68.3 0.2 collective-permute-start.2
  68.5 1.9 %collective-permute-start.7 = (f32[3,8,256]{2,1,0:T(8,128)S(1)}, f32[3,8,256]{2,1,0:T(8,128)S(1)}, u32[]{:S(2)}, u32[]{:S(2)}) collective-permute-start(f32[3,8,256]{2,1,0:T(8,128)S(1)} %pad_maximum_fusion.16), channel_id=1, source_target_pairs={{0,4},{4,0},{8,12},{12,8},{16,20},{20,16},{24,28},{28,24},{1,5},{5... | collective-permute-start | bytes 73736 | tf_op jit(solution)/shard_map/ppermute | solution.py:219
  70.4 1.7 %copy.34 = f32[1,36,32,256]{3,2,1,0:T(8,128)S(1)} copy(f32[1,36,32,256]{3,1,0,2:T(8,128)} %all-to-all-done) | data formatting | bytes 2359296 | tf_op jit(solution)/shard_map/all_to_all | solution.py:202
  72.1 0.4 collective-permute-done.2
  72.5 3.3 %collective-permute-start.3 = (f32[3,8,256]{2,1,0:T(8,128)S(1)}, f32[3,8,256]{2,1,0:T(8,128)S(1)}, u32[]{:S(2)}, u32[]{:S(2)}) collective-permute-start(f32[3,8,256]{2,1,0:T(8,128)S(1)} %fusion.65), channel_id=1, source_target_pairs={{0,8},{4,12},{8,0},{12,4},{16,24},{20,28},{24,16},{28,20},{1,9},{5... | collective-permute-start | bytes 73736 | tf_op jit(solution)/shard_map/ppermute | solution.py:219
  75.8 0.5 collective-permute-start.8
  76.3 1.6 %collective-permute-done.3 = f32[3,8,256]{2,1,0:T(8,128)S(1)} collective-permute-done((f32[3,8,256]{2,1,0:T(8,128)S(1)}, f32[3,8,256]{2,1,0:T(8,128)S(1)}, u32[]{:S(2)}, u32[]{:S(2)}) %collective-permute-start.3) | collective-permute-done | bytes 24608 | tf_op jit(solution)/shard_map/ppermute | solution.py:219
  77.9 5.5 %collective-permute-start.4 = (f32[3,8,256]{2,1,0:T(8,128)S(1)}, f32[3,8,256]{2,1,0:T(8,128)S(1)}, u32[]{:S(2)}, u32[]{:S(2)}) collective-permute-start(f32[3,8,256]{2,1,0:T(8,128)S(1)} %fusion.73), channel_id=1, source_target_pairs={{0,16},{4,20},{8,24},{12,28},{16,0},{20,4},{24,8},{28,12},{1,17},{... | collective-permute-start | bytes 73736 | tf_op jit(solution)/shard_map/ppermute | solution.py:219
  83.4 1.6 %collective-permute-start.9 = (f32[3,8,256]{2,1,0:T(8,128)S(1)}, f32[3,8,256]{2,1,0:T(8,128)S(1)}, u32[]{:S(2)}, u32[]{:S(2)}) collective-permute-start(f32[3,8,256]{2,1,0:T(8,128)S(1)} %fusion.74), channel_id=1, source_target_pairs={{0,16},{4,20},{8,24},{12,28},{16,0},{20,4},{24,8},{28,12},{1,17},{... | collective-permute-start | bytes 73736 | tf_op jit(solution)/shard_map/ppermute | solution.py:219
  85.1 4.5 %collective-permute-start.5 = (f32[2,36,8,256]{3,2,0,1:T(8,128)S(1)}, f32[2,36,8,256]{3,2,0,1:T(8,128)S(1)}, u32[]{:S(2)}, u32[]{:S(2)}) collective-permute-start(f32[2,36,8,256]{3,2,0,1:T(8,128)S(1)} %get-tuple-element.26), channel_id=1, source_target_pairs={{0,4},{4,8},{8,12},{12,16},{16,20},{20,24},{24,28},{1,5},{5,9},{9,... | collective-permute-start | bytes 1769480 | tf_op jit(solution)/shard_map/ppermute | solution.py:205
  89.6 1.9 %collective-permute-start.6 = (f32[2,36,8,256]{3,2,0,1:T(8,128)S(1)}, f32[2,36,8,256]{3,2,0,1:T(8,128)S(1)}, u32[]{:S(2)}, u32[]{:S(2)}) collective-permute-start(f32[2,36,8,256]{3,2,0,1:T(8,128)S(1)} %get-tuple-element.27), channel_id=1, source_target_pairs={{4,0},{8,4},{12,8},{16,12},{20,16},{24,20},{28,24},{5,1},{9,5},{13... | collective-permute-start | bytes 1769480 | tf_op jit(solution)/shard_map/ppermute | solution.py:206
  91.7 15.0 %collective-permute-done.6 = f32[2,36,8,256]{3,2,0,1:T(8,128)S(1)} collective-permute-done((f32[2,36,8,256]{3,2,0,1:T(8,128)S(1)}, f32[2,36,8,256]{3,2,0,1:T(8,128)S(1)}, u32[]{:S(2)}, u32[]{:S(2)}) %collective-permute-start.6) | collective-permute-done | bytes 589856 | tf_op jit(solution)/shard_map/ppermute | solution.py:206
  106.8 0.4 multiply_subtract_fusion.1
  107.5 0.8 copy-done.1
  108.2 0.6 fusion.38
  108.8 1.1 copy.14
  110.0 5.0 %all-to-all-start.1 = ((f32[4,36,8,256]{3,2,1,0:T(8,128)}), f32[4,36,8,256]{3,2,1,0:T(8,128)S(1)}, u32[]{:S(2)}, u32[]{:S(2)}) async-start(f32[4,36,8,256]{3,2,1,0:T(8,128)} %copy.14), calls=%async_computation.1 | async-start | bytes 2359296 | tf_op jit(solution)/shard_map/all_to_all | solution.py:247
  115.2 1.7 %multiply_subtract_fusion = f32[6,36,8,256]{3,2,0,1:T(8,128)S(1)} fusion(f32[2,36,8,256]{3,2,0,1:T(8,128)S(1)} %collective-permute-done.11, f32[4,36,8,256]{3,2,0,1:T(8,128)S(1)} %get-tuple-element.19, f32[6,35,8,256]{3,2,0,1:T(8,128)S(1)} %fusion.27, f32[2,36,8,256]{3,2,0,1:T(8,128)} %collective-permute-done.10), kind=kLoop, calls=%fused_computation.61 | loop fusion | flops 6193152 | bytes 5849088 | tf_op jit(solution)/shard_map/sub | solution.py:225
  117.1 0.6 fusion.33
  117.7 1.1 copy.18
  118.8 11.9 %all-to-all-done.1 = f32[4,36,8,256]{3,2,1,0:T(8,128)S(1)} async-done(((f32[4,36,8,256]{3,2,1,0:T(8,128)}), f32[4,36,8,256]{3,2,1,0:T(8,128)S(1)}, u32[]{:S(2)}, u32[]{:S(2)}) %all-to-all-start.1) | async-done | bytes 1179680 | tf_op jit(solution)/shard_map/all_to_all | solution.py:247
  130.7 3.5 %all-to-all-start.3 = ((f32[4,36,8,256]{3,2,1,0:T(8,128)}), f32[4,36,8,256]{3,2,1,0:T(8,128)S(1)}, u32[]{:S(2)}, u32[]{:S(2)}) async-start(f32[4,36,8,256]{3,2,1,0:T(8,128)} %copy.18), calls=%async_computation.3 | async-start | bytes 2359296 | tf_op jit(solution)/shard_map/all_to_all | solution.py:247
  134.3 0.1 copy.32
  134.4 14.6 %all-to-all-done.3 = f32[4,36,8,256]{3,2,1,0:T(8,128)S(1)} async-done(((f32[4,36,8,256]{3,2,1,0:T(8,128)}), f32[4,36,8,256]{3,2,1,0:T(8,128)S(1)}, u32[]{:S(2)}, u32[]{:S(2)}) %all-to-all-start.3) | async-done | bytes 1179680 | tf_op jit(solution)/shard_map/all_to_all | solution.py:247
  149.1 0.1 copy.31
  149.2 1.7 %pad_maximum_fusion.4 = f32[1,36,32,512]{3,2,1,0:T(8,128)} fusion(f32[1,36,32,256]{3,2,1,0:T(8,128)S(1)} %bitcast.101, f32[1,36,32,256]{3,2,1,0:T(8,128)S(1)} %bitcast.100), kind=kLoop, calls=%fused_computation.42 | loop fusion | flops 589824 | bytes 4718592 | tf_op jit(solution)/shard_map/concatenate | solution.py:195
  (61 shorter events, 1.5 us)
Async XLA Ops:
  3.9 3.4 %collective-permute-start = (f32[1,36,2,512]{3,1,2,0:T(8,128)S(1)}, f32[1,36,2,512]{3,1,2,0:T(8,128)S(1)}, u32[]{:S(2)}, u32[]{:S(2)}) collective-permute-start(f32[1,36,2,512]{3,1,2,0:T(8,128)S(1)} %get-tuple-element.24), channel_id=1, source_target_pairs={{0,32},{32,64},{64,96},{96,128},{128,160},{160,192},{192,224},{1,3... | collective-permute-start | bytes 442376 | tf_op jit(solution)/shard_map/ppermute | solution.py:30
  5.7 4.6 %collective-permute-start.1 = (f32[1,36,2,512]{3,1,2,0:T(8,128)S(1)}, f32[1,36,2,512]{3,1,2,0:T(8,128)S(1)}, u32[]{:S(2)}, u32[]{:S(2)}) collective-permute-start(f32[1,36,2,512]{3,1,2,0:T(8,128)S(1)} %get-tuple-element.25), channel_id=1, source_target_pairs={{32,0},{64,32},{96,64},{128,96},{160,128},{192,160},{224,192},{33,... | collective-permute-start | bytes 442376 | tf_op jit(solution)/shard_map/ppermute | solution.py:32
  10.2 1.7 %copy-start = (f32[1,36,32,512]{3,2,1,0:T(8,128)S(1)}, f32[1,36,32,512]{3,2,1,0:T(8,128)}, u32[]{:S(2)}) copy-start(f32[1,36,32,512]{3,2,1,0:T(8,128)} %param.8) | copy-start | bytes 7077892
  16.4 0.9 copy-start.2
  16.4 0.9 copy-start.3
  22.8 4.6 %copy-start.4 = (f32[32,512]{1,0:T(8,128)S(1)}, f32[32,512]{1,0:T(8,128)}, u32[]{:S(2)}) copy-start(f32[32,512]{1,0:T(8,128)} %param.10) | copy-start | bytes 196612
  22.8 4.7 %copy-start.5 = (f32[32,512]{1,0:T(8,128)S(1)}, f32[32,512]{1,0:T(8,128)}, u32[]{:S(2)}) copy-start(f32[32,512]{1,0:T(8,128)} %param.11) | copy-start | bytes 196612
  22.8 21.2 %all-to-all-start.2 = ((f32[1,36,32,256]{3,1,0,2:T(8,128)}), f32[1,36,32,256]{3,1,0,2:T(8,128)S(1)}, u32[]{:S(2)}, u32[]{:S(2)}) async-start(f32[1,36,32,256]{3,1,0,2:T(8,128)} %get-tuple-element.21), calls=%async_computation.2 | async-start | bytes 2621440 | tf_op jit(solution)/shard_map/all_to_all | solution.py:202
  44.1 22.1 %all-to-all-start = ((f32[1,36,32,256]{3,1,0,2:T(8,128)}), f32[1,36,32,256]{3,1,0,2:T(8,128)}, u32[]{:S(2)}, u32[]{:S(2)}) async-start(f32[1,36,32,256]{3,1,0,2:T(8,128)} %get-tuple-element.20), calls=%async_computation | async-start | bytes 2621440 | tf_op jit(solution)/shard_map/all_to_all | solution.py:202
  52.7 62.5 %collective-permute-start.10 = (f32[2,36,8,256]{3,2,0,1:T(8,128)}, f32[2,36,8,256]{3,2,0,1:T(8,128)}, u32[]{:S(2)}, u32[]{:S(2)}) collective-permute-start(f32[2,36,8,256]{3,2,0,1:T(8,128)} %get-tuple-element.28), channel_id=1, source_target_pairs={{0,4},{4,8},{8,12},{12,16},{16,20},{20,24},{24,28},{1,5},{5,9},{9,... | collective-permute-start | bytes 1769480 | tf_op jit(solution)/shard_map/ppermute | solution.py:205
  56.5 58.5 %collective-permute-start.11 = (f32[2,36,8,256]{3,2,0,1:T(8,128)}, f32[2,36,8,256]{3,2,0,1:T(8,128)S(1)}, u32[]{:S(2)}, u32[]{:S(2)}) collective-permute-start(f32[2,36,8,256]{3,2,0,1:T(8,128)} %get-tuple-element.29), channel_id=1, source_target_pairs={{4,0},{8,4},{12,8},{16,12},{20,16},{24,20},{28,24},{5,1},{9,5},{13... | collective-permute-start | bytes 1769480 | tf_op jit(solution)/shard_map/ppermute | solution.py:206
  68.3 4.2 %collective-permute-start.2 = (f32[3,8,256]{2,1,0:T(8,128)S(1)}, f32[3,8,256]{2,1,0:T(8,128)S(1)}, u32[]{:S(2)}, u32[]{:S(2)}) collective-permute-start(f32[3,8,256]{2,1,0:T(8,128)S(1)} %pad_maximum_fusion.15), channel_id=1, source_target_pairs={{0,4},{4,0},{8,12},{12,8},{16,20},{20,16},{24,28},{28,24},{1,5},{5... | collective-permute-start | bytes 73736 | tf_op jit(solution)/shard_map/ppermute | solution.py:219
  68.5 7.3 %collective-permute-start.7 = (f32[3,8,256]{2,1,0:T(8,128)S(1)}, f32[3,8,256]{2,1,0:T(8,128)S(1)}, u32[]{:S(2)}, u32[]{:S(2)}) collective-permute-start(f32[3,8,256]{2,1,0:T(8,128)S(1)} %pad_maximum_fusion.16), channel_id=1, source_target_pairs={{0,4},{4,0},{8,12},{12,8},{16,20},{20,16},{24,28},{28,24},{1,5},{5... | collective-permute-start | bytes 73736 | tf_op jit(solution)/shard_map/ppermute | solution.py:219
  72.5 5.4 %collective-permute-start.3 = (f32[3,8,256]{2,1,0:T(8,128)S(1)}, f32[3,8,256]{2,1,0:T(8,128)S(1)}, u32[]{:S(2)}, u32[]{:S(2)}) collective-permute-start(f32[3,8,256]{2,1,0:T(8,128)S(1)} %fusion.65), channel_id=1, source_target_pairs={{0,8},{4,12},{8,0},{12,4},{16,24},{20,28},{24,16},{28,20},{1,9},{5... | collective-permute-start | bytes 73736 | tf_op jit(solution)/shard_map/ppermute | solution.py:219
  75.8 7.6 %collective-permute-start.8 = (f32[3,8,256]{2,1,0:T(8,128)S(1)}, f32[3,8,256]{2,1,0:T(8,128)S(1)}, u32[]{:S(2)}, u32[]{:S(2)}) collective-permute-start(f32[3,8,256]{2,1,0:T(8,128)S(1)} %fusion.64), channel_id=1, source_target_pairs={{0,8},{4,12},{8,0},{12,4},{16,24},{20,28},{24,16},{28,20},{1,9},{5... | collective-permute-start | bytes 73736 | tf_op jit(solution)/shard_map/ppermute | solution.py:219
  77.9 11.7 %collective-permute-start.4 = (f32[3,8,256]{2,1,0:T(8,128)S(1)}, f32[3,8,256]{2,1,0:T(8,128)S(1)}, u32[]{:S(2)}, u32[]{:S(2)}) collective-permute-start(f32[3,8,256]{2,1,0:T(8,128)S(1)} %fusion.73), channel_id=1, source_target_pairs={{0,16},{4,20},{8,24},{12,28},{16,0},{20,4},{24,8},{28,12},{1,17},{... | collective-permute-start | bytes 73736 | tf_op jit(solution)/shard_map/ppermute | solution.py:219
  83.4 8.1 %collective-permute-start.9 = (f32[3,8,256]{2,1,0:T(8,128)S(1)}, f32[3,8,256]{2,1,0:T(8,128)S(1)}, u32[]{:S(2)}, u32[]{:S(2)}) collective-permute-start(f32[3,8,256]{2,1,0:T(8,128)S(1)} %fusion.74), channel_id=1, source_target_pairs={{0,16},{4,20},{8,24},{12,28},{16,0},{20,4},{24,8},{28,12},{1,17},{... | collective-permute-start | bytes 73736 | tf_op jit(solution)/shard_map/ppermute | solution.py:219
  85.1 21.7 %collective-permute-start.5 = (f32[2,36,8,256]{3,2,0,1:T(8,128)S(1)}, f32[2,36,8,256]{3,2,0,1:T(8,128)S(1)}, u32[]{:S(2)}, u32[]{:S(2)}) collective-permute-start(f32[2,36,8,256]{3,2,0,1:T(8,128)S(1)} %get-tuple-element.26), channel_id=1, source_target_pairs={{0,4},{4,8},{8,12},{12,16},{16,20},{20,24},{24,28},{1,5},{5,9},{9,... | collective-permute-start | bytes 1769480 | tf_op jit(solution)/shard_map/ppermute | solution.py:205
  89.6 17.1 %collective-permute-start.6 = (f32[2,36,8,256]{3,2,0,1:T(8,128)S(1)}, f32[2,36,8,256]{3,2,0,1:T(8,128)S(1)}, u32[]{:S(2)}, u32[]{:S(2)}) collective-permute-start(f32[2,36,8,256]{3,2,0,1:T(8,128)S(1)} %get-tuple-element.27), channel_id=1, source_target_pairs={{4,0},{8,4},{12,8},{16,12},{20,16},{24,20},{28,24},{5,1},{9,5},{13... | collective-permute-start | bytes 1769480 | tf_op jit(solution)/shard_map/ppermute | solution.py:206
  107.3 1.0 copy-start.1
  110.0 20.8 %all-to-all-start.1 = ((f32[4,36,8,256]{3,2,1,0:T(8,128)}), f32[4,36,8,256]{3,2,1,0:T(8,128)S(1)}, u32[]{:S(2)}, u32[]{:S(2)}) async-start(f32[4,36,8,256]{3,2,1,0:T(8,128)} %copy.14), calls=%async_computation.1 | async-start | bytes 2359296 | tf_op jit(solution)/shard_map/all_to_all | solution.py:247
  130.7 18.3 %all-to-all-start.3 = ((f32[4,36,8,256]{3,2,1,0:T(8,128)}), f32[4,36,8,256]{3,2,1,0:T(8,128)S(1)}, u32[]{:S(2)}, u32[]{:S(2)}) async-start(f32[4,36,8,256]{3,2,1,0:T(8,128)} %copy.18), calls=%async_computation.3 | async-start | bytes 2359296 | tf_op jit(solution)/shard_map/all_to_all | solution.py:247

commit v5 on v2

--- a/solution.py
+++ b/solution.py
@@ -1,8 +1,11 @@
+import functools
 import math
 
 import jax
 import jax.numpy as jnp
 from jax import lax
+from jax.experimental import pallas as pl
+from jax.experimental.pallas import tpu as pltpu
 from jax.sharding import PartitionSpec as P
 
 GRAVITY = 9.81
@@ -145,6 +148,97 @@
 
 
 Y_GROUP = 4
+
+
+def _z_exchange_kernel(z_count, point_ref, part_ref, lower_ref, upper_ref, gathered_ref,
+                       halo_send, halo_recv, gather_send, gather_recv):
+    geo = lax.axis_index("geo")
+    z_pos = lax.axis_index("z")
+    y_pos = lax.axis_index("y")
+    group = point_ref.shape[0]
+    barrier = pltpu.get_barrier_semaphore()
+    for offset in range(1, z_count):
+        target = lax.rem(z_pos + offset, z_count)
+        pl.semaphore_signal(barrier, inc=1, device_id=(geo, target, y_pos),
+                            device_id_type=pl.DeviceIdType.MESH)
+    pl.semaphore_wait(barrier, z_count - 1)
+
+    def halo_copy(src_lo, dst_ref, slot, target):
+        return pltpu.make_async_remote_copy(
+            src_ref=point_ref.at[pl.ds(src_lo, 2)],
+            dst_ref=dst_ref,
+            send_sem=halo_send.at[slot],
+            recv_sem=halo_recv.at[slot],
+            device_id=(geo, target, y_pos),
+            device_id_type=pl.DeviceIdType.MESH,
+        )
+
+    up = halo_copy(group - 2, lower_ref, 0, z_pos + 1)
+    down = halo_copy(0, upper_ref, 1, z_pos - 1)
+
+    @pl.when(z_pos < z_count - 1)
+    def _():
+        up.start()
+
+    @pl.when(z_pos > 0)
+    def _():
+        down.start()
+
+    copies = []
+    for offset in range(1, z_count):
+        target = lax.rem(z_pos + offset, z_count)
+        copy = pltpu.make_async_remote_copy(
+            src_ref=part_ref,
+            dst_ref=gathered_ref.at[z_pos],
+            send_sem=gather_send.at[offset],
+            recv_sem=gather_recv.at[offset],
+            device_id=(geo, target, y_pos),
+            device_id_type=pl.DeviceIdType.MESH,
+        )
+        copy.start()
+        copies.append(copy)
+    gathered_ref[z_pos] = part_ref[...]
+
+    @pl.when(z_pos == 0)
+    def _():
+        lower_ref[...] = jnp.zeros(lower_ref.shape, lower_ref.dtype)
+
+    @pl.when(z_pos == z_count - 1)
+    def _():
+        upper_ref[...] = jnp.zeros(upper_ref.shape, upper_ref.dtype)
+
+    for copy in copies:
+        copy.wait_send()
+        copy.wait_recv()
+
+    @pl.when(z_pos < z_count - 1)
+    def _():
+        up.wait_send()
+        down.wait_recv()
+
+    @pl.when(z_pos > 0)
+    def _():
+        down.wait_send()
+        up.wait_recv()
+
+
+def z_exchange(point, part, z_count):
+    group, dirs, rows, cols = point.shape
+    halo = jax.ShapeDtypeStruct((2, dirs, rows, cols), point.dtype)
+    vmem = pl.BlockSpec(memory_space=pltpu.VMEM)
+    return pl.pallas_call(
+        functools.partial(_z_exchange_kernel, z_count),
+        out_shape=(halo, halo, jax.ShapeDtypeStruct((z_count,) + part.shape, part.dtype)),
+        in_specs=[vmem, vmem],
+        out_specs=(vmem, vmem, vmem),
+        scratch_shapes=[
+            pltpu.SemaphoreType.DMA((2,)),
+            pltpu.SemaphoreType.DMA((2,)),
+            pltpu.SemaphoreType.DMA((z_count,)),
+            pltpu.SemaphoreType.DMA((z_count,)),
+        ],
+        compiler_params=pltpu.CompilerParams(collective_id=0, has_side_effects=True),
+    )(point, part)
 
 
 def shards(spectrum, land_sea, sea_index, sea_count, wind_speed, wind_dir, slope_x, slope_y):
@@ -180,8 +274,6 @@
     point = lax.all_to_all(floored, "y", split_axis=2, concat_axis=0, tiled=True)
     group = point.shape[0]
     part_rows = point.shape[2]
-    lower = lax.ppermute(point[group - 2 :], "z", [(i, i + 1) for i in range(z_count - 1)])
-    upper = lax.ppermute(point[:2], "z", [(i + 1, i) for i in range(z_count - 1)])
     group_ids = (z_pos * group + jnp.arange(group)).astype(jnp.float32)
     radian_freq, wavenum, courant, turn_rate, band_spread = band_table(group_ids)
     scaled = point * (band_spread * dtheta)[:, None, None, None]
@@ -192,7 +284,8 @@
             jnp.sum(scaled / jnp.sqrt(wavenum)[:, None, None, None], axis=(0, 1)),
         ]
     )
-    sums = jnp.sum(lax.all_gather(sums, "z"), axis=0)
+    lower, upper, gathered = z_exchange(point, sums, z_count)
+    sums = jnp.sum(gathered, axis=0)
     energy_sum, first_sum, root_sum = sums[0], sums[1], sums[2]
     energy = energy_sum + EPSILON
     ext = jnp.concatenate([lower, point, upper], axis=0)

time: 157 us -> 156 us (level)
  Pallas kernels: 0 us -> 46.1 us
  blocking collectives: 73.7 us -> 31.2 us
  local copies, waits for them, and re-layouts: 5.31 us -> 12.1 us
  starting transfers between devices: 16.2 us -> 10 us
  waiting for transfers between devices: 32.6 us -> 29.6 us
    all_gather x1 -> x0, blocking collectives: 47.5 us -> none  [shards(): sums = jnp.sum(lax.all_gather(sums, 'z'), axis=0)]
    pallas_call x0 -> x1, Pallas kernels: none -> 46.1 us  [z_exchange(): pl.pallas_call(functools.partial(_z_exchange_kernel, z_count), out_shape=...]
    ppermute x2 -> x0, starting transfers between devices: 6.15 us -> none  [the longest x1 4.87 us: shards(): lax.ppermute(point[group - 2:], 'z', [(i, i + 1) for i in range(z_count -...]
    all_to_all x1, blocking collectives: 26.2 us -> 31.2 us  [shards(): return lax.all_to_all(updated, 'y', split_axis=0, concat_axis=2, tiled=True)]
    max x0 -> x1, local copies, waits for them, and re-layouts: none -> 3.83 us  [shards(): floored = jnp.maximum(advect(padded, turning, 1), 0.0)]
    all_to_all x1, waiting for transfers between devices: 30.1 us -> 27.3 us  [shards(): lax.all_to_all(floored, 'y', split_axis=2, concat_axis=0, tiled=True)]
    mul x1, other arithmetic: 1.43 us -> 3.78 us  [shards(): (sources(point, energy_sum, first_sum, root_sum, radian_freq[:, None, Non...]
    reduce_sum x1, other arithmetic: 3.15 us -> 0.82 us  [shards(): jnp.sum(scaled, axis=(0, 1))]
  transfers between devices with their start and end apart: 5 -> 3, of which waited for: 3 -> 3; matrix products, arithmetic and copies ran while one was open for 5% -> 2% of each run, Pallas kernels for 0% -> 0%
where the time goes in v5:
time: 156 us
  Pallas kernels  46.1 us (30%)
  blocking collectives  31.2 us (20%)
  waiting for transfers between devices  29.6 us (19%)
  other arithmetic  26.5 us (17%)
  local copies, waits for them, and re-layouts  12.1 us (8%)
  starting transfers between devices  10 us (6%)
    pallas_call x1, Pallas kernels, z_exchange(): pl.pallas_call(functools.partial(_z_exchange_kernel, z_count), out_shape=...  46.1 us
    all_to_all x1, blocking collectives, shards(): return lax.all_to_all(updated, 'y', split_axis=0, concat_axis=2, tiled=True)  31.2 us
    all_to_all x1, waiting for transfers between devices, shards(): lax.all_to_all(floored, 'y', split_axis=2, concat_axis=0, tiled=True)  27.3 us
    mul x3, other arithmetic, quick_flux(): return courant * face_value  8.41 us
    all_to_all x1, starting transfers between devices, shards(): lax.all_to_all(floored, 'y', split_axis=2, concat_axis=0, tiled=True)  4.46 us
    max x1, local copies, waits for them, and re-layouts, shards(): floored = jnp.maximum(advect(padded, turning, 1), 0.0)  3.83 us
    mul x1, other arithmetic, shards(): (sources(point, energy_sum, first_sum, root_sum, radian_freq[:, None, Non...  3.78 us
    ppermute x1, starting transfers between devices, extended(): lax.ppermute(head, axis, [((i + 1) % count, i) for i in range(ends)])  3.64 us
  transfers between devices with their start and end apart: 3, of which 3 were waited for; matrix products, arithmetic and copies ran while one was open for 2% of the time, Pallas kernels for 0%

profile of v5, /device:TPU:2, one launch (start us, length us, event | category | flops | bytes accessed | tf_op | source)
XLA Modules:
  0.0 155.9 jit_solution(18085893459202599780)
XLA Ops:
  0.0 0.0 copy-start
  0.0 0.9 convert_element_type.84
  0.9 2.0 %broadcast_multiply_fusion = f32[1,36,32,512]{3,2,1,0:T(8,128)S(1)} fusion(f32[1,36,32,512]{3,2,1,0:T(8,128)} %param.8, f32[32,512]{1,0:T(8,128)S(1)} %convert_element_type.84), kind=kLoop, calls=%fused_computation.64 | loop fusion | flops 589824 | bytes 4784128 | tf_op jit(solution)/shard_map/mul | solution.py:257
  2.9 0.1 fusion.47
  3.0 1.9 %collective-permute-start = (f32[1,36,2,512]{3,2,1,0:T(2,128)S(1)}, f32[1,36,2,512]{3,2,1,0:T(2,128)S(1)}, u32[]{:S(2)}, u32[]{:S(2)}) collective-permute-start(f32[1,36,2,512]{3,2,1,0:T(2,128)S(1)} %get-tuple-element.18), channel_id=1, source_target_pairs={{0,32},{32,64},{64,96},{96,128},{128,160},{160,192},{192,224},{1,3... | collective-permute-start | bytes 442376 | tf_op jit(solution)/shard_map/ppermute | solution.py:33
  5.0 3.6 %collective-permute-start.1 = (f32[1,36,2,512]{3,2,1,0:T(2,128)S(1)}, f32[1,36,2,512]{3,2,1,0:T(2,128)S(1)}, u32[]{:S(2)}, u32[]{:S(2)}) collective-permute-start(f32[1,36,2,512]{3,2,1,0:T(2,128)S(1)} %get-tuple-element.19), channel_id=1, source_target_pairs={{32,0},{64,32},{96,64},{128,96},{160,128},{192,160},{224,192},{33,... | collective-permute-start | bytes 442376 | tf_op jit(solution)/shard_map/ppermute | solution.py:35
  8.9 0.6 collective-permute-done
  9.5 1.8 %collective-permute-done.1 = f32[1,36,2,512]{3,2,1,0:T(2,128)S(1)} collective-permute-done((f32[1,36,2,512]{3,2,1,0:T(2,128)S(1)}, f32[1,36,2,512]{3,2,1,0:T(2,128)S(1)}, u32[]{:S(2)}, u32[]{:S(2)}) %collective-permute-start.1) | collective-permute-done | bytes 147488 | tf_op jit(solution)/shard_map/ppermute | solution.py:35
  11.3 0.0 copy-start.3
  11.3 2.5 %fusion.12 = f32[1,36,33,512]{3,2,1,0:T(8,128)S(1)} fusion(f32[1,36,2,512]{3,2,1,0:T(2,128)S(1)} %collective-permute-done.1, f32[1,36,32,512]{3,2,1,0:T(8,128)S(1)} %broadcast_multiply_fusion, f32[1,36,2,512]{3,2,1,0:T(2,128)S(1)} %collective-permute-done, f32[36]{0:T(128)S(1)} %get-tuple-element.31, f32[36]{0:T(128)S(1)} %get-tuple-element.32, ...), kind=kLoop, calls=%fused_computation.25 | loop fusion | flops 10948608 | bytes 5087700 | tf_op jit(solution)/shard_map/mul | solution.py:65
  13.8 0.0 copy-done.3
  13.8 0.7 fusion.30
  14.5 2.8 %fusion.7 = f32[1,36,32,513]{3,2,1,0:T(8,128)S(1)} fusion(f32[1,36,32,512]{3,2,1,0:T(8,128)S(1)} %fusion.30, f32[36]{0:T(128)S(1)} %get-tuple-element.28, f32[36]{0:T(128)S(1)} %get-tuple-element.29, f32[36]{0:T(128)S(1)} %get-tuple-element.30, pred[36]{0:T(512)(128)(4,1)S(1)} %get-tuple-element.34), kind=kLoop, calls=%fused_computation.19 | loop fusion | flops 8273664 | bytes 4723668 | tf_op jit(solution)/shard_map/mul | solution.py:65
  17.3 0.0 copy-start.6
  17.3 0.0 copy-start.7
  17.3 0.7 fusion.28
  18.1 0.1 copy-done.6
  18.2 0.0 copy-done.7
  18.2 3.1 %fusion.19 = f32[1,37,32,512]{3,2,1,0:T(8,128)S(1)} fusion(f32[1,2,32,512]{3,2,1,0:T(8,128)S(1)} %get-tuple-element.17, f32[1,36,32,512]{3,2,1,0:T(8,128)S(1)} %fusion.28, f32[1,2,32,512]{3,2,1,0:T(8,128)S(1)} %get-tuple-element.16, f32[32,512]{1,0:T(8,128)S(1)} %copy-done.6, f32[37]{0:T(128)S(1)} %get-tuple-element.36, f32[32,512]{1,0:T(8,128)S(1)} %copy-done.7, ...), kind=kLoop, calls=%fused_computation.40 | loop fusion | flops 16973824 | bytes 5177644 | tf_op jit(solution)/shard_map/mul | solution.py:65
  21.3 0.6 fusion.26
  21.9 3.8 %copy.17 = f32[1,36,32,512]{3,0,1,2:T(1,128)} copy(f32[1,36,32,512]{3,2,1,0:T(8,128)S(1)} %fusion.26) | data formatting | bytes 4718592 | tf_op jit(solution)/shard_map/max | solution.py:273
  25.7 4.5 %all-to-all-start = ((f32[1,36,32,512]{3,0,1,2:T(1,128)}), f32[1,36,32,512]{3,0,1,2:T(1,128)S(1)}, u32[]{:S(2)}, u32[]{:S(2)}) async-start(f32[1,36,32,512]{3,0,1,2:T(1,128)} %copy.17), calls=%async_computation | async-start | bytes 4718592 | tf_op jit(solution)/shard_map/all_to_all | solution.py:274
  30.2 0.0 copy-done
  30.3 0.7 dynamic-slice_multiply_fusion
  31.0 0.1 multiply_multiply_fusion
  31.1 1.9 %subtract_cosine_fusion = f32[36,8,512]{2,1,0:T(8,128)S(1)} fusion(f32[8,512]{1,0:T(8,128)S(1)} %constant_dynamic-slice_fusion.1, f32[36]{0:T(128)S(1)} %add_multiply_fusion), kind=kLoop, calls=%fused_computation.65 | loop fusion | flops 147456 | bytes 606352 | tf_op jit(solution)/shard_map/cos | solution.py:301
  33.0 27.3 %all-to-all-done = f32[1,36,32,512]{3,0,1,2:T(1,128)S(1)} async-done(((f32[1,36,32,512]{3,0,1,2:T(1,128)}), f32[1,36,32,512]{3,0,1,2:T(1,128)S(1)}, u32[]{:S(2)}, u32[]{:S(2)}) %all-to-all-start) | async-done | bytes 2359328 | tf_op jit(solution)/shard_map/all_to_all | solution.py:274
  60.3 0.8 multiply_reduce_fusion
  61.1 0.6 pad_maximum_fusion.9.part_ref
  61.8 2.1 %copy_bitcast_fusion.1.point_ref = f32[4,36,8,512]{3,2,1,0:T(8,128)} fusion(f32[1,36,32,512]{3,0,1,2:T(1,128)S(1)} %all-to-all-done), kind=kLoop, calls=%fused_computation.59 | loop fusion | bytes 4718592 | tf_op jit(solution)/shard_map/all_to_all | solution.py:274
  63.9 46.1 %shard_map.64 = (f32[2,36,8,512]{3,2,1,0:T(8,128)}, f32[2,36,8,512]{3,2,1,0:T(8,128)}, f32[8,3,8,512]{3,2,1,0:T(8,128)}) custom-call(f32[4,36,8,512]{3,2,1,0:T(8,128)} %copy_bitcast_fusion.1.point_ref, f32[3,8,512]{2,1,0:T(8,128)} %pad_maximum_fusion.9.part_ref), custom_call_target="tpu_custom_call" | custom-call | tf_op jit(solution)/shard_map/pallas_call | solution.py:229
  110.0 0.0 copy-start.1
  110.0 0.0 copy-start.4
  110.0 0.0 copy-start.5
  110.0 2.5 %fusion.2 = f32[6,35,8,512]{3,2,1,0:T(8,128)S(1)} fusion(f32[4,36,8,512]{3,2,1,0:T(8,128)} %copy_bitcast_fusion.1.point_ref, f32[2,36,8,512]{3,2,1,0:T(8,128)} %get-tuple-element.10), kind=kLoop, calls=%fused_computation.10 | loop fusion | flops 860160 | bytes 6979584 | tf_op jit(solution)/shard_map/concatenate | solution.py:291
  112.5 0.2 copy-done.1
  112.7 0.3 copy-done.4
  113.0 0.4 copy-done.5
  113.4 1.4 multiply_subtract_fusion
  114.8 0.0 copy-start.2
  114.8 1.7 %slice.194 = f32[4,35,8,512]{3,2,1,0:T(8,128)} slice(f32[6,36,8,512]{3,2,1,0:T(8,128)S(1)} %multiply_subtract_fusion), slice={[0:4], [0:35], [0:8], [0:512]} | slice | bytes 4587520 | tf_op jit(solution)/shard_map/jit(_roll_static)/slice | solution.py:295
  116.5 1.5 slice.195
  118.1 0.0 copy-done.2
  118.1 1.0 reduce_sum.39
  119.1 0.1 fusion.33
  119.2 3.8 %fusion.24 = f32[4,36,8,512]{3,2,1,0:T(8,128)S(1)} fusion(f32[6,36,8,512]{3,2,1,0:T(8,128)} %copy-done.2, f32[4,35,8,512]{3,2,1,0:T(8,128)} %slice.194, f32[4,1,8,512]{3,2,1,0:T(8,128)S(1)} %slice.193, f32[4,3,8,512]{3,2,1,0:T(8,128)S(1)} %slice.196, f32[4,33,8,512]{3,2,1,0:T(8,128)} %slice.195, f32[8,512]{1,0:T(8,128)S(1)} %get-tuple-element.39, ...), kind=kLoop, calls=%fused_computation.48 | loop fusion | flops 8847360 | bytes 12550160 | tf_op jit(solution)/shard_map/mul | solution.py:302
  123.0 31.2 %all_to_all.36 = f32[4,36,8,512]{3,2,1,0:T(8,128)S(1)} all-to-all(f32[4,36,8,512]{3,2,1,0:T(8,128)S(1)} %fusion.24), channel_id=1, replica_groups=mesh['geo'=8,'z'=8,'y'=4] {'y'}, dimensions={0} | all-to-all | bytes 4718592 | tf_op jit(solution)/shard_map/all_to_all | solution.py:315
  154.3 1.7 %copy_bitcast_fusion = f32[1,36,32,512]{3,2,1,0:T(8,128)} fusion(f32[4,36,8,512]{3,2,1,0:T(8,128)S(1)} %all_to_all.36), kind=kLoop, calls=%fused_computation.58 | loop fusion | bytes 4718592 | tf_op jit(solution)/shard_map/all_to_all | solution.py:315
  (14 shorter events, 0.3 us)
Async XLA Ops:
  0.0 30.2 %copy-start = (f32[32,512]{1,0:T(8,128)S(1)}, f32[32,512]{1,0:T(8,128)}, u32[]{:S(2)}) copy-start(f32[32,512]{1,0:T(8,128)} %param.11) | copy-start | bytes 196612
  3.0 6.5 %collective-permute-start = (f32[1,36,2,512]{3,2,1,0:T(2,128)S(1)}, f32[1,36,2,512]{3,2,1,0:T(2,128)S(1)}, u32[]{:S(2)}, u32[]{:S(2)}) collective-permute-start(f32[1,36,2,512]{3,2,1,0:T(2,128)S(1)} %get-tuple-element.18), channel_id=1, source_target_pairs={{0,32},{32,64},{64,96},{96,128},{128,160},{160,192},{192,224},{1,3... | collective-permute-start | bytes 442376 | tf_op jit(solution)/shard_map/ppermute | solution.py:33
  5.0 6.3 %collective-permute-start.1 = (f32[1,36,2,512]{3,2,1,0:T(2,128)S(1)}, f32[1,36,2,512]{3,2,1,0:T(2,128)S(1)}, u32[]{:S(2)}, u32[]{:S(2)}) collective-permute-start(f32[1,36,2,512]{3,2,1,0:T(2,128)S(1)} %get-tuple-element.19), channel_id=1, source_target_pairs={{32,0},{64,32},{96,64},{128,96},{160,128},{192,160},{224,192},{33,... | collective-permute-start | bytes 442376 | tf_op jit(solution)/shard_map/ppermute | solution.py:35
  11.3 2.5 %copy-start.3 = (f32[1,36,32,512]{3,2,1,0:T(8,128)S(1)}, f32[1,36,32,512]{3,2,1,0:T(8,128)}, u32[]{:S(2)}) copy-start(f32[1,36,32,512]{3,2,1,0:T(8,128)} %param.8) | copy-start | bytes 7077892
  17.3 0.8 copy-start.6
  17.3 0.9 copy-start.7
  25.7 34.6 %all-to-all-start = ((f32[1,36,32,512]{3,0,1,2:T(1,128)}), f32[1,36,32,512]{3,0,1,2:T(1,128)S(1)}, u32[]{:S(2)}, u32[]{:S(2)}) async-start(f32[1,36,32,512]{3,0,1,2:T(1,128)} %copy.17), calls=%async_computation | async-start | bytes 4718592 | tf_op jit(solution)/shard_map/all_to_all | solution.py:274
  110.0 2.7 %copy-start.1 = (f32[4,36,8,512]{3,2,1,0:T(8,128)S(1)}, f32[4,36,8,512]{3,2,1,0:T(8,128)}, u32[]{:S(2)}) copy-start(f32[4,36,8,512]{3,2,1,0:T(8,128)} %copy_bitcast_fusion.1.point_ref) | copy-start | bytes 7077892
  110.0 3.0 %copy-start.4 = (f32[2,36,8,512]{3,2,1,0:T(8,128)S(1)}, f32[2,36,8,512]{3,2,1,0:T(8,128)}, u32[]{:S(2)}) copy-start(f32[2,36,8,512]{3,2,1,0:T(8,128)} %get-tuple-element.10) | copy-start | bytes 3538948
  110.0 3.4 %copy-start.5 = (f32[2,36,8,512]{3,2,1,0:T(8,128)S(1)}, f32[2,36,8,512]{3,2,1,0:T(8,128)}, u32[]{:S(2)}) copy-start(f32[2,36,8,512]{3,2,1,0:T(8,128)} %get-tuple-element.9) | copy-start | bytes 3538948
  114.8 3.3 %copy-start.2 = (f32[6,36,8,512]{3,2,1,0:T(8,128)}, f32[6,36,8,512]{3,2,1,0:T(8,128)S(1)}, u32[]{:S(2)}) copy-start(f32[6,36,8,512]{3,2,1,0:T(8,128)S(1)} %multiply_subtract_fusion) | copy-start | bytes 10616836

commit v6 on v2

--- a/solution.py
+++ b/solution.py
@@ -1,8 +1,11 @@
+import functools
 import math
 
 import jax
 import jax.numpy as jnp
 from jax import lax
+from jax.experimental import pallas as pl
+from jax.experimental.pallas import tpu as pltpu
 from jax.sharding import PartitionSpec as P
 
 GRAVITY = 9.81
@@ -145,6 +148,184 @@
 
 
 Y_GROUP = 4
+HALO = 2
+
+
+def _z_gather_kernel(z_count, part_ref, gathered_ref, gather_send, gather_recv):
+    geo = lax.axis_index("geo")
+    z_pos = lax.axis_index("z")
+    y_pos = lax.axis_index("y")
+    barrier = pltpu.get_barrier_semaphore()
+    for offset in range(1, z_count):
+        target = lax.rem(z_pos + offset, z_count)
+        pl.semaphore_signal(barrier, inc=1, device_id=(geo, target, y_pos),
+                            device_id_type=pl.DeviceIdType.MESH)
+    pl.semaphore_wait(barrier, z_count - 1)
+    copies = []
+    for offset in range(1, z_count):
+        target = lax.rem(z_pos + offset, z_count)
+        copy = pltpu.make_async_remote_copy(
+            src_ref=part_ref,
+            dst_ref=gathered_ref.at[z_pos],
+            send_sem=gather_send.at[offset],
+            recv_sem=gather_recv.at[offset],
+            device_id=(geo, target, y_pos),
+            device_id_type=pl.DeviceIdType.MESH,
+        )
+        copy.start()
+        copies.append(copy)
+    gathered_ref[z_pos] = part_ref[...]
+    for copy in copies:
+        copy.wait_send()
+        copy.wait_recv()
+
+
+def z_gather(part, z_count):
+    vmem = pl.BlockSpec(memory_space=pltpu.VMEM)
+    return pl.pallas_call(
+        functools.partial(_z_gather_kernel, z_count),
+        out_shape=jax.ShapeDtypeStruct((z_count,) + part.shape, part.dtype),
+        in_specs=[vmem],
+        out_specs=vmem,
+        scratch_shapes=[
+            pltpu.SemaphoreType.DMA((z_count,)),
+            pltpu.SemaphoreType.DMA((z_count,)),
+        ],
+        compiler_params=pltpu.CompilerParams(collective_id=0, has_side_effects=True),
+    )(part)
+
+
+def _spread_kernel(z_count, y_count, floored_ref, ext_ref, y_send, local_sem, slot_recv, z_send):
+    geo = lax.axis_index("geo")
+    z_pos = lax.axis_index("z")
+    y_pos = lax.axis_index("y")
+    rows = ext_ref.shape[2]
+    mesh_id = pl.DeviceIdType.MESH
+    barrier = pltpu.get_barrier_semaphore()
+    for offset in range(1, y_count):
+        pl.semaphore_signal(barrier, inc=1, device_id=(geo, z_pos, lax.rem(y_pos + offset, y_count)),
+                            device_id_type=mesh_id)
+
+    for step in (1, z_count - 1):
+        pl.semaphore_signal(barrier, inc=1, device_id=(geo, lax.rem(z_pos + step, z_count), y_pos),
+                            device_id_type=mesh_id)
+    pl.semaphore_wait(barrier, y_count + 1)
+
+    own_slot = HALO + y_pos
+    sends = []
+    for offset in range(1, y_count):
+        target = lax.rem(y_pos + offset, y_count)
+        copy = pltpu.make_async_remote_copy(
+            src_ref=floored_ref.at[0, :, pl.ds(pl.multiple_of(target * rows, rows), rows)],
+            dst_ref=ext_ref.at[own_slot],
+            send_sem=y_send.at[offset],
+            recv_sem=slot_recv.at[own_slot],
+            device_id=(geo, z_pos, target),
+            device_id_type=mesh_id,
+        )
+        copy.start()
+        sends.append(copy)
+    local = pltpu.make_async_copy(
+        floored_ref.at[0, :, pl.ds(pl.multiple_of(y_pos * rows, rows), rows)],
+        ext_ref.at[own_slot],
+        local_sem.at[0],
+    )
+    local.start()
+
+    @pl.when(z_pos == 0)
+    def _():
+        ext_ref[pl.ds(0, HALO)] = jnp.zeros((HALO,) + ext_ref.shape[1:], ext_ref.dtype)
+
+    @pl.when(z_pos == z_count - 1)
+    def _():
+        ext_ref[pl.ds(HALO + y_count, HALO)] = jnp.zeros((HALO,) + ext_ref.shape[1:], ext_ref.dtype)
+
+    def forward(slot, dst_slot, target_z):
+        return pltpu.make_async_remote_copy(
+            src_ref=ext_ref.at[slot],
+            dst_ref=ext_ref.at[dst_slot],
+            send_sem=z_send.at[slot - HALO],
+            recv_sem=slot_recv.at[dst_slot],
+            device_id=(geo, target_z, y_pos),
+            device_id_type=mesh_id,
+        )
+
+    forwards = []
+    for band in range(y_count):
+        slot = HALO + band
+        arrival = pltpu.make_async_remote_copy(
+            src_ref=ext_ref.at[slot],
+            dst_ref=ext_ref.at[slot],
+            send_sem=y_send.at[0],
+            recv_sem=slot_recv.at[slot],
+            device_id=(geo, z_pos, lax.rem(y_pos + 1, y_count)),
+            device_id_type=mesh_id,
+        )
+
+        @pl.when(y_pos == band)
+        def _():
+            local.wait()
+
+        @pl.when(y_pos != band)
+        def _():
+            arrival.wait_recv()
+
+        if band < HALO:
+            fwd = forward(slot, slot + y_count, z_pos - 1)
+            live = z_pos > 0
+        elif band >= y_count - HALO:
+            fwd = forward(slot, slot - y_count, z_pos + 1)
+            live = z_pos < z_count - 1
+        else:
+            continue
+
+        @pl.when(live)
+        def _():
+            fwd.start()
+
+        forwards.append((fwd, live))
+    for copy in sends:
+        copy.wait_send()
+    for fwd, live in forwards:
+
+        @pl.when(live)
+        def _():
+            fwd.wait_send()
+
+    for slot, live in ((0, z_pos > 0), (1, z_pos > 0),
+                       (HALO + y_count, z_pos < z_count - 1), (HALO + y_count + 1, z_pos < z_count - 1)):
+        incoming = pltpu.make_async_remote_copy(
+            src_ref=ext_ref.at[slot],
+            dst_ref=ext_ref.at[slot],
+            send_sem=z_send.at[0],
+            recv_sem=slot_recv.at[slot],
+            device_id=(geo, lax.rem(z_pos + 1, z_count), y_pos),
+            device_id_type=mesh_id,
+        )
+
+        @pl.when(live)
+        def _():
+            incoming.wait_recv()
+
+
+def spread(floored, z_count, y_count):
+    _, dirs, rows, cols = floored.shape
+    part_rows = rows // y_count
+    vmem = pl.BlockSpec(memory_space=pltpu.VMEM)
+    slots = y_count + 2 * HALO
+    return pl.pallas_call(
+        functools.partial(_spread_kernel, z_count, y_count),
+        out_shape=jax.ShapeDtypeStruct((slots, dirs, part_rows, cols), floored.dtype),
+        in_specs=[vmem],
+        out_specs=vmem,
+        scratch_shapes=[
+            pltpu.SemaphoreType.DMA((y_count,)),
+            pltpu.SemaphoreType.DMA((1,)),
+            pltpu.SemaphoreType.DMA((slots,)),
+            pltpu.SemaphoreType.DMA((y_count,)),
+        ],
+        compiler_params=pltpu.CompilerParams(collective_id=1, has_side_effects=True),
+    )(floored)
 
 
 def shards(spectrum, land_sea, sea_index, sea_count, wind_speed, wind_dir, slope_x, slope_y):
@@ -177,11 +358,10 @@
     )
     padded = jnp.concatenate([density[:, -2:], density, density[:, :2]], axis=1)
     floored = jnp.maximum(advect(padded, turning, 1), 0.0)
-    point = lax.all_to_all(floored, "y", split_axis=2, concat_axis=0, tiled=True)
+    ext = spread(floored, z_count, lax.axis_size("y"))
+    point = ext[HALO:-HALO]
     group = point.shape[0]
     part_rows = point.shape[2]
-    lower = lax.ppermute(point[group - 2 :], "z", [(i, i + 1) for i in range(z_count - 1)])
-    upper = lax.ppermute(point[:2], "z", [(i + 1, i) for i in range(z_count - 1)])
     group_ids = (z_pos * group + jnp.arange(group)).astype(jnp.float32)
     radian_freq, wavenum, courant, turn_rate, band_spread = band_table(group_ids)
     scaled = point * (band_spread * dtheta)[:, None, None, None]
@@ -192,10 +372,9 @@
             jnp.sum(scaled / jnp.sqrt(wavenum)[:, None, None, None], axis=(0, 1)),
         ]
     )
-    sums = jnp.sum(lax.all_gather(sums, "z"), axis=0)
+    sums = jnp.sum(z_gather(sums, z_count), axis=0)
     energy_sum, first_sum, root_sum = sums[0], sums[1], sums[2]
     energy = energy_sum + EPSILON
-    ext = jnp.concatenate([lower, point, upper], axis=0)
     center, plus, minus = ext[1:-1], jnp.roll(ext[2:], -1, axis=1), jnp.roll(ext[:-2], 3, axis=1)
     cubic = center * center * (plus + minus) - 2.0 * center * plus * minus
     extra = (

time: 157 us -> 156 us (level)
  Pallas kernels: 0 us -> 81.8 us
  blocking collectives: 73.7 us -> 31.6 us
  waiting for transfers between devices: 32.6 us -> 0.01 us
  starting transfers between devices: 16.2 us -> 5.55 us
  local copies, waits for them, and re-layouts: 5.31 us -> 11 us
  other arithmetic: 28 us -> 25.2 us
    pallas_call x0 -> x2, Pallas kernels: none -> 81.8 us  [the longest x1 65.3 us: spread(): pl.pallas_call(functools.partial(_spread_kernel, z_count, y_count), out_s...]
    all_gather x1 -> x0, blocking collectives: 47.5 us -> none  [shards(): sums = jnp.sum(lax.all_gather(sums, 'z'), axis=0)]
    all_to_all x1 -> x0, waiting for transfers between devices: 30.1 us -> none  [shards(): lax.all_to_all(floored, 'y', split_axis=2, concat_axis=0, tiled=True)]
    ppermute x2 -> x0, starting transfers between devices: 6.15 us -> none  [the longest x1 4.87 us: shards(): lax.ppermute(point[group - 2:], 'z', [(i, i + 1) for i in range(z_count -...]
    all_to_all x1, blocking collectives: 26.2 us -> 31.6 us  [shards(): return lax.all_to_all(updated, 'y', split_axis=0, concat_axis=2, tiled=True)]
    all_to_all x1 -> x0, starting transfers between devices: 4.46 us -> none  [shards(): lax.all_to_all(floored, 'y', split_axis=2, concat_axis=0, tiled=True)]
    slice x1 -> x4, local copies, waits for them, and re-layouts: 1.6 us -> 4.8 us  [the longest x2 3.38 us: shards(): jnp.roll(ext[:-2], 3, axis=1)]
    reduce_sum x1, other arithmetic: 3.15 us -> 0.69 us  [shards(): jnp.sum(scaled, axis=(0, 1))]
  transfers between devices with their start and end apart: 5 -> 2, of which waited for: 3 -> 0; matrix products, arithmetic and copies ran while one was open for 5% -> 2% of each run, Pallas kernels for 0% -> 0%
where the time goes in v6:
time: 156 us; the launch traced here: 155 us
  Pallas kernels  81.8 us (52%)
  blocking collectives  31.6 us (20%)
  other arithmetic  25.2 us (16%)
  local copies, waits for them, and re-layouts  11 us (7%)
  starting transfers between devices  5.55 us (4%)
    pallas_call x1, Pallas kernels, spread(): pl.pallas_call(functools.partial(_spread_kernel, z_count, y_count), out_s...  65.3 us
    all_to_all x1, blocking collectives, shards(): return lax.all_to_all(updated, 'y', split_axis=0, concat_axis=2, tiled=True)  31.6 us
    pallas_call x1, Pallas kernels, z_gather(): pl.pallas_call(functools.partial(_z_gather_kernel, z_count), out_shape=ja...  16.5 us
    mul x3, other arithmetic, quick_flux(): return courant * face_value  8.44 us
    mul x1, other arithmetic, shards(): (sources(point, energy_sum, first_sum, root_sum, radian_freq[:, None, Non...  3.67 us
    ppermute x1, starting transfers between devices, extended(): lax.ppermute(head, axis, [((i + 1) % count, i) for i in range(ends)])  3.64 us
    slice x2, local copies, waits for them, and re-layouts, shards(): jnp.roll(ext[:-2], 3, axis=1)  3.38 us
  transfers between devices with their start and end apart: 2, of which 0 were waited for; matrix products, arithmetic and copies ran while one was open for 2% of the time, Pallas kernels for 0%

profile of v6, /device:TPU:2, one launch (start us, length us, event | category | flops | bytes accessed | tf_op | source)
XLA Modules:
  0.0 155.5 jit_solution(7535139436744067701)
XLA Ops:
  0.0 0.0 copy-start
  0.0 0.9 convert_element_type.84
  0.9 2.0 %broadcast_multiply_fusion = f32[1,36,32,512]{3,2,1,0:T(8,128)S(1)} fusion(f32[1,36,32,512]{3,2,1,0:T(8,128)} %param.8, f32[32,512]{1,0:T(8,128)S(1)} %convert_element_type.84), kind=kLoop, calls=%fused_computation.55 | loop fusion | flops 589824 | bytes 4784128 | tf_op jit(solution)/shard_map/mul | solution.py:344
  2.9 0.8 fusion.45
  3.7 1.9 %collective-permute-start = (f32[1,36,2,512]{3,2,1,0:T(2,128)}, f32[1,36,2,512]{3,2,1,0:T(2,128)S(1)}, u32[]{:S(2)}, u32[]{:S(2)}) collective-permute-start(f32[1,36,2,512]{3,2,1,0:T(2,128)} %get-tuple-element.12), channel_id=1, source_target_pairs={{0,32},{32,64},{64,96},{96,128},{128,160},{160,192},{192,224},{1,3... | collective-permute-start | bytes 442376 | tf_op jit(solution)/shard_map/ppermute | solution.py:33
  5.6 3.6 %collective-permute-start.1 = (f32[1,36,2,512]{3,2,1,0:T(2,128)}, f32[1,36,2,512]{3,2,1,0:T(2,128)S(1)}, u32[]{:S(2)}, u32[]{:S(2)}) collective-permute-start(f32[1,36,2,512]{3,2,1,0:T(2,128)} %get-tuple-element.13), channel_id=1, source_target_pairs={{32,0},{64,32},{96,64},{128,96},{160,128},{192,160},{224,192},{33,... | collective-permute-start | bytes 442376 | tf_op jit(solution)/shard_map/ppermute | solution.py:35
  9.6 0.0 copy-done
  9.6 0.7 dynamic-slice_multiply_fusion
  10.4 0.1 multiply_multiply_fusion
  10.4 1.9 %subtract_cosine_fusion = f32[36,8,512]{2,1,0:T(8,128)S(1)} fusion(f32[8,512]{1,0:T(8,128)S(1)} %constant_dynamic-slice_fusion.1, f32[36]{0:T(128)S(1)} %add_multiply_fusion), kind=kLoop, calls=%fused_computation.56 | loop fusion | flops 147456 | bytes 606352 | tf_op jit(solution)/shard_map/cos | solution.py:387
  12.5 0.0 collective-permute-done
  12.5 0.0 collective-permute-done.1
  12.5 0.0 copy-start.3
  12.5 2.6 %fusion.9 = f32[1,36,33,512]{3,2,1,0:T(8,128)S(1)} fusion(f32[1,36,2,512]{3,2,1,0:T(2,128)S(1)} %collective-permute-done.1, f32[1,36,32,512]{3,2,1,0:T(8,128)S(1)} %broadcast_multiply_fusion, f32[1,36,2,512]{3,2,1,0:T(2,128)S(1)} %collective-permute-done, f32[36]{0:T(128)S(1)} %get-tuple-element.25, f32[36]{0:T(128)S(1)} %get-tuple-element.26, ...), kind=kLoop, calls=%fused_computation.17 | loop fusion | flops 10948608 | bytes 5087700 | tf_op jit(solution)/shard_map/mul | solution.py:65
  15.1 0.0 copy-done.3
  15.1 0.7 fusion.27
  15.8 2.8 %fusion.4 = f32[1,36,32,513]{3,2,1,0:T(8,128)S(1)} fusion(f32[1,36,32,512]{3,2,1,0:T(8,128)S(1)} %fusion.27, f32[36]{0:T(128)S(1)} %get-tuple-element.22, f32[36]{0:T(128)S(1)} %get-tuple-element.23, f32[36]{0:T(128)S(1)} %get-tuple-element.24, pred[36]{0:T(512)(128)(4,1)S(1)} %get-tuple-element.28), kind=kLoop, calls=%fused_computation.11 | loop fusion | flops 8273664 | bytes 4723668 | tf_op jit(solution)/shard_map/mul | solution.py:65
  18.6 0.0 copy-start.4
  18.6 0.0 copy-start.5
  18.6 0.7 fusion.25
  19.3 0.1 copy-done.4
  19.4 0.0 copy-done.5
  19.5 3.1 %fusion.16 = f32[1,37,32,512]{3,2,1,0:T(8,128)S(1)} fusion(f32[1,2,32,512]{3,2,1,0:T(8,128)S(1)} %get-tuple-element.11, f32[1,36,32,512]{3,2,1,0:T(8,128)S(1)} %fusion.25, f32[1,2,32,512]{3,2,1,0:T(8,128)S(1)} %get-tuple-element.10, f32[32,512]{1,0:T(8,128)S(1)} %copy-done.4, f32[37]{0:T(128)S(1)} %get-tuple-element.30, f32[32,512]{1,0:T(8,128)S(1)} %copy-done.5, ...), kind=kLoop, calls=%fused_computation.32 | loop fusion | flops 16973824 | bytes 5177644 | tf_op jit(solution)/shard_map/mul | solution.py:65
  22.6 2.0 %fusion.23.floored_ref = f32[1,36,32,512]{3,2,1,0:T(8,128)} fusion(f32[1,36,32,512]{3,2,1,0:T(8,128)S(1)} %fusion.25, f32[1,37,32,512]{3,2,1,0:T(8,128)S(1)} %fusion.16), kind=kLoop, calls=%fused_computation.43 | loop fusion | flops 1769472 | bytes 9437184 | tf_op jit(solution)/shard_map/max | solution.py:360
  24.6 65.3 %shard_map.64 = f32[8,36,8,512]{3,2,1,0:T(8,128)} custom-call(f32[1,36,32,512]{3,2,1,0:T(8,128)} %fusion.23.floored_ref), custom_call_target="tpu_custom_call" | custom-call | tf_op jit(solution)/shard_map/pallas_call | solution.py:316
  89.9 0.9 slice.165
  90.8 1.0 slice.166
  91.8 0.0 copy-start.1
  91.8 2.4 %slice.167 = f32[6,33,8,512]{3,2,1,0:T(8,128)S(1)} slice(f32[8,36,8,512]{3,2,1,0:T(8,128)} %shard_map.64), slice={[0:6], [0:33], [0:8], [0:512]} | slice | bytes 6488064 | tf_op jit(solution)/shard_map/jit(_roll_static)/slice | solution.py:378
  94.2 0.9 copy-done.1
  95.1 0.5 slice.164
  95.6 1.4 multiply_subtract_fusion
  97.0 0.0 copy-start.2
  97.0 1.7 %slice.197 = f32[4,33,8,512]{3,2,1,0:T(8,128)} slice(f32[6,36,8,512]{3,2,1,0:T(8,128)S(1)} %multiply_subtract_fusion), slice={[2:6], [3:36], [0:8], [0:512]} | slice | bytes 4325376 | tf_op jit(solution)/shard_map/jit(_roll_static)/slice | solution.py:381
  98.7 0.7 copy-done.2
  99.4 0.2 slice.196
  99.7 0.7 fusion.28
  100.3 0.6 pad_maximum_fusion.6.part_ref
  101.0 16.5 %shard_map.65 = f32[8,3,8,512]{3,2,1,0:T(8,128)} custom-call(f32[3,8,512]{2,1,0:T(8,128)} %pad_maximum_fusion.6.part_ref), custom_call_target="tpu_custom_call" | custom-call | tf_op jit(solution)/shard_map/pallas_call | solution.py:185
  117.4 1.0 reduce_sum.39
  118.5 0.1 fusion.31
  118.6 3.7 %fusion.21 = f32[4,36,8,512]{3,2,1,0:T(8,128)S(1)} fusion(f32[6,36,8,512]{3,2,1,0:T(8,128)} %copy-done.2, f32[4,35,8,512]{3,2,1,0:T(8,128)S(1)} %slice.196, f32[4,1,8,512]{3,2,1,0:T(8,128)S(1)} %slice.195, f32[4,3,8,512]{3,2,1,0:T(8,128)S(1)} %slice.198, f32[4,33,8,512]{3,2,1,0:T(8,128)} %slice.197, f32[8,36,8,512]{3,2,1,0:T(8,128)} %shard_map.64, ...), kind=kLoop, calls=%fused_computation.40 | loop fusion | flops 8847360 | bytes 12550160 | tf_op jit(solution)/shard_map/mul | solution.py:388
  122.3 31.6 %all_to_all.18 = f32[4,36,8,512]{3,2,1,0:T(8,128)S(1)} all-to-all(f32[4,36,8,512]{3,2,1,0:T(8,128)S(1)} %fusion.21), channel_id=1, replica_groups=mesh['geo'=8,'z'=8,'y'=4] {'y'}, dimensions={0} | all-to-all | bytes 4718592 | tf_op jit(solution)/shard_map/all_to_all | solution.py:401
  153.8 1.7 %copy_bitcast_fusion = f32[1,36,32,512]{3,2,1,0:T(8,128)} fusion(f32[4,36,8,512]{3,2,1,0:T(8,128)S(1)} %all_to_all.18), kind=kLoop, calls=%fused_computation.50 | loop fusion | bytes 4718592 | tf_op jit(solution)/shard_map/all_to_all | solution.py:401
  (14 shorter events, 0.3 us)
Async XLA Ops:
  0.0 9.6 %copy-start = (f32[32,512]{1,0:T(8,128)S(1)}, f32[32,512]{1,0:T(8,128)}, u32[]{:S(2)}) copy-start(f32[32,512]{1,0:T(8,128)} %param.11) | copy-start | bytes 196612
  3.7 8.7 %collective-permute-start = (f32[1,36,2,512]{3,2,1,0:T(2,128)}, f32[1,36,2,512]{3,2,1,0:T(2,128)S(1)}, u32[]{:S(2)}, u32[]{:S(2)}) collective-permute-start(f32[1,36,2,512]{3,2,1,0:T(2,128)} %get-tuple-element.12), channel_id=1, source_target_pairs={{0,32},{32,64},{64,96},{96,128},{128,160},{160,192},{192,224},{1,3... | collective-permute-start | bytes 442376 | tf_op jit(solution)/shard_map/ppermute | solution.py:33
  5.6 6.8 %collective-permute-start.1 = (f32[1,36,2,512]{3,2,1,0:T(2,128)}, f32[1,36,2,512]{3,2,1,0:T(2,128)S(1)}, u32[]{:S(2)}, u32[]{:S(2)}) collective-permute-start(f32[1,36,2,512]{3,2,1,0:T(2,128)} %get-tuple-element.13), channel_id=1, source_target_pairs={{32,0},{64,32},{96,64},{128,96},{160,128},{192,160},{224,192},{33,... | collective-permute-start | bytes 442376 | tf_op jit(solution)/shard_map/ppermute | solution.py:35
  12.5 2.6 %copy-start.3 = (f32[1,36,32,512]{3,2,1,0:T(8,128)S(1)}, f32[1,36,32,512]{3,2,1,0:T(8,128)}, u32[]{:S(2)}) copy-start(f32[1,36,32,512]{3,2,1,0:T(8,128)} %param.8) | copy-start | bytes 7077892
  18.6 0.8 copy-start.4
  18.6 0.9 copy-start.5
  91.8 3.3 %copy-start.1 = (f32[8,36,8,512]{3,2,1,0:T(8,128)S(1)}, f32[8,36,8,512]{3,2,1,0:T(8,128)}, u32[]{:S(2)}) copy-start(f32[8,36,8,512]{3,2,1,0:T(8,128)} %shard_map.64) | copy-start | bytes 14155780
  97.0 2.4 %copy-start.2 = (f32[6,36,8,512]{3,2,1,0:T(8,128)}, f32[6,36,8,512]{3,2,1,0:T(8,128)S(1)}, u32[]{:S(2)}) copy-start(f32[6,36,8,512]{3,2,1,0:T(8,128)S(1)} %multiply_subtract_fusion) | copy-start | bytes 10616836

commit v7 on v6

--- a/solution.py
+++ b/solution.py
@@ -325,6 +325,9 @@
             pltpu.SemaphoreType.DMA((y_count,)),
         ],
         compiler_params=pltpu.CompilerParams(collective_id=1, has_side_effects=True),
+        cost_estimate=pl.CostEstimate(
+            flops=0, transcendentals=0, bytes_accessed=40 * floored.size * floored.dtype.itemsize
+        ),
     )(floored)
 
 
@@ -358,21 +361,26 @@
     )
     padded = jnp.concatenate([density[:, -2:], density, density[:, :2]], axis=1)
     floored = jnp.maximum(advect(padded, turning, 1), 0.0)
+    own_freq, own_wavenum, _, _, own_spread = band_table(band_ids)
+    own_scaled = floored * (own_spread * dtheta)[:, None, None, None]
+    total_sums = lax.psum(
+        jnp.stack(
+            [
+                jnp.sum(own_scaled, axis=(0, 1)),
+                jnp.sum(own_scaled / own_freq[:, None, None, None], axis=(0, 1)),
+                jnp.sum(own_scaled / jnp.sqrt(own_wavenum)[:, None, None, None], axis=(0, 1)),
+            ]
+        ),
+        ("z", "y"),
+    )
     ext = spread(floored, z_count, lax.axis_size("y"))
     point = ext[HALO:-HALO]
     group = point.shape[0]
     part_rows = point.shape[2]
     group_ids = (z_pos * group + jnp.arange(group)).astype(jnp.float32)
     radian_freq, wavenum, courant, turn_rate, band_spread = band_table(group_ids)
-    scaled = point * (band_spread * dtheta)[:, None, None, None]
-    sums = jnp.stack(
-        [
-            jnp.sum(scaled, axis=(0, 1)),
-            jnp.sum(scaled / radian_freq[:, None, None, None], axis=(0, 1)),
-            jnp.sum(scaled / jnp.sqrt(wavenum)[:, None, None, None], axis=(0, 1)),
-        ]
-    )
-    sums = jnp.sum(z_gather(sums, z_count), axis=0)
+    row_start = y_pos * part_rows
+    sums = lax.dynamic_slice_in_dim(total_sums, row_start, part_rows, axis=1)
     energy_sum, first_sum, root_sum = sums[0], sums[1], sums[2]
     energy = energy_sum + EPSILON
     center, plus, minus = ext[1:-1], jnp.roll(ext[2:], -1, axis=1), jnp.roll(ext[:-2], 3, axis=1)
@@ -380,7 +388,6 @@
     extra = (
         -2.0 * cubic[1:-1] + jnp.roll(cubic[:-2], 1, axis=1) + jnp.roll(cubic[2:], -3, axis=1)
     ) * (QUAD_COEF / (energy * energy))
-    row_start = y_pos * part_rows
     wind_block = lax.dynamic_slice_in_dim(wind_speed, row_start, part_rows, axis=0)
     wind_angle = lax.dynamic_slice_in_dim(wind_dir, row_start, part_rows, axis=0)
     wet_block = lax.dynamic_slice_in_dim(wet_mask, row_start, part_rows, axis=0)

time: 156 us -> 288 us (1.85)
  waiting for transfers between devices: 0.01 us -> 136 us
  Pallas kernels: 81.8 us -> 63.4 us
  between operations: 0.36 us -> 13.8 us
  blocking collectives: 31.6 us -> 27.5 us
  other arithmetic: 25.2 us -> 29 us
    psum x0 -> x1, waiting for transfers between devices: none -> 136 us  [shards(): lax.psum(jnp.stack([jnp.sum(own_scaled, axis=(0, 1)), jnp.sum(own_scaled...]
    pallas_call x1 -> x0, Pallas kernels: 16.5 us -> none  [z_gather(): pl.pallas_call(functools.partial(_z_gather_kernel, z_count), out_shape=ja...]
    all_to_all x1, blocking collectives: 31.6 us -> 27.5 us  [shards(): return lax.all_to_all(updated, 'y', split_axis=0, concat_axis=2, tiled=True)]
  transfers between devices with their start and end apart: 2 -> 3, of which waited for: 0 -> 1; matrix products, arithmetic and copies ran while one was open for 2% -> 4% of each run, Pallas kernels for 0% -> 0%
where the time goes in v7:
time: 288 us
  waiting for transfers between devices  136 us (47%)
  Pallas kernels  63.4 us (22%)
  other arithmetic  29 us (10%)
  blocking collectives  27.5 us (10%)
  between operations  13.8 us (5%)
  local copies, waits for them, and re-layouts  12.9 us (4%)
  starting transfers between devices  5.56 us (2%)
    psum x1, waiting for transfers between devices, shards(): lax.psum(jnp.stack([jnp.sum(own_scaled, axis=(0, 1)), jnp.sum(own_scaled...  136 us
    pallas_call x1, Pallas kernels, spread(): pl.pallas_call(functools.partial(_spread_kernel, z_count, y_count), out_s...  63.4 us
    all_to_all x1, blocking collectives, shards(): return lax.all_to_all(updated, 'y', split_axis=0, concat_axis=2, tiled=True)  27.5 us
    mul x3, other arithmetic, quick_flux(): return courant * face_value  8.44 us
    slice x2, local copies, waits for them, and re-layouts, shards(): jnp.roll(ext[:-2], 3, axis=1)  5.84 us
  transfers between devices with their start and end apart: 3, of which 1 were waited for; matrix products, arithmetic and copies ran while one was open for 4% of the time, Pallas kernels for 0%

profile of v7, /device:TPU:2, one launch (start us, length us, event | category | flops | bytes accessed | tf_op | source)
XLA Modules:
  0.0 287.7 jit_solution(15617156475327661536)
XLA Ops:
  6.5 0.0 copy-start
  6.5 0.0 all-reduce.3.cloned.1.call-start
  6.5 0.9 convert_element_type.78
  7.4 2.0 broadcast_multiply_fusion
  9.4 0.1 fusion.46
  9.6 1.9 collective-permute-start
  11.5 3.6 %collective-permute-start.1 = (f32[1,36,2,512]{3,2,1,0:T(2,128)S(1)}, f32[1,36,2,512]{3,2,1,0:T(2,128)S(1)}, u32[]{:S(2)}, u32[]{:S(2)}) collective-permute-start(f32[1,36,2,512]{3,2,1,0:T(2,128)S(1)} %get-tuple-element.14), channel_id=1, source_target_pairs={{32,0},{64,32},{96,64},{128,96},{160,128},{192,160},{224,192},{33,... | collective-permute-start | bytes 442376 | tf_op jit(solution)/shard_map/ppermute | solution.py:35
  15.4 0.0 copy-done
  15.5 0.7 dynamic-slice_multiply_fusion
  16.2 0.7 multiply_multiply_fusion
  16.9 2.8 subtract_cosine_fusion
  19.8 0.0 collective-permute-done
  19.8 0.0 collective-permute-done.1
  19.8 0.0 copy-start.3
  19.8 2.6 fusion.9
  22.4 0.0 copy-done.3
  22.4 0.7 fusion.27
  23.1 2.8 fusion.4
  25.9 0.0 copy-start.9
  26.0 0.0 copy-start.10
  26.0 0.7 fusion.25
  26.7 0.1 copy-done.9
  26.8 0.0 copy-done.10
  26.8 3.1 %fusion.16 = f32[1,37,32,512]{3,2,1,0:T(8,128)S(1)} fusion(f32[1,2,32,512]{3,2,1,0:T(8,128)S(1)} %get-tuple-element.12, f32[1,36,32,512]{3,2,1,0:T(8,128)S(1)} %fusion.25, f32[1,2,32,512]{3,2,1,0:T(8,128)S(1)} %get-tuple-element.11, f32[32,512]{1,0:T(8,128)S(1)} %copy-done.9, f32[37]{0:T(128)S(1)} %get-tuple-element.27, f32[32,512]{1,0:T(8,128)S(1)} %copy-done.10, ...), kind=kLoop, calls=%fused_computation.32 | loop fusion | flops 16973824 | bytes 5177644 | tf_op jit(solution)/shard_map/mul | solution.py:65
  29.9 2.8 multiply_reduce_fusion
  32.7 63.4 %shard_map.64 = f32[8,36,8,512]{3,2,1,0:T(8,128)} custom-call(f32[1,36,32,512]{3,2,1,0:T(8,128)} %get-tuple-element.10.floored_ref), custom_call_target="tpu_custom_call" | custom-call | bytes 94371840 | tf_op jit(solution)/shard_map/pallas_call | solution.py:316
  96.1 1.5 slice.165
  97.7 1.7 slice.166
  99.4 4.1 %slice.167 = f32[6,33,8,512]{3,2,1,0:T(8,128)} slice(f32[8,36,8,512]{3,2,1,0:T(8,128)} %shard_map.64), slice={[0:6], [0:33], [0:8], [0:512]} | slice | bytes 6488064 | tf_op jit(solution)/shard_map/jit(_roll_static)/slice | solution.py:386
  103.5 0.0 copy-done.1
  103.5 0.4 slice.164
  103.9 0.5 copy-done.6
  104.4 0.0 copy-done.7
  104.4 0.0 copy-done.8
  104.4 0.7 pad_maximum_fusion.6
  105.1 0.0 all-reduce.3.cloned.1.call-update
  105.1 3.8 %multiply_subtract_fusion = f32[6,36,8,512]{3,2,1,0:T(8,128)S(1)} fusion(f32[6,33,8,512]{3,2,1,0:T(8,128)} %slice.167, f32[6,3,8,512]{3,2,1,0:T(8,128)} %slice.166, f32[6,1,8,512]{3,2,1,0:T(8,128)} %slice.165, f32[6,35,8,512]{3,2,1,0:T(8,128)S(1)} %slice.164, f32[8,36,8,512]{3,2,1,0:T(8,128)} %shard_map.64), kind=kLoop, calls=%fused_computation.2 | loop fusion | flops 7962624 | bytes 14155776 | tf_op jit(solution)/shard_map/sub | solution.py:387
  109.0 0.0 copy-start.2
  109.0 1.7 slice.194
  110.7 0.7 copy-done.2
  111.4 0.2 slice.193
  111.6 135.5 %all-reduce.3.cloned.1.call-done = f32[3,32,512]{2,1,0:T(8,128)} async-done(((f32[3,32,512]{2,1,0:T(8,128)}), f32[3,32,512]{2,1,0:T(8,128)}) %all-reduce.3.cloned.1.call-update) | async-done | bytes 196624 | tf_op jit(solution)/shard_map/psum | solution.py:366
  247.1 0.8 fusion.31
  247.9 0.1 fusion.30
  248.0 0.0 copy-done.4
  248.0 3.7 %fusion.21 = f32[4,36,8,512]{3,2,1,0:T(8,128)S(1)} fusion(f32[6,36,8,512]{3,2,1,0:T(8,128)} %copy-done.2, f32[4,35,8,512]{3,2,1,0:T(8,128)S(1)} %slice.193, f32[4,1,8,512]{3,2,1,0:T(8,128)S(1)} %slice.192, f32[4,3,8,512]{3,2,1,0:T(8,128)S(1)} %slice.195, f32[4,33,8,512]{3,2,1,0:T(8,128)} %slice.194, f32[8,36,8,512]{3,2,1,0:T(8,128)} %shard_map.64, ...), kind=kLoop, calls=%fused_computation.40 | loop fusion | flops 8847360 | bytes 12550160 | tf_op jit(solution)/shard_map/mul | solution.py:395
  251.7 27.5 %all_to_all.18 = f32[4,36,8,512]{3,2,1,0:T(8,128)S(1)} all-to-all(f32[4,36,8,512]{3,2,1,0:T(8,128)S(1)} %fusion.21), channel_id=1, replica_groups=mesh['geo'=8,'z'=8,'y'=4] {'y'}, dimensions={0} | all-to-all | bytes 4718592 | tf_op jit(solution)/shard_map/all_to_all | solution.py:408
  279.2 1.7 copy_bitcast_fusion
  (19 shorter events, 0.3 us)
Async XLA Ops:
  6.5 8.9 %copy-start = (f32[32,512]{1,0:T(8,128)S(1)}, f32[32,512]{1,0:T(8,128)}, u32[]{:S(2)}) copy-start(f32[32,512]{1,0:T(8,128)} %param.11) | copy-start | bytes 196612
  6.5 240.6 %all-reduce.3.cloned.1.call-start = ((), (), s32[]{:S(2)}) async-start(), calls=%async_computation.1 | async-start | bytes 393216 | tf_op jit(solution)/shard_map/psum | solution.py:366
  9.6 10.2 %collective-permute-start = (f32[1,36,2,512]{3,2,1,0:T(2,128)S(1)}, f32[1,36,2,512]{3,2,1,0:T(2,128)S(1)}, u32[]{:S(2)}, u32[]{:S(2)}) collective-permute-start(f32[1,36,2,512]{3,2,1,0:T(2,128)S(1)} %get-tuple-element.13), channel_id=1, source_target_pairs={{0,32},{32,64},{64,96},{96,128},{128,160},{160,192},{192,224},{1,3... | collective-permute-start | bytes 442376 | tf_op jit(solution)/shard_map/ppermute | solution.py:33
  11.5 8.3 %collective-permute-start.1 = (f32[1,36,2,512]{3,2,1,0:T(2,128)S(1)}, f32[1,36,2,512]{3,2,1,0:T(2,128)S(1)}, u32[]{:S(2)}, u32[]{:S(2)}) collective-permute-start(f32[1,36,2,512]{3,2,1,0:T(2,128)S(1)} %get-tuple-element.14), channel_id=1, source_target_pairs={{32,0},{64,32},{96,64},{128,96},{160,128},{192,160},{224,192},{33,... | collective-permute-start | bytes 442376 | tf_op jit(solution)/shard_map/ppermute | solution.py:35
  19.8 2.6 copy-start.3
  25.9 0.8 copy-start.9
  26.0 0.9 copy-start.10
  99.4 4.2 %copy-start.1 = (f32[8,36,8,512]{3,2,1,0:T(8,128)S(1)}, f32[8,36,8,512]{3,2,1,0:T(8,128)}, u32[]{:S(2)}) copy-start(f32[8,36,8,512]{3,2,1,0:T(8,128)} %shard_map.64) | copy-start | bytes 14155780
  103.5 0.8 copy-start.6
  103.5 0.9 copy-start.7
  103.5 0.9 copy-start.8
  109.0 2.4 copy-start.2
  111.4 136.6 %copy-start.4 = (f32[36,8,512]{2,1,0:T(8,128)S(1)}, f32[36,8,512]{2,1,0:T(8,128)}, u32[]{:S(2)}) copy-start(f32[36,8,512]{2,1,0:T(8,128)} %subtract_cosine_fusion) | copy-start | bytes 1769476
  111.4 136.6 %copy-start.5 = (f32[4,8,512]{2,1,0:T(8,128)S(1)}, f32[4,8,512]{2,1,0:T(8,128)}, u32[]{:S(2)}) copy-start(f32[4,8,512]{2,1,0:T(8,128)} %multiply_multiply_fusion) | copy-start | bytes 196612
Sparse Core Ops, SparseCore 0:
  105.3 141.8 all-reduce.2

commit v8 on v6

--- a/solution.py
+++ b/solution.py
@@ -372,7 +372,10 @@
             jnp.sum(scaled / jnp.sqrt(wavenum)[:, None, None, None], axis=(0, 1)),
         ]
     )
-    sums = jnp.sum(z_gather(sums, z_count), axis=0)
+    step = 1
+    while step < z_count:
+        sums = sums + lax.ppermute(sums, "z", [(i, i ^ step) for i in range(z_count)])
+        step *= 2
     energy_sum, first_sum, root_sum = sums[0], sums[1], sums[2]
     energy = energy_sum + EPSILON
     center, plus, minus = ext[1:-1], jnp.roll(ext[2:], -1, axis=1), jnp.roll(ext[:-2], 3, axis=1)

time: 156 us -> 147 us (0.942)
  Pallas kernels: 81.8 us -> 63.4 us
  starting transfers between devices: 5.55 us -> 13.4 us
  waiting for transfers between devices: 0.01 us -> 3.06 us
  local copies, waits for them, and re-layouts: 11 us -> 8.86 us
    pallas_call x1 -> x0, Pallas kernels: 16.5 us -> none  [z_gather(): pl.pallas_call(functools.partial(_z_gather_kernel, z_count), out_shape=ja...]
    ppermute x0 -> x3, starting transfers between devices: none -> 7.82 us  [shards(): lax.ppermute(sums, 'z', [(i, i ^ step) for i in range(z_count)])]
    ppermute x0 -> x3, waiting for transfers between devices: none -> 3.05 us  [shards(): lax.ppermute(sums, 'z', [(i, i ^ step) for i in range(z_count)])]
    mul x1, other arithmetic: 3.67 us -> 1.45 us  [shards(): (sources(point, energy_sum, first_sum, root_sum, radian_freq[:, None, Non...]
    pallas_call x1, Pallas kernels: 65.3 us -> 63.4 us  [spread(): pl.pallas_call(functools.partial(_spread_kernel, z_count, y_count), out_s...]
    reduce_sum x1, other arithmetic: 0.69 us -> 2.34 us  [shards(): jnp.sum(scaled, axis=(0, 1))]
  transfers between devices with their start and end apart: 2 -> 5, of which waited for: 0 -> 2; matrix products, arithmetic and copies ran while one was open for 2% -> 8% of each run, Pallas kernels for 0% -> 0%
where the time goes in v8:
time: 147 us
  Pallas kernels  63.4 us (43%)
  blocking collectives  32 us (22%)
  other arithmetic  25.5 us (17%)
  starting transfers between devices  13.4 us (9%)
  local copies, waits for them, and re-layouts  8.86 us (6%)
  waiting for transfers between devices  3.06 us (2%)
    pallas_call x1, Pallas kernels, spread(): pl.pallas_call(functools.partial(_spread_kernel, z_count, y_count), out_s...  63.4 us
    all_to_all x1, blocking collectives, shards(): return lax.all_to_all(updated, 'y', split_axis=0, concat_axis=2, tiled=True)  32 us
    mul x3, other arithmetic, quick_flux(): return courant * face_value  9.3 us
    ppermute x3, starting transfers between devices, shards(): lax.ppermute(sums, 'z', [(i, i ^ step) for i in range(z_count)])  7.82 us
    ppermute x1, starting transfers between devices, extended(): lax.ppermute(head, axis, [((i + 1) % count, i) for i in range(ends)])  3.64 us
    slice x2, local copies, waits for them, and re-layouts, shards(): jnp.roll(ext[:-2], 3, axis=1)  3.4 us
    ppermute x3, waiting for transfers between devices, shards(): lax.ppermute(sums, 'z', [(i, i ^ step) for i in range(z_count)])  3.05 us
  transfers between devices with their start and end apart: 5, of which 2 were waited for; matrix products, arithmetic and copies ran while one was open for 8% of the time, Pallas kernels for 0%

profile of v8, /device:TPU:2, one launch (start us, length us, event | category | flops | bytes accessed | tf_op | source)
XLA Modules:
  0.0 146.5 jit_solution(9863232622242655266)
XLA Ops:
  0.0 0.8 convert_element_type.84
  0.8 2.0 %broadcast_multiply_fusion = f32[1,36,32,512]{3,2,1,0:T(8,128)S(1)} fusion(f32[1,36,32,512]{3,2,1,0:T(8,128)} %param.8, f32[32,512]{1,0:T(8,128)S(1)} %convert_element_type.84), kind=kLoop, calls=%fused_computation.55 | loop fusion | flops 589824 | bytes 4784128 | tf_op jit(solution)/shard_map/mul | solution.py:344
  2.8 0.8 fusion.46
  3.6 1.9 %collective-permute-start = (f32[1,36,2,512]{3,2,1,0:T(2,128)}, f32[1,36,2,512]{3,2,1,0:T(2,128)S(1)}, u32[]{:S(2)}, u32[]{:S(2)}) collective-permute-start(f32[1,36,2,512]{3,2,1,0:T(2,128)} %get-tuple-element.12), channel_id=1, source_target_pairs={{0,32},{32,64},{64,96},{96,128},{128,160},{160,192},{192,224},{1,3... | collective-permute-start | bytes 442376 | tf_op jit(solution)/shard_map/ppermute | solution.py:33
  5.5 3.6 %collective-permute-start.1 = (f32[1,36,2,512]{3,2,1,0:T(2,128)S(1)}, f32[1,36,2,512]{3,2,1,0:T(2,128)S(1)}, u32[]{:S(2)}, u32[]{:S(2)}) collective-permute-start(f32[1,36,2,512]{3,2,1,0:T(2,128)S(1)} %get-tuple-element.13), channel_id=1, source_target_pairs={{32,0},{64,32},{96,64},{128,96},{160,128},{192,160},{224,192},{33,... | collective-permute-start | bytes 442376 | tf_op jit(solution)/shard_map/ppermute | solution.py:35
  9.2 0.6 abs_multiply_fusion.1
  9.8 0.6 broadcast_compare_fusion
  10.5 0.6 sine_multiply_fusion
  11.1 0.7 dynamic-slice_multiply_fusion
  11.9 0.1 multiply_multiply_fusion
  11.9 1.9 %subtract_cosine_fusion = f32[36,8,512]{2,1,0:T(8,128)S(1)} fusion(f32[8,512]{1,0:T(8,128)S(1)} %get-tuple-element.33, f32[36]{0:T(128)S(1)} %add_multiply_fusion), kind=kLoop, calls=%fused_computation.56 | loop fusion | flops 147456 | bytes 606352 | tf_op jit(solution)/shard_map/cos | solution.py:390
  14.0 0.0 collective-permute-done
  14.0 0.0 collective-permute-done.1
  14.0 0.0 copy-start.1
  14.0 3.4 %fusion.9 = f32[1,36,33,512]{3,2,1,0:T(8,128)S(1)} fusion(f32[1,36,2,512]{3,2,1,0:T(2,128)S(1)} %collective-permute-done.1, f32[1,36,32,512]{3,2,1,0:T(8,128)S(1)} %broadcast_multiply_fusion, f32[1,36,2,512]{3,2,1,0:T(2,128)S(1)} %collective-permute-done, f32[36]{0:T(128)} %get-tuple-element.25, f32[36]{0:T(128)} %get-tuple-element.26, ...), kind=kLoop, calls=%fused_computation.17 | loop fusion | flops 10948608 | bytes 5087700 | tf_op jit(solution)/shard_map/mul | solution.py:65
  17.4 0.0 copy-done.1
  17.4 0.7 fusion.27
  18.2 2.8 %fusion.4 = f32[1,36,32,513]{3,2,1,0:T(8,128)S(1)} fusion(f32[1,36,32,512]{3,2,1,0:T(8,128)S(1)} %fusion.27, f32[36]{0:T(128)S(1)} %get-tuple-element.22, f32[36]{0:T(128)S(1)} %get-tuple-element.23, f32[36]{0:T(128)S(1)} %get-tuple-element.24, pred[36]{0:T(512)(128)(4,1)S(1)} %get-tuple-element.28), kind=kLoop, calls=%fused_computation.11 | loop fusion | flops 8273664 | bytes 4723668 | tf_op jit(solution)/shard_map/mul | solution.py:65
  21.0 0.0 copy-start.2
  21.0 0.0 copy-start.3
  21.0 0.7 fusion.25
  21.7 0.1 copy-done.2
  21.8 0.0 copy-done.3
  21.8 3.1 %fusion.16 = f32[1,37,32,512]{3,2,1,0:T(8,128)S(1)} fusion(f32[1,2,32,512]{3,2,1,0:T(8,128)S(1)} %get-tuple-element.11, f32[1,36,32,512]{3,2,1,0:T(8,128)S(1)} %fusion.25, f32[1,2,32,512]{3,2,1,0:T(8,128)S(1)} %get-tuple-element.10, f32[32,512]{1,0:T(8,128)S(1)} %copy-done.2, f32[37]{0:T(128)S(1)} %get-tuple-element.30, f32[32,512]{1,0:T(8,128)S(1)} %copy-done.3, ...), kind=kLoop, calls=%fused_computation.32 | loop fusion | flops 16973824 | bytes 5177644 | tf_op jit(solution)/shard_map/mul | solution.py:65
  24.9 2.0 %fusion.23.floored_ref = f32[1,36,32,512]{3,2,1,0:T(8,128)} fusion(f32[1,36,32,512]{3,2,1,0:T(8,128)S(1)} %fusion.25, f32[1,37,32,512]{3,2,1,0:T(8,128)S(1)} %fusion.16), kind=kLoop, calls=%fused_computation.43 | loop fusion | flops 1769472 | bytes 9437184 | tf_op jit(solution)/shard_map/max | solution.py:360
  26.9 63.4 %shard_map.64 = f32[8,36,8,512]{3,2,1,0:T(8,128)} custom-call(f32[1,36,32,512]{3,2,1,0:T(8,128)} %fusion.23.floored_ref), custom_call_target="tpu_custom_call" | custom-call | tf_op jit(solution)/shard_map/pallas_call | solution.py:316
  90.3 2.3 %fusion.28 = (f32[8,512]{1,0:T(8,128)S(1)}, f32[8,512]{1,0:T(8,128)S(1)}, f32[8,512]{1,0:T(8,128)S(1)}) fusion(f32[8,36,8,512]{3,2,1,0:T(8,128)} %shard_map.64, f32[4]{0:T(128)S(1)} %get-tuple-element.18, f32[4]{0:T(128)S(1)} %get-tuple-element.19, f32[4]{0:T(128)S(1)} %get-tuple-element.21), kind=kLoop, calls=%fused_computation.54 | loop fusion | flops 3526656 | bytes 2408496 | tf_op jit(solution)/shard_map/reduce_sum | solution.py:370
  92.7 2.6 %collective-permute-start.2 = (f32[3,8,512]{2,1,0:T(8,128)S(1)}, f32[3,8,512]{2,1,0:T(8,128)S(1)}, u32[]{:S(2)}, u32[]{:S(2)}) collective-permute-start(f32[3,8,512]{2,1,0:T(8,128)S(1)} %pad_maximum_fusion.6), channel_id=1, source_target_pairs={{0,4},{4,0},{8,12},{12,8},{16,20},{20,16},{24,28},{28,24},{1,5},{5... | collective-permute-start | bytes 147464 | tf_op jit(solution)/shard_map/ppermute | solution.py:377
  95.3 2.1 %collective-permute-done.2 = f32[3,8,512]{2,1,0:T(8,128)S(1)} collective-permute-done((f32[3,8,512]{2,1,0:T(8,128)S(1)}, f32[3,8,512]{2,1,0:T(8,128)S(1)}, u32[]{:S(2)}, u32[]{:S(2)}) %collective-permute-start.2) | collective-permute-done | bytes 49184 | tf_op jit(solution)/shard_map/ppermute | solution.py:377
  97.3 0.1 collective-permute-start.3
  97.5 0.9 slice.165
  98.4 1.0 slice.166
  99.3 0.0 copy-start
  99.3 2.4 %slice.167 = f32[6,33,8,512]{3,2,1,0:T(8,128)S(1)} slice(f32[8,36,8,512]{3,2,1,0:T(8,128)} %shard_map.64), slice={[0:6], [0:33], [0:8], [0:512]} | slice | bytes 6488064 | tf_op jit(solution)/shard_map/jit(_roll_static)/slice | solution.py:381
  101.8 0.9 copy-done
  102.7 0.5 slice.164
  103.2 0.0 collective-permute-done.3
  103.2 5.2 %collective-permute-start.4 = (f32[3,8,512]{2,1,0:T(8,128)S(1)}, f32[3,8,512]{2,1,0:T(8,128)S(1)}, u32[]{:S(2)}, u32[]{:S(2)}) collective-permute-start(f32[3,8,512]{2,1,0:T(8,128)S(1)} %fusion.47), channel_id=1, source_target_pairs={{0,16},{4,20},{8,24},{12,28},{16,0},{20,4},{24,8},{28,12},{1,17},{... | collective-permute-start | bytes 147464 | tf_op jit(solution)/shard_map/ppermute | solution.py:377
  108.4 1.3 multiply_subtract_fusion
  109.7 0.3 slice.197
  110.0 0.3 slice.196
  110.3 1.0 collective-permute-done.4
  111.3 0.1 fusion.31
  111.4 1.4 fusion.21
  112.9 32.0 %all_to_all.18 = f32[4,36,8,512]{3,2,1,0:T(8,128)S(1)} all-to-all(f32[4,36,8,512]{3,2,1,0:T(8,128)S(1)} %fusion.21), channel_id=1, replica_groups=mesh['geo'=8,'z'=8,'y'=4] {'y'}, dimensions={0} | all-to-all | bytes 4718592 | tf_op jit(solution)/shard_map/all_to_all | solution.py:404
  144.9 1.7 %copy_bitcast_fusion = f32[1,36,32,512]{3,2,1,0:T(8,128)} fusion(f32[4,36,8,512]{3,2,1,0:T(8,128)S(1)} %all_to_all.18), kind=kLoop, calls=%fused_computation.50 | loop fusion | bytes 4718592 | tf_op jit(solution)/shard_map/all_to_all | solution.py:404
  (15 shorter events, 0.2 us)
Async XLA Ops:
  3.6 10.3 %collective-permute-start = (f32[1,36,2,512]{3,2,1,0:T(2,128)}, f32[1,36,2,512]{3,2,1,0:T(2,128)S(1)}, u32[]{:S(2)}, u32[]{:S(2)}) collective-permute-start(f32[1,36,2,512]{3,2,1,0:T(2,128)} %get-tuple-element.12), channel_id=1, source_target_pairs={{0,32},{32,64},{64,96},{96,128},{128,160},{160,192},{192,224},{1,3... | collective-permute-start | bytes 442376 | tf_op jit(solution)/shard_map/ppermute | solution.py:33
  5.5 8.4 %collective-permute-start.1 = (f32[1,36,2,512]{3,2,1,0:T(2,128)S(1)}, f32[1,36,2,512]{3,2,1,0:T(2,128)S(1)}, u32[]{:S(2)}, u32[]{:S(2)}) collective-permute-start(f32[1,36,2,512]{3,2,1,0:T(2,128)S(1)} %get-tuple-element.13), channel_id=1, source_target_pairs={{32,0},{64,32},{96,64},{128,96},{160,128},{192,160},{224,192},{33,... | collective-permute-start | bytes 442376 | tf_op jit(solution)/shard_map/ppermute | solution.py:35
  14.0 3.5 %copy-start.1 = (f32[1,36,32,512]{3,2,1,0:T(8,128)S(1)}, f32[1,36,32,512]{3,2,1,0:T(8,128)}, u32[]{:S(2)}) copy-start(f32[1,36,32,512]{3,2,1,0:T(8,128)} %param.8) | copy-start | bytes 7077892
  21.0 0.8 copy-start.2
  21.0 0.9 copy-start.3
  92.7 4.6 %collective-permute-start.2 = (f32[3,8,512]{2,1,0:T(8,128)S(1)}, f32[3,8,512]{2,1,0:T(8,128)S(1)}, u32[]{:S(2)}, u32[]{:S(2)}) collective-permute-start(f32[3,8,512]{2,1,0:T(8,128)S(1)} %pad_maximum_fusion.6), channel_id=1, source_target_pairs={{0,4},{4,0},{8,12},{12,8},{16,20},{20,16},{24,28},{28,24},{1,5},{5... | collective-permute-start | bytes 147464 | tf_op jit(solution)/shard_map/ppermute | solution.py:377
  97.3 5.8 %collective-permute-start.3 = (f32[3,8,512]{2,1,0:T(8,128)S(1)}, f32[3,8,512]{2,1,0:T(8,128)S(1)}, u32[]{:S(2)}, u32[]{:S(2)}) collective-permute-start(f32[3,8,512]{2,1,0:T(8,128)S(1)} %fusion.43), channel_id=1, source_target_pairs={{0,8},{4,12},{8,0},{12,4},{16,24},{20,28},{24,16},{28,20},{1,9},{5... | collective-permute-start | bytes 147464 | tf_op jit(solution)/shard_map/ppermute | solution.py:377
  99.3 3.3 %copy-start = (f32[8,36,8,512]{3,2,1,0:T(8,128)S(1)}, f32[8,36,8,512]{3,2,1,0:T(8,128)}, u32[]{:S(2)}) copy-start(f32[8,36,8,512]{3,2,1,0:T(8,128)} %shard_map.64) | copy-start | bytes 14155780
  103.2 8.1 %collective-permute-start.4 = (f32[3,8,512]{2,1,0:T(8,128)S(1)}, f32[3,8,512]{2,1,0:T(8,128)S(1)}, u32[]{:S(2)}, u32[]{:S(2)}) collective-permute-start(f32[3,8,512]{2,1,0:T(8,128)S(1)} %fusion.47), channel_id=1, source_target_pairs={{0,16},{4,20},{8,24},{12,28},{16,0},{20,4},{24,8},{28,12},{1,17},{... | collective-permute-start | bytes 147464 | tf_op jit(solution)/shard_map/ppermute | solution.py:377

commit v9 on v8

--- a/solution.py
+++ b/solution.py
@@ -20,6 +20,372 @@
 STEEP_REF = 1.6
 EPSILON = 1e-06
 QUAD_COEF = 100.0
+
+
+def extended(cells, sides, width):
+    for axis, dim in sides:
+        count = lax.axis_size(axis)
+        ends = count - 1
+        head = lax.slice_in_dim(cells, 0, width, axis=dim)
+        tail = lax.slice_in_dim(cells, cells.shape[dim] - width, cells.shape[dim], axis=dim)
+        cells = jnp.concatenate(
+            [
+                lax.ppermute(tail, axis, [(i, (i + 1) % count) for i in range(ends)]),
+                cells,
+                lax.ppermute(head, axis, [((i + 1) % count, i) for i in range(ends)]),
+            ],
+            axis=dim,
+        )
+    return cells
+
+
+def band_table(band_ids):
+    growth_factor = jnp.power(GROWTH, band_ids)
+    radian_freq = 2.0 * math.pi * BASE_FREQ * growth_factor
+    wavenum = radian_freq * radian_freq / GRAVITY
+    return (
+        radian_freq,
+        wavenum,
+        COURANT_TOP / growth_factor,
+        TURN_TOP / growth_factor,
+        SPACING * radian_freq,
+    )
+
+
+def quick_flux(far_left, near_left, near_right, far_right, courant):
+    forward = courant >= 0
+    upwind = jnp.where(forward, far_left, far_right)
+    center = jnp.where(forward, near_left, near_right)
+    downwind = jnp.where(forward, near_right, near_left)
+    face_value = (
+        0.5 * (center + downwind)
+        - 0.5 * jnp.abs(courant) * (downwind - center)
+        - (1.0 - courant * courant) / 6.0 * (downwind - 2.0 * center + upwind)
+    )
+    return courant * face_value
+
+
+def advect(padded, courant, along):
+    face_count = padded.shape[along] - 4
+    shifted = [
+        lax.slice_in_dim(padded, offset, offset + face_count + 1, axis=along) for offset in range(4)
+    ]
+    face_flux = quick_flux(shifted[0], shifted[1], shifted[2], shifted[3], courant)
+    centre_cells = lax.slice_in_dim(padded, 2, 2 + face_count, axis=along)
+    upper_flux = lax.slice_in_dim(face_flux, 1, face_count + 1, axis=along)
+    lower_flux = lax.slice_in_dim(face_flux, 0, face_count, axis=along)
+    return centre_cells - (upper_flux - lower_flux)
+
+
+def quad_delta(center, above, below, energy, dir_axis):
+    plus = jnp.roll(above, -1, axis=dir_axis)
+    minus = jnp.roll(below, 3, axis=dir_axis)
+    return (
+        QUAD_COEF
+        * (center * center * (plus + minus) - 2.0 * center * plus * minus)
+        / (energy * energy)
+    )
+
+
+def quad_term(delta, delta_above, delta_below, dir_axis):
+    return (
+        -2.0 * delta
+        + jnp.roll(delta_below, 1, axis=dir_axis)
+        + jnp.roll(delta_above, -3, axis=dir_axis)
+    )
+
+
+def band_neighbours(values):
+    empty = jnp.zeros((1,) + values.shape[1:], jnp.float32)
+    return (
+        jnp.concatenate([values[1:], empty], axis=0),
+        jnp.concatenate([empty, values[:-1]], axis=0),
+    )
+
+
+def sources(density, energy_sum, first_sum, root_sum, radian_freq, wavenum, cosine, wind_speed):
+    energy = energy_sum + EPSILON
+    mean_sigma = energy / (first_sum + EPSILON)
+    ratio_k = energy / (root_sum + EPSILON)
+    mean_k = ratio_k * ratio_k
+    steepness = energy * mean_k * mean_k / STEEP_REF
+    decay_rate = WHITECAP * mean_sigma * (wavenum / mean_k) * steepness * steepness
+    growth_rate = (
+        WIND_COEF
+        * radian_freq
+        * jnp.maximum(28.0 * USTAR_RATIO * wind_speed * radian_freq / GRAVITY * cosine - 1.0, 0.0)
+    )
+    return density * (1.0 + growth_rate) / (1.0 + decay_rate)
+
+
+def local_sources(point_block, wind_block, wind_angle, angles, dtheta):
+    band_total = point_block.shape[0]
+    band_ids = jnp.arange(band_total).astype(jnp.float32)
+    radian_freq, wavenum, courant, turn_rate, band_spread = band_table(band_ids)
+    scaled = point_block * (band_spread * dtheta)[:, None, None]
+    energy_sum = jnp.sum(scaled, axis=(0, 1))
+    first_sum = jnp.sum(scaled / radian_freq[:, None, None], axis=(0, 1))
+    root_sum = jnp.sum(scaled / jnp.sqrt(wavenum)[:, None, None], axis=(0, 1))
+    energy = energy_sum + EPSILON
+    above, below = band_neighbours(point_block)
+    delta = quad_delta(point_block, above, below, energy, 1)
+    delta_above, delta_below = band_neighbours(delta)
+    extra = quad_term(delta, delta_above, delta_below, 1)
+    cosine = jnp.cos(angles[:, None] - wind_angle[None, :])
+    return (
+        sources(
+            point_block,
+            energy_sum,
+            first_sum,
+            root_sum,
+            radian_freq[:, None, None],
+            wavenum[:, None, None],
+            cosine,
+            wind_block,
+        )
+        + extra
+    )
+
+
+Y_GROUP = 4
+HALO = 2
+
+
+def _z_gather_kernel(z_count, part_ref, gathered_ref, gather_send, gather_recv):
+    geo = lax.axis_index("geo")
+    z_pos = lax.axis_index("z")
+    y_pos = lax.axis_index("y")
+    barrier = pltpu.get_barrier_semaphore()
+    for offset in range(1, z_count):
+        target = lax.rem(z_pos + offset, z_count)
+        pl.semaphore_signal(barrier, inc=1, device_id=(geo, target, y_pos),
+                            device_id_type=pl.DeviceIdType.MESH)
+    pl.semaphore_wait(barrier, z_count - 1)
+    copies = []
+    for offset in range(1, z_count):
+        target = lax.rem(z_pos + offset, z_count)
+        copy = pltpu.make_async_remote_copy(
+            src_ref=part_ref,
+            dst_ref=gathered_ref.at[z_pos],
+            send_sem=gather_send.at[offset],
+            recv_sem=gather_recv.at[offset],
+            device_id=(geo, target, y_pos),
+            device_id_type=pl.DeviceIdType.MESH,
+        )
+        copy.start()
+        copies.append(copy)
+    gathered_ref[z_pos] = part_ref[...]
+    for copy in copies:
+        copy.wait_send()
+        copy.wait_recv()
+
+
+def z_gather(part, z_count):
+    vmem = pl.BlockSpec(memory_space=pltpu.VMEM)
+    return pl.pallas_call(
+        functools.partial(_z_gather_kernel, z_count),
+        out_shape=jax.ShapeDtypeStruct((z_count,) + part.shape, part.dtype),
+        in_specs=[vmem],
+        out_specs=vmem,
+        scratch_shapes=[
+            pltpu.SemaphoreType.DMA((z_count,)),
+            pltpu.SemaphoreType.DMA((z_count,)),
+        ],
+        compiler_params=pltpu.CompilerParams(collective_id=0, has_side_effects=True),
+    )(part)
+
+
+def _spread_kernel(z_count, y_count, floored_ref, ext_ref, relay_ref, y_send, local_sem, slot_recv,
+                   z_send, relay_send, relay_recv, pass_send, pass_recv):
+    geo = lax.axis_index("geo")
+    z_pos = lax.axis_index("z")
+    y_pos = lax.axis_index("y")
+    rows = ext_ref.shape[2]
+    half = relay_ref.shape[1]
+    mesh_id = pl.DeviceIdType.MESH
+    up_y = lax.rem(y_pos + 1, y_count)
+    down_y = lax.rem(y_pos + y_count - 1, y_count)
+    barrier = pltpu.get_barrier_semaphore()
+    for offset in range(1, y_count):
+        pl.semaphore_signal(barrier, inc=1, device_id=(geo, z_pos, lax.rem(y_pos + offset, y_count)),
+                            device_id_type=mesh_id)
+    for step in (1, z_count - 1):
+        pl.semaphore_signal(barrier, inc=1, device_id=(geo, lax.rem(z_pos + step, z_count), y_pos),
+                            device_id_type=mesh_id)
+    pl.semaphore_wait(barrier, y_count + 1)
+
+    def quarter(target):
+        return floored_ref.at[0, :, pl.ds(pl.multiple_of(target * rows, rows), rows)]
+
+    own_slot = HALO + y_pos
+    sends = []
+    for offset in (1, y_count - 1):
+        target = lax.rem(y_pos + offset, y_count)
+        copy = pltpu.make_async_remote_copy(
+            src_ref=quarter(target),
+            dst_ref=ext_ref.at[own_slot],
+            send_sem=y_send.at[offset],
+            recv_sem=slot_recv.at[own_slot],
+            device_id=(geo, z_pos, target),
+            device_id_type=mesh_id,
+        )
+        copy.start()
+        sends.append(copy)
+    far = lax.rem(y_pos + 2, y_count)
+    for side, via in ((0, up_y), (1, down_y)):
+        copy = pltpu.make_async_remote_copy(
+            src_ref=quarter(far).at[pl.ds(side * half, half)],
+            dst_ref=relay_ref.at[side],
+            send_sem=relay_send.at[side],
+            recv_sem=relay_recv.at[side],
+            device_id=(geo, z_pos, via),
+            device_id_type=mesh_id,
+        )
+        copy.start()
+        sends.append(copy)
+    local = pltpu.make_async_copy(quarter(y_pos), ext_ref.at[own_slot], local_sem.at[0])
+    local.start()
+
+    @pl.when(z_pos == 0)
+    def _():
+        ext_ref[pl.ds(0, HALO)] = jnp.zeros((HALO,) + ext_ref.shape[1:], ext_ref.dtype)
+
+    @pl.when(z_pos == z_count - 1)
+    def _():
+        ext_ref[pl.ds(HALO + y_count, HALO)] = jnp.zeros((HALO,) + ext_ref.shape[1:], ext_ref.dtype)
+
+    passes = []
+    for side, origin, onward in ((0, down_y, up_y), (1, up_y, down_y)):
+        relay_in = pltpu.make_async_remote_copy(
+            src_ref=relay_ref.at[side],
+            dst_ref=relay_ref.at[side],
+            send_sem=relay_send.at[side],
+            recv_sem=relay_recv.at[side],
+            device_id=(geo, z_pos, onward),
+            device_id_type=mesh_id,
+        )
+        relay_in.wait_recv()
+        onward_copy = pltpu.make_async_remote_copy(
+            src_ref=relay_ref.at[side],
+            dst_ref=ext_ref.at[HALO + origin, pl.ds(side * half, half)],
+            send_sem=pass_send.at[side],
+            recv_sem=pass_recv.at[side],
+            device_id=(geo, z_pos, onward),
+            device_id_type=mesh_id,
+        )
+        onward_copy.start()
+        passes.append(onward_copy)
+
+    def forward(slot, dst_slot, target_z):
+        return pltpu.make_async_remote_copy(
+            src_ref=ext_ref.at[slot],
+            dst_ref=ext_ref.at[dst_slot],
+            send_sem=z_send.at[slot - HALO],
+            recv_sem=slot_recv.at[dst_slot],
+            device_id=(geo, target_z, y_pos),
+            device_id_type=mesh_id,
+        )
+
+    forwards = []
+    for band in range(y_count):
+        slot = HALO + band
+        distance = lax.rem(band - y_pos + y_count, y_count)
+        arrival = pltpu.make_async_remote_copy(
+            src_ref=ext_ref.at[slot],
+            dst_ref=ext_ref.at[slot],
+            send_sem=y_send.at[0],
+            recv_sem=slot_recv.at[slot],
+            device_id=(geo, z_pos, up_y),
+            device_id_type=mesh_id,
+        )
+        relayed = [
+            pltpu.make_async_remote_copy(
+                src_ref=ext_ref.at[slot, pl.ds(side * half, half)],
+                dst_ref=ext_ref.at[slot, pl.ds(side * half, half)],
+                send_sem=pass_send.at[side],
+                recv_sem=pass_recv.at[side],
+                device_id=(geo, z_pos, up_y),
+                device_id_type=mesh_id,
+            )
+            for side in (0, 1)
+        ]
+
+        @pl.when(distance == 0)
+        def _():
+            local.wait()
+
+        @pl.when((distance == 1) | (distance == y_count - 1))
+        def _():
+            arrival.wait_recv()
+
+        @pl.when(distance == 2)
+        def _():
+            for copy in relayed:
+                copy.wait_recv()
+
+        if band < HALO:
+            fwd = forward(slot, slot + y_count, z_pos - 1)
+            live = z_pos > 0
+        elif band >= y_count - HALO:
+            fwd = forward(slot, slot - y_count, z_pos + 1)
+            live = z_pos < z_count - 1
+        else:
+            continue
+
+        @pl.when(live)
+        def _():
+            fwd.start()
+
+        forwards.append((fwd, live))
+    for copy in sends + passes:
+        copy.wait_send()
+    for fwd, live in forwards:
+
+        @pl.when(live)
+        def _():
+            fwd.wait_send()
+
+    for slot, live in ((0, z_pos > 0), (1, z_pos > 0),
+                       (HALO + y_count, z_pos < z_count - 1), (HALO + y_count + 1, z_pos < z_count - 1)):
+        incoming = pltpu.make_async_remote_copy(
+            src_ref=ext_ref.at[slot],
+            dst_ref=ext_ref.at[slot],
+            send_sem=z_send.at[0],
+            recv_sem=slot_recv.at[slot],
+            device_id=(geo, lax.rem(z_pos + 1, z_count), y_pos),
+            device_id_type=mesh_id,
+        )
+
+        @pl.when(live)
+        def _():
+            incoming.wait_recv()
+
+
+def spread(floored, z_count, y_count):
+    _, dirs, rows, cols = floored.shape
+    part_rows = rows // y_count
+    vmem = pl.BlockSpec(memory_space=pltpu.VMEM)
+    slots = y_count + 2 * HALO
+    half = dirs // 2
+    assert 2 * half == dirs
+    return pl.pallas_call(
+        functools.partial(_spread_kernel, z_count, y_count),
+        out_shape=jax.ShapeDtypeStruct((slots, dirs, part_rows, cols), floored.dtype),
+        in_specs=[vmem],
+        out_specs=vmem,
+        scratch_shapes=[
+            pltpu.VMEM((2, half, part_rows, cols), floored.dtype),
+            pltpu.SemaphoreType.DMA((y_count,)),
+            pltpu.SemaphoreType.DMA((1,)),
+            pltpu.SemaphoreType.DMA((slots,)),
+            pltpu.SemaphoreType.DMA((y_count,)),
+            pltpu.SemaphoreType.DMA((2,)),
+            pltpu.SemaphoreType.DMA((2,)),
+            pltpu.SemaphoreType.DMA((2,)),
+            pltpu.SemaphoreType.DMA((2,)),
+        ],
+        compiler_params=pltpu.CompilerParams(collective_id=1, has_side_effects=True),
+    )(floored)
 
 
 def extended(cells, sides, width):

time: 147 us -> 147 us (level)
  no operation moved by 1% of the time
where the time goes in v9:
time: 147 us
  Pallas kernels  63.4 us (43%)
  blocking collectives  32 us (22%)
  other arithmetic  25.5 us (17%)
  starting transfers between devices  13.4 us (9%)
  local copies, waits for them, and re-layouts  8.86 us (6%)
  waiting for transfers between devices  3.06 us (2%)
    pallas_call x1, Pallas kernels, spread(): pl.pallas_call(functools.partial(_spread_kernel, z_count, y_count), out_s...  63.4 us
    all_to_all x1, blocking collectives, shards(): return lax.all_to_all(updated, 'y', split_axis=0, concat_axis=2, tiled=True)  32 us
    mul x3, other arithmetic, quick_flux(): return courant * face_value  9.3 us
    ppermute x3, starting transfers between devices, shards(): lax.ppermute(sums, 'z', [(i, i ^ step) for i in range(z_count)])  7.82 us
    ppermute x1, starting transfers between devices, extended(): lax.ppermute(head, axis, [((i + 1) % count, i) for i in range(ends)])  3.64 us
    slice x2, local copies, waits for them, and re-layouts, shards(): jnp.roll(ext[:-2], 3, axis=1)  3.4 us
    ppermute x3, waiting for transfers between devices, shards(): lax.ppermute(sums, 'z', [(i, i ^ step) for i in range(z_count)])  3.05 us
  transfers between devices with their start and end apart: 5, of which 2 were waited for; matrix products, arithmetic and copies ran while one was open for 8% of the time, Pallas kernels for 0%

profile of v9, /device:TPU:2, one launch (start us, length us, event | category | flops | bytes accessed | tf_op | source)
XLA Modules:
  0.0 146.5 jit_solution(9863232622242655266)
XLA Ops:
  0.0 0.8 convert_element_type.84
  0.8 2.0 %broadcast_multiply_fusion = f32[1,36,32,512]{3,2,1,0:T(8,128)S(1)} fusion(f32[1,36,32,512]{3,2,1,0:T(8,128)} %param.8, f32[32,512]{1,0:T(8,128)S(1)} %convert_element_type.84), kind=kLoop, calls=%fused_computation.55 | loop fusion | flops 589824 | bytes 4784128 | tf_op jit(solution)/shard_map/mul | solution.py:710
  2.8 0.8 fusion.46
  3.6 1.9 %collective-permute-start = (f32[1,36,2,512]{3,2,1,0:T(2,128)}, f32[1,36,2,512]{3,2,1,0:T(2,128)S(1)}, u32[]{:S(2)}, u32[]{:S(2)}) collective-permute-start(f32[1,36,2,512]{3,2,1,0:T(2,128)} %get-tuple-element.12), channel_id=1, source_target_pairs={{0,32},{32,64},{64,96},{96,128},{128,160},{160,192},{192,224},{1,3... | collective-permute-start | bytes 442376 | tf_op jit(solution)/shard_map/ppermute | solution.py:399
  5.5 3.6 %collective-permute-start.1 = (f32[1,36,2,512]{3,2,1,0:T(2,128)S(1)}, f32[1,36,2,512]{3,2,1,0:T(2,128)S(1)}, u32[]{:S(2)}, u32[]{:S(2)}) collective-permute-start(f32[1,36,2,512]{3,2,1,0:T(2,128)S(1)} %get-tuple-element.13), channel_id=1, source_target_pairs={{32,0},{64,32},{96,64},{128,96},{160,128},{192,160},{224,192},{33,... | collective-permute-start | bytes 442376 | tf_op jit(solution)/shard_map/ppermute | solution.py:401
  9.2 0.6 abs_multiply_fusion.1
  9.8 0.6 broadcast_compare_fusion
  10.5 0.6 sine_multiply_fusion
  11.1 0.7 dynamic-slice_multiply_fusion
  11.9 0.1 multiply_multiply_fusion
  11.9 1.9 %subtract_cosine_fusion = f32[36,8,512]{2,1,0:T(8,128)S(1)} fusion(f32[8,512]{1,0:T(8,128)S(1)} %get-tuple-element.33, f32[36]{0:T(128)S(1)} %add_multiply_fusion), kind=kLoop, calls=%fused_computation.56 | loop fusion | flops 147456 | bytes 606352 | tf_op jit(solution)/shard_map/cos | solution.py:756
  14.0 0.0 collective-permute-done
  14.0 0.0 collective-permute-done.1
  14.0 0.0 copy-start.1
  14.0 3.4 %fusion.9 = f32[1,36,33,512]{3,2,1,0:T(8,128)S(1)} fusion(f32[1,36,2,512]{3,2,1,0:T(2,128)S(1)} %collective-permute-done.1, f32[1,36,32,512]{3,2,1,0:T(8,128)S(1)} %broadcast_multiply_fusion, f32[1,36,2,512]{3,2,1,0:T(2,128)S(1)} %collective-permute-done, f32[36]{0:T(128)} %get-tuple-element.25, f32[36]{0:T(128)} %get-tuple-element.26, ...), kind=kLoop, calls=%fused_computation.17 | loop fusion | flops 10948608 | bytes 5087700 | tf_op jit(solution)/shard_map/mul | solution.py:431
  17.4 0.0 copy-done.1
  17.4 0.7 fusion.27
  18.2 2.8 %fusion.4 = f32[1,36,32,513]{3,2,1,0:T(8,128)S(1)} fusion(f32[1,36,32,512]{3,2,1,0:T(8,128)S(1)} %fusion.27, f32[36]{0:T(128)S(1)} %get-tuple-element.22, f32[36]{0:T(128)S(1)} %get-tuple-element.23, f32[36]{0:T(128)S(1)} %get-tuple-element.24, pred[36]{0:T(512)(128)(4,1)S(1)} %get-tuple-element.28), kind=kLoop, calls=%fused_computation.11 | loop fusion | flops 8273664 | bytes 4723668 | tf_op jit(solution)/shard_map/mul | solution.py:431
  21.0 0.0 copy-start.2
  21.0 0.0 copy-start.3
  21.0 0.7 fusion.25
  21.7 0.1 copy-done.2
  21.8 0.0 copy-done.3
  21.8 3.1 %fusion.16 = f32[1,37,32,512]{3,2,1,0:T(8,128)S(1)} fusion(f32[1,2,32,512]{3,2,1,0:T(8,128)S(1)} %get-tuple-element.11, f32[1,36,32,512]{3,2,1,0:T(8,128)S(1)} %fusion.25, f32[1,2,32,512]{3,2,1,0:T(8,128)S(1)} %get-tuple-element.10, f32[32,512]{1,0:T(8,128)S(1)} %copy-done.2, f32[37]{0:T(128)S(1)} %get-tuple-element.30, f32[32,512]{1,0:T(8,128)S(1)} %copy-done.3, ...), kind=kLoop, calls=%fused_computation.32 | loop fusion | flops 16973824 | bytes 5177644 | tf_op jit(solution)/shard_map/mul | solution.py:431
  24.9 2.0 %fusion.23.floored_ref = f32[1,36,32,512]{3,2,1,0:T(8,128)} fusion(f32[1,36,32,512]{3,2,1,0:T(8,128)S(1)} %fusion.25, f32[1,37,32,512]{3,2,1,0:T(8,128)S(1)} %fusion.16), kind=kLoop, calls=%fused_computation.43 | loop fusion | flops 1769472 | bytes 9437184 | tf_op jit(solution)/shard_map/max | solution.py:726
  26.9 63.4 %shard_map.64 = f32[8,36,8,512]{3,2,1,0:T(8,128)} custom-call(f32[1,36,32,512]{3,2,1,0:T(8,128)} %fusion.23.floored_ref), custom_call_target="tpu_custom_call" | custom-call | tf_op jit(solution)/shard_map/pallas_call | solution.py:682
  90.3 2.3 %fusion.28 = (f32[8,512]{1,0:T(8,128)S(1)}, f32[8,512]{1,0:T(8,128)S(1)}, f32[8,512]{1,0:T(8,128)S(1)}) fusion(f32[8,36,8,512]{3,2,1,0:T(8,128)} %shard_map.64, f32[4]{0:T(128)S(1)} %get-tuple-element.18, f32[4]{0:T(128)S(1)} %get-tuple-element.19, f32[4]{0:T(128)S(1)} %get-tuple-element.21), kind=kLoop, calls=%fused_computation.54 | loop fusion | flops 3526656 | bytes 2408496 | tf_op jit(solution)/shard_map/reduce_sum | solution.py:736
  92.7 2.6 %collective-permute-start.2 = (f32[3,8,512]{2,1,0:T(8,128)S(1)}, f32[3,8,512]{2,1,0:T(8,128)S(1)}, u32[]{:S(2)}, u32[]{:S(2)}) collective-permute-start(f32[3,8,512]{2,1,0:T(8,128)S(1)} %pad_maximum_fusion.6), channel_id=1, source_target_pairs={{0,4},{4,0},{8,12},{12,8},{16,20},{20,16},{24,28},{28,24},{1,5},{5... | collective-permute-start | bytes 147464 | tf_op jit(solution)/shard_map/ppermute | solution.py:743
  95.3 2.1 %collective-permute-done.2 = f32[3,8,512]{2,1,0:T(8,128)S(1)} collective-permute-done((f32[3,8,512]{2,1,0:T(8,128)S(1)}, f32[3,8,512]{2,1,0:T(8,128)S(1)}, u32[]{:S(2)}, u32[]{:S(2)}) %collective-permute-start.2) | collective-permute-done | bytes 49184 | tf_op jit(solution)/shard_map/ppermute | solution.py:743
  97.3 0.1 collective-permute-start.3
  97.5 0.9 slice.165
  98.4 1.0 slice.166
  99.3 0.0 copy-start
  99.3 2.4 %slice.167 = f32[6,33,8,512]{3,2,1,0:T(8,128)S(1)} slice(f32[8,36,8,512]{3,2,1,0:T(8,128)} %shard_map.64), slice={[0:6], [0:33], [0:8], [0:512]} | slice | bytes 6488064 | tf_op jit(solution)/shard_map/jit(_roll_static)/slice | solution.py:747
  101.8 0.9 copy-done
  102.7 0.5 slice.164
  103.2 0.0 collective-permute-done.3
  103.2 5.2 %collective-permute-start.4 = (f32[3,8,512]{2,1,0:T(8,128)S(1)}, f32[3,8,512]{2,1,0:T(8,128)S(1)}, u32[]{:S(2)}, u32[]{:S(2)}) collective-permute-start(f32[3,8,512]{2,1,0:T(8,128)S(1)} %fusion.47), channel_id=1, source_target_pairs={{0,16},{4,20},{8,24},{12,28},{16,0},{20,4},{24,8},{28,12},{1,17},{... | collective-permute-start | bytes 147464 | tf_op jit(solution)/shard_map/ppermute | solution.py:743
  108.4 1.3 multiply_subtract_fusion
  109.7 0.3 slice.197
  110.0 0.3 slice.196
  110.3 1.0 collective-permute-done.4
  111.3 0.1 fusion.31
  111.4 1.4 fusion.21
  112.9 32.0 %all_to_all.18 = f32[4,36,8,512]{3,2,1,0:T(8,128)S(1)} all-to-all(f32[4,36,8,512]{3,2,1,0:T(8,128)S(1)} %fusion.21), channel_id=1, replica_groups=mesh['geo'=8,'z'=8,'y'=4] {'y'}, dimensions={0} | all-to-all | bytes 4718592 | tf_op jit(solution)/shard_map/all_to_all | solution.py:770
  144.9 1.7 %copy_bitcast_fusion = f32[1,36,32,512]{3,2,1,0:T(8,128)} fusion(f32[4,36,8,512]{3,2,1,0:T(8,128)S(1)} %all_to_all.18), kind=kLoop, calls=%fused_computation.50 | loop fusion | bytes 4718592 | tf_op jit(solution)/shard_map/all_to_all | solution.py:770
  (15 shorter events, 0.2 us)
Async XLA Ops:
  3.6 10.3 %collective-permute-start = (f32[1,36,2,512]{3,2,1,0:T(2,128)}, f32[1,36,2,512]{3,2,1,0:T(2,128)S(1)}, u32[]{:S(2)}, u32[]{:S(2)}) collective-permute-start(f32[1,36,2,512]{3,2,1,0:T(2,128)} %get-tuple-element.12), channel_id=1, source_target_pairs={{0,32},{32,64},{64,96},{96,128},{128,160},{160,192},{192,224},{1,3... | collective-permute-start | bytes 442376 | tf_op jit(solution)/shard_map/ppermute | solution.py:399
  5.5 8.4 %collective-permute-start.1 = (f32[1,36,2,512]{3,2,1,0:T(2,128)S(1)}, f32[1,36,2,512]{3,2,1,0:T(2,128)S(1)}, u32[]{:S(2)}, u32[]{:S(2)}) collective-permute-start(f32[1,36,2,512]{3,2,1,0:T(2,128)S(1)} %get-tuple-element.13), channel_id=1, source_target_pairs={{32,0},{64,32},{96,64},{128,96},{160,128},{192,160},{224,192},{33,... | collective-permute-start | bytes 442376 | tf_op jit(solution)/shard_map/ppermute | solution.py:401
  14.0 3.5 %copy-start.1 = (f32[1,36,32,512]{3,2,1,0:T(8,128)S(1)}, f32[1,36,32,512]{3,2,1,0:T(8,128)}, u32[]{:S(2)}) copy-start(f32[1,36,32,512]{3,2,1,0:T(8,128)} %param.8) | copy-start | bytes 7077892
  21.0 0.8 copy-start.2
  21.0 0.9 copy-start.3
  92.7 4.6 %collective-permute-start.2 = (f32[3,8,512]{2,1,0:T(8,128)S(1)}, f32[3,8,512]{2,1,0:T(8,128)S(1)}, u32[]{:S(2)}, u32[]{:S(2)}) collective-permute-start(f32[3,8,512]{2,1,0:T(8,128)S(1)} %pad_maximum_fusion.6), channel_id=1, source_target_pairs={{0,4},{4,0},{8,12},{12,8},{16,20},{20,16},{24,28},{28,24},{1,5},{5... | collective-permute-start | bytes 147464 | tf_op jit(solution)/shard_map/ppermute | solution.py:743
  97.3 5.8 %collective-permute-start.3 = (f32[3,8,512]{2,1,0:T(8,128)S(1)}, f32[3,8,512]{2,1,0:T(8,128)S(1)}, u32[]{:S(2)}, u32[]{:S(2)}) collective-permute-start(f32[3,8,512]{2,1,0:T(8,128)S(1)} %fusion.43), channel_id=1, source_target_pairs={{0,8},{4,12},{8,0},{12,4},{16,24},{20,28},{24,16},{28,20},{1,9},{5... | collective-permute-start | bytes 147464 | tf_op jit(solution)/shard_map/ppermute | solution.py:743
  99.3 3.3 %copy-start = (f32[8,36,8,512]{3,2,1,0:T(8,128)S(1)}, f32[8,36,8,512]{3,2,1,0:T(8,128)}, u32[]{:S(2)}) copy-start(f32[8,36,8,512]{3,2,1,0:T(8,128)} %shard_map.64) | copy-start | bytes 14155780
  103.2 8.1 %collective-permute-start.4 = (f32[3,8,512]{2,1,0:T(8,128)S(1)}, f32[3,8,512]{2,1,0:T(8,128)S(1)}, u32[]{:S(2)}, u32[]{:S(2)}) collective-permute-start(f32[3,8,512]{2,1,0:T(8,128)S(1)} %fusion.47), channel_id=1, source_target_pairs={{0,16},{4,20},{8,24},{12,28},{16,0},{20,4},{24,8},{28,12},{1,17},{... | collective-permute-start | bytes 147464 | tf_op jit(solution)/shard_map/ppermute | solution.py:743

commit v10 on v9

--- a/solution.py
+++ b/solution.py
@@ -20,6 +20,328 @@
 STEEP_REF = 1.6
 EPSILON = 1e-06
 QUAD_COEF = 100.0
+
+
+def extended(cells, sides, width):
+    for axis, dim in sides:
+        count = lax.axis_size(axis)
+        ends = count - 1
+        head = lax.slice_in_dim(cells, 0, width, axis=dim)
+        tail = lax.slice_in_dim(cells, cells.shape[dim] - width, cells.shape[dim], axis=dim)
+        cells = jnp.concatenate(
+            [
+                lax.ppermute(tail, axis, [(i, (i + 1) % count) for i in range(ends)]),
+                cells,
+                lax.ppermute(head, axis, [((i + 1) % count, i) for i in range(ends)]),
+            ],
+            axis=dim,
+        )
+    return cells
+
+
+def band_table(band_ids):
+    growth_factor = jnp.power(GROWTH, band_ids)
+    radian_freq = 2.0 * math.pi * BASE_FREQ * growth_factor
+    wavenum = radian_freq * radian_freq / GRAVITY
+    return (
+        radian_freq,
+        wavenum,
+        COURANT_TOP / growth_factor,
+        TURN_TOP / growth_factor,
+        SPACING * radian_freq,
+    )
+
+
+def quick_flux(far_left, near_left, near_right, far_right, courant):
+    forward = courant >= 0
+    upwind = jnp.where(forward, far_left, far_right)
+    center = jnp.where(forward, near_left, near_right)
+    downwind = jnp.where(forward, near_right, near_left)
+    face_value = (
+        0.5 * (center + downwind)
+        - 0.5 * jnp.abs(courant) * (downwind - center)
+        - (1.0 - courant * courant) / 6.0 * (downwind - 2.0 * center + upwind)
+    )
+    return courant * face_value
+
+
+def advect(padded, courant, along):
+    face_count = padded.shape[along] - 4
+    shifted = [
+        lax.slice_in_dim(padded, offset, offset + face_count + 1, axis=along) for offset in range(4)
+    ]
+    face_flux = quick_flux(shifted[0], shifted[1], shifted[2], shifted[3], courant)
+    centre_cells = lax.slice_in_dim(padded, 2, 2 + face_count, axis=along)
+    upper_flux = lax.slice_in_dim(face_flux, 1, face_count + 1, axis=along)
+    lower_flux = lax.slice_in_dim(face_flux, 0, face_count, axis=along)
+    return centre_cells - (upper_flux - lower_flux)
+
+
+def quad_delta(center, above, below, energy, dir_axis):
+    plus = jnp.roll(above, -1, axis=dir_axis)
+    minus = jnp.roll(below, 3, axis=dir_axis)
+    return (
+        QUAD_COEF
+        * (center * center * (plus + minus) - 2.0 * center * plus * minus)
+        / (energy * energy)
+    )
+
+
+def quad_term(delta, delta_above, delta_below, dir_axis):
+    return (
+        -2.0 * delta
+        + jnp.roll(delta_below, 1, axis=dir_axis)
+        + jnp.roll(delta_above, -3, axis=dir_axis)
+    )
+
+
+def band_neighbours(values):
+    empty = jnp.zeros((1,) + values.shape[1:], jnp.float32)
+    return (
+        jnp.concatenate([values[1:], empty], axis=0),
+        jnp.concatenate([empty, values[:-1]], axis=0),
+    )
+
+
+def sources(density, energy_sum, first_sum, root_sum, radian_freq, wavenum, cosine, wind_speed):
+    energy = energy_sum + EPSILON
+    mean_sigma = energy / (first_sum + EPSILON)
+    ratio_k = energy / (root_sum + EPSILON)
+    mean_k = ratio_k * ratio_k
+    steepness = energy * mean_k * mean_k / STEEP_REF
+    decay_rate = WHITECAP * mean_sigma * (wavenum / mean_k) * steepness * steepness
+    growth_rate = (
+        WIND_COEF
+        * radian_freq
+        * jnp.maximum(28.0 * USTAR_RATIO * wind_speed * radian_freq / GRAVITY * cosine - 1.0, 0.0)
+    )
+    return density * (1.0 + growth_rate) / (1.0 + decay_rate)
+
+
+def local_sources(point_block, wind_block, wind_angle, angles, dtheta):
+    band_total = point_block.shape[0]
+    band_ids = jnp.arange(band_total).astype(jnp.float32)
+    radian_freq, wavenum, courant, turn_rate, band_spread = band_table(band_ids)
+    scaled = point_block * (band_spread * dtheta)[:, None, None]
+    energy_sum = jnp.sum(scaled, axis=(0, 1))
+    first_sum = jnp.sum(scaled / radian_freq[:, None, None], axis=(0, 1))
+    root_sum = jnp.sum(scaled / jnp.sqrt(wavenum)[:, None, None], axis=(0, 1))
+    energy = energy_sum + EPSILON
+    above, below = band_neighbours(point_block)
+    delta = quad_delta(point_block, above, below, energy, 1)
+    delta_above, delta_below = band_neighbours(delta)
+    extra = quad_term(delta, delta_above, delta_below, 1)
+    cosine = jnp.cos(angles[:, None] - wind_angle[None, :])
+    return (
+        sources(
+            point_block,
+            energy_sum,
+            first_sum,
+            root_sum,
+            radian_freq[:, None, None],
+            wavenum[:, None, None],
+            cosine,
+            wind_block,
+        )
+        + extra
+    )
+
+
+Y_GROUP = 4
+HALO = 2
+SPREAD_CHUNKS = 4
+
+
+def _z_gather_kernel(z_count, part_ref, gathered_ref, gather_send, gather_recv):
+    geo = lax.axis_index("geo")
+    z_pos = lax.axis_index("z")
+    y_pos = lax.axis_index("y")
+    barrier = pltpu.get_barrier_semaphore()
+    for offset in range(1, z_count):
+        target = lax.rem(z_pos + offset, z_count)
+        pl.semaphore_signal(barrier, inc=1, device_id=(geo, target, y_pos),
+                            device_id_type=pl.DeviceIdType.MESH)
+    pl.semaphore_wait(barrier, z_count - 1)
+    copies = []
+    for offset in range(1, z_count):
+        target = lax.rem(z_pos + offset, z_count)
+        copy = pltpu.make_async_remote_copy(
+            src_ref=part_ref,
+            dst_ref=gathered_ref.at[z_pos],
+            send_sem=gather_send.at[offset],
+            recv_sem=gather_recv.at[offset],
+            device_id=(geo, target, y_pos),
+            device_id_type=pl.DeviceIdType.MESH,
+        )
+        copy.start()
+        copies.append(copy)
+    gathered_ref[z_pos] = part_ref[...]
+    for copy in copies:
+        copy.wait_send()
+        copy.wait_recv()
+
+
+def z_gather(part, z_count):
+    vmem = pl.BlockSpec(memory_space=pltpu.VMEM)
+    return pl.pallas_call(
+        functools.partial(_z_gather_kernel, z_count),
+        out_shape=jax.ShapeDtypeStruct((z_count,) + part.shape, part.dtype),
+        in_specs=[vmem],
+        out_specs=vmem,
+        scratch_shapes=[
+            pltpu.SemaphoreType.DMA((z_count,)),
+            pltpu.SemaphoreType.DMA((z_count,)),
+        ],
+        compiler_params=pltpu.CompilerParams(collective_id=0, has_side_effects=True),
+    )(part)
+
+
+def _spread_kernel(z_count, y_count, chunks, floored_ref, ext_ref, y_send, local_sem, slot_recv, z_send):
+    geo = lax.axis_index("geo")
+    z_pos = lax.axis_index("z")
+    y_pos = lax.axis_index("y")
+    rows = ext_ref.shape[2]
+    width = ext_ref.shape[1] // chunks
+    mesh_id = pl.DeviceIdType.MESH
+    barrier = pltpu.get_barrier_semaphore()
+    for offset in range(1, y_count):
+        pl.semaphore_signal(barrier, inc=1, device_id=(geo, z_pos, lax.rem(y_pos + offset, y_count)),
+                            device_id_type=mesh_id)
+    for step in (1, z_count - 1):
+        pl.semaphore_signal(barrier, inc=1, device_id=(geo, lax.rem(z_pos + step, z_count), y_pos),
+                            device_id_type=mesh_id)
+    pl.semaphore_wait(barrier, y_count + 1)
+
+    own_slot = HALO + y_pos
+
+    def planes(chunk):
+        return pl.ds(chunk * width, width)
+
+    def y_sends(chunk):
+        copies = []
+        for offset in range(1, y_count):
+            target = lax.rem(y_pos + offset, y_count)
+            copies.append(pltpu.make_async_remote_copy(
+                src_ref=floored_ref.at[0, planes(chunk), pl.ds(pl.multiple_of(target * rows, rows), rows)],
+                dst_ref=ext_ref.at[own_slot, planes(chunk)],
+                send_sem=y_send.at[offset * chunks + chunk],
+                recv_sem=slot_recv.at[own_slot * chunks + chunk],
+                device_id=(geo, z_pos, target),
+                device_id_type=mesh_id,
+            ))
+        copies.append(pltpu.make_async_copy(
+            floored_ref.at[0, planes(chunk), pl.ds(pl.multiple_of(y_pos * rows, rows), rows)],
+            ext_ref.at[own_slot, planes(chunk)],
+            local_sem.at[chunk],
+        ))
+        return copies
+
+    def forward(slot, dst_slot, target_z, chunk):
+        return pltpu.make_async_remote_copy(
+            src_ref=ext_ref.at[slot, planes(chunk)],
+            dst_ref=ext_ref.at[dst_slot, planes(chunk)],
+            send_sem=z_send.at[(slot - HALO) * chunks + chunk],
+            recv_sem=slot_recv.at[dst_slot * chunks + chunk],
+            device_id=(geo, target_z, y_pos),
+            device_id_type=mesh_id,
+        )
+
+    @pl.when(z_pos == 0)
+    def _():
+        ext_ref[pl.ds(0, HALO)] = jnp.zeros((HALO,) + ext_ref.shape[1:], ext_ref.dtype)
+
+    @pl.when(z_pos == z_count - 1)
+    def _():
+        ext_ref[pl.ds(HALO + y_count, HALO)] = jnp.zeros((HALO,) + ext_ref.shape[1:], ext_ref.dtype)
+
+    pending = y_sends(0)
+    for copy in pending:
+        copy.start()
+    forwards = []
+    for chunk in range(chunks):
+        for band in range(y_count):
+            slot = HALO + band
+            arrival = pltpu.make_async_remote_copy(
+                src_ref=ext_ref.at[slot, planes(chunk)],
+                dst_ref=ext_ref.at[slot, planes(chunk)],
+                send_sem=y_send.at[chunk],
+                recv_sem=slot_recv.at[slot * chunks + chunk],
+                device_id=(geo, z_pos, lax.rem(y_pos + 1, y_count)),
+                device_id_type=mesh_id,
+            )
+            local = pending[-1]
+
+            @pl.when(y_pos == band)
+            def _():
+                local.wait()
+
+            @pl.when(y_pos != band)
+            def _():
+                arrival.wait_recv()
+
+            if band < HALO:
+                fwd = forward(slot, slot + y_count, z_pos - 1, chunk)
+                live = z_pos > 0
+            elif band >= y_count - HALO:
+                fwd = forward(slot, slot - y_count, z_pos + 1, chunk)
+                live = z_pos < z_count - 1
+            else:
+                continue
+
+            @pl.when(live)
+            def _():
+                fwd.start()
+
+            forwards.append((fwd, live))
+        for copy in pending[:-1]:
+            copy.wait_send()
+        if chunk + 1 < chunks:
+            pending = y_sends(chunk + 1)
+            for copy in pending:
+                copy.start()
+    for fwd, live in forwards:
+
+        @pl.when(live)
+        def _():
+            fwd.wait_send()
+
+    for chunk in range(chunks):
+        for slot, live in ((0, z_pos > 0), (1, z_pos > 0),
+                           (HALO + y_count, z_pos < z_count - 1), (HALO + y_count + 1, z_pos < z_count - 1)):
+            incoming = pltpu.make_async_remote_copy(
+                src_ref=ext_ref.at[slot, planes(chunk)],
+                dst_ref=ext_ref.at[slot, planes(chunk)],
+                send_sem=z_send.at[chunk],
+                recv_sem=slot_recv.at[slot * chunks + chunk],
+                device_id=(geo, lax.rem(z_pos + 1, z_count), y_pos),
+                device_id_type=mesh_id,
+            )
+
+            @pl.when(live)
+            def _():
+                incoming.wait_recv()
+
+
+def spread(floored, z_count, y_count):
+    _, dirs, rows, cols = floored.shape
+    part_rows = rows // y_count
+    chunks = SPREAD_CHUNKS
+    assert dirs % chunks == 0
+    vmem = pl.BlockSpec(memory_space=pltpu.VMEM)
+    slots = y_count + 2 * HALO
+    return pl.pallas_call(
+        functools.partial(_spread_kernel, z_count, y_count, chunks),
+        out_shape=jax.ShapeDtypeStruct((slots, dirs, part_rows, cols), floored.dtype),
+        in_specs=[vmem],
+        out_specs=vmem,
+        scratch_shapes=[
+            pltpu.SemaphoreType.DMA((y_count * chunks,)),
+            pltpu.SemaphoreType.DMA((chunks,)),
+            pltpu.SemaphoreType.DMA((slots * chunks,)),
+            pltpu.SemaphoreType.DMA((y_count * chunks,)),
+        ],
+        compiler_params=pltpu.CompilerParams(collective_id=1, has_side_effects=True),
+    )(floored)
 
 
 def extended(cells, sides, width):

time: 147 us -> 147 us (level)
  no operation moved by 1% of the time
where the time goes in v10:
time: 147 us
  Pallas kernels  63.4 us (43%)
  blocking collectives  32 us (22%)
  other arithmetic  25.5 us (17%)
  starting transfers between devices  13.4 us (9%)
  local copies, waits for them, and re-layouts  8.86 us (6%)
  waiting for transfers between devices  3.06 us (2%)
    pallas_call x1, Pallas kernels, spread(): pl.pallas_call(functools.partial(_spread_kernel, z_count, y_count), out_s...  63.4 us
    all_to_all x1, blocking collectives, shards(): return lax.all_to_all(updated, 'y', split_axis=0, concat_axis=2, tiled=True)  32 us
    mul x3, other arithmetic, quick_flux(): return courant * face_value  9.3 us
    ppermute x3, starting transfers between devices, shards(): lax.ppermute(sums, 'z', [(i, i ^ step) for i in range(z_count)])  7.82 us
    ppermute x1, starting transfers between devices, extended(): lax.ppermute(head, axis, [((i + 1) % count, i) for i in range(ends)])  3.64 us
    slice x2, local copies, waits for them, and re-layouts, shards(): jnp.roll(ext[:-2], 3, axis=1)  3.4 us
    ppermute x3, waiting for transfers between devices, shards(): lax.ppermute(sums, 'z', [(i, i ^ step) for i in range(z_count)])  3.05 us
  transfers between devices with their start and end apart: 5, of which 2 were waited for; matrix products, arithmetic and copies ran while one was open for 8% of the time, Pallas kernels for 0%

profile of v10, /device:TPU:2, one launch (start us, length us, event | category | flops | bytes accessed | tf_op | source)
XLA Modules:
  0.0 146.5 jit_solution(9863232622242655266)
XLA Ops:
  0.0 0.8 convert_element_type.84
  0.8 2.0 %broadcast_multiply_fusion = f32[1,36,32,512]{3,2,1,0:T(8,128)S(1)} fusion(f32[1,36,32,512]{3,2,1,0:T(8,128)} %param.8, f32[32,512]{1,0:T(8,128)S(1)} %convert_element_type.84), kind=kLoop, calls=%fused_computation.55 | loop fusion | flops 589824 | bytes 4784128 | tf_op jit(solution)/shard_map/mul | solution.py:1032
  2.8 0.8 fusion.46
  3.6 1.9 %collective-permute-start = (f32[1,36,2,512]{3,2,1,0:T(2,128)}, f32[1,36,2,512]{3,2,1,0:T(2,128)S(1)}, u32[]{:S(2)}, u32[]{:S(2)}) collective-permute-start(f32[1,36,2,512]{3,2,1,0:T(2,128)} %get-tuple-element.12), channel_id=1, source_target_pairs={{0,32},{32,64},{64,96},{96,128},{128,160},{160,192},{192,224},{1,3... | collective-permute-start | bytes 442376 | tf_op jit(solution)/shard_map/ppermute | solution.py:721
  5.5 3.6 %collective-permute-start.1 = (f32[1,36,2,512]{3,2,1,0:T(2,128)S(1)}, f32[1,36,2,512]{3,2,1,0:T(2,128)S(1)}, u32[]{:S(2)}, u32[]{:S(2)}) collective-permute-start(f32[1,36,2,512]{3,2,1,0:T(2,128)S(1)} %get-tuple-element.13), channel_id=1, source_target_pairs={{32,0},{64,32},{96,64},{128,96},{160,128},{192,160},{224,192},{33,... | collective-permute-start | bytes 442376 | tf_op jit(solution)/shard_map/ppermute | solution.py:723
  9.2 0.6 abs_multiply_fusion.1
  9.8 0.6 broadcast_compare_fusion
  10.5 0.6 sine_multiply_fusion
  11.1 0.7 dynamic-slice_multiply_fusion
  11.9 0.1 multiply_multiply_fusion
  11.9 1.9 %subtract_cosine_fusion = f32[36,8,512]{2,1,0:T(8,128)S(1)} fusion(f32[8,512]{1,0:T(8,128)S(1)} %get-tuple-element.33, f32[36]{0:T(128)S(1)} %add_multiply_fusion), kind=kLoop, calls=%fused_computation.56 | loop fusion | flops 147456 | bytes 606352 | tf_op jit(solution)/shard_map/cos | solution.py:1078
  14.0 0.0 collective-permute-done
  14.0 0.0 collective-permute-done.1
  14.0 0.0 copy-start.1
  14.0 3.4 %fusion.9 = f32[1,36,33,512]{3,2,1,0:T(8,128)S(1)} fusion(f32[1,36,2,512]{3,2,1,0:T(2,128)S(1)} %collective-permute-done.1, f32[1,36,32,512]{3,2,1,0:T(8,128)S(1)} %broadcast_multiply_fusion, f32[1,36,2,512]{3,2,1,0:T(2,128)S(1)} %collective-permute-done, f32[36]{0:T(128)} %get-tuple-element.25, f32[36]{0:T(128)} %get-tuple-element.26, ...), kind=kLoop, calls=%fused_computation.17 | loop fusion | flops 10948608 | bytes 5087700 | tf_op jit(solution)/shard_map/mul | solution.py:753
  17.4 0.0 copy-done.1
  17.4 0.7 fusion.27
  18.2 2.8 %fusion.4 = f32[1,36,32,513]{3,2,1,0:T(8,128)S(1)} fusion(f32[1,36,32,512]{3,2,1,0:T(8,128)S(1)} %fusion.27, f32[36]{0:T(128)S(1)} %get-tuple-element.22, f32[36]{0:T(128)S(1)} %get-tuple-element.23, f32[36]{0:T(128)S(1)} %get-tuple-element.24, pred[36]{0:T(512)(128)(4,1)S(1)} %get-tuple-element.28), kind=kLoop, calls=%fused_computation.11 | loop fusion | flops 8273664 | bytes 4723668 | tf_op jit(solution)/shard_map/mul | solution.py:753
  21.0 0.0 copy-start.2
  21.0 0.0 copy-start.3
  21.0 0.7 fusion.25
  21.7 0.1 copy-done.2
  21.8 0.0 copy-done.3
  21.8 3.1 %fusion.16 = f32[1,37,32,512]{3,2,1,0:T(8,128)S(1)} fusion(f32[1,2,32,512]{3,2,1,0:T(8,128)S(1)} %get-tuple-element.11, f32[1,36,32,512]{3,2,1,0:T(8,128)S(1)} %fusion.25, f32[1,2,32,512]{3,2,1,0:T(8,128)S(1)} %get-tuple-element.10, f32[32,512]{1,0:T(8,128)S(1)} %copy-done.2, f32[37]{0:T(128)S(1)} %get-tuple-element.30, f32[32,512]{1,0:T(8,128)S(1)} %copy-done.3, ...), kind=kLoop, calls=%fused_computation.32 | loop fusion | flops 16973824 | bytes 5177644 | tf_op jit(solution)/shard_map/mul | solution.py:753
  24.9 2.0 %fusion.23.floored_ref = f32[1,36,32,512]{3,2,1,0:T(8,128)} fusion(f32[1,36,32,512]{3,2,1,0:T(8,128)S(1)} %fusion.25, f32[1,37,32,512]{3,2,1,0:T(8,128)S(1)} %fusion.16), kind=kLoop, calls=%fused_computation.43 | loop fusion | flops 1769472 | bytes 9437184 | tf_op jit(solution)/shard_map/max | solution.py:1048
  26.9 63.4 %shard_map.64 = f32[8,36,8,512]{3,2,1,0:T(8,128)} custom-call(f32[1,36,32,512]{3,2,1,0:T(8,128)} %fusion.23.floored_ref), custom_call_target="tpu_custom_call" | custom-call | tf_op jit(solution)/shard_map/pallas_call | solution.py:1004
  90.3 2.3 %fusion.28 = (f32[8,512]{1,0:T(8,128)S(1)}, f32[8,512]{1,0:T(8,128)S(1)}, f32[8,512]{1,0:T(8,128)S(1)}) fusion(f32[8,36,8,512]{3,2,1,0:T(8,128)} %shard_map.64, f32[4]{0:T(128)S(1)} %get-tuple-element.18, f32[4]{0:T(128)S(1)} %get-tuple-element.19, f32[4]{0:T(128)S(1)} %get-tuple-element.21), kind=kLoop, calls=%fused_computation.54 | loop fusion | flops 3526656 | bytes 2408496 | tf_op jit(solution)/shard_map/reduce_sum | solution.py:1058
  92.7 2.6 %collective-permute-start.2 = (f32[3,8,512]{2,1,0:T(8,128)S(1)}, f32[3,8,512]{2,1,0:T(8,128)S(1)}, u32[]{:S(2)}, u32[]{:S(2)}) collective-permute-start(f32[3,8,512]{2,1,0:T(8,128)S(1)} %pad_maximum_fusion.6), channel_id=1, source_target_pairs={{0,4},{4,0},{8,12},{12,8},{16,20},{20,16},{24,28},{28,24},{1,5},{5... | collective-permute-start | bytes 147464 | tf_op jit(solution)/shard_map/ppermute | solution.py:1065
  95.3 2.1 %collective-permute-done.2 = f32[3,8,512]{2,1,0:T(8,128)S(1)} collective-permute-done((f32[3,8,512]{2,1,0:T(8,128)S(1)}, f32[3,8,512]{2,1,0:T(8,128)S(1)}, u32[]{:S(2)}, u32[]{:S(2)}) %collective-permute-start.2) | collective-permute-done | bytes 49184 | tf_op jit(solution)/shard_map/ppermute | solution.py:1065
  97.3 0.1 collective-permute-start.3
  97.5 0.9 slice.165
  98.4 1.0 slice.166
  99.3 0.0 copy-start
  99.3 2.4 %slice.167 = f32[6,33,8,512]{3,2,1,0:T(8,128)S(1)} slice(f32[8,36,8,512]{3,2,1,0:T(8,128)} %shard_map.64), slice={[0:6], [0:33], [0:8], [0:512]} | slice | bytes 6488064 | tf_op jit(solution)/shard_map/jit(_roll_static)/slice | solution.py:1069
  101.8 0.9 copy-done
  102.7 0.5 slice.164
  103.2 0.0 collective-permute-done.3
  103.2 5.2 %collective-permute-start.4 = (f32[3,8,512]{2,1,0:T(8,128)S(1)}, f32[3,8,512]{2,1,0:T(8,128)S(1)}, u32[]{:S(2)}, u32[]{:S(2)}) collective-permute-start(f32[3,8,512]{2,1,0:T(8,128)S(1)} %fusion.47), channel_id=1, source_target_pairs={{0,16},{4,20},{8,24},{12,28},{16,0},{20,4},{24,8},{28,12},{1,17},{... | collective-permute-start | bytes 147464 | tf_op jit(solution)/shard_map/ppermute | solution.py:1065
  108.4 1.3 multiply_subtract_fusion
  109.7 0.3 slice.197
  110.0 0.3 slice.196
  110.3 1.0 collective-permute-done.4
  111.3 0.1 fusion.31
  111.4 1.4 fusion.21
  112.9 32.0 %all_to_all.18 = f32[4,36,8,512]{3,2,1,0:T(8,128)S(1)} all-to-all(f32[4,36,8,512]{3,2,1,0:T(8,128)S(1)} %fusion.21), channel_id=1, replica_groups=mesh['geo'=8,'z'=8,'y'=4] {'y'}, dimensions={0} | all-to-all | bytes 4718592 | tf_op jit(solution)/shard_map/all_to_all | solution.py:1092
  144.9 1.7 %copy_bitcast_fusion = f32[1,36,32,512]{3,2,1,0:T(8,128)} fusion(f32[4,36,8,512]{3,2,1,0:T(8,128)S(1)} %all_to_all.18), kind=kLoop, calls=%fused_computation.50 | loop fusion | bytes 4718592 | tf_op jit(solution)/shard_map/all_to_all | solution.py:1092
  (15 shorter events, 0.2 us)
Async XLA Ops:
  3.6 10.3 %collective-permute-start = (f32[1,36,2,512]{3,2,1,0:T(2,128)}, f32[1,36,2,512]{3,2,1,0:T(2,128)S(1)}, u32[]{:S(2)}, u32[]{:S(2)}) collective-permute-start(f32[1,36,2,512]{3,2,1,0:T(2,128)} %get-tuple-element.12), channel_id=1, source_target_pairs={{0,32},{32,64},{64,96},{96,128},{128,160},{160,192},{192,224},{1,3... | collective-permute-start | bytes 442376 | tf_op jit(solution)/shard_map/ppermute | solution.py:721
  5.5 8.4 %collective-permute-start.1 = (f32[1,36,2,512]{3,2,1,0:T(2,128)S(1)}, f32[1,36,2,512]{3,2,1,0:T(2,128)S(1)}, u32[]{:S(2)}, u32[]{:S(2)}) collective-permute-start(f32[1,36,2,512]{3,2,1,0:T(2,128)S(1)} %get-tuple-element.13), channel_id=1, source_target_pairs={{32,0},{64,32},{96,64},{128,96},{160,128},{192,160},{224,192},{33,... | collective-permute-start | bytes 442376 | tf_op jit(solution)/shard_map/ppermute | solution.py:723
  14.0 3.5 %copy-start.1 = (f32[1,36,32,512]{3,2,1,0:T(8,128)S(1)}, f32[1,36,32,512]{3,2,1,0:T(8,128)}, u32[]{:S(2)}) copy-start(f32[1,36,32,512]{3,2,1,0:T(8,128)} %param.8) | copy-start | bytes 7077892
  21.0 0.8 copy-start.2
  21.0 0.9 copy-start.3
  92.7 4.6 %collective-permute-start.2 = (f32[3,8,512]{2,1,0:T(8,128)S(1)}, f32[3,8,512]{2,1,0:T(8,128)S(1)}, u32[]{:S(2)}, u32[]{:S(2)}) collective-permute-start(f32[3,8,512]{2,1,0:T(8,128)S(1)} %pad_maximum_fusion.6), channel_id=1, source_target_pairs={{0,4},{4,0},{8,12},{12,8},{16,20},{20,16},{24,28},{28,24},{1,5},{5... | collective-permute-start | bytes 147464 | tf_op jit(solution)/shard_map/ppermute | solution.py:1065
  97.3 5.8 %collective-permute-start.3 = (f32[3,8,512]{2,1,0:T(8,128)S(1)}, f32[3,8,512]{2,1,0:T(8,128)S(1)}, u32[]{:S(2)}, u32[]{:S(2)}) collective-permute-start(f32[3,8,512]{2,1,0:T(8,128)S(1)} %fusion.43), channel_id=1, source_target_pairs={{0,8},{4,12},{8,0},{12,4},{16,24},{20,28},{24,16},{28,20},{1,9},{5... | collective-permute-start | bytes 147464 | tf_op jit(solution)/shard_map/ppermute | solution.py:1065
  99.3 3.3 %copy-start = (f32[8,36,8,512]{3,2,1,0:T(8,128)S(1)}, f32[8,36,8,512]{3,2,1,0:T(8,128)}, u32[]{:S(2)}) copy-start(f32[8,36,8,512]{3,2,1,0:T(8,128)} %shard_map.64) | copy-start | bytes 14155780
  103.2 8.1 %collective-permute-start.4 = (f32[3,8,512]{2,1,0:T(8,128)S(1)}, f32[3,8,512]{2,1,0:T(8,128)S(1)}, u32[]{:S(2)}, u32[]{:S(2)}) collective-permute-start(f32[3,8,512]{2,1,0:T(8,128)S(1)} %fusion.47), channel_id=1, source_target_pairs={{0,16},{4,20},{8,24},{12,28},{16,0},{20,4},{24,8},{28,12},{1,17},{... | collective-permute-start | bytes 147464 | tf_op jit(solution)/shard_map/ppermute | solution.py:1065

commit v11 on v10

--- a/solution.py
+++ b/solution.py
@@ -1060,10 +1060,7 @@
             jnp.sum(scaled / jnp.sqrt(wavenum)[:, None, None, None], axis=(0, 1)),
         ]
     )
-    step = 1
-    while step < z_count:
-        sums = sums + lax.ppermute(sums, "z", [(i, i ^ step) for i in range(z_count)])
-        step *= 2
+    sums = lax.psum(sums, "z")
     energy_sum, first_sum, root_sum = sums[0], sums[1], sums[2]
     energy = energy_sum + EPSILON
     center, plus, minus = ext[1:-1], jnp.roll(ext[2:], -1, axis=1), jnp.roll(ext[:-2], 3, axis=1)

time: 147 us -> 163 us (1.11)
  blocking collectives: 32 us -> 55.5 us
  starting transfers between devices: 13.4 us -> 5.55 us
  waiting for transfers between devices: 3.06 us -> 0.01 us
  local copies, waits for them, and re-layouts: 8.86 us -> 11 us
  Pallas kernels: 63.4 us -> 65.3 us
    psum x0 -> x1, blocking collectives: none -> 30.1 us  [shards(): sums = lax.psum(sums, 'z')]
    ppermute x3 -> x0, starting transfers between devices: 7.82 us -> none  [shards(): lax.ppermute(sums, 'z', [(i, i ^ step) for i in range(z_count)])]
    all_to_all x1, blocking collectives: 32 us -> 25.4 us  [shards(): return lax.all_to_all(updated, 'y', split_axis=0, concat_axis=2, tiled=True)]
    ppermute x3 -> x0, waiting for transfers between devices: 3.05 us -> none  [shards(): lax.ppermute(sums, 'z', [(i, i ^ step) for i in range(z_count)])]
    mul x1, other arithmetic: 1.45 us -> 3.67 us  [shards(): (sources(point, energy_sum, first_sum, root_sum, radian_freq[:, None, Non...]
    pallas_call x1, Pallas kernels: 63.4 us -> 65.3 us  [spread(): pl.pallas_call(functools.partial(_spread_kernel, z_count, y_count), out_s...]
    reduce_sum x1, other arithmetic: 2.34 us -> 0.69 us  [shards(): jnp.sum(scaled, axis=(0, 1))]
  transfers between devices with their start and end apart: 5 -> 2, of which waited for: 2 -> 0; matrix products, arithmetic and copies ran while one was open for 8% -> 2% of each run, Pallas kernels for 0% -> 0%
where the time goes in v11:
time: 163 us; the launch traced here: 162 us
  Pallas kernels  65.3 us (40%)
  blocking collectives  55.5 us (34%)
  other arithmetic  24.6 us (15%)
  local copies, waits for them, and re-layouts  11 us (7%)
  starting transfers between devices  5.55 us (3%)
    pallas_call x1, Pallas kernels, spread(): pl.pallas_call(functools.partial(_spread_kernel, z_count, y_count), out_s...  65.3 us
    psum x1, blocking collectives, shards(): sums = lax.psum(sums, 'z')  30.1 us
    all_to_all x1, blocking collectives, shards(): return lax.all_to_all(updated, 'y', split_axis=0, concat_axis=2, tiled=True)  25.4 us
    mul x3, other arithmetic, quick_flux(): return courant * face_value  9.44 us
    mul x1, other arithmetic, shards(): (sources(point, energy_sum, first_sum, root_sum, radian_freq[:, None, Non...  3.67 us
    ppermute x1, starting transfers between devices, extended(): lax.ppermute(head, axis, [((i + 1) % count, i) for i in range(ends)])  3.64 us
    slice x2, local copies, waits for them, and re-layouts, shards(): jnp.roll(ext[:-2], 3, axis=1)  3.38 us
  transfers between devices with their start and end apart: 2, of which 0 were waited for; matrix products, arithmetic and copies ran while one was open for 2% of the time, Pallas kernels for 0%

profile of v11, /device:TPU:2, one launch (start us, length us, event | category | flops | bytes accessed | tf_op | source)
XLA Modules:
  0.0 162.3 jit_solution(6264373270705687029)
XLA Ops:
  0.0 0.0 copy-start
  0.0 0.9 convert_element_type.84
  0.9 2.0 %broadcast_multiply_fusion = f32[1,36,32,512]{3,2,1,0:T(8,128)S(1)} fusion(f32[1,36,32,512]{3,2,1,0:T(8,128)} %param.8, f32[32,512]{1,0:T(8,128)S(1)} %convert_element_type.84), kind=kLoop, calls=%fused_computation.55 | loop fusion | flops 589824 | bytes 4784128 | tf_op jit(solution)/shard_map/mul | solution.py:1032
  2.9 0.8 fusion.45
  3.7 1.9 %collective-permute-start = (f32[1,36,2,512]{3,2,1,0:T(2,128)}, f32[1,36,2,512]{3,2,1,0:T(2,128)S(1)}, u32[]{:S(2)}, u32[]{:S(2)}) collective-permute-start(f32[1,36,2,512]{3,2,1,0:T(2,128)} %get-tuple-element.12), channel_id=1, source_target_pairs={{0,32},{32,64},{64,96},{96,128},{128,160},{160,192},{192,224},{1,3... | collective-permute-start | bytes 442376 | tf_op jit(solution)/shard_map/ppermute | solution.py:721
  5.6 3.6 %collective-permute-start.1 = (f32[1,36,2,512]{3,2,1,0:T(2,128)}, f32[1,36,2,512]{3,2,1,0:T(2,128)}, u32[]{:S(2)}, u32[]{:S(2)}) collective-permute-start(f32[1,36,2,512]{3,2,1,0:T(2,128)} %get-tuple-element.13), channel_id=1, source_target_pairs={{32,0},{64,32},{96,64},{128,96},{160,128},{192,160},{224,192},{33,... | collective-permute-start | bytes 442376 | tf_op jit(solution)/shard_map/ppermute | solution.py:723
  9.6 0.0 copy-done
  9.6 0.7 dynamic-slice_multiply_fusion
  10.4 0.1 multiply_multiply_fusion
  10.4 1.9 %subtract_cosine_fusion = f32[36,8,512]{2,1,0:T(8,128)S(1)} fusion(f32[8,512]{1,0:T(8,128)S(1)} %constant_dynamic-slice_fusion.1, f32[36]{0:T(128)S(1)} %add_multiply_fusion), kind=kLoop, calls=%fused_computation.56 | loop fusion | flops 147456 | bytes 606352 | tf_op jit(solution)/shard_map/cos | solution.py:1075
  12.5 0.0 collective-permute-done
  12.5 0.0 collective-permute-done.1
  12.5 0.0 copy-start.3
  12.5 3.6 %fusion.9 = f32[1,36,33,512]{3,2,1,0:T(8,128)S(1)} fusion(f32[1,36,2,512]{3,2,1,0:T(2,128)} %collective-permute-done.1, f32[1,36,32,512]{3,2,1,0:T(8,128)S(1)} %broadcast_multiply_fusion, f32[1,36,2,512]{3,2,1,0:T(2,128)S(1)} %collective-permute-done, f32[36]{0:T(128)S(1)} %get-tuple-element.25, f32[36]{0:T(128)S(1)} %get-tuple-element.26, ...), kind=kLoop, calls=%fused_computation.17 | loop fusion | flops 10948608 | bytes 5087700 | tf_op jit(solution)/shard_map/mul | solution.py:753
  16.1 0.0 copy-done.3
  16.1 0.7 fusion.27
  16.8 2.8 %fusion.4 = f32[1,36,32,513]{3,2,1,0:T(8,128)S(1)} fusion(f32[1,36,32,512]{3,2,1,0:T(8,128)S(1)} %fusion.27, f32[36]{0:T(128)S(1)} %get-tuple-element.22, f32[36]{0:T(128)S(1)} %get-tuple-element.23, f32[36]{0:T(128)S(1)} %get-tuple-element.24, pred[36]{0:T(512)(128)(4,1)S(1)} %get-tuple-element.28), kind=kLoop, calls=%fused_computation.11 | loop fusion | flops 8273664 | bytes 4723668 | tf_op jit(solution)/shard_map/mul | solution.py:753
  19.6 0.0 copy-start.4
  19.6 0.0 copy-start.5
  19.6 0.7 fusion.25
  20.3 0.1 copy-done.4
  20.4 0.0 copy-done.5
  20.5 3.1 %fusion.16 = f32[1,37,32,512]{3,2,1,0:T(8,128)S(1)} fusion(f32[1,2,32,512]{3,2,1,0:T(8,128)S(1)} %get-tuple-element.11, f32[1,36,32,512]{3,2,1,0:T(8,128)S(1)} %fusion.25, f32[1,2,32,512]{3,2,1,0:T(8,128)S(1)} %get-tuple-element.10, f32[32,512]{1,0:T(8,128)S(1)} %copy-done.4, f32[37]{0:T(128)S(1)} %get-tuple-element.30, f32[32,512]{1,0:T(8,128)S(1)} %copy-done.5, ...), kind=kLoop, calls=%fused_computation.32 | loop fusion | flops 16973824 | bytes 5177644 | tf_op jit(solution)/shard_map/mul | solution.py:753
  23.6 2.0 %fusion.23.floored_ref = f32[1,36,32,512]{3,2,1,0:T(8,128)} fusion(f32[1,36,32,512]{3,2,1,0:T(8,128)S(1)} %fusion.25, f32[1,37,32,512]{3,2,1,0:T(8,128)S(1)} %fusion.16), kind=kLoop, calls=%fused_computation.43 | loop fusion | flops 1769472 | bytes 9437184 | tf_op jit(solution)/shard_map/max | solution.py:1048
  25.6 65.3 %shard_map.64 = f32[8,36,8,512]{3,2,1,0:T(8,128)} custom-call(f32[1,36,32,512]{3,2,1,0:T(8,128)} %fusion.23.floored_ref), custom_call_target="tpu_custom_call" | custom-call | tf_op jit(solution)/shard_map/pallas_call | solution.py:1004
  90.9 0.9 slice.165
  91.8 1.0 slice.166
  92.8 0.0 copy-start.1
  92.8 2.4 %slice.167 = f32[6,33,8,512]{3,2,1,0:T(8,128)S(1)} slice(f32[8,36,8,512]{3,2,1,0:T(8,128)} %shard_map.64), slice={[0:6], [0:33], [0:8], [0:512]} | slice | bytes 6488064 | tf_op jit(solution)/shard_map/jit(_roll_static)/slice | solution.py:1066
  95.2 0.9 copy-done.1
  96.1 0.5 slice.164
  96.6 1.4 multiply_subtract_fusion
  98.0 0.0 copy-start.2
  98.0 1.7 %slice.197 = f32[4,33,8,512]{3,2,1,0:T(8,128)} slice(f32[6,36,8,512]{3,2,1,0:T(8,128)S(1)} %multiply_subtract_fusion), slice={[2:6], [3:36], [0:8], [0:512]} | slice | bytes 4325376 | tf_op jit(solution)/shard_map/jit(_roll_static)/slice | solution.py:1069
  99.8 0.7 copy-done.2
  100.4 0.2 slice.196
  100.7 0.7 fusion.28
  101.4 30.1 %psum.7 = f32[3,8,512]{2,1,0:T(8,128)S(1)} all-reduce(f32[3,8,512]{2,1,0:T(8,128)S(1)} %pad_maximum_fusion.6), channel_id=1, replica_groups=mesh['geo'=8,'z'=8,'y'=4] {'z'}, use_global_device_ids=true, to_apply=%region_3.4 | all-reduce | flops 12288 | bytes 98304 | tf_op jit(solution)/shard_map/psum | solution.py:1063
  131.5 0.1 fusion.31
  131.6 3.7 %fusion.21 = f32[4,36,8,512]{3,2,1,0:T(8,128)S(1)} fusion(f32[6,36,8,512]{3,2,1,0:T(8,128)} %copy-done.2, f32[4,35,8,512]{3,2,1,0:T(8,128)S(1)} %slice.196, f32[4,1,8,512]{3,2,1,0:T(8,128)S(1)} %slice.195, f32[4,3,8,512]{3,2,1,0:T(8,128)S(1)} %slice.198, f32[4,33,8,512]{3,2,1,0:T(8,128)} %slice.197, f32[8,36,8,512]{3,2,1,0:T(8,128)} %shard_map.64, ...), kind=kLoop, calls=%fused_computation.40 | loop fusion | flops 8847360 | bytes 12550160 | tf_op jit(solution)/shard_map/mul | solution.py:1076
  135.3 25.4 %all_to_all.18 = f32[4,36,8,512]{3,2,1,0:T(8,128)S(1)} all-to-all(f32[4,36,8,512]{3,2,1,0:T(8,128)S(1)} %fusion.21), channel_id=1, replica_groups=mesh['geo'=8,'z'=8,'y'=4] {'y'}, dimensions={0} | all-to-all | bytes 4718592 | tf_op jit(solution)/shard_map/all_to_all | solution.py:1089
  160.7 1.7 %copy_bitcast_fusion = f32[1,36,32,512]{3,2,1,0:T(8,128)} fusion(f32[4,36,8,512]{3,2,1,0:T(8,128)S(1)} %all_to_all.18), kind=kLoop, calls=%fused_computation.50 | loop fusion | bytes 4718592 | tf_op jit(solution)/shard_map/all_to_all | solution.py:1089
  (15 shorter events, 0.4 us)
Async XLA Ops:
  0.0 9.6 %copy-start = (f32[32,512]{1,0:T(8,128)S(1)}, f32[32,512]{1,0:T(8,128)}, u32[]{:S(2)}) copy-start(f32[32,512]{1,0:T(8,128)} %param.11) | copy-start | bytes 196612
  3.7 8.7 %collective-permute-start = (f32[1,36,2,512]{3,2,1,0:T(2,128)}, f32[1,36,2,512]{3,2,1,0:T(2,128)S(1)}, u32[]{:S(2)}, u32[]{:S(2)}) collective-permute-start(f32[1,36,2,512]{3,2,1,0:T(2,128)} %get-tuple-element.12), channel_id=1, source_target_pairs={{0,32},{32,64},{64,96},{96,128},{128,160},{160,192},{192,224},{1,3... | collective-permute-start | bytes 442376 | tf_op jit(solution)/shard_map/ppermute | solution.py:721
  5.6 6.8 %collective-permute-start.1 = (f32[1,36,2,512]{3,2,1,0:T(2,128)}, f32[1,36,2,512]{3,2,1,0:T(2,128)}, u32[]{:S(2)}, u32[]{:S(2)}) collective-permute-start(f32[1,36,2,512]{3,2,1,0:T(2,128)} %get-tuple-element.13), channel_id=1, source_target_pairs={{32,0},{64,32},{96,64},{128,96},{160,128},{192,160},{224,192},{33,... | collective-permute-start | bytes 442376 | tf_op jit(solution)/shard_map/ppermute | solution.py:723
  12.5 3.6 %copy-start.3 = (f32[1,36,32,512]{3,2,1,0:T(8,128)S(1)}, f32[1,36,32,512]{3,2,1,0:T(8,128)}, u32[]{:S(2)}) copy-start(f32[1,36,32,512]{3,2,1,0:T(8,128)} %param.8) | copy-start | bytes 7077892
  19.6 0.8 copy-start.4
  19.6 0.9 copy-start.5
  92.8 3.3 %copy-start.1 = (f32[8,36,8,512]{3,2,1,0:T(8,128)S(1)}, f32[8,36,8,512]{3,2,1,0:T(8,128)}, u32[]{:S(2)}) copy-start(f32[8,36,8,512]{3,2,1,0:T(8,128)} %shard_map.64) | copy-start | bytes 14155780
  98.0 2.4 %copy-start.2 = (f32[6,36,8,512]{3,2,1,0:T(8,128)}, f32[6,36,8,512]{3,2,1,0:T(8,128)S(1)}, u32[]{:S(2)}) copy-start(f32[6,36,8,512]{3,2,1,0:T(8,128)S(1)} %multiply_subtract_fusion) | copy-start | bytes 10616836

commit v12 on v0

--- a/solution.py
+++ b/solution.py
@@ -1,8 +1,11 @@
+import functools
 import math
 
 import jax
 import jax.numpy as jnp
 from jax import lax
+from jax.experimental import pallas as pl
+from jax.experimental.pallas import tpu as pltpu
 from jax.sharding import PartitionSpec as P
 
 GRAVITY = 9.81
@@ -144,12 +147,65 @@
     )
 
 
+Y_GROUP = 4
+
+
+def _exchange_kernel(y_count, x_ref, out_ref, local_sem, send_sems, recv_sems):
+    geo = lax.axis_index("geo")
+    me = lax.axis_index("z") * y_count + lax.axis_index("y")
+    count = x_ref.shape[0]
+    mesh_id = pl.DeviceIdType.MESH
+    barrier = pltpu.get_barrier_semaphore()
+    for offset in range(1, count):
+        target = lax.rem(me + offset, count)
+        pl.semaphore_signal(barrier, inc=1, device_id=(geo, target // y_count, target % y_count),
+                            device_id_type=mesh_id)
+    pl.semaphore_wait(barrier, count - 1)
+    local = pltpu.make_async_copy(x_ref.at[me], out_ref.at[me], local_sem.at[0])
+    local.start()
+    copies = []
+    for offset in range(1, count):
+        target = lax.rem(me + offset, count)
+        copy = pltpu.make_async_remote_copy(
+            src_ref=x_ref.at[target],
+            dst_ref=out_ref.at[me],
+            send_sem=send_sems.at[offset],
+            recv_sem=recv_sems.at[offset],
+            device_id=(geo, target // y_count, target % y_count),
+            device_id_type=mesh_id,
+        )
+        copy.start()
+        copies.append(copy)
+    local.wait()
+    for copy in copies:
+        copy.wait_send()
+        copy.wait_recv()
+
+
+def exchange(x, y_count, collective_id):
+    count = x.shape[0]
+    vmem = pl.BlockSpec(memory_space=pltpu.VMEM)
+    return pl.pallas_call(
+        functools.partial(_exchange_kernel, y_count),
+        out_shape=jax.ShapeDtypeStruct(x.shape, x.dtype),
+        in_specs=[vmem],
+        out_specs=vmem,
+        scratch_shapes=[
+            pltpu.SemaphoreType.DMA((1,)),
+            pltpu.SemaphoreType.DMA((count,)),
+            pltpu.SemaphoreType.DMA((count,)),
+        ],
+        compiler_params=pltpu.CompilerParams(collective_id=collective_id, has_side_effects=True),
+    )(x)
+
+
 def shards(spectrum, land_sea, sea_index, sea_count, wind_speed, wind_dir, slope_x, slope_y):
     local_bands, dir_count, row_count, col_count = spectrum.shape
-    spec_count = lax.axis_size("spec")
-    spec_pos = lax.axis_index("spec")
-    band_total = local_bands * spec_count
-    tile_cells = row_count * col_count
+    z_count = lax.axis_size("z")
+    y_count = lax.axis_size("y")
+    z_pos = lax.axis_index("z")
+    y_pos = lax.axis_index("y")
+    spec_pos = z_pos * y_count + y_pos
     dtheta = 2.0 * math.pi / dir_count
     angles = (jnp.arange(dir_count).astype(jnp.float32) + 0.5) * dtheta
     face_angles = jnp.arange(dir_count + 1).astype(jnp.float32) * dtheta
@@ -173,33 +229,27 @@
     )
     padded = jnp.concatenate([density[:, -2:], density, density[:, :2]], axis=1)
     floored = jnp.maximum(advect(padded, turning, 1), 0.0)
-    per_device = tile_cells // spec_count
-    point_block = lax.all_to_all(floored, "spec", split_axis=2, concat_axis=0, tiled=True).reshape(
-        band_total, dir_count, per_device
-    )
-    wind_block = lax.dynamic_slice_in_dim(
-        wind_speed.reshape(tile_cells), spec_pos * per_device, per_device
-    )
-    wind_angle = lax.dynamic_slice_in_dim(
-        wind_dir.reshape(tile_cells), spec_pos * per_device, per_device
-    )
-    wet_block = lax.dynamic_slice_in_dim(
-        wet_mask.reshape(tile_cells), spec_pos * per_device, per_device
-    )
-    updated = local_sources(point_block, wind_block, wind_angle, angles, dtheta) * wet_block
-    returned = lax.all_to_all(
-        updated.reshape(band_total, dir_count, 1, per_device),
-        "spec",
-        split_axis=0,
-        concat_axis=2,
-        tiled=True,
-    )
-    return returned
+    y_count = lax.axis_size("y")
+    band_total = local_bands * z_count * y_count
+    by_row = jnp.transpose(floored[0], (1, 0, 2))
+    point_block = exchange(by_row, y_count, 0)
+    row = lax.dynamic_slice_in_dim(wind_speed, spec_pos, 1, axis=0)[0]
+    angle = lax.dynamic_slice_in_dim(wind_dir, spec_pos, 1, axis=0)[0]
+    wet_row = lax.dynamic_slice_in_dim(wet_mask, spec_pos, 1, axis=0)[0]
+    updated = local_sources(point_block, row, angle, angles, dtheta) * wet_row
+    by_band = exchange(updated, y_count, 1)
+    return jnp.transpose(by_band, (1, 0, 2))[None]
 
 
 def solution(mesh):
+    geo_count = mesh.shape["geo"]
+    spec_count = mesh.shape["spec"]
+    local = jax.sharding.Mesh(
+        mesh.devices.reshape(geo_count, spec_count // Y_GROUP, Y_GROUP), ("geo", "z", "y")
+    )
+    spec = ("z", "y")
     placed = (
-        P("spec", None, "geo", None),
+        P(spec, None, "geo", None),
         P("geo", None),
         P("geo", None),
         P("geo"),
@@ -209,5 +259,5 @@
         P("geo", None),
     )
     return jax.shard_map(
-        shards, mesh=mesh, in_specs=placed, out_specs=P("spec", None, "geo", None), check_vma=False
-    )
+        shards, mesh=local, in_specs=placed, out_specs=P(spec, None, "geo", None), check_vma=False
+    )

time: 172 us -> 194 us (1.13)
  the two profiles are of different devices: /device:TPU:2 before, /device:TPU:92 now
where the time goes in v12:
time: 194 us; the launch traced here: 193 us
  Pallas kernels  148 us (76%)
  other arithmetic  29.2 us (15%)
  local copies, waits for them, and re-layouts  11.2 us (6%)
  starting transfers between devices  4.33 us (2%)
    pallas_call x2, Pallas kernels, exchange(): pl.pallas_call(functools.partial(_exchange_kernel, y_count), out_shape=ja...  148 us
    mul x3, other arithmetic, quick_flux(): return courant * face_value  8.28 us
    broadcast_in_dim x1, local copies, waits for them, and re-layouts, shards(): return jnp.transpose(by_band, (1, 0, 2))[None]  4.51 us
  transfers between devices with their start and end apart: 2, of which 0 were waited for; matrix products, arithmetic and copies ran while one was open for 4% of the time, Pallas kernels for 0%

profile of v12, /device:TPU:92, one launch (start us, length us, event | category | flops | bytes accessed | tf_op | source)
XLA Modules:
  0.0 193.4 jit_solution(5981690947334654387)
XLA Ops:
  0.0 0.9 convert_element_type.94
  0.9 3.0 %copy_multiply_fusion = f32[1,36,32,512]{3,1,2,0:T(8,128)S(1)} fusion(f32[1,36,32,512]{3,2,1,0:T(8,128)} %param.8, f32[32,512]{1,0:T(8,128)S(1)} %convert_element_type.94), kind=kLoop, calls=%fused_computation.47 | loop fusion | flops 589824 | bytes 4784128 | tf_op jit(solution)/shard_map/mul | solution.py:215
  4.0 1.9 collective-permute-start.1
  5.9 2.4 %collective-permute-start = (f32[1,36,2,512]{3,1,2,0:T(8,128)S(1)}, f32[1,36,2,512]{3,1,2,0:T(8,128)S(1)}, u32[]{:S(2)}, u32[]{:S(2)}) collective-permute-start(f32[1,36,2,512]{3,1,2,0:T(8,128)S(1)} %get-tuple-element.14), channel_id=1, source_target_pairs={{0,32},{32,64},{64,96},{96,128},{128,160},{160,192},{192,224},{1,3... | collective-permute-start | bytes 442376 | tf_op jit(solution)/shard_map/ppermute | solution.py:33
  8.4 0.6 sine_multiply_fusion
  9.0 0.6 abs_multiply_fusion.1
  9.6 0.6 broadcast_compare_fusion
  10.2 0.6 subtract_multiply_fusion
  10.9 0.6 fusion.32
  11.4 0.6 fusion.37
  12.1 0.5 multiply_multiply_fusion.2
  12.6 1.3 dynamic-slice_multiply_fusion
  13.9 0.0 copy-done
  13.9 0.3 subtract_cosine_fusion
  14.2 0.7 multiply_multiply_fusion
  14.9 0.6 fusion.34
  15.6 0.0 collective-permute-done.1
  15.6 0.0 collective-permute-done
  15.6 0.0 copy-start.2
  15.6 2.5 %fusion.11 = f32[1,36,33,512]{3,1,2,0:T(8,128)S(1)} fusion(f32[1,36,2,512]{3,1,2,0:T(8,128)S(1)} %collective-permute-done.1, f32[1,36,32,512]{3,1,2,0:T(8,128)S(1)} %copy_multiply_fusion, f32[1,36,2,512]{3,1,2,0:T(8,128)S(1)} %collective-permute-done, f32[36]{0:T(128)} %get-tuple-element.23, f32[36]{0:T(128)} %get-tuple-element.24, f32[36]{0:T(128)} %get-tuple-element.25, ...), kind=kLoop, calls=%fused_computation.20 | loop fusion | flops 10948608 | bytes 5087700 | tf_op jit(solution)/shard_map/mul | solution.py:65
  18.1 1.7 fusion.23
  19.9 2.8 %fusion.4 = f32[1,36,32,513]{3,1,2,0:T(8,128)S(1)} fusion(f32[1,36,32,512]{3,1,2,0:T(8,128)S(1)} %fusion.23, f32[36]{0:T(128)S(1)} %copy-done.13, f32[36]{0:T(128)S(1)} %copy-done.14, f32[36]{0:T(128)S(1)} %copy-done.11, pred[36]{0:T(512)(128)(4,1)S(1)} %copy-done.12), kind=kLoop, calls=%fused_computation.8 | loop fusion | flops 8273664 | bytes 4723668 | tf_op jit(solution)/shard_map/mul | solution.py:65
  22.7 0.0 copy-start.3
  22.7 0.0 copy-start.4
  22.7 0.8 fusion.21
  23.5 0.1 fusion.40
  23.6 3.0 %fusion.19 = f32[1,37,32,512]{3,1,2,0:T(8,128)S(1)} fusion(f32[1,2,32,512]{3,1,2,0:T(2,128)S(1)} %get-tuple-element.13, f32[1,36,32,512]{3,1,2,0:T(8,128)S(1)} %fusion.21, f32[1,2,32,512]{3,1,2,0:T(2,128)S(1)} %get-tuple-element.12, f32[32,512]{1,0:T(8,128)S(1)} %copy-done.3, f32[37]{0:T(128)S(1)} %get-tuple-element.28, f32[32,512]{1,0:T(8,128)S(1)} %copy-done.4, ...), kind=kLoop, calls=%fused_computation.31 | loop fusion | flops 16973824 | bytes 5177644 | tf_op jit(solution)/shard_map/mul | solution.py:65
  26.7 2.2 %fusion.14.x_ref = f32[32,36,512]{2,1,0:T(8,128)} fusion(f32[1,36,32,512]{3,1,2,0:T(8,128)S(1)} %fusion.21, f32[1,37,32,512]{3,1,2,0:T(8,128)S(1)} %fusion.19), kind=kLoop, calls=%fused_computation.25 | loop fusion | flops 1769472 | bytes 9437184 | tf_op jit(solution)/shard_map/transpose | solution.py:234
  28.8 76.5 %shard_map.64 = f32[32,36,512]{2,1,0:T(8,128)} custom-call(f32[32,36,512]{2,1,0:T(8,128)} %fusion.14.x_ref), custom_call_target="tpu_custom_call" | custom-call | tf_op jit(solution)/shard_map/pallas_call | solution.py:188
  105.3 3.1 %fusion.39 = (f32[31,36,512]{2,1,0:T(8,128)S(1)}, f32[31,36,512]{2,1,0:T(8,128)S(1)}) fusion(f32[32,36,512]{2,1,0:T(8,128)} %shard_map.64), kind=kLoop, calls=%fused_computation.95 | loop fusion | bytes 9142272 | tf_op jit(solution)/shard_map/slice | solution.py:101
  108.4 0.3 pad_slice_fusion.10
  108.7 0.1 pad_slice_fusion.11
  108.8 0.4 pad_slice_fusion.15
  109.2 1.3 copy-done.1
  110.6 1.0 divide_reduce_fusion.1
  111.5 1.2 multiply_divide_fusion
  112.7 0.3 fusion.38
  113.1 0.3 pad_slice_fusion.12
  113.4 0.1 pad_slice_fusion.13
  113.5 0.0 copy-start.5
  113.5 0.4 pad_slice_fusion.9
  113.9 0.2 copy-done.7
  114.1 0.1 fusion.29
  114.2 0.0 copy-done.5
  114.2 0.0 copy-done.8
  114.2 2.9 %fusion.26.x_ref = f32[32,36,512]{2,1,0:T(8,128)} fusion(f32[32,35,512]{2,1,0:T(8,128)S(1)} %pad_slice_fusion.12, f32[32,1,512]{2,1,0:T(1,128)S(1)} %pad_slice_fusion.13, f32[32,3,512]{2,1,0:T(4,128)S(1)} %pad_slice_fusion.8, f32[32,33,512]{2,1,0:T(8,128)S(1)} %pad_slice_fusion.9, f32[32,36,512]{2,1,0:T(8,128)S(1)} %multiply_divide_fusion, ...), kind=kLoop, calls=%fused_computation.46 | loop fusion | flops 8257536 | bytes 12003456 | tf_op jit(solution)/shard_map/mul | solution.py:239
  117.0 71.8 %shard_map.65 = f32[32,36,512]{2,1,0:T(8,128)} custom-call(f32[32,36,512]{2,1,0:T(8,128)} %fusion.26.x_ref), custom_call_target="tpu_custom_call" | custom-call | tf_op jit(solution)/shard_map/pallas_call | solution.py:188
  188.9 4.5 %copy.8 = f32[1,36,32,512]{3,2,1,0:T(8,128)} copy(f32[1,36,32,512]{3,1,2,0:T(8,128)} %bitcast.10) | data formatting | bytes 4718592 | tf_op jit(solution)/shard_map/broadcast_in_dim | solution.py:241
  (28 shorter events, 0.2 us)
Async XLA Ops:
  0.0 13.9 %copy-start = (f32[32,512]{1,0:T(8,128)S(1)}, f32[32,512]{1,0:T(8,128)}, u32[]{:S(2)}) copy-start(f32[32,512]{1,0:T(8,128)} %param.11) | copy-start | bytes 196612
  4.0 11.6 %collective-permute-start.1 = (f32[1,36,2,512]{3,1,2,0:T(8,128)S(1)}, f32[1,36,2,512]{3,1,2,0:T(8,128)S(1)}, u32[]{:S(2)}, u32[]{:S(2)}) collective-permute-start(f32[1,36,2,512]{3,1,2,0:T(8,128)S(1)} %get-tuple-element.15), channel_id=1, source_target_pairs={{32,0},{64,32},{96,64},{128,96},{160,128},{192,160},{224,192},{33,... | collective-permute-start | bytes 442376 | tf_op jit(solution)/shard_map/ppermute | solution.py:35
  5.9 9.7 %collective-permute-start = (f32[1,36,2,512]{3,1,2,0:T(8,128)S(1)}, f32[1,36,2,512]{3,1,2,0:T(8,128)S(1)}, u32[]{:S(2)}, u32[]{:S(2)}) collective-permute-start(f32[1,36,2,512]{3,1,2,0:T(8,128)S(1)} %get-tuple-element.14), channel_id=1, source_target_pairs={{0,32},{32,64},{64,96},{96,128},{128,160},{160,192},{192,224},{1,3... | collective-permute-start | bytes 442376 | tf_op jit(solution)/shard_map/ppermute | solution.py:33
  15.6 2.5 %copy-start.2 = (f32[1,36,32,512]{3,2,1,0:T(8,128)S(1)}, f32[1,36,32,512]{3,2,1,0:T(8,128)}, u32[]{:S(2)}) copy-start(f32[1,36,32,512]{3,2,1,0:T(8,128)} %param.8) | copy-start | bytes 7077892
  18.1 1.8 copy-start.11
  18.1 1.8 copy-start.12
  18.1 1.8 copy-start.13
  18.1 1.8 copy-start.14
  22.7 0.9 copy-start.3
  22.7 0.9 copy-start.4
  108.8 1.7 copy-start.1
  108.8 1.7 copy-start.6
  108.8 1.7 copy-start.9
  108.8 1.7 copy-start.10
  113.5 0.6 copy-start.7
  113.5 0.7 copy-start.5
  113.5 0.7 copy-start.8

commit v13 on v10

--- a/solution.py
+++ b/solution.py
@@ -20,6 +20,56 @@
 STEEP_REF = 1.6
 EPSILON = 1e-06
 QUAD_COEF = 100.0
+
+
+def _gather_rows_kernel(y_count, x_ref, out_ref, local_sem, send_sems, recv_sems):
+    geo = lax.axis_index("geo")
+    z_pos = lax.axis_index("z")
+    y_pos = lax.axis_index("y")
+    rows = x_ref.shape[2]
+    mesh_id = pl.DeviceIdType.MESH
+    barrier = pltpu.get_barrier_semaphore()
+    for offset in range(1, y_count):
+        pl.semaphore_signal(barrier, inc=1, device_id=(geo, z_pos, lax.rem(y_pos + offset, y_count)),
+                            device_id_type=mesh_id)
+    pl.semaphore_wait(barrier, y_count - 1)
+    mine = out_ref.at[0, :, pl.ds(pl.multiple_of(y_pos * rows, rows), rows)]
+    local = pltpu.make_async_copy(x_ref.at[y_pos], mine, local_sem.at[0])
+    local.start()
+    copies = []
+    for offset in range(1, y_count):
+        target = lax.rem(y_pos + offset, y_count)
+        copy = pltpu.make_async_remote_copy(
+            src_ref=x_ref.at[target],
+            dst_ref=mine,
+            send_sem=send_sems.at[offset],
+            recv_sem=recv_sems.at[offset],
+            device_id=(geo, z_pos, target),
+            device_id_type=mesh_id,
+        )
+        copy.start()
+        copies.append(copy)
+    local.wait()
+    for copy in copies:
+        copy.wait_send()
+        copy.wait_recv()
+
+
+def gather_rows(x, y_count):
+    group, dirs, rows, cols = x.shape
+    vmem = pl.BlockSpec(memory_space=pltpu.VMEM)
+    return pl.pallas_call(
+        functools.partial(_gather_rows_kernel, y_count),
+        out_shape=jax.ShapeDtypeStruct((1, dirs, rows * y_count, cols), x.dtype),
+        in_specs=[vmem],
+        out_specs=vmem,
+        scratch_shapes=[
+            pltpu.SemaphoreType.DMA((1,)),
+            pltpu.SemaphoreType.DMA((y_count,)),
+            pltpu.SemaphoreType.DMA((y_count,)),
+        ],
+        compiler_params=pltpu.CompilerParams(collective_id=2, has_side_effects=True),
+    )(x)
 
 
 def extended(cells, sides, width):
@@ -1089,7 +1139,7 @@
         )
         + extra
     ) * wet_block
-    return lax.all_to_all(updated, "y", split_axis=0, concat_axis=2, tiled=True)
+    return gather_rows(updated, lax.axis_size("y"))
 
 
 def solution(mesh):

time: 147 us -> 150 us (1.020)
  Pallas kernels: 63.4 us -> 95.5 us
  blocking collectives: 32 us -> 0 us
  local copies, waits for them, and re-layouts: 8.86 us -> 10.6 us
    pallas_call x0 -> x1, Pallas kernels: none -> 32.1 us  [gather_rows(): pl.pallas_call(functools.partial(_gather_rows_kernel, y_count), out_shape...]
    all_to_all x1 -> x0, blocking collectives: 32 us -> none  [shards(): return lax.all_to_all(updated, 'y', split_axis=0, concat_axis=2, tiled=True)]
    unnamed x8 -> x9, local copies, waits for them, and re-layouts: 1.03 us -> 4.44 us
    all_to_all x1 -> x0, local copies, waits for them, and re-layouts: 1.66 us -> none  [shards(): return lax.all_to_all(updated, 'y', split_axis=0, concat_axis=2, tiled=True)]
where the time goes in v13:
time: 150 us
  Pallas kernels  95.5 us (64%)
  other arithmetic  26.5 us (18%)
  starting transfers between devices  13.6 us (9%)
  local copies, waits for them, and re-layouts  10.6 us (7%)
  waiting for transfers between devices  3.06 us (2%)
    pallas_call x1, Pallas kernels, spread(): pl.pallas_call(functools.partial(_spread_kernel, z_count, y_count), out_s...  63.4 us
    pallas_call x1, Pallas kernels, gather_rows(): pl.pallas_call(functools.partial(_gather_rows_kernel, y_count), out_shape...  32.1 us
    mul x3, other arithmetic, quick_flux(): return courant * face_value  9.3 us
    ppermute x3, starting transfers between devices, shards(): lax.ppermute(sums, 'z', [(i, i ^ step) for i in range(z_count)])  8 us
    unnamed x9, local copies, waits for them, and re-layouts  4.44 us
    ppermute x1, starting transfers between devices, extended(): lax.ppermute(head, axis, [((i + 1) % count, i) for i in range(ends)])  3.64 us
    slice x2, local copies, waits for them, and re-layouts, shards(): jnp.roll(ext[:-2], 3, axis=1)  3.4 us
    ppermute x3, waiting for transfers between devices, shards(): lax.ppermute(sums, 'z', [(i, i ^ step) for i in range(z_count)])  3.05 us
  transfers between devices with their start and end apart: 5, of which 2 were waited for; matrix products, arithmetic and copies ran while one was open for 8% of the time, Pallas kernels for 0%

profile of v13, /device:TPU:2, one launch (start us, length us, event | category | flops | bytes accessed | tf_op | source)
XLA Modules:
  0.0 149.6 jit_solution(5051491909347702543)
XLA Ops:
  0.0 0.8 convert_element_type.84
  0.8 2.0 %broadcast_multiply_fusion = f32[1,36,32,512]{3,2,1,0:T(8,128)S(1)} fusion(f32[1,36,32,512]{3,2,1,0:T(8,128)} %param.8, f32[32,512]{1,0:T(8,128)S(1)} %convert_element_type.84), kind=kLoop, calls=%fused_computation.54 | loop fusion | flops 589824 | bytes 4784128 | tf_op jit(solution)/shard_map/mul | solution.py:1082
  2.8 0.8 fusion.46
  3.6 1.9 %collective-permute-start = (f32[1,36,2,512]{3,2,1,0:T(2,128)}, f32[1,36,2,512]{3,2,1,0:T(2,128)S(1)}, u32[]{:S(2)}, u32[]{:S(2)}) collective-permute-start(f32[1,36,2,512]{3,2,1,0:T(2,128)} %get-tuple-element.12), channel_id=1, source_target_pairs={{0,32},{32,64},{64,96},{96,128},{128,160},{160,192},{192,224},{1,3... | collective-permute-start | bytes 442376 | tf_op jit(solution)/shard_map/ppermute | solution.py:771
  5.5 3.6 %collective-permute-start.1 = (f32[1,36,2,512]{3,2,1,0:T(2,128)S(1)}, f32[1,36,2,512]{3,2,1,0:T(2,128)S(1)}, u32[]{:S(2)}, u32[]{:S(2)}) collective-permute-start(f32[1,36,2,512]{3,2,1,0:T(2,128)S(1)} %get-tuple-element.13), channel_id=1, source_target_pairs={{32,0},{64,32},{96,64},{128,96},{160,128},{192,160},{224,192},{33,... | collective-permute-start | bytes 442376 | tf_op jit(solution)/shard_map/ppermute | solution.py:773
  9.2 0.6 abs_multiply_fusion.1
  9.8 0.6 broadcast_compare_fusion
  10.5 0.6 sine_multiply_fusion
  11.1 0.7 dynamic-slice_multiply_fusion
  11.9 0.1 multiply_multiply_fusion
  11.9 1.9 %subtract_cosine_fusion = f32[36,8,512]{2,1,0:T(8,128)S(1)} fusion(f32[8,512]{1,0:T(8,128)S(1)} %get-tuple-element.33, f32[36]{0:T(128)S(1)} %add_multiply_fusion), kind=kLoop, calls=%fused_computation.55 | loop fusion | flops 147456 | bytes 606352 | tf_op jit(solution)/shard_map/cos | solution.py:1128
  14.0 0.0 collective-permute-done
  14.0 0.0 collective-permute-done.1
  14.0 0.0 copy-start.1
  14.0 3.4 %fusion.9 = f32[1,36,33,512]{3,2,1,0:T(8,128)S(1)} fusion(f32[1,36,2,512]{3,2,1,0:T(2,128)S(1)} %collective-permute-done.1, f32[1,36,32,512]{3,2,1,0:T(8,128)S(1)} %broadcast_multiply_fusion, f32[1,36,2,512]{3,2,1,0:T(2,128)S(1)} %collective-permute-done, f32[36]{0:T(128)} %get-tuple-element.25, f32[36]{0:T(128)} %get-tuple-element.26, ...), kind=kLoop, calls=%fused_computation.17 | loop fusion | flops 10948608 | bytes 5087700 | tf_op jit(solution)/shard_map/mul | solution.py:803
  17.4 0.0 copy-done.1
  17.4 0.7 fusion.27
  18.2 2.8 %fusion.4 = f32[1,36,32,513]{3,2,1,0:T(8,128)S(1)} fusion(f32[1,36,32,512]{3,2,1,0:T(8,128)S(1)} %fusion.27, f32[36]{0:T(128)S(1)} %get-tuple-element.22, f32[36]{0:T(128)S(1)} %get-tuple-element.23, f32[36]{0:T(128)S(1)} %get-tuple-element.24, pred[36]{0:T(512)(128)(4,1)S(1)} %get-tuple-element.28), kind=kLoop, calls=%fused_computation.11 | loop fusion | flops 8273664 | bytes 4723668 | tf_op jit(solution)/shard_map/mul | solution.py:803
  21.0 0.0 copy-start.2
  21.0 0.0 copy-start.3
  21.0 0.7 fusion.25
  21.7 0.1 copy-done.2
  21.8 0.0 copy-done.3
  21.8 3.1 %fusion.16 = f32[1,37,32,512]{3,2,1,0:T(8,128)S(1)} fusion(f32[1,2,32,512]{3,2,1,0:T(8,128)S(1)} %get-tuple-element.11, f32[1,36,32,512]{3,2,1,0:T(8,128)S(1)} %fusion.25, f32[1,2,32,512]{3,2,1,0:T(8,128)S(1)} %get-tuple-element.10, f32[32,512]{1,0:T(8,128)S(1)} %copy-done.2, f32[37]{0:T(128)S(1)} %get-tuple-element.30, f32[32,512]{1,0:T(8,128)S(1)} %copy-done.3, ...), kind=kLoop, calls=%fused_computation.32 | loop fusion | flops 16973824 | bytes 5177644 | tf_op jit(solution)/shard_map/mul | solution.py:803
  24.9 2.0 %fusion.23.floored_ref = f32[1,36,32,512]{3,2,1,0:T(8,128)} fusion(f32[1,36,32,512]{3,2,1,0:T(8,128)S(1)} %fusion.25, f32[1,37,32,512]{3,2,1,0:T(8,128)S(1)} %fusion.16), kind=kLoop, calls=%fused_computation.43 | loop fusion | flops 1769472 | bytes 9437184 | tf_op jit(solution)/shard_map/max | solution.py:1098
  26.9 63.4 %shard_map.64 = f32[8,36,8,512]{3,2,1,0:T(8,128)} custom-call(f32[1,36,32,512]{3,2,1,0:T(8,128)} %fusion.23.floored_ref), custom_call_target="tpu_custom_call" | custom-call | tf_op jit(solution)/shard_map/pallas_call | solution.py:1054
  90.3 2.3 %fusion.28 = (f32[8,512]{1,0:T(8,128)S(1)}, f32[8,512]{1,0:T(8,128)S(1)}, f32[8,512]{1,0:T(8,128)S(1)}) fusion(f32[8,36,8,512]{3,2,1,0:T(8,128)} %shard_map.64, f32[4]{0:T(128)S(1)} %get-tuple-element.18, f32[4]{0:T(128)S(1)} %get-tuple-element.19, f32[4]{0:T(128)S(1)} %get-tuple-element.21), kind=kLoop, calls=%fused_computation.53 | loop fusion | flops 3526656 | bytes 2408496 | tf_op jit(solution)/shard_map/reduce_sum | solution.py:1108
  92.7 2.6 %collective-permute-start.2 = (f32[3,8,512]{2,1,0:T(8,128)S(1)}, f32[3,8,512]{2,1,0:T(8,128)S(1)}, u32[]{:S(2)}, u32[]{:S(2)}) collective-permute-start(f32[3,8,512]{2,1,0:T(8,128)S(1)} %pad_maximum_fusion.6), channel_id=1, source_target_pairs={{0,4},{4,0},{8,12},{12,8},{16,20},{20,16},{24,28},{28,24},{1,5},{5... | collective-permute-start | bytes 147464 | tf_op jit(solution)/shard_map/ppermute | solution.py:1115
  95.3 2.1 %collective-permute-done.2 = f32[3,8,512]{2,1,0:T(8,128)S(1)} collective-permute-done((f32[3,8,512]{2,1,0:T(8,128)S(1)}, f32[3,8,512]{2,1,0:T(8,128)S(1)}, u32[]{:S(2)}, u32[]{:S(2)}) %collective-permute-start.2) | collective-permute-done | bytes 49184 | tf_op jit(solution)/shard_map/ppermute | solution.py:1115
  97.3 0.1 collective-permute-start.3
  97.5 0.9 slice.165
  98.4 1.0 slice.166
  99.3 0.0 copy-start
  99.3 2.4 %slice.167 = f32[6,33,8,512]{3,2,1,0:T(8,128)S(1)} slice(f32[8,36,8,512]{3,2,1,0:T(8,128)} %shard_map.64), slice={[0:6], [0:33], [0:8], [0:512]} | slice | bytes 6488064 | tf_op jit(solution)/shard_map/jit(_roll_static)/slice | solution.py:1119
  101.8 0.9 copy-done
  102.7 0.5 slice.164
  103.2 0.0 collective-permute-done.3
  103.2 5.3 %collective-permute-start.4 = (f32[3,8,512]{2,1,0:T(8,128)S(1)}, f32[3,8,512]{2,1,0:T(8,128)S(1)}, u32[]{:S(2)}, u32[]{:S(2)}) collective-permute-start(f32[3,8,512]{2,1,0:T(8,128)S(1)} %fusion.47), channel_id=1, source_target_pairs={{0,16},{4,20},{8,24},{12,28},{16,0},{20,4},{24,8},{28,12},{1,17},{... | collective-permute-start | bytes 147464 | tf_op jit(solution)/shard_map/ppermute | solution.py:1115
  108.5 1.3 multiply_subtract_fusion
  109.9 0.3 slice.197
  110.2 0.3 slice.196
  110.5 1.0 collective-permute-done.4
  111.5 0.1 fusion.31
  111.6 2.4 %fusion.21.x_ref = f32[4,36,8,512]{3,2,1,0:T(8,128)} fusion(f32[6,36,8,512]{3,2,1,0:T(8,128)S(1)} %multiply_subtract_fusion, f32[4,35,8,512]{3,2,1,0:T(8,128)S(1)} %slice.196, f32[4,1,8,512]{3,2,1,0:T(8,128)S(1)} %slice.195, f32[4,3,8,512]{3,2,1,0:T(8,128)S(1)} %slice.198, f32[4,33,8,512]{3,2,1,0:T(8,128)S(1)} %slice.197, f32[8,36,8,512]{3,2,1,0:T(8,128)S(1)} %copy-done, ...), kind=kLoop, calls=%fused_computation.40 | loop fusion | flops 8847360 | bytes 12550160 | tf_op jit(solution)/shard_map/mul | solution.py:1129
  114.0 32.1 %shard_map.65 = f32[1,36,32,512]{3,2,1,0:T(8,128)} custom-call(f32[4,36,8,512]{3,2,1,0:T(8,128)} %fusion.21.x_ref), custom_call_target="tpu_custom_call" | custom-call | tf_op jit(solution)/shard_map/pallas_call | solution.py:61
  146.2 3.4 %copy.8 = f32[1,36,32,512]{3,2,1,0:T(8,128)} copy(f32[1,36,32,512]{3,2,1,0:T(8,128)} %shard_map.65) | data formatting | bytes 4718592
  (15 shorter events, 0.2 us)
Async XLA Ops:
  3.6 10.3 %collective-permute-start = (f32[1,36,2,512]{3,2,1,0:T(2,128)}, f32[1,36,2,512]{3,2,1,0:T(2,128)S(1)}, u32[]{:S(2)}, u32[]{:S(2)}) collective-permute-start(f32[1,36,2,512]{3,2,1,0:T(2,128)} %get-tuple-element.12), channel_id=1, source_target_pairs={{0,32},{32,64},{64,96},{96,128},{128,160},{160,192},{192,224},{1,3... | collective-permute-start | bytes 442376 | tf_op jit(solution)/shard_map/ppermute | solution.py:771
  5.5 8.4 %collective-permute-start.1 = (f32[1,36,2,512]{3,2,1,0:T(2,128)S(1)}, f32[1,36,2,512]{3,2,1,0:T(2,128)S(1)}, u32[]{:S(2)}, u32[]{:S(2)}) collective-permute-start(f32[1,36,2,512]{3,2,1,0:T(2,128)S(1)} %get-tuple-element.13), channel_id=1, source_target_pairs={{32,0},{64,32},{96,64},{128,96},{160,128},{192,160},{224,192},{33,... | collective-permute-start | bytes 442376 | tf_op jit(solution)/shard_map/ppermute | solution.py:773
  14.0 3.5 %copy-start.1 = (f32[1,36,32,512]{3,2,1,0:T(8,128)S(1)}, f32[1,36,32,512]{3,2,1,0:T(8,128)}, u32[]{:S(2)}) copy-start(f32[1,36,32,512]{3,2,1,0:T(8,128)} %param.8) | copy-start | bytes 7077892
  21.0 0.8 copy-start.2
  21.0 0.9 copy-start.3
  92.7 4.6 %collective-permute-start.2 = (f32[3,8,512]{2,1,0:T(8,128)S(1)}, f32[3,8,512]{2,1,0:T(8,128)S(1)}, u32[]{:S(2)}, u32[]{:S(2)}) collective-permute-start(f32[3,8,512]{2,1,0:T(8,128)S(1)} %pad_maximum_fusion.6), channel_id=1, source_target_pairs={{0,4},{4,0},{8,12},{12,8},{16,20},{20,16},{24,28},{28,24},{1,5},{5... | collective-permute-start | bytes 147464 | tf_op jit(solution)/shard_map/ppermute | solution.py:1115
  97.3 5.8 %collective-permute-start.3 = (f32[3,8,512]{2,1,0:T(8,128)S(1)}, f32[3,8,512]{2,1,0:T(8,128)S(1)}, u32[]{:S(2)}, u32[]{:S(2)}) collective-permute-start(f32[3,8,512]{2,1,0:T(8,128)S(1)} %fusion.43), channel_id=1, source_target_pairs={{0,8},{4,12},{8,0},{12,4},{16,24},{20,28},{24,16},{28,20},{1,9},{5... | collective-permute-start | bytes 147464 | tf_op jit(solution)/shard_map/ppermute | solution.py:1115
  99.3 3.3 %copy-start = (f32[8,36,8,512]{3,2,1,0:T(8,128)S(1)}, f32[8,36,8,512]{3,2,1,0:T(8,128)}, u32[]{:S(2)}) copy-start(f32[8,36,8,512]{3,2,1,0:T(8,128)} %shard_map.64) | copy-start | bytes 14155780
  103.2 8.3 %collective-permute-start.4 = (f32[3,8,512]{2,1,0:T(8,128)S(1)}, f32[3,8,512]{2,1,0:T(8,128)S(1)}, u32[]{:S(2)}, u32[]{:S(2)}) collective-permute-start(f32[3,8,512]{2,1,0:T(8,128)S(1)} %fusion.47), channel_id=1, source_target_pairs={{0,16},{4,20},{8,24},{12,28},{16,0},{20,4},{24,8},{28,12},{1,17},{... | collective-permute-start | bytes 147464 | tf_op jit(solution)/shard_map/ppermute | solution.py:1115

commit v14 on v5

--- a/solution.py
+++ b/solution.py
@@ -20,6 +20,204 @@
 STEEP_REF = 1.6
 EPSILON = 1e-06
 QUAD_COEF = 100.0
+
+
+def extended(cells, sides, width):
+    for axis, dim in sides:
+        count = lax.axis_size(axis)
+        ends = count - 1
+        head = lax.slice_in_dim(cells, 0, width, axis=dim)
+        tail = lax.slice_in_dim(cells, cells.shape[dim] - width, cells.shape[dim], axis=dim)
+        cells = jnp.concatenate(
+            [
+                lax.ppermute(tail, axis, [(i, (i + 1) % count) for i in range(ends)]),
+                cells,
+                lax.ppermute(head, axis, [((i + 1) % count, i) for i in range(ends)]),
+            ],
+            axis=dim,
+        )
+    return cells
+
+
+def band_table(band_ids):
+    growth_factor = jnp.power(GROWTH, band_ids)
+    radian_freq = 2.0 * math.pi * BASE_FREQ * growth_factor
+    wavenum = radian_freq * radian_freq / GRAVITY
+    return (
+        radian_freq,
+        wavenum,
+        COURANT_TOP / growth_factor,
+        TURN_TOP / growth_factor,
+        SPACING * radian_freq,
+    )
+
+
+def quick_flux(far_left, near_left, near_right, far_right, courant):
+    forward = courant >= 0
+    upwind = jnp.where(forward, far_left, far_right)
+    center = jnp.where(forward, near_left, near_right)
+    downwind = jnp.where(forward, near_right, near_left)
+    face_value = (
+        0.5 * (center + downwind)
+        - 0.5 * jnp.abs(courant) * (downwind - center)
+        - (1.0 - courant * courant) / 6.0 * (downwind - 2.0 * center + upwind)
+    )
+    return courant * face_value
+
+
+def advect(padded, courant, along):
+    face_count = padded.shape[along] - 4
+    shifted = [
+        lax.slice_in_dim(padded, offset, offset + face_count + 1, axis=along) for offset in range(4)
+    ]
+    face_flux = quick_flux(shifted[0], shifted[1], shifted[2], shifted[3], courant)
+    centre_cells = lax.slice_in_dim(padded, 2, 2 + face_count, axis=along)
+    upper_flux = lax.slice_in_dim(face_flux, 1, face_count + 1, axis=along)
+    lower_flux = lax.slice_in_dim(face_flux, 0, face_count, axis=along)
+    return centre_cells - (upper_flux - lower_flux)
+
+
+def quad_delta(center, above, below, energy, dir_axis):
+    plus = jnp.roll(above, -1, axis=dir_axis)
+    minus = jnp.roll(below, 3, axis=dir_axis)
+    return (
+        QUAD_COEF
+        * (center * center * (plus + minus) - 2.0 * center * plus * minus)
+        / (energy * energy)
+    )
+
+
+def quad_term(delta, delta_above, delta_below, dir_axis):
+    return (
+        -2.0 * delta
+        + jnp.roll(delta_below, 1, axis=dir_axis)
+        + jnp.roll(delta_above, -3, axis=dir_axis)
+    )
+
+
+def band_neighbours(values):
+    empty = jnp.zeros((1,) + values.shape[1:], jnp.float32)
+    return (
+        jnp.concatenate([values[1:], empty], axis=0),
+        jnp.concatenate([empty, values[:-1]], axis=0),
+    )
+
+
+def sources(density, energy_sum, first_sum, root_sum, radian_freq, wavenum, cosine, wind_speed):
+    energy = energy_sum + EPSILON
+    mean_sigma = energy / (first_sum + EPSILON)
+    ratio_k = energy / (root_sum + EPSILON)
+    mean_k = ratio_k * ratio_k
+    steepness = energy * mean_k * mean_k / STEEP_REF
+    decay_rate = WHITECAP * mean_sigma * (wavenum / mean_k) * steepness * steepness
+    growth_rate = (
+        WIND_COEF
+        * radian_freq
+        * jnp.maximum(28.0 * USTAR_RATIO * wind_speed * radian_freq / GRAVITY * cosine - 1.0, 0.0)
+    )
+    return density * (1.0 + growth_rate) / (1.0 + decay_rate)
+
+
+def local_sources(point_block, wind_block, wind_angle, angles, dtheta):
+    band_total = point_block.shape[0]
+    band_ids = jnp.arange(band_total).astype(jnp.float32)
+    radian_freq, wavenum, courant, turn_rate, band_spread = band_table(band_ids)
+    scaled = point_block * (band_spread * dtheta)[:, None, None]
+    energy_sum = jnp.sum(scaled, axis=(0, 1))
+    first_sum = jnp.sum(scaled / radian_freq[:, None, None], axis=(0, 1))
+    root_sum = jnp.sum(scaled / jnp.sqrt(wavenum)[:, None, None], axis=(0, 1))
+    energy = energy_sum + EPSILON
+    above, below = band_neighbours(point_block)
+    delta = quad_delta(point_block, above, below, energy, 1)
+    delta_above, delta_below = band_neighbours(delta)
+    extra = quad_term(delta, delta_above, delta_below, 1)
+    cosine = jnp.cos(angles[:, None] - wind_angle[None, :])
+    return (
+        sources(
+            point_block,
+            energy_sum,
+            first_sum,
+            root_sum,
+            radian_freq[:, None, None],
+            wavenum[:, None, None],
+            cosine,
+            wind_block,
+        )
+        + extra
+    )
+
+
+Y_GROUP = 4
+HALO = 2
+
+
+def _z_halo_kernel(z_count, point_ref, lower_ref, upper_ref, halo_send, halo_recv):
+    geo = lax.axis_index("geo")
+    z_pos = lax.axis_index("z")
+    y_pos = lax.axis_index("y")
+    group = point_ref.shape[0]
+    mesh_id = pl.DeviceIdType.MESH
+    barrier = pltpu.get_barrier_semaphore()
+    for step in (1, z_count - 1):
+        pl.semaphore_signal(barrier, inc=1, device_id=(geo, lax.rem(z_pos + step, z_count), y_pos),
+                            device_id_type=mesh_id)
+    pl.semaphore_wait(barrier, 2)
+
+    def halo_copy(src_lo, dst_ref, slot, target):
+        return pltpu.make_async_remote_copy(
+            src_ref=point_ref.at[pl.ds(src_lo, HALO)],
+            dst_ref=dst_ref,
+            send_sem=halo_send.at[slot],
+            recv_sem=halo_recv.at[slot],
+            device_id=(geo, target, y_pos),
+            device_id_type=mesh_id,
+        )
+
+    up = halo_copy(group - HALO, lower_ref, 0, lax.rem(z_pos + 1, z_count))
+    down = halo_copy(0, upper_ref, 1, lax.rem(z_pos + z_count - 1, z_count))
+
+    @pl.when(z_pos < z_count - 1)
+    def _():
+        up.start()
+
+    @pl.when(z_pos > 0)
+    def _():
+        down.start()
+
+    @pl.when(z_pos == 0)
+    def _():
+        lower_ref[...] = jnp.zeros(lower_ref.shape, lower_ref.dtype)
+
+    @pl.when(z_pos == z_count - 1)
+    def _():
+        upper_ref[...] = jnp.zeros(upper_ref.shape, upper_ref.dtype)
+
+    @pl.when(z_pos < z_count - 1)
+    def _():
+        up.wait_send()
+        down.wait_recv()
+
+    @pl.when(z_pos > 0)
+    def _():
+        down.wait_send()
+        up.wait_recv()
+
+
+def z_halo(point, z_count):
+    group, dirs, rows, cols = point.shape
+    halo = jax.ShapeDtypeStruct((HALO, dirs, rows, cols), point.dtype)
+    vmem = pl.BlockSpec(memory_space=pltpu.VMEM)
+    return pl.pallas_call(
+        functools.partial(_z_halo_kernel, z_count),
+        out_shape=(halo, halo),
+        in_specs=[vmem],
+        out_specs=(vmem, vmem),
+        scratch_shapes=[
+            pltpu.SemaphoreType.DMA((2,)),
+            pltpu.SemaphoreType.DMA((2,)),
+        ],
+        compiler_params=pltpu.CompilerParams(collective_id=0, has_side_effects=True),
+    )(point)
 
 
 def extended(cells, sides, width):
@@ -284,8 +482,11 @@
             jnp.sum(scaled / jnp.sqrt(wavenum)[:, None, None, None], axis=(0, 1)),
         ]
     )
-    lower, upper, gathered = z_exchange(point, sums, z_count)
-    sums = jnp.sum(gathered, axis=0)
+    lower, upper = z_halo(point, z_count)
+    step = 1
+    while step < z_count:
+        sums = sums + lax.ppermute(sums, "z", [(i, i ^ step) for i in range(z_count)])
+        step *= 2
     energy_sum, first_sum, root_sum = sums[0], sums[1], sums[2]
     energy = energy_sum + EPSILON
     ext = jnp.concatenate([lower, point, upper], axis=0)

time: 156 us -> 143 us (0.917)
  the two profiles are of different devices: /device:TPU:2 before, /device:TPU:32 now
where the time goes in v14:
time: 143 us
  Pallas kernels  34.6 us (24%)
  waiting for transfers between devices  32.2 us (23%)
  blocking collectives  29.5 us (21%)
  other arithmetic  23 us (16%)
  starting transfers between devices  14.9 us (10%)
  local copies, waits for them, and re-layouts  8.39 us (6%)
    pallas_call x1, Pallas kernels, z_halo(): pl.pallas_call(functools.partial(_z_halo_kernel, z_count), out_shape=(hal...  34.6 us
    all_to_all x1, blocking collectives, shards(): return lax.all_to_all(updated, 'y', split_axis=0, concat_axis=2, tiled=True)  29.5 us
    all_to_all x1, waiting for transfers between devices, shards(): lax.all_to_all(floored, 'y', split_axis=2, concat_axis=0, tiled=True)  26.8 us
    mul x3, other arithmetic, quick_flux(): return courant * face_value  8.41 us
    ppermute x3, starting transfers between devices, shards(): lax.ppermute(sums, 'z', [(i, i ^ step) for i in range(z_count)])  6.07 us
    ppermute x3, waiting for transfers between devices, shards(): lax.ppermute(sums, 'z', [(i, i ^ step) for i in range(z_count)])  4.79 us
    all_to_all x1, starting transfers between devices, shards(): lax.all_to_all(floored, 'y', split_axis=2, concat_axis=0, tiled=True)  4.46 us
    max x1, local copies, waits for them, and re-layouts, shards(): floored = jnp.maximum(advect(padded, turning, 1), 0.0)  3.83 us
  transfers between devices with their start and end apart: 6, of which 4 were waited for; matrix products, arithmetic and copies ran while one was open for 7% of the time, Pallas kernels for 24%

profile of v14, /device:TPU:32, one launch (start us, length us, event | category | flops | bytes accessed | tf_op | source)
XLA Modules:
  0.0 143.0 jit_solution(1219822765193621862)
XLA Ops:
  0.0 0.8 convert_element_type.84
  0.8 2.0 %broadcast_multiply_fusion = f32[1,36,32,512]{3,2,1,0:T(8,128)S(1)} fusion(f32[1,36,32,512]{3,2,1,0:T(8,128)} %param.8, f32[32,512]{1,0:T(8,128)S(1)} %convert_element_type.84), kind=kLoop, calls=%fused_computation.64 | loop fusion | flops 589824 | bytes 4784128 | tf_op jit(solution)/shard_map/mul | solution.py:455
  2.9 0.1 fusion.48
  3.0 1.3 collective-permute-start.1
  4.3 3.0 %collective-permute-start = (f32[1,36,2,512]{3,2,1,0:T(2,128)S(1)}, f32[1,36,2,512]{3,2,1,0:T(2,128)S(1)}, u32[]{:S(2)}, u32[]{:S(2)}) collective-permute-start(f32[1,36,2,512]{3,2,1,0:T(2,128)S(1)} %get-tuple-element.16), channel_id=1, source_target_pairs={{0,32},{32,64},{64,96},{96,128},{128,160},{160,192},{192,224},{1,3... | collective-permute-start | bytes 442376 | tf_op jit(solution)/shard_map/ppermute | solution.py:231
  7.6 0.0 collective-permute-done.1
  7.7 0.7 collective-permute-done
  8.3 0.0 copy-start.1
  8.3 2.5 %fusion.12 = f32[1,36,33,512]{3,2,1,0:T(8,128)S(1)} fusion(f32[1,36,2,512]{3,2,1,0:T(2,128)S(1)} %collective-permute-done.1, f32[1,36,32,512]{3,2,1,0:T(8,128)S(1)} %broadcast_multiply_fusion, f32[1,36,2,512]{3,2,1,0:T(2,128)S(1)} %collective-permute-done, f32[36]{0:T(128)S(1)} %get-tuple-element.29, f32[36]{0:T(128)S(1)} %get-tuple-element.30, ...), kind=kLoop, calls=%fused_computation.25 | loop fusion | flops 10948608 | bytes 5087700 | tf_op jit(solution)/shard_map/mul | solution.py:263
  10.8 0.0 copy-done.1
  10.9 0.7 fusion.30
  11.6 2.8 %fusion.7 = f32[1,36,32,513]{3,2,1,0:T(8,128)S(1)} fusion(f32[1,36,32,512]{3,2,1,0:T(8,128)S(1)} %fusion.30, f32[36]{0:T(128)S(1)} %get-tuple-element.26, f32[36]{0:T(128)S(1)} %get-tuple-element.27, f32[36]{0:T(128)S(1)} %get-tuple-element.28, pred[36]{0:T(512)(128)(4,1)S(1)} %get-tuple-element.32), kind=kLoop, calls=%fused_computation.19 | loop fusion | flops 8273664 | bytes 4723668 | tf_op jit(solution)/shard_map/mul | solution.py:263
  14.4 0.0 copy-start.4
  14.4 0.0 copy-start.5
  14.4 0.7 fusion.28
  15.1 0.1 copy-done.4
  15.2 0.0 copy-done.5
  15.3 3.1 %fusion.19 = f32[1,37,32,512]{3,2,1,0:T(8,128)S(1)} fusion(f32[1,2,32,512]{3,2,1,0:T(8,128)S(1)} %get-tuple-element.15, f32[1,36,32,512]{3,2,1,0:T(8,128)S(1)} %fusion.28, f32[1,2,32,512]{3,2,1,0:T(8,128)S(1)} %get-tuple-element.14, f32[32,512]{1,0:T(8,128)S(1)} %copy-done.4, f32[37]{0:T(128)S(1)} %get-tuple-element.34, f32[32,512]{1,0:T(8,128)S(1)} %copy-done.5, ...), kind=kLoop, calls=%fused_computation.40 | loop fusion | flops 16973824 | bytes 5177644 | tf_op jit(solution)/shard_map/mul | solution.py:263
  18.4 0.6 fusion.26
  19.0 3.8 %copy.17 = f32[1,36,32,512]{3,0,1,2:T(1,128)} copy(f32[1,36,32,512]{3,2,1,0:T(8,128)S(1)} %fusion.26) | data formatting | bytes 4718592 | tf_op jit(solution)/shard_map/max | solution.py:471
  22.8 4.5 %all-to-all-start = ((f32[1,36,32,512]{3,0,1,2:T(1,128)}), f32[1,36,32,512]{3,0,1,2:T(1,128)S(1)}, u32[]{:S(2)}, u32[]{:S(2)}) async-start(f32[1,36,32,512]{3,0,1,2:T(1,128)} %copy.17), calls=%async_computation | async-start | bytes 4718592 | tf_op jit(solution)/shard_map/all_to_all | solution.py:472
  27.3 0.7 dynamic-slice_multiply_fusion
  28.1 0.1 multiply_multiply_fusion
  28.1 1.9 %subtract_cosine_fusion = f32[36,8,512]{2,1,0:T(8,128)S(1)} fusion(f32[8,512]{1,0:T(8,128)S(1)} %get-tuple-element.37, f32[36]{0:T(128)S(1)} %add_multiply_fusion), kind=kLoop, calls=%fused_computation.65 | loop fusion | flops 147456 | bytes 606352 | tf_op jit(solution)/shard_map/cos | solution.py:502
  30.1 26.8 %all-to-all-done = f32[1,36,32,512]{3,0,1,2:T(1,128)S(1)} async-done(((f32[1,36,32,512]{3,0,1,2:T(1,128)}), f32[1,36,32,512]{3,0,1,2:T(1,128)S(1)}, u32[]{:S(2)}, u32[]{:S(2)}) %all-to-all-start) | async-done | bytes 2359328 | tf_op jit(solution)/shard_map/all_to_all | solution.py:472
  56.9 0.8 multiply_reduce_fusion
  57.7 2.1 %collective-permute-start.2 = (f32[3,8,512]{2,1,0:T(8,128)S(1)}, f32[3,8,512]{2,1,0:T(8,128)S(1)}, u32[]{:S(2)}, u32[]{:S(2)}) collective-permute-start(f32[3,8,512]{2,1,0:T(8,128)S(1)} %pad_maximum_fusion.9), channel_id=1, source_target_pairs={{0,4},{4,0},{8,12},{12,8},{16,20},{20,16},{24,28},{28,24},{1,5},{5... | collective-permute-start | bytes 147464 | tf_op jit(solution)/shard_map/ppermute | solution.py:488
  59.8 2.1 %copy_bitcast_fusion.1.point_ref = f32[4,36,8,512]{3,2,1,0:T(8,128)} fusion(f32[1,36,32,512]{3,0,1,2:T(1,128)S(1)} %all-to-all-done), kind=kLoop, calls=%fused_computation.59 | loop fusion | bytes 4718592 | tf_op jit(solution)/shard_map/all_to_all | solution.py:472
  61.9 34.6 %shard_map.64 = (f32[2,36,8,512]{3,2,1,0:T(8,128)}, f32[2,36,8,512]{3,2,1,0:T(8,128)}) custom-call(f32[4,36,8,512]{3,2,1,0:T(8,128)} %copy_bitcast_fusion.1.point_ref), custom_call_target="tpu_custom_call" | custom-call | tf_op jit(solution)/shard_map/pallas_call | solution.py:210
  96.5 0.0 collective-permute-done.2
  96.6 1.5 %collective-permute-start.3 = (f32[3,8,512]{2,1,0:T(8,128)S(1)}, f32[3,8,512]{2,1,0:T(8,128)S(1)}, u32[]{:S(2)}, u32[]{:S(2)}) collective-permute-start(f32[3,8,512]{2,1,0:T(8,128)S(1)} %fusion.45), channel_id=1, source_target_pairs={{0,8},{4,12},{8,0},{12,4},{16,24},{20,28},{24,16},{28,20},{1,9},{5... | collective-permute-start | bytes 147464 | tf_op jit(solution)/shard_map/ppermute | solution.py:488
  98.1 0.0 copy-start
  98.1 0.0 copy-start.2
  98.1 0.0 copy-start.3
  98.1 2.4 %fusion.2 = f32[6,35,8,512]{3,2,1,0:T(8,128)S(1)} fusion(f32[4,36,8,512]{3,2,1,0:T(8,128)} %copy_bitcast_fusion.1.point_ref, f32[2,36,8,512]{3,2,1,0:T(8,128)} %get-tuple-element.8), kind=kLoop, calls=%fused_computation.10 | loop fusion | flops 860160 | bytes 6979584 | tf_op jit(solution)/shard_map/concatenate | solution.py:492
  100.6 1.1 collective-permute-done.3
  101.7 2.5 %collective-permute-start.4 = (f32[3,8,512]{2,1,0:T(8,128)S(1)}, f32[3,8,512]{2,1,0:T(8,128)S(1)}, u32[]{:S(2)}, u32[]{:S(2)}) collective-permute-start(f32[3,8,512]{2,1,0:T(8,128)S(1)} %fusion.49), channel_id=1, source_target_pairs={{0,16},{4,20},{8,24},{12,28},{16,0},{20,4},{24,8},{28,12},{1,17},{... | collective-permute-start | bytes 147464 | tf_op jit(solution)/shard_map/ppermute | solution.py:488
  104.1 0.0 copy-done
  104.1 0.0 copy-done.2
  104.1 0.0 copy-done.3
  104.1 1.4 multiply_subtract_fusion
  105.5 0.2 slice.194
  105.8 0.2 slice.195
  106.0 3.7 %collective-permute-done.4 = f32[3,8,512]{2,1,0:T(8,128)S(1)} collective-permute-done((f32[3,8,512]{2,1,0:T(8,128)S(1)}, f32[3,8,512]{2,1,0:T(8,128)S(1)}, u32[]{:S(2)}, u32[]{:S(2)}) %collective-permute-start.4) | collective-permute-done | bytes 49184 | tf_op jit(solution)/shard_map/ppermute | solution.py:488
  109.8 0.1 fusion.33
  109.9 1.9 %fusion.24 = f32[4,36,8,512]{3,2,1,0:T(8,128)S(1)} fusion(f32[6,36,8,512]{3,2,1,0:T(8,128)S(1)} %multiply_subtract_fusion, f32[4,35,8,512]{3,2,1,0:T(8,128)S(1)} %slice.194, f32[4,1,8,512]{3,2,1,0:T(8,128)S(1)} %slice.193, f32[4,3,8,512]{3,2,1,0:T(8,128)S(1)} %slice.196, f32[4,33,8,512]{3,2,1,0:T(8,128)S(1)} %slice.195, ...), kind=kLoop, calls=%fused_computation.48 | loop fusion | flops 8847360 | bytes 12550160 | tf_op jit(solution)/shard_map/mul | solution.py:503
  111.8 29.5 %all_to_all.36 = f32[4,36,8,512]{3,2,1,0:T(8,128)S(1)} all-to-all(f32[4,36,8,512]{3,2,1,0:T(8,128)S(1)} %fusion.24), channel_id=1, replica_groups=mesh['geo'=8,'z'=8,'y'=4] {'y'}, dimensions={0} | all-to-all | bytes 4718592 | tf_op jit(solution)/shard_map/all_to_all | solution.py:516
  141.3 1.7 %copy_bitcast_fusion = f32[1,36,32,512]{3,2,1,0:T(8,128)} fusion(f32[4,36,8,512]{3,2,1,0:T(8,128)S(1)} %all_to_all.36), kind=kLoop, calls=%fused_computation.58 | loop fusion | bytes 4718592 | tf_op jit(solution)/shard_map/all_to_all | solution.py:516
  (18 shorter events, 0.4 us)
Async XLA Ops:
  3.0 4.7 %collective-permute-start.1 = (f32[1,36,2,512]{3,2,1,0:T(2,128)S(1)}, f32[1,36,2,512]{3,2,1,0:T(2,128)S(1)}, u32[]{:S(2)}, u32[]{:S(2)}) collective-permute-start(f32[1,36,2,512]{3,2,1,0:T(2,128)S(1)} %get-tuple-element.17), channel_id=1, source_target_pairs={{32,0},{64,32},{96,64},{128,96},{160,128},{192,160},{224,192},{33,... | collective-permute-start | bytes 442376 | tf_op jit(solution)/shard_map/ppermute | solution.py:233
  4.3 4.0 %collective-permute-start = (f32[1,36,2,512]{3,2,1,0:T(2,128)S(1)}, f32[1,36,2,512]{3,2,1,0:T(2,128)S(1)}, u32[]{:S(2)}, u32[]{:S(2)}) collective-permute-start(f32[1,36,2,512]{3,2,1,0:T(2,128)S(1)} %get-tuple-element.16), channel_id=1, source_target_pairs={{0,32},{32,64},{64,96},{96,128},{128,160},{160,192},{192,224},{1,3... | collective-permute-start | bytes 442376 | tf_op jit(solution)/shard_map/ppermute | solution.py:231
  8.3 2.5 %copy-start.1 = (f32[1,36,32,512]{3,2,1,0:T(8,128)S(1)}, f32[1,36,32,512]{3,2,1,0:T(8,128)}, u32[]{:S(2)}) copy-start(f32[1,36,32,512]{3,2,1,0:T(8,128)} %param.8) | copy-start | bytes 7077892
  14.4 0.8 copy-start.4
  14.4 0.9 copy-start.5
  22.8 34.1 %all-to-all-start = ((f32[1,36,32,512]{3,0,1,2:T(1,128)}), f32[1,36,32,512]{3,0,1,2:T(1,128)S(1)}, u32[]{:S(2)}, u32[]{:S(2)}) async-start(f32[1,36,32,512]{3,0,1,2:T(1,128)} %copy.17), calls=%async_computation | async-start | bytes 4718592 | tf_op jit(solution)/shard_map/all_to_all | solution.py:472
  57.7 38.8 %collective-permute-start.2 = (f32[3,8,512]{2,1,0:T(8,128)S(1)}, f32[3,8,512]{2,1,0:T(8,128)S(1)}, u32[]{:S(2)}, u32[]{:S(2)}) collective-permute-start(f32[3,8,512]{2,1,0:T(8,128)S(1)} %pad_maximum_fusion.9), channel_id=1, source_target_pairs={{0,4},{4,0},{8,12},{12,8},{16,20},{20,16},{24,28},{28,24},{1,5},{5... | collective-permute-start | bytes 147464 | tf_op jit(solution)/shard_map/ppermute | solution.py:488
  96.6 5.1 %collective-permute-start.3 = (f32[3,8,512]{2,1,0:T(8,128)S(1)}, f32[3,8,512]{2,1,0:T(8,128)S(1)}, u32[]{:S(2)}, u32[]{:S(2)}) collective-permute-start(f32[3,8,512]{2,1,0:T(8,128)S(1)} %fusion.45), channel_id=1, source_target_pairs={{0,8},{4,12},{8,0},{12,4},{16,24},{20,28},{24,16},{28,20},{1,9},{5... | collective-permute-start | bytes 147464 | tf_op jit(solution)/shard_map/ppermute | solution.py:488
  98.1 6.0 %copy-start = (f32[4,36,8,512]{3,2,1,0:T(8,128)S(1)}, f32[4,36,8,512]{3,2,1,0:T(8,128)}, u32[]{:S(2)}) copy-start(f32[4,36,8,512]{3,2,1,0:T(8,128)} %copy_bitcast_fusion.1.point_ref) | copy-start | bytes 7077892
  98.1 6.0 %copy-start.2 = (f32[2,36,8,512]{3,2,1,0:T(8,128)S(1)}, f32[2,36,8,512]{3,2,1,0:T(8,128)}, u32[]{:S(2)}) copy-start(f32[2,36,8,512]{3,2,1,0:T(8,128)} %get-tuple-element.8) | copy-start | bytes 3538948
  98.1 6.0 %copy-start.3 = (f32[2,36,8,512]{3,2,1,0:T(8,128)S(1)}, f32[2,36,8,512]{3,2,1,0:T(8,128)}, u32[]{:S(2)}) copy-start(f32[2,36,8,512]{3,2,1,0:T(8,128)} %get-tuple-element.7) | copy-start | bytes 3538948
  101.7 8.1 %collective-permute-start.4 = (f32[3,8,512]{2,1,0:T(8,128)S(1)}, f32[3,8,512]{2,1,0:T(8,128)S(1)}, u32[]{:S(2)}, u32[]{:S(2)}) collective-permute-start(f32[3,8,512]{2,1,0:T(8,128)S(1)} %fusion.49), channel_id=1, source_target_pairs={{0,16},{4,20},{8,24},{12,28},{16,0},{20,4},{24,8},{28,12},{1,17},{... | collective-permute-start | bytes 147464 | tf_op jit(solution)/shard_map/ppermute | solution.py:488

commit v15 on v14

--- a/solution.py
+++ b/solution.py
@@ -483,10 +483,11 @@
         ]
     )
     lower, upper = z_halo(point, z_count)
-    step = 1
-    while step < z_count:
-        sums = sums + lax.ppermute(sums, "z", [(i, i ^ step) for i in range(z_count)])
-        step *= 2
+    shifted = [
+        lax.ppermute(sums, "z", [(i, (i + shift) % z_count) for i in range(z_count)])
+        for shift in range(1, z_count)
+    ]
+    sums = sums + sum(shifted)
     energy_sum, first_sum, root_sum = sums[0], sums[1], sums[2]
     energy = energy_sum + EPSILON
     ext = jnp.concatenate([lower, point, upper], axis=0)

time: 143 us -> 148 us (1.035)
  the two profiles are of different devices: /device:TPU:32 before, /device:TPU:2 now
where the time goes in v15:
time: 148 us; the launch traced here: 147 us
  waiting for transfers between devices  32.5 us (22%)
  Pallas kernels  28.8 us (19%)
  blocking collectives  28.3 us (19%)
  starting transfers between devices  25.6 us (17%)
  other arithmetic  23.1 us (16%)
  local copies, waits for them, and re-layouts  8.39 us (6%)
    pallas_call x1, Pallas kernels, z_halo(): pl.pallas_call(functools.partial(_z_halo_kernel, z_count), out_shape=(hal...  28.8 us
    all_to_all x1, blocking collectives, shards(): return lax.all_to_all(updated, 'y', split_axis=0, concat_axis=2, tiled=True)  28.3 us
    all_to_all x1, waiting for transfers between devices, shards(): lax.all_to_all(floored, 'y', split_axis=2, concat_axis=0, tiled=True)  25.6 us
    ppermute x7, starting transfers between devices, shards(): lax.ppermute(sums, 'z', [(i, (i + shift) % z_count) for i in range(z_coun...  17.4 us
    mul x3, other arithmetic, quick_flux(): return courant * face_value  8.41 us
    ppermute x1, waiting for transfers between devices, extended(): lax.ppermute(tail, axis, [(i, (i + 1) % count) for i in range(ends)])  4.37 us
    max x1, local copies, waits for them, and re-layouts, shards(): floored = jnp.maximum(advect(padded, turning, 1), 0.0)  3.83 us
    all_to_all x1, starting transfers between devices, shards(): lax.all_to_all(floored, 'y', split_axis=2, concat_axis=0, tiled=True)  3.82 us
  transfers between devices with their start and end apart: 10, of which 3 were waited for; matrix products, arithmetic and copies ran while one was open for 6% of the time, Pallas kernels for 20%

profile of v15, /device:TPU:2, one launch (start us, length us, event | category | flops | bytes accessed | tf_op | source)
XLA Modules:
  0.0 147.0 jit_solution(12583998555175902182)
XLA Ops:
  0.0 0.8 convert_element_type.84
  0.8 2.0 %broadcast_multiply_fusion = f32[1,36,32,512]{3,2,1,0:T(8,128)S(1)} fusion(f32[1,36,32,512]{3,2,1,0:T(8,128)} %param.8, f32[32,512]{1,0:T(8,128)S(1)} %convert_element_type.84), kind=kLoop, calls=%fused_computation.64 | loop fusion | flops 589824 | bytes 4784128 | tf_op jit(solution)/shard_map/mul | solution.py:455
  2.9 0.1 fusion.47
  3.0 1.9 %collective-permute-start.1 = (f32[1,36,2,512]{3,2,1,0:T(2,128)S(1)}, f32[1,36,2,512]{3,2,1,0:T(2,128)S(1)}, u32[]{:S(2)}, u32[]{:S(2)}) collective-permute-start(f32[1,36,2,512]{3,2,1,0:T(2,128)S(1)} %get-tuple-element.17), channel_id=1, source_target_pairs={{32,0},{64,32},{96,64},{128,96},{160,128},{192,160},{224,192},{33,... | collective-permute-start | bytes 442376 | tf_op jit(solution)/shard_map/ppermute | solution.py:233
  4.9 2.4 %collective-permute-start = (f32[1,36,2,512]{3,2,1,0:T(2,128)S(1)}, f32[1,36,2,512]{3,2,1,0:T(2,128)S(1)}, u32[]{:S(2)}, u32[]{:S(2)}) collective-permute-start(f32[1,36,2,512]{3,2,1,0:T(2,128)S(1)} %get-tuple-element.16), channel_id=1, source_target_pairs={{0,32},{32,64},{64,96},{96,128},{128,160},{160,192},{192,224},{1,3... | collective-permute-start | bytes 442376 | tf_op jit(solution)/shard_map/ppermute | solution.py:231
  7.6 0.0 collective-permute-done.1
  7.6 4.4 %collective-permute-done = f32[1,36,2,512]{3,2,1,0:T(2,128)S(1)} collective-permute-done((f32[1,36,2,512]{3,2,1,0:T(2,128)S(1)}, f32[1,36,2,512]{3,2,1,0:T(2,128)S(1)}, u32[]{:S(2)}, u32[]{:S(2)}) %collective-permute-start) | collective-permute-done | bytes 147488 | tf_op jit(solution)/shard_map/ppermute | solution.py:231
  12.0 2.5 %fusion.12 = f32[1,36,33,512]{3,2,1,0:T(8,128)S(1)} fusion(f32[1,36,2,512]{3,2,1,0:T(2,128)S(1)} %collective-permute-done.1, f32[1,36,32,512]{3,2,1,0:T(8,128)S(1)} %broadcast_multiply_fusion, f32[1,36,2,512]{3,2,1,0:T(2,128)S(1)} %collective-permute-done, f32[36]{0:T(128)S(1)} %get-tuple-element.29, f32[36]{0:T(128)S(1)} %get-tuple-element.30, ...), kind=kLoop, calls=%fused_computation.25 | loop fusion | flops 10948608 | bytes 5087700 | tf_op jit(solution)/shard_map/mul | solution.py:263
  14.6 0.7 fusion.30
  15.3 2.8 %fusion.7 = f32[1,36,32,513]{3,2,1,0:T(8,128)S(1)} fusion(f32[1,36,32,512]{3,2,1,0:T(8,128)S(1)} %fusion.30, f32[36]{0:T(128)S(1)} %get-tuple-element.26, f32[36]{0:T(128)S(1)} %get-tuple-element.27, f32[36]{0:T(128)S(1)} %get-tuple-element.28, pred[36]{0:T(512)(128)(4,1)S(1)} %get-tuple-element.32), kind=kLoop, calls=%fused_computation.19 | loop fusion | flops 8273664 | bytes 4723668 | tf_op jit(solution)/shard_map/mul | solution.py:263
  18.1 0.0 copy-start.4
  18.1 0.0 copy-start.5
  18.1 0.7 fusion.28
  18.8 0.1 copy-done.4
  18.9 0.0 copy-done.5
  19.0 3.1 %fusion.19 = f32[1,37,32,512]{3,2,1,0:T(8,128)S(1)} fusion(f32[1,2,32,512]{3,2,1,0:T(8,128)S(1)} %get-tuple-element.15, f32[1,36,32,512]{3,2,1,0:T(8,128)S(1)} %fusion.28, f32[1,2,32,512]{3,2,1,0:T(8,128)S(1)} %get-tuple-element.14, f32[32,512]{1,0:T(8,128)S(1)} %copy-done.4, f32[37]{0:T(128)S(1)} %get-tuple-element.34, f32[32,512]{1,0:T(8,128)S(1)} %copy-done.5, ...), kind=kLoop, calls=%fused_computation.40 | loop fusion | flops 16973824 | bytes 5177644 | tf_op jit(solution)/shard_map/mul | solution.py:263
  22.1 0.6 fusion.26
  22.7 3.8 %copy.17 = f32[1,36,32,512]{3,0,1,2:T(1,128)} copy(f32[1,36,32,512]{3,2,1,0:T(8,128)S(1)} %fusion.26) | data formatting | bytes 4718592 | tf_op jit(solution)/shard_map/max | solution.py:471
  26.5 3.8 %all-to-all-start = ((f32[1,36,32,512]{3,0,1,2:T(1,128)}), f32[1,36,32,512]{3,0,1,2:T(1,128)S(1)}, u32[]{:S(2)}, u32[]{:S(2)}) async-start(f32[1,36,32,512]{3,0,1,2:T(1,128)} %copy.17), calls=%async_computation | async-start | bytes 4718592 | tf_op jit(solution)/shard_map/all_to_all | solution.py:472
  30.4 0.7 dynamic-slice_multiply_fusion
  31.1 0.1 multiply_multiply_fusion
  31.2 1.9 %subtract_cosine_fusion = f32[36,8,512]{2,1,0:T(8,128)S(1)} fusion(f32[8,512]{1,0:T(8,128)S(1)} %get-tuple-element.37, f32[36]{0:T(128)S(1)} %add_multiply_fusion), kind=kLoop, calls=%fused_computation.65 | loop fusion | flops 147456 | bytes 606352 | tf_op jit(solution)/shard_map/cos | solution.py:503
  33.2 25.6 %all-to-all-done = f32[1,36,32,512]{3,0,1,2:T(1,128)S(1)} async-done(((f32[1,36,32,512]{3,0,1,2:T(1,128)}), f32[1,36,32,512]{3,0,1,2:T(1,128)S(1)}, u32[]{:S(2)}, u32[]{:S(2)}) %all-to-all-start) | async-done | bytes 2359328 | tf_op jit(solution)/shard_map/all_to_all | solution.py:472
  58.8 0.8 multiply_reduce_fusion
  59.6 6.1 %collective-permute-start.8 = (f32[3,8,512]{2,1,0:T(8,128)S(1)}, f32[3,8,512]{2,1,0:T(8,128)S(1)}, u32[]{:S(2)}, u32[]{:S(2)}) collective-permute-start(f32[3,8,512]{2,1,0:T(8,128)S(1)} %pad_maximum_fusion.9), channel_id=1, source_target_pairs={{0,28},{4,0},{8,4},{12,8},{16,12},{20,16},{24,20},{28,24},{1,29},{... | collective-permute-start | bytes 147464 | tf_op jit(solution)/shard_map/ppermute | solution.py:487
  65.7 1.5 collective-permute-start.7
  67.2 0.4 collective-permute-start.6
  67.6 5.0 %collective-permute-start.5 = (f32[3,8,512]{2,1,0:T(8,128)S(1)}, f32[3,8,512]{2,1,0:T(8,128)S(1)}, u32[]{:S(2)}, u32[]{:S(2)}) collective-permute-start(f32[3,8,512]{2,1,0:T(8,128)S(1)} %pad_maximum_fusion.9), channel_id=1, source_target_pairs={{0,16},{4,20},{8,24},{12,28},{16,0},{20,4},{24,8},{28,12},{1,17},{... | collective-permute-start | bytes 147464 | tf_op jit(solution)/shard_map/ppermute | solution.py:487
  72.6 0.0 collective-permute-start.4
  72.7 2.1 %copy_bitcast_fusion.1.point_ref = f32[4,36,8,512]{3,2,1,0:T(8,128)} fusion(f32[1,36,32,512]{3,0,1,2:T(1,128)S(1)} %all-to-all-done), kind=kLoop, calls=%fused_computation.59 | loop fusion | bytes 4718592 | tf_op jit(solution)/shard_map/all_to_all | solution.py:472
  74.8 28.8 %shard_map.64 = (f32[2,36,8,512]{3,2,1,0:T(8,128)}, f32[2,36,8,512]{3,2,1,0:T(8,128)}) custom-call(f32[4,36,8,512]{3,2,1,0:T(8,128)} %copy_bitcast_fusion.1.point_ref), custom_call_target="tpu_custom_call" | custom-call | tf_op jit(solution)/shard_map/pallas_call | solution.py:210
  103.6 0.0 copy-start
  103.7 2.5 %fusion.2 = f32[6,35,8,512]{3,2,1,0:T(8,128)S(1)} fusion(f32[4,36,8,512]{3,2,1,0:T(8,128)} %copy_bitcast_fusion.1.point_ref, f32[2,36,8,512]{3,2,1,0:T(8,128)} %get-tuple-element.8), kind=kLoop, calls=%fused_computation.10 | loop fusion | flops 860160 | bytes 6979584 | tf_op jit(solution)/shard_map/concatenate | solution.py:493
  106.1 0.0 collective-permute-done.8
  106.1 2.6 %collective-permute-start.2 = (f32[3,8,512]{2,1,0:T(8,128)S(1)}, f32[3,8,512]{2,1,0:T(8,128)S(1)}, u32[]{:S(2)}, u32[]{:S(2)}) collective-permute-start(f32[3,8,512]{2,1,0:T(8,128)S(1)} %pad_maximum_fusion.9), channel_id=1, source_target_pairs={{0,4},{4,8},{8,12},{12,16},{16,20},{20,24},{24,28},{28,0},{1,5},{5... | collective-permute-start | bytes 147464 | tf_op jit(solution)/shard_map/ppermute | solution.py:487
  108.7 0.0 collective-permute-done.7
  108.7 1.8 %collective-permute-start.3 = (f32[3,8,512]{2,1,0:T(8,128)S(1)}, f32[3,8,512]{2,1,0:T(8,128)S(1)}, u32[]{:S(2)}, u32[]{:S(2)}) collective-permute-start(f32[3,8,512]{2,1,0:T(8,128)S(1)} %pad_maximum_fusion.9), channel_id=1, source_target_pairs={{0,8},{4,12},{8,16},{12,20},{16,24},{20,28},{24,0},{28,4},{1,9},{5... | collective-permute-start | bytes 147464 | tf_op jit(solution)/shard_map/ppermute | solution.py:487
  110.5 1.4 multiply_subtract_fusion
  111.9 0.2 slice.194
  112.2 0.2 slice.195
  112.4 0.0 collective-permute-done.6
  112.4 0.0 collective-permute-done.5
  112.5 0.0 collective-permute-done.4
  112.5 2.5 %collective-permute-done.3 = f32[3,8,512]{2,1,0:T(8,128)S(1)} collective-permute-done((f32[3,8,512]{2,1,0:T(8,128)S(1)}, f32[3,8,512]{2,1,0:T(8,128)S(1)}, u32[]{:S(2)}, u32[]{:S(2)}) %collective-permute-start.3) | collective-permute-done | bytes 49184 | tf_op jit(solution)/shard_map/ppermute | solution.py:487
  115.1 0.1 fusion.33
  115.1 1.9 %fusion.24 = f32[4,36,8,512]{3,2,1,0:T(8,128)S(1)} fusion(f32[6,36,8,512]{3,2,1,0:T(8,128)S(1)} %multiply_subtract_fusion, f32[4,35,8,512]{3,2,1,0:T(8,128)S(1)} %slice.194, f32[4,1,8,512]{3,2,1,0:T(8,128)S(1)} %slice.193, f32[4,3,8,512]{3,2,1,0:T(8,128)S(1)} %slice.196, f32[4,33,8,512]{3,2,1,0:T(8,128)S(1)} %slice.195, ...), kind=kLoop, calls=%fused_computation.48 | loop fusion | flops 8847360 | bytes 12550160 | tf_op jit(solution)/shard_map/mul | solution.py:504
  117.1 28.3 %all_to_all.36 = f32[4,36,8,512]{3,2,1,0:T(8,128)S(1)} all-to-all(f32[4,36,8,512]{3,2,1,0:T(8,128)S(1)} %fusion.24), channel_id=1, replica_groups=mesh['geo'=8,'z'=8,'y'=4] {'y'}, dimensions={0} | all-to-all | bytes 4718592 | tf_op jit(solution)/shard_map/all_to_all | solution.py:517
  145.4 1.7 %copy_bitcast_fusion = f32[1,36,32,512]{3,2,1,0:T(8,128)} fusion(f32[4,36,8,512]{3,2,1,0:T(8,128)S(1)} %all_to_all.36), kind=kLoop, calls=%fused_computation.58 | loop fusion | bytes 4718592 | tf_op jit(solution)/shard_map/all_to_all | solution.py:517
  (24 shorter events, 0.4 us)
Async XLA Ops:
  3.0 4.6 %collective-permute-start.1 = (f32[1,36,2,512]{3,2,1,0:T(2,128)S(1)}, f32[1,36,2,512]{3,2,1,0:T(2,128)S(1)}, u32[]{:S(2)}, u32[]{:S(2)}) collective-permute-start(f32[1,36,2,512]{3,2,1,0:T(2,128)S(1)} %get-tuple-element.17), channel_id=1, source_target_pairs={{32,0},{64,32},{96,64},{128,96},{160,128},{192,160},{224,192},{33,... | collective-permute-start | bytes 442376 | tf_op jit(solution)/shard_map/ppermute | solution.py:233
  4.9 7.1 %collective-permute-start = (f32[1,36,2,512]{3,2,1,0:T(2,128)S(1)}, f32[1,36,2,512]{3,2,1,0:T(2,128)S(1)}, u32[]{:S(2)}, u32[]{:S(2)}) collective-permute-start(f32[1,36,2,512]{3,2,1,0:T(2,128)S(1)} %get-tuple-element.16), channel_id=1, source_target_pairs={{0,32},{32,64},{64,96},{96,128},{128,160},{160,192},{192,224},{1,3... | collective-permute-start | bytes 442376 | tf_op jit(solution)/shard_map/ppermute | solution.py:231
  12.0 2.5 %copy-start.1 = (f32[1,36,32,512]{3,2,1,0:T(8,128)S(1)}, f32[1,36,32,512]{3,2,1,0:T(8,128)}, u32[]{:S(2)}) copy-start(f32[1,36,32,512]{3,2,1,0:T(8,128)} %param.8) | copy-start | bytes 7077892
  18.1 0.8 copy-start.4
  18.1 0.9 copy-start.5
  26.5 32.3 %all-to-all-start = ((f32[1,36,32,512]{3,0,1,2:T(1,128)}), f32[1,36,32,512]{3,0,1,2:T(1,128)S(1)}, u32[]{:S(2)}, u32[]{:S(2)}) async-start(f32[1,36,32,512]{3,0,1,2:T(1,128)} %copy.17), calls=%async_computation | async-start | bytes 4718592 | tf_op jit(solution)/shard_map/all_to_all | solution.py:472
  59.6 46.5 %collective-permute-start.8 = (f32[3,8,512]{2,1,0:T(8,128)S(1)}, f32[3,8,512]{2,1,0:T(8,128)S(1)}, u32[]{:S(2)}, u32[]{:S(2)}) collective-permute-start(f32[3,8,512]{2,1,0:T(8,128)S(1)} %pad_maximum_fusion.9), channel_id=1, source_target_pairs={{0,28},{4,0},{8,4},{12,8},{16,12},{20,16},{24,20},{28,24},{1,29},{... | collective-permute-start | bytes 147464 | tf_op jit(solution)/shard_map/ppermute | solution.py:487
  65.7 43.0 %collective-permute-start.7 = (f32[3,8,512]{2,1,0:T(8,128)S(1)}, f32[3,8,512]{2,1,0:T(8,128)S(1)}, u32[]{:S(2)}, u32[]{:S(2)}) collective-permute-start(f32[3,8,512]{2,1,0:T(8,128)S(1)} %pad_maximum_fusion.9), channel_id=1, source_target_pairs={{0,24},{4,28},{8,0},{12,4},{16,8},{20,12},{24,16},{28,20},{1,25},{... | collective-permute-start | bytes 147464 | tf_op jit(solution)/shard_map/ppermute | solution.py:487
  67.2 45.3 %collective-permute-start.6 = (f32[3,8,512]{2,1,0:T(8,128)S(1)}, f32[3,8,512]{2,1,0:T(8,128)S(1)}, u32[]{:S(2)}, u32[]{:S(2)}) collective-permute-start(f32[3,8,512]{2,1,0:T(8,128)S(1)} %pad_maximum_fusion.9), channel_id=1, source_target_pairs={{0,20},{4,24},{8,28},{12,0},{16,4},{20,8},{24,12},{28,16},{1,21},{... | collective-permute-start | bytes 147464 | tf_op jit(solution)/shard_map/ppermute | solution.py:487
  67.6 44.8 %collective-permute-start.5 = (f32[3,8,512]{2,1,0:T(8,128)S(1)}, f32[3,8,512]{2,1,0:T(8,128)S(1)}, u32[]{:S(2)}, u32[]{:S(2)}) collective-permute-start(f32[3,8,512]{2,1,0:T(8,128)S(1)} %pad_maximum_fusion.9), channel_id=1, source_target_pairs={{0,16},{4,20},{8,24},{12,28},{16,0},{20,4},{24,8},{28,12},{1,17},{... | collective-permute-start | bytes 147464 | tf_op jit(solution)/shard_map/ppermute | solution.py:487
  72.6 39.8 %collective-permute-start.4 = (f32[3,8,512]{2,1,0:T(8,128)S(1)}, f32[3,8,512]{2,1,0:T(8,128)S(1)}, u32[]{:S(2)}, u32[]{:S(2)}) collective-permute-start(f32[3,8,512]{2,1,0:T(8,128)S(1)} %pad_maximum_fusion.9), channel_id=1, source_target_pairs={{0,12},{4,16},{8,20},{12,24},{16,28},{20,0},{24,4},{28,8},{1,13},{... | collective-permute-start | bytes 147464 | tf_op jit(solution)/shard_map/ppermute | solution.py:487
  103.6 6.9 %copy-start = (f32[4,36,8,512]{3,2,1,0:T(8,128)S(1)}, f32[4,36,8,512]{3,2,1,0:T(8,128)}, u32[]{:S(2)}) copy-start(f32[4,36,8,512]{3,2,1,0:T(8,128)} %copy_bitcast_fusion.1.point_ref) | copy-start | bytes 7077892
  103.6 6.9 %copy-start.2 = (f32[2,36,8,512]{3,2,1,0:T(8,128)S(1)}, f32[2,36,8,512]{3,2,1,0:T(8,128)}, u32[]{:S(2)}) copy-start(f32[2,36,8,512]{3,2,1,0:T(8,128)} %get-tuple-element.8) | copy-start | bytes 3538948
  103.7 6.9 %copy-start.3 = (f32[2,36,8,512]{3,2,1,0:T(8,128)S(1)}, f32[2,36,8,512]{3,2,1,0:T(8,128)}, u32[]{:S(2)}) copy-start(f32[2,36,8,512]{3,2,1,0:T(8,128)} %get-tuple-element.7) | copy-start | bytes 3538948
  106.1 6.3 %collective-permute-start.2 = (f32[3,8,512]{2,1,0:T(8,128)S(1)}, f32[3,8,512]{2,1,0:T(8,128)S(1)}, u32[]{:S(2)}, u32[]{:S(2)}) collective-permute-start(f32[3,8,512]{2,1,0:T(8,128)S(1)} %pad_maximum_fusion.9), channel_id=1, source_target_pairs={{0,4},{4,8},{8,12},{12,16},{16,20},{20,24},{24,28},{28,0},{1,5},{5... | collective-permute-start | bytes 147464 | tf_op jit(solution)/shard_map/ppermute | solution.py:487
  108.7 6.3 %collective-permute-start.3 = (f32[3,8,512]{2,1,0:T(8,128)S(1)}, f32[3,8,512]{2,1,0:T(8,128)S(1)}, u32[]{:S(2)}, u32[]{:S(2)}) collective-permute-start(f32[3,8,512]{2,1,0:T(8,128)S(1)} %pad_maximum_fusion.9), channel_id=1, source_target_pairs={{0,8},{4,12},{8,16},{12,20},{16,24},{20,28},{24,0},{28,4},{1,9},{5... | collective-permute-start | bytes 147464 | tf_op jit(solution)/shard_map/ppermute | solution.py:487

commit v16 on v14

--- a/solution.py
+++ b/solution.py
@@ -210,7 +210,7 @@
     return pl.pallas_call(
         functools.partial(_z_halo_kernel, z_count),
         out_shape=(halo, halo),
-        in_specs=[vmem],
+        in_specs=[pl.BlockSpec(memory_space=pl.ANY)],
         out_specs=(vmem, vmem),
         scratch_shapes=[
             pltpu.SemaphoreType.DMA((2,)),

time: 143 us -> 142 us (level)
    pallas_call x1, Pallas kernels: 34.6 us -> 33.2 us  [z_halo(): pl.pallas_call(functools.partial(_z_halo_kernel, z_count), out_shape=(hal...]
  transfers between devices with their start and end apart: 6 -> 6, of which waited for: 4 -> 4; matrix products, arithmetic and copies ran while one was open for 7% -> 7% of each run, Pallas kernels for 24% -> 23%
where the time goes in v16:
time: 142 us
  Pallas kernels  33.2 us (23%)
  waiting for transfers between devices  32.2 us (23%)
  blocking collectives  29.5 us (21%)
  other arithmetic  23 us (16%)
  starting transfers between devices  14.9 us (10%)
  local copies, waits for them, and re-layouts  8.39 us (6%)
    pallas_call x1, Pallas kernels, z_halo(): pl.pallas_call(functools.partial(_z_halo_kernel, z_count), out_shape=(hal...  33.2 us
    all_to_all x1, blocking collectives, shards(): return lax.all_to_all(updated, 'y', split_axis=0, concat_axis=2, tiled=True)  29.5 us
    all_to_all x1, waiting for transfers between devices, shards(): lax.all_to_all(floored, 'y', split_axis=2, concat_axis=0, tiled=True)  26.8 us
    mul x3, other arithmetic, quick_flux(): return courant * face_value  8.41 us
    ppermute x3, starting transfers between devices, shards(): lax.ppermute(sums, 'z', [(i, i ^ step) for i in range(z_count)])  6.07 us
    ppermute x3, waiting for transfers between devices, shards(): lax.ppermute(sums, 'z', [(i, i ^ step) for i in range(z_count)])  4.79 us
    all_to_all x1, starting transfers between devices, shards(): lax.all_to_all(floored, 'y', split_axis=2, concat_axis=0, tiled=True)  4.46 us
    max x1, local copies, waits for them, and re-layouts, shards(): floored = jnp.maximum(advect(padded, turning, 1), 0.0)  3.83 us
  transfers between devices with their start and end apart: 6, of which 4 were waited for; matrix products, arithmetic and copies ran while one was open for 7% of the time, Pallas kernels for 23%

profile of v16, /device:TPU:32, one launch (start us, length us, event | category | flops | bytes accessed | tf_op | source)
XLA Modules:
  0.0 141.5 jit_solution(6730159767085044791)
XLA Ops:
  0.0 0.8 convert_element_type.84
  0.8 2.0 %broadcast_multiply_fusion = f32[1,36,32,512]{3,2,1,0:T(8,128)S(1)} fusion(f32[1,36,32,512]{3,2,1,0:T(8,128)} %param.8, f32[32,512]{1,0:T(8,128)S(1)} %convert_element_type.84), kind=kLoop, calls=%fused_computation.64 | loop fusion | flops 589824 | bytes 4784128 | tf_op jit(solution)/shard_map/mul | solution.py:455
  2.9 0.1 fusion.48
  3.0 1.3 collective-permute-start.1
  4.3 3.0 %collective-permute-start = (f32[1,36,2,512]{3,2,1,0:T(2,128)S(1)}, f32[1,36,2,512]{3,2,1,0:T(2,128)S(1)}, u32[]{:S(2)}, u32[]{:S(2)}) collective-permute-start(f32[1,36,2,512]{3,2,1,0:T(2,128)S(1)} %get-tuple-element.16), channel_id=1, source_target_pairs={{0,32},{32,64},{64,96},{96,128},{128,160},{160,192},{192,224},{1,3... | collective-permute-start | bytes 442376 | tf_op jit(solution)/shard_map/ppermute | solution.py:231
  7.6 0.0 collective-permute-done.1
  7.7 0.7 collective-permute-done
  8.3 0.0 copy-start.1
  8.3 2.5 %fusion.12 = f32[1,36,33,512]{3,2,1,0:T(8,128)S(1)} fusion(f32[1,36,2,512]{3,2,1,0:T(2,128)S(1)} %collective-permute-done.1, f32[1,36,32,512]{3,2,1,0:T(8,128)S(1)} %broadcast_multiply_fusion, f32[1,36,2,512]{3,2,1,0:T(2,128)S(1)} %collective-permute-done, f32[36]{0:T(128)S(1)} %get-tuple-element.29, f32[36]{0:T(128)S(1)} %get-tuple-element.30, ...), kind=kLoop, calls=%fused_computation.25 | loop fusion | flops 10948608 | bytes 5087700 | tf_op jit(solution)/shard_map/mul | solution.py:263
  10.8 0.0 copy-done.1
  10.9 0.7 fusion.30
  11.6 2.8 %fusion.7 = f32[1,36,32,513]{3,2,1,0:T(8,128)S(1)} fusion(f32[1,36,32,512]{3,2,1,0:T(8,128)S(1)} %fusion.30, f32[36]{0:T(128)S(1)} %get-tuple-element.26, f32[36]{0:T(128)S(1)} %get-tuple-element.27, f32[36]{0:T(128)S(1)} %get-tuple-element.28, pred[36]{0:T(512)(128)(4,1)S(1)} %get-tuple-element.32), kind=kLoop, calls=%fused_computation.19 | loop fusion | flops 8273664 | bytes 4723668 | tf_op jit(solution)/shard_map/mul | solution.py:263
  14.4 0.0 copy-start.4
  14.4 0.0 copy-start.5
  14.4 0.7 fusion.28
  15.1 0.1 copy-done.4
  15.2 0.0 copy-done.5
  15.3 3.1 %fusion.19 = f32[1,37,32,512]{3,2,1,0:T(8,128)S(1)} fusion(f32[1,2,32,512]{3,2,1,0:T(8,128)S(1)} %get-tuple-element.15, f32[1,36,32,512]{3,2,1,0:T(8,128)S(1)} %fusion.28, f32[1,2,32,512]{3,2,1,0:T(8,128)S(1)} %get-tuple-element.14, f32[32,512]{1,0:T(8,128)S(1)} %copy-done.4, f32[37]{0:T(128)S(1)} %get-tuple-element.34, f32[32,512]{1,0:T(8,128)S(1)} %copy-done.5, ...), kind=kLoop, calls=%fused_computation.40 | loop fusion | flops 16973824 | bytes 5177644 | tf_op jit(solution)/shard_map/mul | solution.py:263
  18.4 0.6 fusion.26
  19.0 3.8 %copy.17 = f32[1,36,32,512]{3,0,1,2:T(1,128)} copy(f32[1,36,32,512]{3,2,1,0:T(8,128)S(1)} %fusion.26) | data formatting | bytes 4718592 | tf_op jit(solution)/shard_map/max | solution.py:471
  22.8 4.5 %all-to-all-start = ((f32[1,36,32,512]{3,0,1,2:T(1,128)}), f32[1,36,32,512]{3,0,1,2:T(1,128)S(1)}, u32[]{:S(2)}, u32[]{:S(2)}) async-start(f32[1,36,32,512]{3,0,1,2:T(1,128)} %copy.17), calls=%async_computation | async-start | bytes 4718592 | tf_op jit(solution)/shard_map/all_to_all | solution.py:472
  27.3 0.7 dynamic-slice_multiply_fusion
  28.1 0.1 multiply_multiply_fusion
  28.1 1.9 %subtract_cosine_fusion = f32[36,8,512]{2,1,0:T(8,128)S(1)} fusion(f32[8,512]{1,0:T(8,128)S(1)} %get-tuple-element.37, f32[36]{0:T(128)S(1)} %add_multiply_fusion), kind=kLoop, calls=%fused_computation.65 | loop fusion | flops 147456 | bytes 606352 | tf_op jit(solution)/shard_map/cos | solution.py:502
  30.1 26.8 %all-to-all-done = f32[1,36,32,512]{3,0,1,2:T(1,128)S(1)} async-done(((f32[1,36,32,512]{3,0,1,2:T(1,128)}), f32[1,36,32,512]{3,0,1,2:T(1,128)S(1)}, u32[]{:S(2)}, u32[]{:S(2)}) %all-to-all-start) | async-done | bytes 2359328 | tf_op jit(solution)/shard_map/all_to_all | solution.py:472
  56.9 0.8 multiply_reduce_fusion
  57.7 2.1 %collective-permute-start.2 = (f32[3,8,512]{2,1,0:T(8,128)S(1)}, f32[3,8,512]{2,1,0:T(8,128)S(1)}, u32[]{:S(2)}, u32[]{:S(2)}) collective-permute-start(f32[3,8,512]{2,1,0:T(8,128)S(1)} %pad_maximum_fusion.9), channel_id=1, source_target_pairs={{0,4},{4,0},{8,12},{12,8},{16,20},{20,16},{24,28},{28,24},{1,5},{5... | collective-permute-start | bytes 147464 | tf_op jit(solution)/shard_map/ppermute | solution.py:488
  59.8 2.1 %copy_bitcast_fusion.1.point_ref = f32[4,36,8,512]{3,2,1,0:T(8,128)} fusion(f32[1,36,32,512]{3,0,1,2:T(1,128)S(1)} %all-to-all-done), kind=kLoop, calls=%fused_computation.59 | loop fusion | bytes 4718592 | tf_op jit(solution)/shard_map/all_to_all | solution.py:472
  61.9 33.2 %shard_map.64 = (f32[2,36,8,512]{3,2,1,0:T(8,128)}, f32[2,36,8,512]{3,2,1,0:T(8,128)}) custom-call(f32[4,36,8,512]{3,2,1,0:T(8,128)} %copy_bitcast_fusion.1.point_ref), custom_call_target="tpu_custom_call" | custom-call | tf_op jit(solution)/shard_map/pallas_call | solution.py:210
  95.1 0.0 collective-permute-done.2
  95.1 1.5 %collective-permute-start.3 = (f32[3,8,512]{2,1,0:T(8,128)S(1)}, f32[3,8,512]{2,1,0:T(8,128)S(1)}, u32[]{:S(2)}, u32[]{:S(2)}) collective-permute-start(f32[3,8,512]{2,1,0:T(8,128)S(1)} %fusion.45), channel_id=1, source_target_pairs={{0,8},{4,12},{8,0},{12,4},{16,24},{20,28},{24,16},{28,20},{1,9},{5... | collective-permute-start | bytes 147464 | tf_op jit(solution)/shard_map/ppermute | solution.py:488
  96.7 0.0 copy-start
  96.7 0.0 copy-start.2
  96.7 0.0 copy-start.3
  96.7 2.4 %fusion.2 = f32[6,35,8,512]{3,2,1,0:T(8,128)S(1)} fusion(f32[4,36,8,512]{3,2,1,0:T(8,128)} %copy_bitcast_fusion.1.point_ref, f32[2,36,8,512]{3,2,1,0:T(8,128)} %get-tuple-element.8), kind=kLoop, calls=%fused_computation.10 | loop fusion | flops 860160 | bytes 6979584 | tf_op jit(solution)/shard_map/concatenate | solution.py:492
  99.1 1.1 collective-permute-done.3
  100.2 2.5 %collective-permute-start.4 = (f32[3,8,512]{2,1,0:T(8,128)S(1)}, f32[3,8,512]{2,1,0:T(8,128)S(1)}, u32[]{:S(2)}, u32[]{:S(2)}) collective-permute-start(f32[3,8,512]{2,1,0:T(8,128)S(1)} %fusion.49), channel_id=1, source_target_pairs={{0,16},{4,20},{8,24},{12,28},{16,0},{20,4},{24,8},{28,12},{1,17},{... | collective-permute-start | bytes 147464 | tf_op jit(solution)/shard_map/ppermute | solution.py:488
  102.7 0.0 copy-done
  102.7 0.0 copy-done.2
  102.7 0.0 copy-done.3
  102.7 1.4 multiply_subtract_fusion
  104.1 0.2 slice.194
  104.4 0.2 slice.195
  104.6 3.7 %collective-permute-done.4 = f32[3,8,512]{2,1,0:T(8,128)S(1)} collective-permute-done((f32[3,8,512]{2,1,0:T(8,128)S(1)}, f32[3,8,512]{2,1,0:T(8,128)S(1)}, u32[]{:S(2)}, u32[]{:S(2)}) %collective-permute-start.4) | collective-permute-done | bytes 49184 | tf_op jit(solution)/shard_map/ppermute | solution.py:488
  108.3 0.1 fusion.33
  108.4 1.9 %fusion.24 = f32[4,36,8,512]{3,2,1,0:T(8,128)S(1)} fusion(f32[6,36,8,512]{3,2,1,0:T(8,128)S(1)} %multiply_subtract_fusion, f32[4,35,8,512]{3,2,1,0:T(8,128)S(1)} %slice.194, f32[4,1,8,512]{3,2,1,0:T(8,128)S(1)} %slice.193, f32[4,3,8,512]{3,2,1,0:T(8,128)S(1)} %slice.196, f32[4,33,8,512]{3,2,1,0:T(8,128)S(1)} %slice.195, ...), kind=kLoop, calls=%fused_computation.48 | loop fusion | flops 8847360 | bytes 12550160 | tf_op jit(solution)/shard_map/mul | solution.py:503
  110.4 29.5 %all_to_all.36 = f32[4,36,8,512]{3,2,1,0:T(8,128)S(1)} all-to-all(f32[4,36,8,512]{3,2,1,0:T(8,128)S(1)} %fusion.24), channel_id=1, replica_groups=mesh['geo'=8,'z'=8,'y'=4] {'y'}, dimensions={0} | all-to-all | bytes 4718592 | tf_op jit(solution)/shard_map/all_to_all | solution.py:516
  139.9 1.7 %copy_bitcast_fusion = f32[1,36,32,512]{3,2,1,0:T(8,128)} fusion(f32[4,36,8,512]{3,2,1,0:T(8,128)S(1)} %all_to_all.36), kind=kLoop, calls=%fused_computation.58 | loop fusion | bytes 4718592 | tf_op jit(solution)/shard_map/all_to_all | solution.py:516
  (18 shorter events, 0.4 us)
Async XLA Ops:
  3.0 4.7 %collective-permute-start.1 = (f32[1,36,2,512]{3,2,1,0:T(2,128)S(1)}, f32[1,36,2,512]{3,2,1,0:T(2,128)S(1)}, u32[]{:S(2)}, u32[]{:S(2)}) collective-permute-start(f32[1,36,2,512]{3,2,1,0:T(2,128)S(1)} %get-tuple-element.17), channel_id=1, source_target_pairs={{32,0},{64,32},{96,64},{128,96},{160,128},{192,160},{224,192},{33,... | collective-permute-start | bytes 442376 | tf_op jit(solution)/shard_map/ppermute | solution.py:233
  4.3 4.0 %collective-permute-start = (f32[1,36,2,512]{3,2,1,0:T(2,128)S(1)}, f32[1,36,2,512]{3,2,1,0:T(2,128)S(1)}, u32[]{:S(2)}, u32[]{:S(2)}) collective-permute-start(f32[1,36,2,512]{3,2,1,0:T(2,128)S(1)} %get-tuple-element.16), channel_id=1, source_target_pairs={{0,32},{32,64},{64,96},{96,128},{128,160},{160,192},{192,224},{1,3... | collective-permute-start | bytes 442376 | tf_op jit(solution)/shard_map/ppermute | solution.py:231
  8.3 2.5 %copy-start.1 = (f32[1,36,32,512]{3,2,1,0:T(8,128)S(1)}, f32[1,36,32,512]{3,2,1,0:T(8,128)}, u32[]{:S(2)}) copy-start(f32[1,36,32,512]{3,2,1,0:T(8,128)} %param.8) | copy-start | bytes 7077892
  14.4 0.8 copy-start.4
  14.4 0.9 copy-start.5
  22.8 34.1 %all-to-all-start = ((f32[1,36,32,512]{3,0,1,2:T(1,128)}), f32[1,36,32,512]{3,0,1,2:T(1,128)S(1)}, u32[]{:S(2)}, u32[]{:S(2)}) async-start(f32[1,36,32,512]{3,0,1,2:T(1,128)} %copy.17), calls=%async_computation | async-start | bytes 4718592 | tf_op jit(solution)/shard_map/all_to_all | solution.py:472
  57.7 37.4 %collective-permute-start.2 = (f32[3,8,512]{2,1,0:T(8,128)S(1)}, f32[3,8,512]{2,1,0:T(8,128)S(1)}, u32[]{:S(2)}, u32[]{:S(2)}) collective-permute-start(f32[3,8,512]{2,1,0:T(8,128)S(1)} %pad_maximum_fusion.9), channel_id=1, source_target_pairs={{0,4},{4,0},{8,12},{12,8},{16,20},{20,16},{24,28},{28,24},{1,5},{5... | collective-permute-start | bytes 147464 | tf_op jit(solution)/shard_map/ppermute | solution.py:488
  95.1 5.1 %collective-permute-start.3 = (f32[3,8,512]{2,1,0:T(8,128)S(1)}, f32[3,8,512]{2,1,0:T(8,128)S(1)}, u32[]{:S(2)}, u32[]{:S(2)}) collective-permute-start(f32[3,8,512]{2,1,0:T(8,128)S(1)} %fusion.45), channel_id=1, source_target_pairs={{0,8},{4,12},{8,0},{12,4},{16,24},{20,28},{24,16},{28,20},{1,9},{5... | collective-permute-start | bytes 147464 | tf_op jit(solution)/shard_map/ppermute | solution.py:488
  96.7 6.0 %copy-start = (f32[4,36,8,512]{3,2,1,0:T(8,128)S(1)}, f32[4,36,8,512]{3,2,1,0:T(8,128)}, u32[]{:S(2)}) copy-start(f32[4,36,8,512]{3,2,1,0:T(8,128)} %copy_bitcast_fusion.1.point_ref) | copy-start | bytes 7077892
  96.7 6.0 %copy-start.2 = (f32[2,36,8,512]{3,2,1,0:T(8,128)S(1)}, f32[2,36,8,512]{3,2,1,0:T(8,128)}, u32[]{:S(2)}) copy-start(f32[2,36,8,512]{3,2,1,0:T(8,128)} %get-tuple-element.8) | copy-start | bytes 3538948
  96.7 6.0 %copy-start.3 = (f32[2,36,8,512]{3,2,1,0:T(8,128)S(1)}, f32[2,36,8,512]{3,2,1,0:T(8,128)}, u32[]{:S(2)}) copy-start(f32[2,36,8,512]{3,2,1,0:T(8,128)} %get-tuple-element.7) | copy-start | bytes 3538948
  100.2 8.1 %collective-permute-start.4 = (f32[3,8,512]{2,1,0:T(8,128)S(1)}, f32[3,8,512]{2,1,0:T(8,128)S(1)}, u32[]{:S(2)}, u32[]{:S(2)}) collective-permute-start(f32[3,8,512]{2,1,0:T(8,128)S(1)} %fusion.49), channel_id=1, source_target_pairs={{0,16},{4,20},{8,24},{12,28},{16,0},{20,4},{24,8},{28,12},{1,17},{... | collective-permute-start | bytes 147464 | tf_op jit(solution)/shard_map/ppermute | solution.py:488

commit v17 on v16

--- a/solution.py
+++ b/solution.py
@@ -469,7 +469,11 @@
     )
     padded = jnp.concatenate([density[:, -2:], density, density[:, :2]], axis=1)
     floored = jnp.maximum(advect(padded, turning, 1), 0.0)
-    point = lax.all_to_all(floored, "y", split_axis=2, concat_axis=0, tiled=True)
+    y_count = lax.axis_size("y")
+    quarters = jnp.transpose(
+        floored[0].reshape(dir_count, y_count, row_count // y_count, col_count), (1, 0, 2, 3)
+    )
+    point = lax.all_to_all(quarters, "y", split_axis=0, concat_axis=0, tiled=True)
     group = point.shape[0]
     part_rows = point.shape[2]
     group_ids = (z_pos * group + jnp.arange(group)).astype(jnp.float32)

time: 142 us -> 143 us (level)
  waiting for transfers between devices: 32.2 us -> 37.4 us
  starting transfers between devices: 14.9 us -> 13.1 us
    ppermute x3, waiting for transfers between devices: 4.79 us -> 9.91 us  [shards(): lax.ppermute(sums, 'z', [(i, i ^ step) for i in range(z_count)])]
    max x1 -> x0, local copies, waits for them, and re-layouts: 3.83 us -> none  [shards(): floored = jnp.maximum(advect(padded, turning, 1), 0.0)]
    unnamed x12 -> x15, local copies, waits for them, and re-layouts: 0.15 us -> 3.56 us
    concatenate x1 -> x0, other arithmetic: 2.44 us -> none  [shards(): ext = jnp.concatenate([lower, point, upper], axis=0)]
    all_to_all x1 -> x0, local copies, waits for them, and re-layouts: 2.13 us -> none  [shards(): lax.all_to_all(floored, 'y', split_axis=2, concat_axis=0, tiled=True)]
    transpose x0 -> x1, other arithmetic: none -> 1.98 us  [shards(): jnp.transpose(floored[0].reshape(dir_count, y_count, row_count // y_count...]
    ppermute x3, starting transfers between devices: 6.07 us -> 4.27 us  [shards(): lax.ppermute(sums, 'z', [(i, i ^ step) for i in range(z_count)])]
  transfers between devices with their start and end apart: 6 -> 6, of which waited for: 4 -> 5; matrix products, arithmetic and copies ran while one was open for 7% -> 4% of each run, Pallas kernels for 23% -> 0%
where the time goes in v17:
time: 143 us; the launch traced here: 142 us
  waiting for transfers between devices  37.4 us (26%)
  Pallas kernels  34.3 us (24%)
  blocking collectives  28.5 us (20%)
  other arithmetic  21.6 us (15%)
  starting transfers between devices  13.1 us (9%)
  local copies, waits for them, and re-layouts  7.04 us (5%)
    pallas_call x1, Pallas kernels, z_halo(): pl.pallas_call(functools.partial(_z_halo_kernel, z_count), out_shape=(hal...  34.3 us
    all_to_all x1, blocking collectives, shards(): return lax.all_to_all(updated, 'y', split_axis=0, concat_axis=2, tiled=True)  28.5 us
    all_to_all x1, waiting for transfers between devices, shards(): lax.all_to_all(quarters, 'y', split_axis=0, concat_axis=0, tiled=True)  26.8 us
    ppermute x3, waiting for transfers between devices, shards(): lax.ppermute(sums, 'z', [(i, i ^ step) for i in range(z_count)])  9.91 us
    mul x3, other arithmetic, quick_flux(): return courant * face_value  8.41 us
    all_to_all x1, starting transfers between devices, shards(): lax.all_to_all(quarters, 'y', split_axis=0, concat_axis=0, tiled=True)  4.46 us
    ppermute x3, starting transfers between devices, shards(): lax.ppermute(sums, 'z', [(i, i ^ step) for i in range(z_count)])  4.27 us
    unnamed x15, local copies, waits for them, and re-layouts  3.56 us
  transfers between devices with their start and end apart: 6, of which 5 were waited for; matrix products, arithmetic and copies ran while one was open for 4% of the time, Pallas kernels for 0%

profile of v17, /device:TPU:32, one launch (start us, length us, event | category | flops | bytes accessed | tf_op | source)
XLA Modules:
  0.0 142.2 jit_solution(12176505456958088345)
XLA Ops:
  0.0 0.8 convert_element_type.84
  0.8 2.0 %broadcast_multiply_fusion = f32[1,36,32,512]{3,2,1,0:T(8,128)S(1)} fusion(f32[1,36,32,512]{3,2,1,0:T(8,128)} %param.8, f32[32,512]{1,0:T(8,128)S(1)} %convert_element_type.84), kind=kLoop, calls=%fused_computation.58 | loop fusion | flops 589824 | bytes 4784128 | tf_op jit(solution)/shard_map/mul | solution.py:455
  2.9 0.1 fusion.46
  3.0 1.3 collective-permute-start.1
  4.3 3.0 %collective-permute-start = (f32[1,36,2,512]{3,2,1,0:T(2,128)S(1)}, f32[1,36,2,512]{3,2,1,0:T(2,128)S(1)}, u32[]{:S(2)}, u32[]{:S(2)}) collective-permute-start(f32[1,36,2,512]{3,2,1,0:T(2,128)S(1)} %get-tuple-element.18), channel_id=1, source_target_pairs={{0,32},{32,64},{64,96},{96,128},{128,160},{160,192},{192,224},{1,3... | collective-permute-start | bytes 442376 | tf_op jit(solution)/shard_map/ppermute | solution.py:231
  7.6 0.0 collective-permute-done.1
  7.7 0.7 collective-permute-done
  8.3 2.5 %fusion.9 = f32[1,36,33,512]{3,2,1,0:T(8,128)S(1)} fusion(f32[1,36,2,512]{3,2,1,0:T(2,128)S(1)} %collective-permute-done.1, f32[1,36,32,512]{3,2,1,0:T(8,128)S(1)} %broadcast_multiply_fusion, f32[1,36,2,512]{3,2,1,0:T(2,128)S(1)} %collective-permute-done, f32[36]{0:T(128)S(1)} %get-tuple-element.31, f32[36]{0:T(128)S(1)} %get-tuple-element.32, ...), kind=kLoop, calls=%fused_computation.19 | loop fusion | flops 10948608 | bytes 5087700 | tf_op jit(solution)/shard_map/mul | solution.py:263
  10.8 0.0 copy-done.2
  10.9 0.7 fusion.28
  11.6 2.8 %fusion.4 = f32[1,36,32,513]{3,2,1,0:T(8,128)S(1)} fusion(f32[1,36,32,512]{3,2,1,0:T(8,128)S(1)} %fusion.28, f32[36]{0:T(128)S(1)} %get-tuple-element.28, f32[36]{0:T(128)S(1)} %get-tuple-element.29, f32[36]{0:T(128)S(1)} %get-tuple-element.30, pred[36]{0:T(512)(128)(4,1)S(1)} %get-tuple-element.34), kind=kLoop, calls=%fused_computation.13 | loop fusion | flops 8273664 | bytes 4723668 | tf_op jit(solution)/shard_map/mul | solution.py:263
  14.4 0.0 copy-start.5
  14.4 0.0 copy-start.6
  14.4 0.7 fusion.26
  15.1 0.1 copy-done.5
  15.2 0.0 copy-done.6
  15.3 3.1 %fusion.16 = f32[1,37,32,512]{3,2,1,0:T(8,128)S(1)} fusion(f32[1,2,32,512]{3,2,1,0:T(8,128)S(1)} %get-tuple-element.17, f32[1,36,32,512]{3,2,1,0:T(8,128)S(1)} %fusion.26, f32[1,2,32,512]{3,2,1,0:T(8,128)S(1)} %get-tuple-element.16, f32[32,512]{1,0:T(8,128)S(1)} %copy-done.5, f32[37]{0:T(128)S(1)} %get-tuple-element.36, f32[32,512]{1,0:T(8,128)S(1)} %copy-done.6, ...), kind=kLoop, calls=%fused_computation.34 | loop fusion | flops 16973824 | bytes 5177644 | tf_op jit(solution)/shard_map/mul | solution.py:263
  18.4 2.0 %copy_bitcast_fusion.1 = f32[4,36,8,512]{3,2,1,0:T(8,128)} fusion(f32[1,36,32,512]{3,2,1,0:T(8,128)S(1)} %fusion.26, f32[1,37,32,512]{3,2,1,0:T(8,128)S(1)} %fusion.16), kind=kLoop, calls=%fused_computation.54 | loop fusion | flops 1769472 | bytes 9437184 | tf_op jit(solution)/shard_map/transpose | solution.py:473
  20.4 4.5 %all-to-all-start = ((f32[4,36,8,512]{3,2,1,0:T(8,128)}), f32[4,36,8,512]{3,2,1,0:T(8,128)S(1)}, u32[]{:S(2)}, u32[]{:S(2)}) async-start(f32[4,36,8,512]{3,2,1,0:T(8,128)} %copy_bitcast_fusion.1), calls=%async_computation | async-start | bytes 4718592 | tf_op jit(solution)/shard_map/all_to_all | solution.py:476
  24.9 0.7 dynamic-slice_multiply_fusion
  25.6 0.1 multiply_multiply_fusion
  25.7 1.9 %subtract_cosine_fusion = f32[36,8,512]{2,1,0:T(8,128)S(1)} fusion(f32[8,512]{1,0:T(8,128)S(1)} %get-tuple-element.39, f32[36]{0:T(128)S(1)} %add_multiply_fusion), kind=kLoop, calls=%fused_computation.59 | loop fusion | flops 147456 | bytes 606352 | tf_op jit(solution)/shard_map/cos | solution.py:506
  27.6 26.8 %all-to-all-done.point_ref = f32[4,36,8,512]{3,2,1,0:T(8,128)S(1)} async-done(((f32[4,36,8,512]{3,2,1,0:T(8,128)}), f32[4,36,8,512]{3,2,1,0:T(8,128)S(1)}, u32[]{:S(2)}, u32[]{:S(2)}) %all-to-all-start) | async-done | bytes 2359328 | tf_op jit(solution)/shard_map/all_to_all | solution.py:476
  54.4 1.4 copy-done
  55.8 34.3 %shard_map.64 = (f32[2,36,8,512]{3,2,1,0:T(8,128)}, f32[2,36,8,512]{3,2,1,0:T(8,128)}) custom-call(f32[4,36,8,512]{3,2,1,0:T(8,128)} %copy-done), custom_call_target="tpu_custom_call" | custom-call | tf_op jit(solution)/shard_map/pallas_call | solution.py:210
  90.1 0.0 copy-start.1
  90.1 1.5 %constant_dynamic-update-slice_fusion.3 = f32[6,36,8,512]{3,2,1,0:T(8,128)S(1)} fusion(f32[2,36,8,512]{3,2,1,0:T(8,128)} %get-tuple-element.7), kind=kLoop, calls=%fused_computation.83 | loop fusion | bytes 2359296
  91.6 0.5 copy-done.1
  92.1 0.9 multiply_reduce_fusion
  93.1 0.1 collective-permute-start.2
  93.2 4.1 %collective-permute-done.2 = f32[3,8,512]{2,1,0:T(8,128)S(1)} collective-permute-done((f32[3,8,512]{2,1,0:T(8,128)S(1)}, f32[3,8,512]{2,1,0:T(8,128)S(1)}, u32[]{:S(2)}, u32[]{:S(2)}) %collective-permute-start.2) | collective-permute-done | bytes 49184 | tf_op jit(solution)/shard_map/ppermute | solution.py:492
  97.2 1.5 %collective-permute-start.3 = (f32[3,8,512]{2,1,0:T(8,128)S(1)}, f32[3,8,512]{2,1,0:T(8,128)S(1)}, u32[]{:S(2)}, u32[]{:S(2)}) collective-permute-start(f32[3,8,512]{2,1,0:T(8,128)S(1)} %fusion.43), channel_id=1, source_target_pairs={{0,8},{4,12},{8,0},{12,4},{16,24},{20,28},{24,16},{28,20},{1,9},{5... | collective-permute-start | bytes 147464 | tf_op jit(solution)/shard_map/ppermute | solution.py:492
  98.8 0.0 copy-done.4
  98.8 0.1 constant_dynamic-update-slice_fusion
  98.9 0.5 slice.193
  99.4 0.0 copy-start.3
  99.4 0.5 slice.190
  99.9 2.4 %collective-permute-done.3 = f32[3,8,512]{2,1,0:T(8,128)S(1)} collective-permute-done((f32[3,8,512]{2,1,0:T(8,128)S(1)}, f32[3,8,512]{2,1,0:T(8,128)S(1)}, u32[]{:S(2)}, u32[]{:S(2)}) %collective-permute-start.3) | collective-permute-done | bytes 49184 | tf_op jit(solution)/shard_map/ppermute | solution.py:492
  102.3 2.6 %collective-permute-start.4 = (f32[3,8,512]{2,1,0:T(8,128)S(1)}, f32[3,8,512]{2,1,0:T(8,128)S(1)}, u32[]{:S(2)}, u32[]{:S(2)}) collective-permute-start(f32[3,8,512]{2,1,0:T(8,128)S(1)} %fusion.47), channel_id=1, source_target_pairs={{0,16},{4,20},{8,24},{12,28},{16,0},{20,4},{24,8},{28,12},{1,17},{... | collective-permute-start | bytes 147464 | tf_op jit(solution)/shard_map/ppermute | solution.py:492
  105.0 0.0 copy-done.3
  105.0 1.4 multiply_subtract_fusion
  106.4 0.3 slice.196
  106.7 0.3 slice.197
  107.0 3.5 %collective-permute-done.4 = f32[3,8,512]{2,1,0:T(8,128)S(1)} collective-permute-done((f32[3,8,512]{2,1,0:T(8,128)S(1)}, f32[3,8,512]{2,1,0:T(8,128)S(1)}, u32[]{:S(2)}, u32[]{:S(2)}) %collective-permute-start.4) | collective-permute-done | bytes 49184 | tf_op jit(solution)/shard_map/ppermute | solution.py:492
  110.5 0.1 fusion.31
  110.6 1.4 %fusion.21 = f32[4,36,8,512]{3,2,1,0:T(8,128)S(1)} fusion(f32[6,36,8,512]{3,2,1,0:T(8,128)S(1)} %multiply_subtract_fusion, f32[4,35,8,512]{3,2,1,0:T(8,128)S(1)} %slice.196, f32[4,1,8,512]{3,2,1,0:T(8,128)S(1)} %slice.195, f32[4,3,8,512]{3,2,1,0:T(8,128)S(1)} %slice.198, f32[4,33,8,512]{3,2,1,0:T(8,128)S(1)} %slice.197, f32[4,36,8,512]{3,2,1,0:T(8,128)S(1)} %copy-done.1, ...), kind=kLoop, calls=%fused_computation.42 | loop fusion | flops 8847360 | bytes 12550160 | tf_op jit(solution)/shard_map/mul | solution.py:507
  112.0 28.5 %all_to_all.23 = f32[4,36,8,512]{3,2,1,0:T(8,128)S(1)} all-to-all(f32[4,36,8,512]{3,2,1,0:T(8,128)S(1)} %fusion.21), channel_id=1, replica_groups=mesh['geo'=8,'z'=8,'y'=4] {'y'}, dimensions={0} | all-to-all | bytes 4718592 | tf_op jit(solution)/shard_map/all_to_all | solution.py:520
  140.5 1.7 %copy_bitcast_fusion = f32[1,36,32,512]{3,2,1,0:T(8,128)} fusion(f32[4,36,8,512]{3,2,1,0:T(8,128)S(1)} %all_to_all.23), kind=kLoop, calls=%fused_computation.53 | loop fusion | bytes 4718592 | tf_op jit(solution)/shard_map/all_to_all | solution.py:520
  (23 shorter events, 0.4 us)
Async XLA Ops:
  3.0 4.7 %collective-permute-start.1 = (f32[1,36,2,512]{3,2,1,0:T(2,128)S(1)}, f32[1,36,2,512]{3,2,1,0:T(2,128)S(1)}, u32[]{:S(2)}, u32[]{:S(2)}) collective-permute-start(f32[1,36,2,512]{3,2,1,0:T(2,128)S(1)} %get-tuple-element.19), channel_id=1, source_target_pairs={{32,0},{64,32},{96,64},{128,96},{160,128},{192,160},{224,192},{33,... | collective-permute-start | bytes 442376 | tf_op jit(solution)/shard_map/ppermute | solution.py:233
  4.3 4.0 %collective-permute-start = (f32[1,36,2,512]{3,2,1,0:T(2,128)S(1)}, f32[1,36,2,512]{3,2,1,0:T(2,128)S(1)}, u32[]{:S(2)}, u32[]{:S(2)}) collective-permute-start(f32[1,36,2,512]{3,2,1,0:T(2,128)S(1)} %get-tuple-element.18), channel_id=1, source_target_pairs={{0,32},{32,64},{64,96},{96,128},{128,160},{160,192},{192,224},{1,3... | collective-permute-start | bytes 442376 | tf_op jit(solution)/shard_map/ppermute | solution.py:231
  8.3 2.5 %copy-start.2 = (f32[1,36,32,512]{3,2,1,0:T(8,128)S(1)}, f32[1,36,32,512]{3,2,1,0:T(8,128)}, u32[]{:S(2)}) copy-start(f32[1,36,32,512]{3,2,1,0:T(8,128)} %param.8) | copy-start | bytes 7077892
  14.4 0.8 copy-start.5
  14.4 0.9 copy-start.6
  20.4 34.1 %all-to-all-start = ((f32[4,36,8,512]{3,2,1,0:T(8,128)}), f32[4,36,8,512]{3,2,1,0:T(8,128)S(1)}, u32[]{:S(2)}, u32[]{:S(2)}) async-start(f32[4,36,8,512]{3,2,1,0:T(8,128)} %copy_bitcast_fusion.1), calls=%async_computation | async-start | bytes 4718592 | tf_op jit(solution)/shard_map/all_to_all | solution.py:476
  54.4 1.4 copy-start
  90.1 2.0 %copy-start.1 = (f32[4,36,8,512]{3,2,1,0:T(8,128)S(1)}, f32[4,36,8,512]{3,2,1,0:T(8,128)}, u32[]{:S(2)}) copy-start(f32[4,36,8,512]{3,2,1,0:T(8,128)} %copy-done) | copy-start | bytes 7077892
  92.1 6.7 %copy-start.4 = (f32[2,36,8,512]{3,2,1,0:T(8,128)S(1)}, f32[2,36,8,512]{3,2,1,0:T(8,128)}, u32[]{:S(2)}) copy-start(f32[2,36,8,512]{3,2,1,0:T(8,128)} %get-tuple-element.8) | copy-start | bytes 3538948
  93.1 4.2 %collective-permute-start.2 = (f32[3,8,512]{2,1,0:T(8,128)S(1)}, f32[3,8,512]{2,1,0:T(8,128)S(1)}, u32[]{:S(2)}, u32[]{:S(2)}) collective-permute-start(f32[3,8,512]{2,1,0:T(8,128)S(1)} %pad_maximum_fusion.8), channel_id=1, source_target_pairs={{0,4},{4,0},{8,12},{12,8},{16,20},{20,16},{24,28},{28,24},{1,5},{5... | collective-permute-start | bytes 147464 | tf_op jit(solution)/shard_map/ppermute | solution.py:492
  97.2 5.1 %collective-permute-start.3 = (f32[3,8,512]{2,1,0:T(8,128)S(1)}, f32[3,8,512]{2,1,0:T(8,128)S(1)}, u32[]{:S(2)}, u32[]{:S(2)}) collective-permute-start(f32[3,8,512]{2,1,0:T(8,128)S(1)} %fusion.43), channel_id=1, source_target_pairs={{0,8},{4,12},{8,0},{12,4},{16,24},{20,28},{24,16},{28,20},{1,9},{5... | collective-permute-start | bytes 147464 | tf_op jit(solution)/shard_map/ppermute | solution.py:492
  99.4 5.6 %copy-start.3 = (f32[2,36,8,512]{3,2,1,0:T(8,128)S(1)}, f32[2,36,8,512]{3,2,1,0:T(8,128)}, u32[]{:S(2)}) copy-start(f32[2,36,8,512]{3,2,1,0:T(8,128)} %get-tuple-element.7) | copy-start | bytes 3538948
  102.3 8.1 %collective-permute-start.4 = (f32[3,8,512]{2,1,0:T(8,128)S(1)}, f32[3,8,512]{2,1,0:T(8,128)S(1)}, u32[]{:S(2)}, u32[]{:S(2)}) collective-permute-start(f32[3,8,512]{2,1,0:T(8,128)S(1)} %fusion.47), channel_id=1, source_target_pairs={{0,16},{4,20},{8,24},{12,28},{16,0},{20,4},{24,8},{28,12},{1,17},{... | collective-permute-start | bytes 147464 | tf_op jit(solution)/shard_map/ppermute | solution.py:492

commit v18 on v16

--- a/solution.py
+++ b/solution.py
@@ -469,24 +469,28 @@
     )
     padded = jnp.concatenate([density[:, -2:], density, density[:, :2]], axis=1)
     floored = jnp.maximum(advect(padded, turning, 1), 0.0)
+    own_scaled = floored * (band_spread * dtheta)[:, None, None, None]
+    tile_sums = jnp.stack(
+        [
+            jnp.sum(own_scaled, axis=(0, 1)),
+            jnp.sum(own_scaled / radian_freq[:, None, None, None], axis=(0, 1)),
+            jnp.sum(own_scaled / jnp.sqrt(wavenum)[:, None, None, None], axis=(0, 1)),
+        ]
+    )
+    for axis, size in (("z", z_count), ("y", lax.axis_size("y"))):
+        step = 1
+        while step < size:
+            tile_sums = tile_sums + lax.ppermute(
+                tile_sums, axis, [(i, i ^ step) for i in range(size)]
+            )
+            step *= 2
     point = lax.all_to_all(floored, "y", split_axis=2, concat_axis=0, tiled=True)
     group = point.shape[0]
     part_rows = point.shape[2]
     group_ids = (z_pos * group + jnp.arange(group)).astype(jnp.float32)
     radian_freq, wavenum, courant, turn_rate, band_spread = band_table(group_ids)
-    scaled = point * (band_spread * dtheta)[:, None, None, None]
-    sums = jnp.stack(
-        [
-            jnp.sum(scaled, axis=(0, 1)),
-            jnp.sum(scaled / radian_freq[:, None, None, None], axis=(0, 1)),
-            jnp.sum(scaled / jnp.sqrt(wavenum)[:, None, None, None], axis=(0, 1)),
-        ]
-    )
     lower, upper = z_halo(point, z_count)
-    step = 1
-    while step < z_count:
-        sums = sums + lax.ppermute(sums, "z", [(i, i ^ step) for i in range(z_count)])
-        step *= 2
+    sums = lax.dynamic_slice_in_dim(tile_sums, y_pos * part_rows, part_rows, axis=1)
     energy_sum, first_sum, root_sum = sums[0], sums[1], sums[2]
     energy = energy_sum + EPSILON
     ext = jnp.concatenate([lower, point, upper], axis=0)

time: 142 us -> 149 us (1.049)
  the two profiles are of different devices: /device:TPU:32 before, /device:TPU:2 now
where the time goes in v18:
time: 149 us; the launch traced here: 148 us
  blocking collectives  31.2 us (21%)
  Pallas kernels  30.6 us (21%)
  starting transfers between devices  27 us (18%)
  waiting for transfers between devices  26.2 us (18%)
  other arithmetic  21.6 us (14%)
  local copies, waits for them, and re-layouts  11.4 us (8%)
    all_to_all x1, blocking collectives, shards(): return lax.all_to_all(updated, 'y', split_axis=0, concat_axis=2, tiled=True)  31.2 us
    pallas_call x1, Pallas kernels, z_halo(): pl.pallas_call(functools.partial(_z_halo_kernel, z_count), out_shape=(hal...  30.6 us
    ppermute x5, waiting for transfers between devices, shards(): lax.ppermute(tile_sums, axis, [(i, i ^ step) for i in range(size)])  23.9 us
    ppermute x5, starting transfers between devices, shards(): lax.ppermute(tile_sums, axis, [(i, i ^ step) for i in range(size)])  17 us
    mul x3, other arithmetic, quick_flux(): return courant * face_value  8.41 us
    all_to_all x1, starting transfers between devices, shards(): lax.all_to_all(floored, 'y', split_axis=2, concat_axis=0, tiled=True)  4.46 us
    max x1, local copies, waits for them, and re-layouts, shards(): floored = jnp.maximum(advect(padded, turning, 1), 0.0)  3.84 us
    ppermute x1, starting transfers between devices, extended(): lax.ppermute(head, axis, [((i + 1) % count, i) for i in range(ends)])  3.64 us
  transfers between devices with their start and end apart: 8, of which 6 were waited for; matrix products, arithmetic and copies ran while one was open for 5% of the time, Pallas kernels for 0%

profile of v18, /device:TPU:2, one launch (start us, length us, event | category | flops | bytes accessed | tf_op | source)
XLA Modules:
  0.0 148.4 jit_solution(17064355745345559391)
XLA Ops:
  0.0 0.8 convert_element_type.78
  0.8 2.0 %broadcast_multiply_fusion = f32[1,36,32,512]{3,2,1,0:T(8,128)S(1)} fusion(f32[1,36,32,512]{3,2,1,0:T(8,128)} %param.8, f32[32,512]{1,0:T(8,128)S(1)} %convert_element_type.78), kind=kLoop, calls=%fused_computation.64 | loop fusion | flops 589824 | bytes 4784128 | tf_op jit(solution)/shard_map/mul | solution.py:455
  2.9 0.1 fusion.50
  3.0 1.9 %collective-permute-start = (f32[1,36,2,512]{3,2,1,0:T(2,128)S(1)}, f32[1,36,2,512]{3,2,1,0:T(2,128)S(1)}, u32[]{:S(2)}, u32[]{:S(2)}) collective-permute-start(f32[1,36,2,512]{3,2,1,0:T(2,128)S(1)} %get-tuple-element.17), channel_id=1, source_target_pairs={{0,32},{32,64},{64,96},{96,128},{128,160},{160,192},{192,224},{1,3... | collective-permute-start | bytes 442376 | tf_op jit(solution)/shard_map/ppermute | solution.py:231
  4.9 3.6 %collective-permute-start.1 = (f32[1,36,2,512]{3,2,1,0:T(2,128)S(1)}, f32[1,36,2,512]{3,2,1,0:T(2,128)S(1)}, u32[]{:S(2)}, u32[]{:S(2)}) collective-permute-start(f32[1,36,2,512]{3,2,1,0:T(2,128)S(1)} %get-tuple-element.18), channel_id=1, source_target_pairs={{32,0},{64,32},{96,64},{128,96},{160,128},{192,160},{224,192},{33,... | collective-permute-start | bytes 442376 | tf_op jit(solution)/shard_map/ppermute | solution.py:233
  9.0 0.5 collective-permute-done
  9.5 1.8 %collective-permute-done.1 = f32[1,36,2,512]{3,2,1,0:T(2,128)S(1)} collective-permute-done((f32[1,36,2,512]{3,2,1,0:T(2,128)S(1)}, f32[1,36,2,512]{3,2,1,0:T(2,128)S(1)}, u32[]{:S(2)}, u32[]{:S(2)}) %collective-permute-start.1) | collective-permute-done | bytes 147488 | tf_op jit(solution)/shard_map/ppermute | solution.py:233
  11.2 2.5 %fusion.12 = f32[1,36,33,512]{3,2,1,0:T(8,128)S(1)} fusion(f32[1,36,2,512]{3,2,1,0:T(2,128)S(1)} %collective-permute-done.1, f32[1,36,32,512]{3,2,1,0:T(8,128)S(1)} %broadcast_multiply_fusion, f32[1,36,2,512]{3,2,1,0:T(2,128)S(1)} %collective-permute-done, f32[36]{0:T(128)S(1)} %get-tuple-element.26, f32[36]{0:T(128)S(1)} %get-tuple-element.27, ...), kind=kLoop, calls=%fused_computation.25 | loop fusion | flops 10948608 | bytes 5087700 | tf_op jit(solution)/shard_map/mul | solution.py:263
  13.8 0.0 copy-done.3
  13.8 0.7 fusion.30
  14.5 2.8 %fusion.7 = f32[1,36,32,513]{3,2,1,0:T(8,128)S(1)} fusion(f32[1,36,32,512]{3,2,1,0:T(8,128)S(1)} %fusion.30, f32[36]{0:T(128)S(1)} %get-tuple-element.23, f32[36]{0:T(128)S(1)} %get-tuple-element.24, f32[36]{0:T(128)S(1)} %get-tuple-element.25, pred[36]{0:T(512)(128)(4,1)S(1)} %get-tuple-element.29), kind=kLoop, calls=%fused_computation.19 | loop fusion | flops 8273664 | bytes 4723668 | tf_op jit(solution)/shard_map/mul | solution.py:263
  17.3 0.0 copy-start.6
  17.3 0.0 copy-start.7
  17.3 0.7 fusion.28
  18.0 0.1 copy-done.6
  18.1 0.0 copy-done.7
  18.2 3.1 %fusion.19 = f32[1,37,32,512]{3,2,1,0:T(8,128)S(1)} fusion(f32[1,2,32,512]{3,2,1,0:T(8,128)S(1)} %get-tuple-element.16, f32[1,36,32,512]{3,2,1,0:T(8,128)S(1)} %fusion.28, f32[1,2,32,512]{3,2,1,0:T(8,128)S(1)} %get-tuple-element.15, f32[32,512]{1,0:T(8,128)S(1)} %copy-done.6, f32[37]{0:T(128)S(1)} %get-tuple-element.31, f32[32,512]{1,0:T(8,128)S(1)} %copy-done.7, ...), kind=kLoop, calls=%fused_computation.40 | loop fusion | flops 16973824 | bytes 5177644 | tf_op jit(solution)/shard_map/mul | solution.py:263
  21.3 0.7 multiply_reduce_fusion
  22.0 2.0 %collective-permute-start.2 = (f32[3,32,512]{2,1,0:T(8,128)S(1)}, f32[3,32,512]{2,1,0:T(8,128)S(1)}, u32[]{:S(2)}, u32[]{:S(2)}) collective-permute-start(f32[3,32,512]{2,1,0:T(8,128)S(1)} %pad_maximum_fusion.9), channel_id=1, source_target_pairs={{0,4},{4,0},{8,12},{12,8},{16,20},{20,16},{24,28},{28,24},{1,5},{5... | collective-permute-start | bytes 589832 | tf_op jit(solution)/shard_map/ppermute | solution.py:483
  24.0 3.8 %copy.17 = f32[1,36,32,512]{3,0,1,2:T(1,128)} copy(f32[1,36,32,512]{3,2,1,0:T(8,128)S(1)} %get-tuple-element.14) | data formatting | bytes 4718592 | tf_op jit(solution)/shard_map/max | solution.py:471
  27.8 4.5 %all-to-all-start = ((f32[1,36,32,512]{3,0,1,2:T(1,128)}), f32[1,36,32,512]{3,0,1,2:T(1,128)S(1)}, u32[]{:S(2)}, u32[]{:S(2)}) async-start(f32[1,36,32,512]{3,0,1,2:T(1,128)} %copy.17), calls=%async_computation | async-start | bytes 4718592 | tf_op jit(solution)/shard_map/all_to_all | solution.py:487
  32.3 0.0 collective-permute-done.2
  32.3 3.4 %collective-permute-start.3 = (f32[3,32,512]{2,1,0:T(8,128)S(1)}, f32[3,32,512]{2,1,0:T(8,128)S(1)}, u32[]{:S(2)}, u32[]{:S(2)}) collective-permute-start(f32[3,32,512]{2,1,0:T(8,128)S(1)} %fusion.46), channel_id=1, source_target_pairs={{0,8},{4,12},{8,0},{12,4},{16,24},{20,28},{24,16},{28,20},{1,9},{5... | collective-permute-start | bytes 589832 | tf_op jit(solution)/shard_map/ppermute | solution.py:483
  35.7 9.5 %collective-permute-done.3 = f32[3,32,512]{2,1,0:T(8,128)S(1)} collective-permute-done((f32[3,32,512]{2,1,0:T(8,128)S(1)}, f32[3,32,512]{2,1,0:T(8,128)S(1)}, u32[]{:S(2)}, u32[]{:S(2)}) %collective-permute-start.3) | collective-permute-done | bytes 196640 | tf_op jit(solution)/shard_map/ppermute | solution.py:483
  45.2 6.3 %collective-permute-start.4 = (f32[3,32,512]{2,1,0:T(8,128)S(1)}, f32[3,32,512]{2,1,0:T(8,128)S(1)}, u32[]{:S(2)}, u32[]{:S(2)}) collective-permute-start(f32[3,32,512]{2,1,0:T(8,128)S(1)} %fusion.51), channel_id=1, source_target_pairs={{0,16},{4,20},{8,24},{12,28},{16,0},{20,4},{24,8},{28,12},{1,17},{... | collective-permute-start | bytes 589832 | tf_op jit(solution)/shard_map/ppermute | solution.py:483
  51.5 0.7 dynamic-slice_multiply_fusion
  52.3 7.6 %collective-permute-done.4 = f32[3,32,512]{2,1,0:T(8,128)S(1)} collective-permute-done((f32[3,32,512]{2,1,0:T(8,128)S(1)}, f32[3,32,512]{2,1,0:T(8,128)S(1)}, u32[]{:S(2)}, u32[]{:S(2)}) %collective-permute-start.4) | collective-permute-done | bytes 196640 | tf_op jit(solution)/shard_map/ppermute | solution.py:483
  59.9 2.2 %collective-permute-start.5 = (f32[3,32,512]{2,1,0:T(8,128)S(1)}, f32[3,32,512]{2,1,0:T(8,128)S(1)}, u32[]{:S(2)}, u32[]{:S(2)}) collective-permute-start(f32[3,32,512]{2,1,0:T(8,128)S(1)} %add.193), channel_id=1, source_target_pairs={{0,1},{1,0},{2,3},{3,2},{4,5},{5,4},{6,7},{7,6},{8,9},{9,8},{10,11... | collective-permute-start | bytes 589832 | tf_op jit(solution)/shard_map/ppermute | solution.py:483
  62.1 1.9 %subtract_cosine_fusion = f32[36,8,512]{2,1,0:T(8,128)S(1)} fusion(f32[8,512]{1,0:T(8,128)S(1)} %get-tuple-element.34, f32[36]{0:T(128)S(1)} %add_multiply_fusion), kind=kLoop, calls=%fused_computation.65 | loop fusion | flops 147456 | bytes 606352 | tf_op jit(solution)/shard_map/cos | solution.py:506
  64.1 2.8 %collective-permute-done.5 = f32[3,32,512]{2,1,0:T(8,128)S(1)} collective-permute-done((f32[3,32,512]{2,1,0:T(8,128)S(1)}, f32[3,32,512]{2,1,0:T(8,128)S(1)}, u32[]{:S(2)}, u32[]{:S(2)}) %collective-permute-start.5) | collective-permute-done | bytes 196640 | tf_op jit(solution)/shard_map/ppermute | solution.py:483
  66.8 3.2 %collective-permute-start.6 = (f32[3,32,512]{2,1,0:T(8,128)S(1)}, f32[3,32,512]{2,1,0:T(8,128)S(1)}, u32[]{:S(2)}, u32[]{:S(2)}) collective-permute-start(f32[3,32,512]{2,1,0:T(8,128)S(1)} %add.194), channel_id=1, source_target_pairs={{0,2},{1,3},{2,0},{3,1},{4,6},{5,7},{6,4},{7,5},{8,10},{9,11},{10,... | collective-permute-start | bytes 589832 | tf_op jit(solution)/shard_map/ppermute | solution.py:483
  70.0 0.1 multiply_multiply_fusion
  70.1 4.1 %collective-permute-done.6 = f32[3,32,512]{2,1,0:T(8,128)S(1)} collective-permute-done((f32[3,32,512]{2,1,0:T(8,128)S(1)}, f32[3,32,512]{2,1,0:T(8,128)S(1)}, u32[]{:S(2)}, u32[]{:S(2)}) %collective-permute-start.6) | collective-permute-done | bytes 196640 | tf_op jit(solution)/shard_map/ppermute | solution.py:483
  74.2 0.1 fusion.33
  74.3 0.0 all-to-all-done
  74.3 1.4 copy-done.1
  75.7 2.1 %copy_bitcast_fusion.1.point_ref = f32[4,36,8,512]{3,2,1,0:T(8,128)} fusion(f32[1,36,32,512]{3,0,1,2:T(1,128)S(1)} %all-to-all-done), kind=kLoop, calls=%fused_computation.59 | loop fusion | bytes 4718592 | tf_op jit(solution)/shard_map/all_to_all | solution.py:487
  77.9 30.6 %shard_map.64 = (f32[2,36,8,512]{3,2,1,0:T(8,128)}, f32[2,36,8,512]{3,2,1,0:T(8,128)}) custom-call(f32[4,36,8,512]{3,2,1,0:T(8,128)} %copy_bitcast_fusion.1.point_ref), custom_call_target="tpu_custom_call" | custom-call | tf_op jit(solution)/shard_map/pallas_call | solution.py:210
  108.5 1.8 %fusion.2 = f32[6,35,8,512]{3,2,1,0:T(8,128)S(1)} fusion(f32[4,36,8,512]{3,2,1,0:T(8,128)S(1)} %copy-done, f32[2,36,8,512]{3,2,1,0:T(8,128)} %get-tuple-element.8), kind=kLoop, calls=%fused_computation.10 | loop fusion | flops 860160 | bytes 6979584 | tf_op jit(solution)/shard_map/concatenate | solution.py:496
  110.2 0.2 copy-done.5
  110.4 1.4 multiply_subtract_fusion
  111.8 0.2 slice.194
  112.0 0.0 copy-start.2
  112.1 0.2 slice.195
  112.3 1.4 copy-done.2
  113.7 1.8 %fusion.24 = f32[4,36,8,512]{3,2,1,0:T(8,128)S(1)} fusion(f32[6,36,8,512]{3,2,1,0:T(8,128)S(1)} %multiply_subtract_fusion, f32[4,35,8,512]{3,2,1,0:T(8,128)S(1)} %slice.194, f32[4,1,8,512]{3,2,1,0:T(8,128)S(1)} %slice.193, f32[4,3,8,512]{3,2,1,0:T(8,128)S(1)} %slice.196, f32[4,33,8,512]{3,2,1,0:T(8,128)S(1)} %slice.195, ...), kind=kLoop, calls=%fused_computation.48 | loop fusion | flops 8847360 | bytes 12550160 | tf_op jit(solution)/shard_map/mul | solution.py:507
  115.6 31.2 %all_to_all.36 = f32[4,36,8,512]{3,2,1,0:T(8,128)S(1)} all-to-all(f32[4,36,8,512]{3,2,1,0:T(8,128)S(1)} %fusion.24), channel_id=1, replica_groups=mesh['geo'=8,'z'=8,'y'=4] {'y'}, dimensions={0} | all-to-all | bytes 4718592 | tf_op jit(solution)/shard_map/all_to_all | solution.py:520
  146.7 1.7 %copy_bitcast_fusion = f32[1,36,32,512]{3,2,1,0:T(8,128)} fusion(f32[4,36,8,512]{3,2,1,0:T(8,128)S(1)} %all_to_all.36), kind=kLoop, calls=%fused_computation.58 | loop fusion | bytes 4718592 | tf_op jit(solution)/shard_map/all_to_all | solution.py:520
  (26 shorter events, 0.5 us)
Async XLA Ops:
  3.0 6.5 %collective-permute-start = (f32[1,36,2,512]{3,2,1,0:T(2,128)S(1)}, f32[1,36,2,512]{3,2,1,0:T(2,128)S(1)}, u32[]{:S(2)}, u32[]{:S(2)}) collective-permute-start(f32[1,36,2,512]{3,2,1,0:T(2,128)S(1)} %get-tuple-element.17), channel_id=1, source_target_pairs={{0,32},{32,64},{64,96},{96,128},{128,160},{160,192},{192,224},{1,3... | collective-permute-start | bytes 442376 | tf_op jit(solution)/shard_map/ppermute | solution.py:231
  4.9 6.3 %collective-permute-start.1 = (f32[1,36,2,512]{3,2,1,0:T(2,128)S(1)}, f32[1,36,2,512]{3,2,1,0:T(2,128)S(1)}, u32[]{:S(2)}, u32[]{:S(2)}) collective-permute-start(f32[1,36,2,512]{3,2,1,0:T(2,128)S(1)} %get-tuple-element.18), channel_id=1, source_target_pairs={{32,0},{64,32},{96,64},{128,96},{160,128},{192,160},{224,192},{33,... | collective-permute-start | bytes 442376 | tf_op jit(solution)/shard_map/ppermute | solution.py:233
  11.2 2.5 %copy-start.3 = (f32[1,36,32,512]{3,2,1,0:T(8,128)S(1)}, f32[1,36,32,512]{3,2,1,0:T(8,128)}, u32[]{:S(2)}) copy-start(f32[1,36,32,512]{3,2,1,0:T(8,128)} %param.8) | copy-start | bytes 7077892
  17.3 0.8 copy-start.6
  17.3 0.9 copy-start.7
  22.0 10.3 %collective-permute-start.2 = (f32[3,32,512]{2,1,0:T(8,128)S(1)}, f32[3,32,512]{2,1,0:T(8,128)S(1)}, u32[]{:S(2)}, u32[]{:S(2)}) collective-permute-start(f32[3,32,512]{2,1,0:T(8,128)S(1)} %pad_maximum_fusion.9), channel_id=1, source_target_pairs={{0,4},{4,0},{8,12},{12,8},{16,20},{20,16},{24,28},{28,24},{1,5},{5... | collective-permute-start | bytes 589832 | tf_op jit(solution)/shard_map/ppermute | solution.py:483
  27.8 46.5 %all-to-all-start = ((f32[1,36,32,512]{3,0,1,2:T(1,128)}), f32[1,36,32,512]{3,0,1,2:T(1,128)S(1)}, u32[]{:S(2)}, u32[]{:S(2)}) async-start(f32[1,36,32,512]{3,0,1,2:T(1,128)} %copy.17), calls=%async_computation | async-start | bytes 4718592 | tf_op jit(solution)/shard_map/all_to_all | solution.py:487
  32.3 12.8 %collective-permute-start.3 = (f32[3,32,512]{2,1,0:T(8,128)S(1)}, f32[3,32,512]{2,1,0:T(8,128)S(1)}, u32[]{:S(2)}, u32[]{:S(2)}) collective-permute-start(f32[3,32,512]{2,1,0:T(8,128)S(1)} %fusion.46), channel_id=1, source_target_pairs={{0,8},{4,12},{8,0},{12,4},{16,24},{20,28},{24,16},{28,20},{1,9},{5... | collective-permute-start | bytes 589832 | tf_op jit(solution)/shard_map/ppermute | solution.py:483
  45.2 14.7 %collective-permute-start.4 = (f32[3,32,512]{2,1,0:T(8,128)S(1)}, f32[3,32,512]{2,1,0:T(8,128)S(1)}, u32[]{:S(2)}, u32[]{:S(2)}) collective-permute-start(f32[3,32,512]{2,1,0:T(8,128)S(1)} %fusion.51), channel_id=1, source_target_pairs={{0,16},{4,20},{8,24},{12,28},{16,0},{20,4},{24,8},{28,12},{1,17},{... | collective-permute-start | bytes 589832 | tf_op jit(solution)/shard_map/ppermute | solution.py:483
  59.9 6.9 %collective-permute-start.5 = (f32[3,32,512]{2,1,0:T(8,128)S(1)}, f32[3,32,512]{2,1,0:T(8,128)S(1)}, u32[]{:S(2)}, u32[]{:S(2)}) collective-permute-start(f32[3,32,512]{2,1,0:T(8,128)S(1)} %add.193), channel_id=1, source_target_pairs={{0,1},{1,0},{2,3},{3,2},{4,5},{5,4},{6,7},{7,6},{8,9},{9,8},{10,11... | collective-permute-start | bytes 589832 | tf_op jit(solution)/shard_map/ppermute | solution.py:483
  66.8 7.3 %collective-permute-start.6 = (f32[3,32,512]{2,1,0:T(8,128)S(1)}, f32[3,32,512]{2,1,0:T(8,128)S(1)}, u32[]{:S(2)}, u32[]{:S(2)}) collective-permute-start(f32[3,32,512]{2,1,0:T(8,128)S(1)} %add.194), channel_id=1, source_target_pairs={{0,2},{1,3},{2,0},{3,1},{4,6},{5,7},{6,4},{7,5},{8,10},{9,11},{10,... | collective-permute-start | bytes 589832 | tf_op jit(solution)/shard_map/ppermute | solution.py:483
  74.3 1.4 copy-start.1
  77.9 30.6 %copy-start = (f32[4,36,8,512]{3,2,1,0:T(8,128)S(1)}, f32[4,36,8,512]{3,2,1,0:T(8,128)}, u32[]{:S(2)}) copy-start(f32[4,36,8,512]{3,2,1,0:T(8,128)} %copy_bitcast_fusion.1.point_ref) | copy-start | bytes 7077892
  108.4 1.8 %copy-start.4 = (f32[2,36,8,512]{3,2,1,0:T(8,128)S(1)}, f32[2,36,8,512]{3,2,1,0:T(8,128)}, u32[]{:S(2)}) copy-start(f32[2,36,8,512]{3,2,1,0:T(8,128)} %get-tuple-element.8) | copy-start | bytes 3538948
  108.5 2.0 %copy-start.5 = (f32[2,36,8,512]{3,2,1,0:T(8,128)S(1)}, f32[2,36,8,512]{3,2,1,0:T(8,128)}, u32[]{:S(2)}) copy-start(f32[2,36,8,512]{3,2,1,0:T(8,128)} %get-tuple-element.7) | copy-start | bytes 3538948
  112.0 1.7 %copy-start.2 = (f32[1,36,32,512]{3,0,1,2:T(1,128)S(1)}, f32[1,36,32,512]{3,0,1,2:T(1,128)}, u32[]{:S(2)}) copy-start(f32[1,36,32,512]{3,0,1,2:T(1,128)} %copy-done.1) | copy-start | bytes 7077892

commit v19 on v17

--- a/solution.py
+++ b/solution.py
@@ -151,7 +151,8 @@
 HALO = 2
 
 
-def _z_halo_kernel(z_count, point_ref, lower_ref, upper_ref, halo_send, halo_recv):
+def _z_halo_kernel(z_count, point_ref, sums_ref, lower_ref, upper_ref, pair_ref, halo_send, halo_recv,
+                   pair_send, pair_recv):
     geo = lax.axis_index("geo")
     z_pos = lax.axis_index("z")
     y_pos = lax.axis_index("y")
@@ -176,6 +177,16 @@
     up = halo_copy(group - HALO, lower_ref, 0, lax.rem(z_pos + 1, z_count))
     down = halo_copy(0, upper_ref, 1, lax.rem(z_pos + z_count - 1, z_count))
 
+    pair = pltpu.make_async_remote_copy(
+        src_ref=sums_ref,
+        dst_ref=pair_ref,
+        send_sem=pair_send.at[0],
+        recv_sem=pair_recv.at[0],
+        device_id=(geo, z_pos + 1 - 2 * lax.rem(z_pos, 2), y_pos),
+        device_id_type=mesh_id,
+    )
+    pair.start()
+
     @pl.when(z_pos < z_count - 1)
     def _():
         up.start()
@@ -191,6 +202,9 @@
     @pl.when(z_pos == z_count - 1)
     def _():
         upper_ref[...] = jnp.zeros(upper_ref.shape, upper_ref.dtype)
+
+    pair.wait_send()
+    pair.wait_recv()
 
     @pl.when(z_pos < z_count - 1)
     def _():
@@ -203,21 +217,24 @@
         up.wait_recv()
 
 
-def z_halo(point, z_count):
+def z_halo(point, sums, z_count):
     group, dirs, rows, cols = point.shape
     halo = jax.ShapeDtypeStruct((HALO, dirs, rows, cols), point.dtype)
     vmem = pl.BlockSpec(memory_space=pltpu.VMEM)
+    hbm = pl.BlockSpec(memory_space=pl.ANY)
     return pl.pallas_call(
         functools.partial(_z_halo_kernel, z_count),
-        out_shape=(halo, halo),
-        in_specs=[pl.BlockSpec(memory_space=pl.ANY)],
-        out_specs=(vmem, vmem),
+        out_shape=(halo, halo, jax.ShapeDtypeStruct(sums.shape, sums.dtype)),
+        in_specs=[hbm, hbm],
+        out_specs=(vmem, vmem, vmem),
         scratch_shapes=[
             pltpu.SemaphoreType.DMA((2,)),
             pltpu.SemaphoreType.DMA((2,)),
+            pltpu.SemaphoreType.DMA((1,)),
+            pltpu.SemaphoreType.DMA((1,)),
         ],
         compiler_params=pltpu.CompilerParams(collective_id=0, has_side_effects=True),
-    )(point)
+    )(point, sums)
 
 
 def extended(cells, sides, width):
@@ -486,8 +503,9 @@
             jnp.sum(scaled / jnp.sqrt(wavenum)[:, None, None, None], axis=(0, 1)),
         ]
     )
-    lower, upper = z_halo(point, z_count)
-    step = 1
+    lower, upper, paired = z_halo(point, sums, z_count)
+    sums = sums + paired
+    step = 2
     while step < z_count:
         sums = sums + lax.ppermute(sums, "z", [(i, i ^ step) for i in range(z_count)])
         step *= 2

time: 143 us -> 143 us (level)
  the two profiles are of different devices: /device:TPU:32 before, /device:TPU:2 now
where the time goes in v19:
time: 143 us
  Pallas kernels  34.4 us (24%)
  waiting for transfers between devices  33.1 us (23%)
  blocking collectives  30.1 us (21%)
  other arithmetic  23 us (16%)
  starting transfers between devices  15.4 us (11%)
  local copies, waits for them, and re-layouts  6.51 us (5%)
    pallas_call x1, Pallas kernels, z_halo(): pl.pallas_call(functools.partial(_z_halo_kernel, z_count), out_shape=(hal...  34.4 us
    all_to_all x1, blocking collectives, shards(): return lax.all_to_all(updated, 'y', split_axis=0, concat_axis=2, tiled=True)  30.1 us
    all_to_all x1, waiting for transfers between devices, shards(): lax.all_to_all(quarters, 'y', split_axis=0, concat_axis=0, tiled=True)  27.3 us
    mul x3, other arithmetic, quick_flux(): return courant * face_value  8.41 us
    ppermute x2, starting transfers between devices, shards(): lax.ppermute(sums, 'z', [(i, i ^ step) for i in range(z_count)])  5.4 us
    all_to_all x1, starting transfers between devices, shards(): lax.all_to_all(quarters, 'y', split_axis=0, concat_axis=0, tiled=True)  4.46 us
    ppermute x1, starting transfers between devices, extended(): lax.ppermute(head, axis, [((i + 1) % count, i) for i in range(ends)])  3.64 us
    ppermute x2, waiting for transfers between devices, shards(): lax.ppermute(sums, 'z', [(i, i ^ step) for i in range(z_count)])  3.51 us
  transfers between devices with their start and end apart: 5, of which 4 were waited for; matrix products, arithmetic and copies ran while one was open for 5% of the time, Pallas kernels for 0%

profile of v19, /device:TPU:2, one launch (start us, length us, event | category | flops | bytes accessed | tf_op | source)
XLA Modules:
  0.0 142.9 jit_solution(14917581639682532203)
XLA Ops:
  0.0 0.8 convert_element_type.84
  0.8 2.0 %broadcast_multiply_fusion = f32[1,36,32,512]{3,2,1,0:T(8,128)S(1)} fusion(f32[1,36,32,512]{3,2,1,0:T(8,128)} %param.8, f32[32,512]{1,0:T(8,128)S(1)} %convert_element_type.84), kind=kLoop, calls=%fused_computation.58 | loop fusion | flops 589824 | bytes 4784128 | tf_op jit(solution)/shard_map/mul | solution.py:472
  2.9 0.1 fusion.46
  3.0 1.9 %collective-permute-start = (f32[1,36,2,512]{3,2,1,0:T(2,128)S(1)}, f32[1,36,2,512]{3,2,1,0:T(2,128)S(1)}, u32[]{:S(2)}, u32[]{:S(2)}) collective-permute-start(f32[1,36,2,512]{3,2,1,0:T(2,128)S(1)} %get-tuple-element.20), channel_id=1, source_target_pairs={{0,32},{32,64},{64,96},{96,128},{128,160},{160,192},{192,224},{1,3... | collective-permute-start | bytes 442376 | tf_op jit(solution)/shard_map/ppermute | solution.py:248
  4.9 3.6 %collective-permute-start.1 = (f32[1,36,2,512]{3,2,1,0:T(2,128)S(1)}, f32[1,36,2,512]{3,2,1,0:T(2,128)S(1)}, u32[]{:S(2)}, u32[]{:S(2)}) collective-permute-start(f32[1,36,2,512]{3,2,1,0:T(2,128)S(1)} %get-tuple-element.21), channel_id=1, source_target_pairs={{32,0},{64,32},{96,64},{128,96},{160,128},{192,160},{224,192},{33,... | collective-permute-start | bytes 442376 | tf_op jit(solution)/shard_map/ppermute | solution.py:250
  8.9 0.6 collective-permute-done
  9.5 1.8 %collective-permute-done.1 = f32[1,36,2,512]{3,2,1,0:T(2,128)S(1)} collective-permute-done((f32[1,36,2,512]{3,2,1,0:T(2,128)S(1)}, f32[1,36,2,512]{3,2,1,0:T(2,128)S(1)}, u32[]{:S(2)}, u32[]{:S(2)}) %collective-permute-start.1) | collective-permute-done | bytes 147488 | tf_op jit(solution)/shard_map/ppermute | solution.py:250
  11.2 2.5 %fusion.9 = f32[1,36,33,512]{3,2,1,0:T(8,128)S(1)} fusion(f32[1,36,2,512]{3,2,1,0:T(2,128)S(1)} %collective-permute-done.1, f32[1,36,32,512]{3,2,1,0:T(8,128)S(1)} %broadcast_multiply_fusion, f32[1,36,2,512]{3,2,1,0:T(2,128)S(1)} %collective-permute-done, f32[36]{0:T(128)S(1)} %get-tuple-element.33, f32[36]{0:T(128)S(1)} %get-tuple-element.34, ...), kind=kLoop, calls=%fused_computation.19 | loop fusion | flops 10948608 | bytes 5087700 | tf_op jit(solution)/shard_map/mul | solution.py:280
  13.8 0.0 copy-done.2
  13.8 0.7 fusion.28
  14.5 2.8 %fusion.4 = f32[1,36,32,513]{3,2,1,0:T(8,128)S(1)} fusion(f32[1,36,32,512]{3,2,1,0:T(8,128)S(1)} %fusion.28, f32[36]{0:T(128)S(1)} %get-tuple-element.30, f32[36]{0:T(128)S(1)} %get-tuple-element.31, f32[36]{0:T(128)S(1)} %get-tuple-element.32, pred[36]{0:T(512)(128)(4,1)S(1)} %get-tuple-element.36), kind=kLoop, calls=%fused_computation.13 | loop fusion | flops 8273664 | bytes 4723668 | tf_op jit(solution)/shard_map/mul | solution.py:280
  17.3 0.0 copy-start.6
  17.3 0.0 copy-start.7
  17.3 0.7 fusion.26
  18.0 0.1 copy-done.6
  18.1 0.0 copy-done.7
  18.2 3.1 %fusion.16 = f32[1,37,32,512]{3,2,1,0:T(8,128)S(1)} fusion(f32[1,2,32,512]{3,2,1,0:T(8,128)S(1)} %get-tuple-element.19, f32[1,36,32,512]{3,2,1,0:T(8,128)S(1)} %fusion.26, f32[1,2,32,512]{3,2,1,0:T(8,128)S(1)} %get-tuple-element.18, f32[32,512]{1,0:T(8,128)S(1)} %copy-done.6, f32[37]{0:T(128)S(1)} %get-tuple-element.38, f32[32,512]{1,0:T(8,128)S(1)} %copy-done.7, ...), kind=kLoop, calls=%fused_computation.34 | loop fusion | flops 16973824 | bytes 5177644 | tf_op jit(solution)/shard_map/mul | solution.py:280
  21.3 2.0 %copy_bitcast_fusion.1 = f32[4,36,8,512]{3,2,1,0:T(8,128)} fusion(f32[1,36,32,512]{3,2,1,0:T(8,128)S(1)} %fusion.26, f32[1,37,32,512]{3,2,1,0:T(8,128)S(1)} %fusion.16), kind=kLoop, calls=%fused_computation.54 | loop fusion | flops 1769472 | bytes 9437184 | tf_op jit(solution)/shard_map/transpose | solution.py:490
  23.3 4.5 %all-to-all-start = ((f32[4,36,8,512]{3,2,1,0:T(8,128)}), f32[4,36,8,512]{3,2,1,0:T(8,128)S(1)}, u32[]{:S(2)}, u32[]{:S(2)}) async-start(f32[4,36,8,512]{3,2,1,0:T(8,128)} %copy_bitcast_fusion.1), calls=%async_computation | async-start | bytes 4718592 | tf_op jit(solution)/shard_map/all_to_all | solution.py:493
  27.8 0.7 dynamic-slice_multiply_fusion
  28.5 0.1 multiply_multiply_fusion
  28.6 1.9 %subtract_cosine_fusion = f32[36,8,512]{2,1,0:T(8,128)S(1)} fusion(f32[8,512]{1,0:T(8,128)S(1)} %get-tuple-element.41, f32[36]{0:T(128)S(1)} %add_multiply_fusion), kind=kLoop, calls=%fused_computation.59 | loop fusion | flops 147456 | bytes 606352 | tf_op jit(solution)/shard_map/cos | solution.py:524
  30.6 27.3 %all-to-all-done.point_ref = f32[4,36,8,512]{3,2,1,0:T(8,128)S(1)} async-done(((f32[4,36,8,512]{3,2,1,0:T(8,128)}), f32[4,36,8,512]{3,2,1,0:T(8,128)S(1)}, u32[]{:S(2)}, u32[]{:S(2)}) %all-to-all-start) | async-done | bytes 2359328 | tf_op jit(solution)/shard_map/all_to_all | solution.py:493
  57.8 0.7 multiply_reduce_fusion
  58.5 0.7 pad_maximum_fusion.8.sums_ref
  59.2 0.0 copy-done
  59.2 34.4 %shard_map.64 = (f32[2,36,8,512]{3,2,1,0:T(8,128)}, f32[2,36,8,512]{3,2,1,0:T(8,128)}, f32[3,8,512]{2,1,0:T(8,128)}) custom-call(f32[4,36,8,512]{3,2,1,0:T(8,128)} %copy-done, f32[3,8,512]{2,1,0:T(8,128)} %pad_maximum_fusion.8.sums_ref), custom_call_target="tpu_custom_call" | custom-call | tf_op jit(solution)/shard_map/pallas_call | solution.py:225
  93.6 0.0 copy-start.1
  93.6 1.0 fusion.43
  94.6 2.8 %collective-permute-start.2 = (f32[3,8,512]{2,1,0:T(8,128)S(1)}, f32[3,8,512]{2,1,0:T(8,128)S(1)}, u32[]{:S(2)}, u32[]{:S(2)}) collective-permute-start(f32[3,8,512]{2,1,0:T(8,128)S(1)} %fusion.43), channel_id=1, source_target_pairs={{0,8},{4,12},{8,0},{12,4},{16,24},{20,28},{24,16},{28,20},{1,9},{5... | collective-permute-start | bytes 147464 | tf_op jit(solution)/shard_map/ppermute | solution.py:510
  97.4 1.4 constant_dynamic-update-slice_fusion.3
  98.8 0.0 copy-done.1
  98.8 0.4 constant_dynamic-update-slice_fusion.1
  99.2 0.8 copy-done.4
  100.0 0.1 constant_dynamic-update-slice_fusion
  100.1 0.5 slice.190
  100.7 0.3 slice.193
  101.1 0.0 collective-permute-done.2
  101.1 0.4 copy-done.5
  101.5 2.6 %collective-permute-start.3 = (f32[3,8,512]{2,1,0:T(8,128)S(1)}, f32[3,8,512]{2,1,0:T(8,128)S(1)}, u32[]{:S(2)}, u32[]{:S(2)}) collective-permute-start(f32[3,8,512]{2,1,0:T(8,128)S(1)} %fusion.47), channel_id=1, source_target_pairs={{0,16},{4,20},{8,24},{12,28},{16,0},{20,4},{24,8},{28,12},{1,17},{... | collective-permute-start | bytes 147464 | tf_op jit(solution)/shard_map/ppermute | solution.py:510
  104.1 1.4 multiply_subtract_fusion
  105.5 0.3 slice.196
  105.8 0.3 slice.197
  106.1 3.5 %collective-permute-done.3 = f32[3,8,512]{2,1,0:T(8,128)S(1)} collective-permute-done((f32[3,8,512]{2,1,0:T(8,128)S(1)}, f32[3,8,512]{2,1,0:T(8,128)S(1)}, u32[]{:S(2)}, u32[]{:S(2)}) %collective-permute-start.3) | collective-permute-done | bytes 49184 | tf_op jit(solution)/shard_map/ppermute | solution.py:510
  109.6 0.1 fusion.31
  109.7 1.4 %fusion.21 = f32[4,36,8,512]{3,2,1,0:T(8,128)S(1)} fusion(f32[6,36,8,512]{3,2,1,0:T(8,128)S(1)} %multiply_subtract_fusion, f32[4,35,8,512]{3,2,1,0:T(8,128)S(1)} %slice.196, f32[4,1,8,512]{3,2,1,0:T(8,128)S(1)} %slice.195, f32[4,3,8,512]{3,2,1,0:T(8,128)S(1)} %slice.198, f32[4,33,8,512]{3,2,1,0:T(8,128)S(1)} %slice.197, f32[4,36,8,512]{3,2,1,0:T(8,128)S(1)} %copy-done.1, ...), kind=kLoop, calls=%fused_computation.42 | loop fusion | flops 8847360 | bytes 12550160 | tf_op jit(solution)/shard_map/mul | solution.py:525
  111.1 30.1 %all_to_all.23 = f32[4,36,8,512]{3,2,1,0:T(8,128)S(1)} all-to-all(f32[4,36,8,512]{3,2,1,0:T(8,128)S(1)} %fusion.21), channel_id=1, replica_groups=mesh['geo'=8,'z'=8,'y'=4] {'y'}, dimensions={0} | all-to-all | bytes 4718592 | tf_op jit(solution)/shard_map/all_to_all | solution.py:538
  141.2 1.7 %copy_bitcast_fusion = f32[1,36,32,512]{3,2,1,0:T(8,128)} fusion(f32[4,36,8,512]{3,2,1,0:T(8,128)S(1)} %all_to_all.23), kind=kLoop, calls=%fused_computation.53 | loop fusion | bytes 4718592 | tf_op jit(solution)/shard_map/all_to_all | solution.py:538
  (24 shorter events, 0.4 us)
Async XLA Ops:
  3.0 6.5 %collective-permute-start = (f32[1,36,2,512]{3,2,1,0:T(2,128)S(1)}, f32[1,36,2,512]{3,2,1,0:T(2,128)S(1)}, u32[]{:S(2)}, u32[]{:S(2)}) collective-permute-start(f32[1,36,2,512]{3,2,1,0:T(2,128)S(1)} %get-tuple-element.20), channel_id=1, source_target_pairs={{0,32},{32,64},{64,96},{96,128},{128,160},{160,192},{192,224},{1,3... | collective-permute-start | bytes 442376 | tf_op jit(solution)/shard_map/ppermute | solution.py:248
  4.9 6.3 %collective-permute-start.1 = (f32[1,36,2,512]{3,2,1,0:T(2,128)S(1)}, f32[1,36,2,512]{3,2,1,0:T(2,128)S(1)}, u32[]{:S(2)}, u32[]{:S(2)}) collective-permute-start(f32[1,36,2,512]{3,2,1,0:T(2,128)S(1)} %get-tuple-element.21), channel_id=1, source_target_pairs={{32,0},{64,32},{96,64},{128,96},{160,128},{192,160},{224,192},{33,... | collective-permute-start | bytes 442376 | tf_op jit(solution)/shard_map/ppermute | solution.py:250
  11.2 2.5 %copy-start.2 = (f32[1,36,32,512]{3,2,1,0:T(8,128)S(1)}, f32[1,36,32,512]{3,2,1,0:T(8,128)}, u32[]{:S(2)}) copy-start(f32[1,36,32,512]{3,2,1,0:T(8,128)} %param.8) | copy-start | bytes 7077892
  17.3 0.8 copy-start.6
  17.3 0.9 copy-start.7
  23.3 34.6 %all-to-all-start = ((f32[4,36,8,512]{3,2,1,0:T(8,128)}), f32[4,36,8,512]{3,2,1,0:T(8,128)S(1)}, u32[]{:S(2)}, u32[]{:S(2)}) async-start(f32[4,36,8,512]{3,2,1,0:T(8,128)} %copy_bitcast_fusion.1), calls=%async_computation | async-start | bytes 4718592 | tf_op jit(solution)/shard_map/all_to_all | solution.py:493
  57.8 1.4 copy-start
  93.6 5.1 %copy-start.1 = (f32[4,36,8,512]{3,2,1,0:T(8,128)S(1)}, f32[4,36,8,512]{3,2,1,0:T(8,128)}, u32[]{:S(2)}) copy-start(f32[4,36,8,512]{3,2,1,0:T(8,128)} %copy-done) | copy-start | bytes 7077892
  94.6 6.5 %collective-permute-start.2 = (f32[3,8,512]{2,1,0:T(8,128)S(1)}, f32[3,8,512]{2,1,0:T(8,128)S(1)}, u32[]{:S(2)}, u32[]{:S(2)}) collective-permute-start(f32[3,8,512]{2,1,0:T(8,128)S(1)} %fusion.43), channel_id=1, source_target_pairs={{0,8},{4,12},{8,0},{12,4},{16,24},{20,28},{24,16},{28,20},{1,9},{5... | collective-permute-start | bytes 147464 | tf_op jit(solution)/shard_map/ppermute | solution.py:510
  98.8 1.3 copy-start.4
  100.7 0.8 copy-start.5
  100.7 3.4 %copy-start.3 = (f32[2,36,8,512]{3,2,1,0:T(8,128)S(1)}, f32[2,36,8,512]{3,2,1,0:T(8,128)}, u32[]{:S(2)}) copy-start(f32[2,36,8,512]{3,2,1,0:T(8,128)} %get-tuple-element.9) | copy-start | bytes 3538948
  101.5 8.1 %collective-permute-start.3 = (f32[3,8,512]{2,1,0:T(8,128)S(1)}, f32[3,8,512]{2,1,0:T(8,128)S(1)}, u32[]{:S(2)}, u32[]{:S(2)}) collective-permute-start(f32[3,8,512]{2,1,0:T(8,128)S(1)} %fusion.47), channel_id=1, source_target_pairs={{0,16},{4,20},{8,24},{12,28},{16,0},{20,4},{24,8},{28,12},{1,17},{... | collective-permute-start | bytes 147464 | tf_op jit(solution)/shard_map/ppermute | solution.py:510

commit v20 on v19

--- a/solution.py
+++ b/solution.py
@@ -159,10 +159,16 @@
     group = point_ref.shape[0]
     mesh_id = pl.DeviceIdType.MESH
     barrier = pltpu.get_barrier_semaphore()
-    for step in (1, z_count - 1):
-        pl.semaphore_signal(barrier, inc=1, device_id=(geo, lax.rem(z_pos + step, z_count), y_pos),
-                            device_id_type=mesh_id)
-    pl.semaphore_wait(barrier, 2)
+    pair_bit = lax.rem(z_pos, 2)
+    quad_bit = lax.rem(z_pos // 2, 2)
+    partners = [
+        z_pos + 1 - 2 * pair_bit,
+        z_pos + 2 - 4 * quad_bit,
+        z_pos + 1 - 2 * pair_bit + 2 - 4 * quad_bit,
+    ]
+    for target in [lax.rem(z_pos + 1, z_count), lax.rem(z_pos + z_count - 1, z_count)] + partners[1:]:
+        pl.semaphore_signal(barrier, inc=1, device_id=(geo, target, y_pos), device_id_type=mesh_id)
+    pl.semaphore_wait(barrier, 4)
 
     def halo_copy(src_lo, dst_ref, slot, target):
         return pltpu.make_async_remote_copy(
@@ -177,15 +183,18 @@
     up = halo_copy(group - HALO, lower_ref, 0, lax.rem(z_pos + 1, z_count))
     down = halo_copy(0, upper_ref, 1, lax.rem(z_pos + z_count - 1, z_count))
 
-    pair = pltpu.make_async_remote_copy(
-        src_ref=sums_ref,
-        dst_ref=pair_ref,
-        send_sem=pair_send.at[0],
-        recv_sem=pair_recv.at[0],
-        device_id=(geo, z_pos + 1 - 2 * lax.rem(z_pos, 2), y_pos),
-        device_id_type=mesh_id,
-    )
-    pair.start()
+    pairs = []
+    for index, partner in enumerate(partners):
+        pair = pltpu.make_async_remote_copy(
+            src_ref=sums_ref,
+            dst_ref=pair_ref.at[index],
+            send_sem=pair_send.at[index],
+            recv_sem=pair_recv.at[index],
+            device_id=(geo, partner, y_pos),
+            device_id_type=mesh_id,
+        )
+        pair.start()
+        pairs.append(pair)
 
     @pl.when(z_pos < z_count - 1)
     def _():
@@ -203,8 +212,9 @@
     def _():
         upper_ref[...] = jnp.zeros(upper_ref.shape, upper_ref.dtype)
 
-    pair.wait_send()
-    pair.wait_recv()
+    for pair in pairs:
+        pair.wait_send()
+        pair.wait_recv()
 
     @pl.when(z_pos < z_count - 1)
     def _():
@@ -224,14 +234,14 @@
     hbm = pl.BlockSpec(memory_space=pl.ANY)
     return pl.pallas_call(
         functools.partial(_z_halo_kernel, z_count),
-        out_shape=(halo, halo, jax.ShapeDtypeStruct(sums.shape, sums.dtype)),
+        out_shape=(halo, halo, jax.ShapeDtypeStruct((3,) + sums.shape, sums.dtype)),
         in_specs=[hbm, hbm],
         out_specs=(vmem, vmem, vmem),
         scratch_shapes=[
             pltpu.SemaphoreType.DMA((2,)),
             pltpu.SemaphoreType.DMA((2,)),
-            pltpu.SemaphoreType.DMA((1,)),
-            pltpu.SemaphoreType.DMA((1,)),
+            pltpu.SemaphoreType.DMA((3,)),
+            pltpu.SemaphoreType.DMA((3,)),
         ],
         compiler_params=pltpu.CompilerParams(collective_id=0, has_side_effects=True),
     )(point, sums)
@@ -504,8 +514,8 @@
         ]
     )
     lower, upper, paired = z_halo(point, sums, z_count)
-    sums = sums + paired
-    step = 2
+    sums = sums + jnp.sum(paired, axis=0)
+    step = 4
     while step < z_count:
         sums = sums + lax.ppermute(sums, "z", [(i, i ^ step) for i in range(z_count)])
         step *= 2

time: 143 us -> 152 us (1.063)
  waiting for transfers between devices: 33.1 us -> 26.5 us
  other arithmetic: 23 us -> 29.3 us
  local copies, waits for them, and re-layouts: 6.51 us -> 12.6 us
  Pallas kernels: 34.4 us -> 36.5 us
    ppermute x2 -> x1, waiting for transfers between devices: 3.51 us -> 0.01 us  [shards(): lax.ppermute(sums, 'z', [(i, i ^ step) for i in range(z_count)])]
    all_to_all x1, waiting for transfers between devices: 27.3 us -> 24.1 us  [shards(): lax.all_to_all(quarters, 'y', split_axis=0, concat_axis=0, tiled=True)]
    slice x2, local copies, waits for them, and re-layouts: 0.36 us -> 2.79 us  [shards(): jnp.roll(ext[:-2], 3, axis=1)]
    sub x1, other arithmetic: 1.38 us -> 3.76 us  [shards(): cubic = center * center * (plus + minus) - 2.0 * center * plus * minus]
    slice x2, local copies, waits for them, and re-layouts: 0.53 us -> 2.76 us  [shards(): jnp.roll(ext[2:], -1, axis=1)]
    pallas_call x1, Pallas kernels: 34.4 us -> 36.5 us  [z_halo(): pl.pallas_call(functools.partial(_z_halo_kernel, z_count), out_shape=(hal...]
    reduce_sum x0 -> x1, other arithmetic: none -> 1.54 us  [shards(): sums = sums + jnp.sum(paired, axis=0)]
    ppermute x2 -> x1, starting transfers between devices: 5.4 us -> 4.26 us  [shards(): lax.ppermute(sums, 'z', [(i, i ^ step) for i in range(z_count)])]
  transfers between devices with their start and end apart: 5 -> 4, of which waited for: 4 -> 3; matrix products, arithmetic and copies ran while one was open for 5% -> 7% of each run, Pallas kernels for 0% -> 0%
where the time goes in v20:
time: 152 us; the launch traced here: 151 us
  Pallas kernels  36.5 us (24%)
  blocking collectives  31.4 us (21%)
  other arithmetic  29.3 us (19%)
  waiting for transfers between devices  26.5 us (17%)
  starting transfers between devices  14.3 us (9%)
  local copies, waits for them, and re-layouts  12.6 us (8%)
    pallas_call x1, Pallas kernels, z_halo(): pl.pallas_call(functools.partial(_z_halo_kernel, z_count), out_shape=(hal...  36.5 us
    all_to_all x1, blocking collectives, shards(): return lax.all_to_all(updated, 'y', split_axis=0, concat_axis=2, tiled=True)  31.4 us
    all_to_all x1, waiting for transfers between devices, shards(): lax.all_to_all(quarters, 'y', split_axis=0, concat_axis=0, tiled=True)  24.1 us
    mul x3, other arithmetic, quick_flux(): return courant * face_value  8.41 us
    all_to_all x1, starting transfers between devices, shards(): lax.all_to_all(quarters, 'y', split_axis=0, concat_axis=0, tiled=True)  4.46 us
    ppermute x1, starting transfers between devices, shards(): lax.ppermute(sums, 'z', [(i, i ^ step) for i in range(z_count)])  4.26 us
    unnamed x36, local copies, waits for them, and re-layouts  4.02 us
    sub x1, other arithmetic, shards(): cubic = center * center * (plus + minus) - 2.0 * center * plus * minus  3.76 us
  transfers between devices with their start and end apart: 4, of which 3 were waited for; matrix products, arithmetic and copies ran while one was open for 7% of the time, Pallas kernels for 0%

profile of v20, /device:TPU:2, one launch (start us, length us, event | category | flops | bytes accessed | tf_op | source)
XLA Modules:
  0.0 150.9 jit_solution(9595459923027772776)
XLA Ops:
  0.0 0.8 convert_element_type.84
  0.8 2.0 %broadcast_multiply_fusion = f32[1,36,32,512]{3,2,1,0:T(8,128)S(1)} fusion(f32[1,36,32,512]{3,2,1,0:T(8,128)} %param.8, f32[32,512]{1,0:T(8,128)S(1)} %convert_element_type.84), kind=kLoop, calls=%fused_computation.58 | loop fusion | flops 589824 | bytes 4784128 | tf_op jit(solution)/shard_map/mul | solution.py:482
  2.9 0.1 fusion.46
  3.0 1.9 %collective-permute-start = (f32[1,36,2,512]{3,2,1,0:T(2,128)S(1)}, f32[1,36,2,512]{3,2,1,0:T(2,128)S(1)}, u32[]{:S(2)}, u32[]{:S(2)}) collective-permute-start(f32[1,36,2,512]{3,2,1,0:T(2,128)S(1)} %get-tuple-element.20), channel_id=1, source_target_pairs={{0,32},{32,64},{64,96},{96,128},{128,160},{160,192},{192,224},{1,3... | collective-permute-start | bytes 442376 | tf_op jit(solution)/shard_map/ppermute | solution.py:258
  4.9 3.6 %collective-permute-start.1 = (f32[1,36,2,512]{3,2,1,0:T(2,128)S(1)}, f32[1,36,2,512]{3,2,1,0:T(2,128)S(1)}, u32[]{:S(2)}, u32[]{:S(2)}) collective-permute-start(f32[1,36,2,512]{3,2,1,0:T(2,128)S(1)} %get-tuple-element.21), channel_id=1, source_target_pairs={{32,0},{64,32},{96,64},{128,96},{160,128},{192,160},{224,192},{33,... | collective-permute-start | bytes 442376 | tf_op jit(solution)/shard_map/ppermute | solution.py:260
  8.9 0.6 collective-permute-done
  9.5 1.8 %collective-permute-done.1 = f32[1,36,2,512]{3,2,1,0:T(2,128)S(1)} collective-permute-done((f32[1,36,2,512]{3,2,1,0:T(2,128)S(1)}, f32[1,36,2,512]{3,2,1,0:T(2,128)S(1)}, u32[]{:S(2)}, u32[]{:S(2)}) %collective-permute-start.1) | collective-permute-done | bytes 147488 | tf_op jit(solution)/shard_map/ppermute | solution.py:260
  11.2 2.5 %fusion.9 = f32[1,36,33,512]{3,2,1,0:T(8,128)S(1)} fusion(f32[1,36,2,512]{3,2,1,0:T(2,128)S(1)} %collective-permute-done.1, f32[1,36,32,512]{3,2,1,0:T(8,128)S(1)} %broadcast_multiply_fusion, f32[1,36,2,512]{3,2,1,0:T(2,128)S(1)} %collective-permute-done, f32[36]{0:T(128)S(1)} %get-tuple-element.33, f32[36]{0:T(128)S(1)} %get-tuple-element.34, ...), kind=kLoop, calls=%fused_computation.19 | loop fusion | flops 10948608 | bytes 5087700 | tf_op jit(solution)/shard_map/mul | solution.py:290
  13.8 0.7 fusion.28
  14.5 2.8 %fusion.4 = f32[1,36,32,513]{3,2,1,0:T(8,128)S(1)} fusion(f32[1,36,32,512]{3,2,1,0:T(8,128)S(1)} %fusion.28, f32[36]{0:T(128)S(1)} %get-tuple-element.30, f32[36]{0:T(128)S(1)} %get-tuple-element.31, f32[36]{0:T(128)S(1)} %get-tuple-element.32, pred[36]{0:T(512)(128)(4,1)S(1)} %get-tuple-element.36), kind=kLoop, calls=%fused_computation.13 | loop fusion | flops 8273664 | bytes 4723668 | tf_op jit(solution)/shard_map/mul | solution.py:290
  17.3 0.7 fusion.26
  18.0 0.1 copy-done.12
  18.1 0.0 copy-done.13
  18.2 3.1 %fusion.16 = f32[1,37,32,512]{3,2,1,0:T(8,128)S(1)} fusion(f32[1,2,32,512]{3,2,1,0:T(8,128)S(1)} %get-tuple-element.19, f32[1,36,32,512]{3,2,1,0:T(8,128)S(1)} %fusion.26, f32[1,2,32,512]{3,2,1,0:T(8,128)S(1)} %get-tuple-element.18, f32[32,512]{1,0:T(8,128)S(1)} %copy-done.12, f32[37]{0:T(128)S(1)} %get-tuple-element.38, f32[32,512]{1,0:T(8,128)S(1)} %copy-done.13, ...), kind=kLoop, calls=%fused_computation.34 | loop fusion | flops 16973824 | bytes 5177644 | tf_op jit(solution)/shard_map/mul | solution.py:290
  21.3 2.0 %copy_bitcast_fusion.1 = f32[4,36,8,512]{3,2,1,0:T(8,128)} fusion(f32[1,36,32,512]{3,2,1,0:T(8,128)S(1)} %fusion.26, f32[1,37,32,512]{3,2,1,0:T(8,128)S(1)} %fusion.16), kind=kLoop, calls=%fused_computation.54 | loop fusion | flops 1769472 | bytes 9437184 | tf_op jit(solution)/shard_map/transpose | solution.py:500
  23.3 4.5 %all-to-all-start = ((f32[4,36,8,512]{3,2,1,0:T(8,128)}), f32[4,36,8,512]{3,2,1,0:T(8,128)S(1)}, u32[]{:S(2)}, u32[]{:S(2)}) async-start(f32[4,36,8,512]{3,2,1,0:T(8,128)} %copy_bitcast_fusion.1), calls=%async_computation | async-start | bytes 4718592 | tf_op jit(solution)/shard_map/all_to_all | solution.py:503
  27.7 0.6 multiply_multiply_fusion.2
  28.3 0.6 broadcast_multiply_fusion.3
  28.9 0.6 constant_dynamic-slice_fusion
  29.5 0.7 dynamic-slice_multiply_fusion
  30.2 0.7 multiply_multiply_fusion
  30.9 2.8 %subtract_cosine_fusion = f32[36,8,512]{2,1,0:T(8,128)} fusion(f32[8,512]{1,0:T(8,128)S(1)} %get-tuple-element.41, f32[36]{0:T(128)S(1)} %add_multiply_fusion), kind=kLoop, calls=%fused_computation.59 | loop fusion | flops 147456 | bytes 606352 | tf_op jit(solution)/shard_map/cos | solution.py:534
  33.7 24.1 %all-to-all-done.point_ref = f32[4,36,8,512]{3,2,1,0:T(8,128)S(1)} async-done(((f32[4,36,8,512]{3,2,1,0:T(8,128)}), f32[4,36,8,512]{3,2,1,0:T(8,128)S(1)}, u32[]{:S(2)}, u32[]{:S(2)}) %all-to-all-start) | async-done | bytes 2359328 | tf_op jit(solution)/shard_map/all_to_all | solution.py:503
  57.8 0.7 multiply_reduce_fusion
  58.5 0.7 pad_maximum_fusion.8.sums_ref
  59.2 0.0 copy-done
  59.2 36.5 %shard_map.64 = (f32[2,36,8,512]{3,2,1,0:T(8,128)}, f32[2,36,8,512]{3,2,1,0:T(8,128)}, f32[3,3,8,512]{3,2,1,0:T(8,128)}) custom-call(f32[4,36,8,512]{3,2,1,0:T(8,128)} %copy-done, f32[3,8,512]{2,1,0:T(8,128)} %pad_maximum_fusion.8.sums_ref), custom_call_target="tpu_custom_call" | custom-call | tf_op jit(solution)/shard_map/pallas_call | solution.py:235
  95.8 1.5 constant_dynamic-update-slice_fusion.3
  97.3 0.5 copy-done.1
  97.8 0.6 constant_dynamic-update-slice_fusion.1
  98.4 0.6 copy-done.4
  99.0 0.1 constant_dynamic-update-slice_fusion
  99.1 2.1 %slice.190 = f32[6,35,8,512]{3,2,1,0:T(8,128)} slice(f32[6,36,8,512]{3,2,1,0:T(8,128)S(1)} %constant_dynamic-update-slice_fusion), slice={[0:6], [1:36], [0:8], [0:512]} | slice | bytes 6881280 | tf_op jit(solution)/shard_map/jit(_roll_static)/slice | solution.py:525
  101.2 0.6 slice.191
  101.9 2.1 %slice.193 = f32[6,33,8,512]{3,2,1,0:T(8,128)} slice(f32[6,36,8,512]{3,2,1,0:T(8,128)S(1)} %get-tuple-element.17), slice={[0:6], [0:33], [0:8], [0:512]} | slice | bytes 6488064 | tf_op jit(solution)/shard_map/jit(_roll_static)/slice | solution.py:525
  103.9 0.7 slice.192
  104.7 1.5 %reduce_sum.39 = f32[3,8,512]{2,1,0:T(8,128)} reduce(f32[3,3,8,512]{3,2,1,0:T(8,128)} %get-tuple-element.8, f32[]{:T(128)} %constant.35.clone.1), dimensions={0}, to_apply=%region_3.4 | reduce | flops 24576 | bytes 196612 | tf_op jit(solution)/shard_map/reduce_sum | solution.py:517
  106.2 0.8 fusion.43
  107.0 4.3 %collective-permute-start.2 = (f32[3,8,512]{2,1,0:T(8,128)S(1)}, f32[3,8,512]{2,1,0:T(8,128)S(1)}, u32[]{:S(2)}, u32[]{:S(2)}) collective-permute-start(f32[3,8,512]{2,1,0:T(8,128)S(1)} %fusion.43), channel_id=1, source_target_pairs={{0,16},{4,20},{8,24},{12,28},{16,0},{20,4},{24,8},{28,12},{1,17},{... | collective-permute-start | bytes 147464 | tf_op jit(solution)/shard_map/ppermute | solution.py:520
  111.3 3.8 %multiply_subtract_fusion = f32[6,36,8,512]{3,2,1,0:T(8,128)S(1)} fusion(f32[6,33,8,512]{3,2,1,0:T(8,128)} %slice.193, f32[6,3,8,512]{3,2,1,0:T(8,128)} %slice.192, f32[6,1,8,512]{3,2,1,0:T(8,128)} %slice.191, f32[6,35,8,512]{3,2,1,0:T(8,128)} %slice.190, f32[2,36,8,512]{3,2,1,0:T(8,128)} %get-tuple-element.10, f32[4,36,8,512]{3,2,1,0:T(8,128)S(1)} %copy-done.1, ...), kind=kLoop, calls=%fused_computation.4 | loop fusion | flops 9732096 | bytes 15335424 | tf_op jit(solution)/shard_map/sub | solution.py:526
  115.1 0.2 slice.196
  115.4 0.3 slice.197
  115.7 0.4 copy-done.6
  116.2 0.1 fusion.31
  116.3 0.2 copy-done.5
  116.5 1.4 fusion.21
  117.9 31.4 %all_to_all.23 = f32[4,36,8,512]{3,2,1,0:T(8,128)S(1)} all-to-all(f32[4,36,8,512]{3,2,1,0:T(8,128)S(1)} %fusion.21), channel_id=1, replica_groups=mesh['geo'=8,'z'=8,'y'=4] {'y'}, dimensions={0} | all-to-all | bytes 4718592 | tf_op jit(solution)/shard_map/all_to_all | solution.py:548
  149.3 1.7 %copy_bitcast_fusion = f32[1,36,32,512]{3,2,1,0:T(8,128)} fusion(f32[4,36,8,512]{3,2,1,0:T(8,128)S(1)} %all_to_all.23), kind=kLoop, calls=%fused_computation.53 | loop fusion | bytes 4718592 | tf_op jit(solution)/shard_map/all_to_all | solution.py:548
  (40 shorter events, 0.4 us)
Async XLA Ops:
  3.0 6.5 %collective-permute-start = (f32[1,36,2,512]{3,2,1,0:T(2,128)S(1)}, f32[1,36,2,512]{3,2,1,0:T(2,128)S(1)}, u32[]{:S(2)}, u32[]{:S(2)}) collective-permute-start(f32[1,36,2,512]{3,2,1,0:T(2,128)S(1)} %get-tuple-element.20), channel_id=1, source_target_pairs={{0,32},{32,64},{64,96},{96,128},{128,160},{160,192},{192,224},{1,3... | collective-permute-start | bytes 442376 | tf_op jit(solution)/shard_map/ppermute | solution.py:258
  4.9 6.3 %collective-permute-start.1 = (f32[1,36,2,512]{3,2,1,0:T(2,128)S(1)}, f32[1,36,2,512]{3,2,1,0:T(2,128)S(1)}, u32[]{:S(2)}, u32[]{:S(2)}) collective-permute-start(f32[1,36,2,512]{3,2,1,0:T(2,128)S(1)} %get-tuple-element.21), channel_id=1, source_target_pairs={{32,0},{64,32},{96,64},{128,96},{160,128},{192,160},{224,192},{33,... | collective-permute-start | bytes 442376 | tf_op jit(solution)/shard_map/ppermute | solution.py:260
  11.2 2.5 %copy-start.2 = (f32[1,36,32,512]{3,2,1,0:T(8,128)S(1)}, f32[1,36,32,512]{3,2,1,0:T(8,128)}, u32[]{:S(2)}) copy-start(f32[1,36,32,512]{3,2,1,0:T(8,128)} %param.8) | copy-start | bytes 7077892
  17.3 0.8 copy-start.12
  17.3 0.9 copy-start.13
  23.3 34.6 %all-to-all-start = ((f32[4,36,8,512]{3,2,1,0:T(8,128)}), f32[4,36,8,512]{3,2,1,0:T(8,128)S(1)}, u32[]{:S(2)}, u32[]{:S(2)}) async-start(f32[4,36,8,512]{3,2,1,0:T(8,128)} %copy_bitcast_fusion.1), calls=%async_computation | async-start | bytes 4718592 | tf_op jit(solution)/shard_map/all_to_all | solution.py:503
  57.8 1.4 copy-start
  58.5 38.8 %copy-start.8 = (f32[8,512]{1,0:T(8,128)}, f32[8,512]{1,0:T(8,128)S(1)}, u32[]{:S(2)}) copy-start(f32[8,512]{1,0:T(8,128)S(1)} %get-tuple-element.12) | copy-start | bytes 49156
  58.5 38.8 %copy-start.10 = (f32[8,512]{1,0:T(8,128)}, f32[8,512]{1,0:T(8,128)S(1)}, u32[]{:S(2)}) copy-start(f32[8,512]{1,0:T(8,128)S(1)} %get-tuple-element.13) | copy-start | bytes 49156
  95.7 2.0 %copy-start.1 = (f32[4,36,8,512]{3,2,1,0:T(8,128)S(1)}, f32[4,36,8,512]{3,2,1,0:T(8,128)}, u32[]{:S(2)}) copy-start(f32[4,36,8,512]{3,2,1,0:T(8,128)} %copy-done) | copy-start | bytes 7077892
  97.8 1.3 copy-start.4
  101.9 9.4 %copy-start.3 = (f32[2,36,8,512]{3,2,1,0:T(8,128)S(1)}, f32[2,36,8,512]{3,2,1,0:T(8,128)}, u32[]{:S(2)}) copy-start(f32[2,36,8,512]{3,2,1,0:T(8,128)} %get-tuple-element.9) | copy-start | bytes 3538948
  107.0 8.7 %collective-permute-start.2 = (f32[3,8,512]{2,1,0:T(8,128)S(1)}, f32[3,8,512]{2,1,0:T(8,128)S(1)}, u32[]{:S(2)}, u32[]{:S(2)}) collective-permute-start(f32[3,8,512]{2,1,0:T(8,128)S(1)} %fusion.43), channel_id=1, source_target_pairs={{0,16},{4,20},{8,24},{12,28},{16,0},{20,4},{24,8},{28,12},{1,17},{... | collective-permute-start | bytes 147464 | tf_op jit(solution)/shard_map/ppermute | solution.py:520
  115.3 0.8 copy-start.6
  115.3 0.8 copy-start.9
  115.3 0.8 copy-start.11
  115.3 0.8 copy-start.16
  115.4 1.1 copy-start.5
  115.4 1.1 copy-start.7
  115.4 1.1 copy-start.14
  115.4 1.1 copy-start.15

commit v21 on v16

--- a/solution.py
+++ b/solution.py
@@ -483,10 +483,10 @@
         ]
     )
     lower, upper = z_halo(point, z_count)
-    step = 1
-    while step < z_count:
+    step = z_count // 2
+    while step >= 1:
         sums = sums + lax.ppermute(sums, "z", [(i, i ^ step) for i in range(z_count)])
-        step *= 2
+        step //= 2
     energy_sum, first_sum, root_sum = sums[0], sums[1], sums[2]
     energy = energy_sum + EPSILON
     ext = jnp.concatenate([lower, point, upper], axis=0)

time: 142 us -> 140 us (0.986)
  the two profiles are of different devices: /device:TPU:32 before, /device:TPU:2 now
where the time goes in v21:
time: 140 us; the launch traced here: 138 us
  waiting for transfers between devices  34.1 us (24%)
  Pallas kernels  28.2 us (20%)
  blocking collectives  27.4 us (20%)
  other arithmetic  23 us (16%)
  starting transfers between devices  16.9 us (12%)
  local copies, waits for them, and re-layouts  8.39 us (6%)
    pallas_call x1, Pallas kernels, z_halo(): pl.pallas_call(functools.partial(_z_halo_kernel, z_count), out_shape=(hal...  28.2 us
    all_to_all x1, blocking collectives, shards(): return lax.all_to_all(updated, 'y', split_axis=0, concat_axis=2, tiled=True)  27.4 us
    all_to_all x1, waiting for transfers between devices, shards(): lax.all_to_all(floored, 'y', split_axis=2, concat_axis=0, tiled=True)  25.6 us
    ppermute x3, starting transfers between devices, shards(): lax.ppermute(sums, 'z', [(i, i ^ step) for i in range(z_count)])  8.78 us
    mul x3, other arithmetic, quick_flux(): return courant * face_value  8.41 us
    ppermute x1, waiting for transfers between devices, extended(): lax.ppermute(tail, axis, [(i, (i + 1) % count) for i in range(ends)])  4.37 us
    ppermute x3, waiting for transfers between devices, shards(): lax.ppermute(sums, 'z', [(i, i ^ step) for i in range(z_count)])  4.09 us
    max x1, local copies, waits for them, and re-layouts, shards(): floored = jnp.maximum(advect(padded, turning, 1), 0.0)  3.83 us
  transfers between devices with their start and end apart: 6, of which 4 were waited for; matrix products, arithmetic and copies ran while one was open for 7% of the time, Pallas kernels for 20%

profile of v21, /device:TPU:2, one launch (start us, length us, event | category | flops | bytes accessed | tf_op | source)
XLA Modules:
  0.0 138.3 jit_solution(4792576416295670157)
XLA Ops:
  0.0 0.8 convert_element_type.84
  0.8 2.0 %broadcast_multiply_fusion = f32[1,36,32,512]{3,2,1,0:T(8,128)S(1)} fusion(f32[1,36,32,512]{3,2,1,0:T(8,128)} %param.8, f32[32,512]{1,0:T(8,128)S(1)} %convert_element_type.84), kind=kLoop, calls=%fused_computation.64 | loop fusion | flops 589824 | bytes 4784128 | tf_op jit(solution)/shard_map/mul | solution.py:455
  2.9 0.1 fusion.48
  3.0 1.9 %collective-permute-start.1 = (f32[1,36,2,512]{3,2,1,0:T(2,128)S(1)}, f32[1,36,2,512]{3,2,1,0:T(2,128)S(1)}, u32[]{:S(2)}, u32[]{:S(2)}) collective-permute-start(f32[1,36,2,512]{3,2,1,0:T(2,128)S(1)} %get-tuple-element.17), channel_id=1, source_target_pairs={{32,0},{64,32},{96,64},{128,96},{160,128},{192,160},{224,192},{33,... | collective-permute-start | bytes 442376 | tf_op jit(solution)/shard_map/ppermute | solution.py:233
  4.9 2.4 %collective-permute-start = (f32[1,36,2,512]{3,2,1,0:T(2,128)S(1)}, f32[1,36,2,512]{3,2,1,0:T(2,128)S(1)}, u32[]{:S(2)}, u32[]{:S(2)}) collective-permute-start(f32[1,36,2,512]{3,2,1,0:T(2,128)S(1)} %get-tuple-element.16), channel_id=1, source_target_pairs={{0,32},{32,64},{64,96},{96,128},{128,160},{160,192},{192,224},{1,3... | collective-permute-start | bytes 442376 | tf_op jit(solution)/shard_map/ppermute | solution.py:231
  7.6 0.0 collective-permute-done.1
  7.6 4.4 %collective-permute-done = f32[1,36,2,512]{3,2,1,0:T(2,128)S(1)} collective-permute-done((f32[1,36,2,512]{3,2,1,0:T(2,128)S(1)}, f32[1,36,2,512]{3,2,1,0:T(2,128)S(1)}, u32[]{:S(2)}, u32[]{:S(2)}) %collective-permute-start) | collective-permute-done | bytes 147488 | tf_op jit(solution)/shard_map/ppermute | solution.py:231
  12.0 0.0 copy-start.1
  12.0 2.5 %fusion.12 = f32[1,36,33,512]{3,2,1,0:T(8,128)S(1)} fusion(f32[1,36,2,512]{3,2,1,0:T(2,128)S(1)} %collective-permute-done.1, f32[1,36,32,512]{3,2,1,0:T(8,128)S(1)} %broadcast_multiply_fusion, f32[1,36,2,512]{3,2,1,0:T(2,128)S(1)} %collective-permute-done, f32[36]{0:T(128)S(1)} %get-tuple-element.29, f32[36]{0:T(128)S(1)} %get-tuple-element.30, ...), kind=kLoop, calls=%fused_computation.25 | loop fusion | flops 10948608 | bytes 5087700 | tf_op jit(solution)/shard_map/mul | solution.py:263
  14.6 0.0 copy-done.1
  14.6 0.7 fusion.30
  15.3 2.8 %fusion.7 = f32[1,36,32,513]{3,2,1,0:T(8,128)S(1)} fusion(f32[1,36,32,512]{3,2,1,0:T(8,128)S(1)} %fusion.30, f32[36]{0:T(128)S(1)} %get-tuple-element.26, f32[36]{0:T(128)S(1)} %get-tuple-element.27, f32[36]{0:T(128)S(1)} %get-tuple-element.28, pred[36]{0:T(512)(128)(4,1)S(1)} %get-tuple-element.32), kind=kLoop, calls=%fused_computation.19 | loop fusion | flops 8273664 | bytes 4723668 | tf_op jit(solution)/shard_map/mul | solution.py:263
  18.1 0.0 copy-start.4
  18.1 0.0 copy-start.5
  18.1 0.7 fusion.28
  18.8 0.1 copy-done.4
  18.9 0.0 copy-done.5
  19.0 3.1 %fusion.19 = f32[1,37,32,512]{3,2,1,0:T(8,128)S(1)} fusion(f32[1,2,32,512]{3,2,1,0:T(8,128)S(1)} %get-tuple-element.15, f32[1,36,32,512]{3,2,1,0:T(8,128)S(1)} %fusion.28, f32[1,2,32,512]{3,2,1,0:T(8,128)S(1)} %get-tuple-element.14, f32[32,512]{1,0:T(8,128)S(1)} %copy-done.4, f32[37]{0:T(128)S(1)} %get-tuple-element.34, f32[32,512]{1,0:T(8,128)S(1)} %copy-done.5, ...), kind=kLoop, calls=%fused_computation.40 | loop fusion | flops 16973824 | bytes 5177644 | tf_op jit(solution)/shard_map/mul | solution.py:263
  22.1 0.6 fusion.26
  22.7 3.8 %copy.17 = f32[1,36,32,512]{3,0,1,2:T(1,128)} copy(f32[1,36,32,512]{3,2,1,0:T(8,128)S(1)} %fusion.26) | data formatting | bytes 4718592 | tf_op jit(solution)/shard_map/max | solution.py:471
  26.5 3.8 %all-to-all-start = ((f32[1,36,32,512]{3,0,1,2:T(1,128)}), f32[1,36,32,512]{3,0,1,2:T(1,128)S(1)}, u32[]{:S(2)}, u32[]{:S(2)}) async-start(f32[1,36,32,512]{3,0,1,2:T(1,128)} %copy.17), calls=%async_computation | async-start | bytes 4718592 | tf_op jit(solution)/shard_map/all_to_all | solution.py:472
  30.4 0.7 dynamic-slice_multiply_fusion
  31.1 0.1 multiply_multiply_fusion
  31.2 1.9 %subtract_cosine_fusion = f32[36,8,512]{2,1,0:T(8,128)S(1)} fusion(f32[8,512]{1,0:T(8,128)S(1)} %get-tuple-element.37, f32[36]{0:T(128)S(1)} %add_multiply_fusion), kind=kLoop, calls=%fused_computation.65 | loop fusion | flops 147456 | bytes 606352 | tf_op jit(solution)/shard_map/cos | solution.py:502
  33.2 25.6 %all-to-all-done = f32[1,36,32,512]{3,0,1,2:T(1,128)S(1)} async-done(((f32[1,36,32,512]{3,0,1,2:T(1,128)}), f32[1,36,32,512]{3,0,1,2:T(1,128)S(1)}, u32[]{:S(2)}, u32[]{:S(2)}) %all-to-all-start) | async-done | bytes 2359328 | tf_op jit(solution)/shard_map/all_to_all | solution.py:472
  58.8 0.8 multiply_reduce_fusion
  59.6 7.5 %collective-permute-start.2 = (f32[3,8,512]{2,1,0:T(8,128)S(1)}, f32[3,8,512]{2,1,0:T(8,128)S(1)}, u32[]{:S(2)}, u32[]{:S(2)}) collective-permute-start(f32[3,8,512]{2,1,0:T(8,128)S(1)} %pad_maximum_fusion.9), channel_id=1, source_target_pairs={{0,16},{4,20},{8,24},{12,28},{16,0},{20,4},{24,8},{28,12},{1,17},{... | collective-permute-start | bytes 147464 | tf_op jit(solution)/shard_map/ppermute | solution.py:488
  67.0 2.1 %copy_bitcast_fusion.1.point_ref = f32[4,36,8,512]{3,2,1,0:T(8,128)} fusion(f32[1,36,32,512]{3,0,1,2:T(1,128)S(1)} %all-to-all-done), kind=kLoop, calls=%fused_computation.59 | loop fusion | bytes 4718592 | tf_op jit(solution)/shard_map/all_to_all | solution.py:472
  69.2 28.2 %shard_map.64 = (f32[2,36,8,512]{3,2,1,0:T(8,128)}, f32[2,36,8,512]{3,2,1,0:T(8,128)}) custom-call(f32[4,36,8,512]{3,2,1,0:T(8,128)} %copy_bitcast_fusion.1.point_ref), custom_call_target="tpu_custom_call" | custom-call | tf_op jit(solution)/shard_map/pallas_call | solution.py:210
  97.4 0.0 collective-permute-done.2
  97.4 1.1 collective-permute-start.3
  98.6 0.0 copy-start
  98.6 0.0 copy-start.2
  98.6 0.0 copy-start.3
  98.6 2.4 %fusion.2 = f32[6,35,8,512]{3,2,1,0:T(8,128)S(1)} fusion(f32[4,36,8,512]{3,2,1,0:T(8,128)} %copy_bitcast_fusion.1.point_ref, f32[2,36,8,512]{3,2,1,0:T(8,128)} %get-tuple-element.8), kind=kLoop, calls=%fused_computation.10 | loop fusion | flops 860160 | bytes 6979584 | tf_op jit(solution)/shard_map/concatenate | solution.py:492
  101.0 2.0 %collective-permute-done.3 = f32[3,8,512]{2,1,0:T(8,128)S(1)} collective-permute-done((f32[3,8,512]{2,1,0:T(8,128)S(1)}, f32[3,8,512]{2,1,0:T(8,128)S(1)}, u32[]{:S(2)}, u32[]{:S(2)}) %collective-permute-start.3) | collective-permute-done | bytes 49184 | tf_op jit(solution)/shard_map/ppermute | solution.py:488
  103.0 0.2 collective-permute-start.4
  103.2 0.0 copy-done
  103.2 0.0 copy-done.2
  103.2 0.0 copy-done.3
  103.2 1.4 %multiply_subtract_fusion = f32[6,36,8,512]{3,2,1,0:T(8,128)S(1)} fusion(f32[2,36,8,512]{3,2,1,0:T(8,128)S(1)} %copy-done.2, f32[4,36,8,512]{3,2,1,0:T(8,128)S(1)} %copy-done, f32[6,35,8,512]{3,2,1,0:T(8,128)S(1)} %fusion.2, f32[2,36,8,512]{3,2,1,0:T(8,128)S(1)} %copy-done.3), kind=kLoop, calls=%fused_computation.9 | loop fusion | flops 12386304 | bytes 11698176 | tf_op jit(solution)/shard_map/sub | solution.py:494
  104.6 0.2 slice.194
  104.9 0.2 slice.195
  105.1 2.1 %collective-permute-done.4 = f32[3,8,512]{2,1,0:T(8,128)S(1)} collective-permute-done((f32[3,8,512]{2,1,0:T(8,128)S(1)}, f32[3,8,512]{2,1,0:T(8,128)S(1)}, u32[]{:S(2)}, u32[]{:S(2)}) %collective-permute-start.4) | collective-permute-done | bytes 49184 | tf_op jit(solution)/shard_map/ppermute | solution.py:488
  107.3 0.1 fusion.33
  107.4 1.9 %fusion.24 = f32[4,36,8,512]{3,2,1,0:T(8,128)S(1)} fusion(f32[6,36,8,512]{3,2,1,0:T(8,128)S(1)} %multiply_subtract_fusion, f32[4,35,8,512]{3,2,1,0:T(8,128)S(1)} %slice.194, f32[4,1,8,512]{3,2,1,0:T(8,128)S(1)} %slice.193, f32[4,3,8,512]{3,2,1,0:T(8,128)S(1)} %slice.196, f32[4,33,8,512]{3,2,1,0:T(8,128)S(1)} %slice.195, ...), kind=kLoop, calls=%fused_computation.48 | loop fusion | flops 8847360 | bytes 12550160 | tf_op jit(solution)/shard_map/mul | solution.py:503
  109.3 27.4 %all_to_all.36 = f32[4,36,8,512]{3,2,1,0:T(8,128)S(1)} all-to-all(f32[4,36,8,512]{3,2,1,0:T(8,128)S(1)} %fusion.24), channel_id=1, replica_groups=mesh['geo'=8,'z'=8,'y'=4] {'y'}, dimensions={0} | all-to-all | bytes 4718592 | tf_op jit(solution)/shard_map/all_to_all | solution.py:516
  136.7 1.7 %copy_bitcast_fusion = f32[1,36,32,512]{3,2,1,0:T(8,128)} fusion(f32[4,36,8,512]{3,2,1,0:T(8,128)S(1)} %all_to_all.36), kind=kLoop, calls=%fused_computation.58 | loop fusion | bytes 4718592 | tf_op jit(solution)/shard_map/all_to_all | solution.py:516
  (18 shorter events, 0.4 us)
Async XLA Ops:
  3.0 4.6 %collective-permute-start.1 = (f32[1,36,2,512]{3,2,1,0:T(2,128)S(1)}, f32[1,36,2,512]{3,2,1,0:T(2,128)S(1)}, u32[]{:S(2)}, u32[]{:S(2)}) collective-permute-start(f32[1,36,2,512]{3,2,1,0:T(2,128)S(1)} %get-tuple-element.17), channel_id=1, source_target_pairs={{32,0},{64,32},{96,64},{128,96},{160,128},{192,160},{224,192},{33,... | collective-permute-start | bytes 442376 | tf_op jit(solution)/shard_map/ppermute | solution.py:233
  4.9 7.1 %collective-permute-start = (f32[1,36,2,512]{3,2,1,0:T(2,128)S(1)}, f32[1,36,2,512]{3,2,1,0:T(2,128)S(1)}, u32[]{:S(2)}, u32[]{:S(2)}) collective-permute-start(f32[1,36,2,512]{3,2,1,0:T(2,128)S(1)} %get-tuple-element.16), channel_id=1, source_target_pairs={{0,32},{32,64},{64,96},{96,128},{128,160},{160,192},{192,224},{1,3... | collective-permute-start | bytes 442376 | tf_op jit(solution)/shard_map/ppermute | solution.py:231
  12.0 2.5 %copy-start.1 = (f32[1,36,32,512]{3,2,1,0:T(8,128)S(1)}, f32[1,36,32,512]{3,2,1,0:T(8,128)}, u32[]{:S(2)}) copy-start(f32[1,36,32,512]{3,2,1,0:T(8,128)} %param.8) | copy-start | bytes 7077892
  18.1 0.8 copy-start.4
  18.1 0.9 copy-start.5
  26.5 32.3 %all-to-all-start = ((f32[1,36,32,512]{3,0,1,2:T(1,128)}), f32[1,36,32,512]{3,0,1,2:T(1,128)S(1)}, u32[]{:S(2)}, u32[]{:S(2)}) async-start(f32[1,36,32,512]{3,0,1,2:T(1,128)} %copy.17), calls=%async_computation | async-start | bytes 4718592 | tf_op jit(solution)/shard_map/all_to_all | solution.py:472
  59.6 37.8 %collective-permute-start.2 = (f32[3,8,512]{2,1,0:T(8,128)S(1)}, f32[3,8,512]{2,1,0:T(8,128)S(1)}, u32[]{:S(2)}, u32[]{:S(2)}) collective-permute-start(f32[3,8,512]{2,1,0:T(8,128)S(1)} %pad_maximum_fusion.9), channel_id=1, source_target_pairs={{0,16},{4,20},{8,24},{12,28},{16,0},{20,4},{24,8},{28,12},{1,17},{... | collective-permute-start | bytes 147464 | tf_op jit(solution)/shard_map/ppermute | solution.py:488
  97.4 5.6 %collective-permute-start.3 = (f32[3,8,512]{2,1,0:T(8,128)S(1)}, f32[3,8,512]{2,1,0:T(8,128)S(1)}, u32[]{:S(2)}, u32[]{:S(2)}) collective-permute-start(f32[3,8,512]{2,1,0:T(8,128)S(1)} %fusion.45), channel_id=1, source_target_pairs={{0,8},{4,12},{8,0},{12,4},{16,24},{20,28},{24,16},{28,20},{1,9},{5... | collective-permute-start | bytes 147464 | tf_op jit(solution)/shard_map/ppermute | solution.py:488
  98.6 4.6 %copy-start = (f32[4,36,8,512]{3,2,1,0:T(8,128)S(1)}, f32[4,36,8,512]{3,2,1,0:T(8,128)}, u32[]{:S(2)}) copy-start(f32[4,36,8,512]{3,2,1,0:T(8,128)} %copy_bitcast_fusion.1.point_ref) | copy-start | bytes 7077892
  98.6 4.6 %copy-start.2 = (f32[2,36,8,512]{3,2,1,0:T(8,128)S(1)}, f32[2,36,8,512]{3,2,1,0:T(8,128)}, u32[]{:S(2)}) copy-start(f32[2,36,8,512]{3,2,1,0:T(8,128)} %get-tuple-element.8) | copy-start | bytes 3538948
  98.6 4.6 %copy-start.3 = (f32[2,36,8,512]{3,2,1,0:T(8,128)S(1)}, f32[2,36,8,512]{3,2,1,0:T(8,128)}, u32[]{:S(2)}) copy-start(f32[2,36,8,512]{3,2,1,0:T(8,128)} %get-tuple-element.7) | copy-start | bytes 3538948
  103.0 4.2 %collective-permute-start.4 = (f32[3,8,512]{2,1,0:T(8,128)S(1)}, f32[3,8,512]{2,1,0:T(8,128)S(1)}, u32[]{:S(2)}, u32[]{:S(2)}) collective-permute-start(f32[3,8,512]{2,1,0:T(8,128)S(1)} %fusion.49), channel_id=1, source_target_pairs={{0,4},{4,0},{8,12},{12,8},{16,20},{20,16},{24,28},{28,24},{1,5},{5... | collective-permute-start | bytes 147464 | tf_op jit(solution)/shard_map/ppermute | solution.py:488

commit v22 on v2

--- a/solution.py
+++ b/solution.py
@@ -1,8 +1,11 @@
+import functools
 import math
 
 import jax
 import jax.numpy as jnp
 from jax import lax
+from jax.experimental import pallas as pl
+from jax.experimental.pallas import tpu as pltpu
 from jax.sharding import PartitionSpec as P
 
 GRAVITY = 9.81
@@ -145,6 +148,81 @@
 
 
 Y_GROUP = 4
+HALO = 2
+
+
+def _z_halo_kernel(z_count, point_ref, ext_ref, local_sem, halo_send, halo_recv):
+    geo = lax.axis_index("geo")
+    z_pos = lax.axis_index("z")
+    y_pos = lax.axis_index("y")
+    group = point_ref.shape[0]
+    mesh_id = pl.DeviceIdType.MESH
+    barrier = pltpu.get_barrier_semaphore()
+    for step in (1, z_count - 1):
+        pl.semaphore_signal(barrier, inc=1, device_id=(geo, lax.rem(z_pos + step, z_count), y_pos),
+                            device_id_type=mesh_id)
+    pl.semaphore_wait(barrier, 2)
+
+    def halo_copy(src_lo, dst_lo, slot, target):
+        return pltpu.make_async_remote_copy(
+            src_ref=point_ref.at[pl.ds(src_lo, HALO)],
+            dst_ref=ext_ref.at[pl.ds(dst_lo, HALO)],
+            send_sem=halo_send.at[slot],
+            recv_sem=halo_recv.at[slot],
+            device_id=(geo, target, y_pos),
+            device_id_type=mesh_id,
+        )
+
+    up = halo_copy(group - HALO, 0, 0, lax.rem(z_pos + 1, z_count))
+    down = halo_copy(0, HALO + group, 1, lax.rem(z_pos + z_count - 1, z_count))
+
+    @pl.when(z_pos < z_count - 1)
+    def _():
+        up.start()
+
+    @pl.when(z_pos > 0)
+    def _():
+        down.start()
+
+    local = pltpu.make_async_copy(point_ref, ext_ref.at[pl.ds(HALO, group)], local_sem.at[0])
+    local.start()
+
+    @pl.when(z_pos == 0)
+    def _():
+        ext_ref[pl.ds(0, HALO)] = jnp.zeros((HALO,) + ext_ref.shape[1:], ext_ref.dtype)
+
+    @pl.when(z_pos == z_count - 1)
+    def _():
+        ext_ref[pl.ds(HALO + group, HALO)] = jnp.zeros((HALO,) + ext_ref.shape[1:], ext_ref.dtype)
+
+    local.wait()
+
+    @pl.when(z_pos < z_count - 1)
+    def _():
+        up.wait_send()
+        down.wait_recv()
+
+    @pl.when(z_pos > 0)
+    def _():
+        down.wait_send()
+        up.wait_recv()
+
+
+def z_halo(point, z_count):
+    group, dirs, rows, cols = point.shape
+    vmem = pl.BlockSpec(memory_space=pltpu.VMEM)
+    return pl.pallas_call(
+        functools.partial(_z_halo_kernel, z_count),
+        out_shape=jax.ShapeDtypeStruct((group + 2 * HALO, dirs, rows, cols), point.dtype),
+        in_specs=[pl.BlockSpec(memory_space=pl.ANY)],
+        out_specs=vmem,
+        scratch_shapes=[
+            pltpu.SemaphoreType.DMA((1,)),
+            pltpu.SemaphoreType.DMA((2,)),
+            pltpu.SemaphoreType.DMA((2,)),
+        ],
+        compiler_params=pltpu.CompilerParams(collective_id=0, has_side_effects=True),
+    )(point)
 
 
 def shards(spectrum, land_sea, sea_index, sea_count, wind_speed, wind_dir, slope_x, slope_y):
@@ -180,8 +258,6 @@
     point = lax.all_to_all(floored, "y", split_axis=2, concat_axis=0, tiled=True)
     group = point.shape[0]
     part_rows = point.shape[2]
-    lower = lax.ppermute(point[group - 2 :], "z", [(i, i + 1) for i in range(z_count - 1)])
-    upper = lax.ppermute(point[:2], "z", [(i + 1, i) for i in range(z_count - 1)])
     group_ids = (z_pos * group + jnp.arange(group)).astype(jnp.float32)
     radian_freq, wavenum, courant, turn_rate, band_spread = band_table(group_ids)
     scaled = point * (band_spread * dtheta)[:, None, None, None]
@@ -192,10 +268,13 @@
             jnp.sum(scaled / jnp.sqrt(wavenum)[:, None, None, None], axis=(0, 1)),
         ]
     )
-    sums = jnp.sum(lax.all_gather(sums, "z"), axis=0)
+    ext = z_halo(point, z_count)
+    step = z_count // 2
+    while step >= 1:
+        sums = sums + lax.ppermute(sums, "z", [(i, i ^ step) for i in range(z_count)])
+        step //= 2
     energy_sum, first_sum, root_sum = sums[0], sums[1], sums[2]
     energy = energy_sum + EPSILON
-    ext = jnp.concatenate([lower, point, upper], axis=0)
     center, plus, minus = ext[1:-1], jnp.roll(ext[2:], -1, axis=1), jnp.roll(ext[:-2], 3, axis=1)
     cubic = center * center * (plus + minus) - 2.0 * center * plus * minus
     extra = (

time: 157 us -> 146 us (0.930)
  the two profiles are of different devices: /device:TPU:2 before, /device:TPU:32 now
where the time goes in v22:
time: 146 us
  waiting for transfers between devices  32.1 us (22%)
  Pallas kernels  32 us (22%)
  blocking collectives  29.9 us (20%)
  other arithmetic  20.7 us (14%)
  starting transfers between devices  18.3 us (13%)
  local copies, waits for them, and re-layouts  12.3 us (8%)
    pallas_call x1, Pallas kernels, z_halo(): pl.pallas_call(functools.partial(_z_halo_kernel, z_count), out_shape=jax....  32 us
    all_to_all x1, blocking collectives, shards(): return lax.all_to_all(updated, 'y', split_axis=0, concat_axis=2, tiled=True)  29.9 us
    all_to_all x1, waiting for transfers between devices, shards(): lax.all_to_all(floored, 'y', split_axis=2, concat_axis=0, tiled=True)  26.8 us
    ppermute x3, starting transfers between devices, shards(): lax.ppermute(sums, 'z', [(i, i ^ step) for i in range(z_count)])  9.52 us
    mul x3, other arithmetic, quick_flux(): return courant * face_value  8.41 us
    ppermute x3, waiting for transfers between devices, shards(): lax.ppermute(sums, 'z', [(i, i ^ step) for i in range(z_count)])  4.62 us
    all_to_all x1, starting transfers between devices, shards(): lax.all_to_all(floored, 'y', split_axis=2, concat_axis=0, tiled=True)  4.46 us
    max x1, local copies, waits for them, and re-layouts, shards(): floored = jnp.maximum(advect(padded, turning, 1), 0.0)  3.83 us
  transfers between devices with their start and end apart: 6, of which 4 were waited for; matrix products, arithmetic and copies ran while one was open for 7% of the time, Pallas kernels for 22%

profile of v22, /device:TPU:32, one launch (start us, length us, event | category | flops | bytes accessed | tf_op | source)
XLA Modules:
  0.0 145.7 jit_solution(6722189152082608973)
XLA Ops:
  0.0 0.8 convert_element_type.84
  0.8 2.0 %broadcast_multiply_fusion = f32[1,36,32,512]{3,2,1,0:T(8,128)S(1)} fusion(f32[1,36,32,512]{3,2,1,0:T(8,128)} %param.8, f32[32,512]{1,0:T(8,128)S(1)} %convert_element_type.84), kind=kLoop, calls=%fused_computation.56 | loop fusion | flops 589824 | bytes 4784128 | tf_op jit(solution)/shard_map/mul | solution.py:241
  2.9 0.1 fusion.45
  3.0 1.3 collective-permute-start.1
  4.3 3.0 %collective-permute-start = (f32[1,36,2,512]{3,2,1,0:T(2,128)S(1)}, f32[1,36,2,512]{3,2,1,0:T(2,128)S(1)}, u32[]{:S(2)}, u32[]{:S(2)}) collective-permute-start(f32[1,36,2,512]{3,2,1,0:T(2,128)S(1)} %get-tuple-element.12), channel_id=1, source_target_pairs={{0,32},{32,64},{64,96},{96,128},{128,160},{160,192},{192,224},{1,3... | collective-permute-start | bytes 442376 | tf_op jit(solution)/shard_map/ppermute | solution.py:33
  7.6 0.0 collective-permute-done.1
  7.7 0.7 collective-permute-done
  8.3 0.0 copy-start.1
  8.3 2.5 %fusion.9 = f32[1,36,33,512]{3,2,1,0:T(8,128)S(1)} fusion(f32[1,36,2,512]{3,2,1,0:T(2,128)S(1)} %collective-permute-done.1, f32[1,36,32,512]{3,2,1,0:T(8,128)S(1)} %broadcast_multiply_fusion, f32[1,36,2,512]{3,2,1,0:T(2,128)S(1)} %collective-permute-done, f32[36]{0:T(128)S(1)} %get-tuple-element.25, f32[36]{0:T(128)S(1)} %get-tuple-element.26, ...), kind=kLoop, calls=%fused_computation.17 | loop fusion | flops 10948608 | bytes 5087700 | tf_op jit(solution)/shard_map/mul | solution.py:65
  10.8 0.0 copy-done.1
  10.9 0.7 fusion.27
  11.6 2.8 %fusion.4 = f32[1,36,32,513]{3,2,1,0:T(8,128)S(1)} fusion(f32[1,36,32,512]{3,2,1,0:T(8,128)S(1)} %fusion.27, f32[36]{0:T(128)S(1)} %get-tuple-element.22, f32[36]{0:T(128)S(1)} %get-tuple-element.23, f32[36]{0:T(128)S(1)} %get-tuple-element.24, pred[36]{0:T(512)(128)(4,1)S(1)} %get-tuple-element.28), kind=kLoop, calls=%fused_computation.11 | loop fusion | flops 8273664 | bytes 4723668 | tf_op jit(solution)/shard_map/mul | solution.py:65
  14.4 0.0 copy-start.2
  14.4 0.0 copy-start.3
  14.4 0.7 fusion.25
  15.1 0.1 copy-done.2
  15.2 0.0 copy-done.3
  15.3 3.1 %fusion.16 = f32[1,37,32,512]{3,2,1,0:T(8,128)S(1)} fusion(f32[1,2,32,512]{3,2,1,0:T(8,128)S(1)} %get-tuple-element.11, f32[1,36,32,512]{3,2,1,0:T(8,128)S(1)} %fusion.25, f32[1,2,32,512]{3,2,1,0:T(8,128)S(1)} %get-tuple-element.10, f32[32,512]{1,0:T(8,128)S(1)} %copy-done.2, f32[37]{0:T(128)S(1)} %get-tuple-element.30, f32[32,512]{1,0:T(8,128)S(1)} %copy-done.3, ...), kind=kLoop, calls=%fused_computation.32 | loop fusion | flops 16973824 | bytes 5177644 | tf_op jit(solution)/shard_map/mul | solution.py:65
  18.4 0.6 fusion.23
  19.0 3.8 %copy.17 = f32[1,36,32,512]{3,0,1,2:T(1,128)} copy(f32[1,36,32,512]{3,2,1,0:T(8,128)S(1)} %fusion.23) | data formatting | bytes 4718592 | tf_op jit(solution)/shard_map/max | solution.py:257
  22.8 4.5 %all-to-all-start = ((f32[1,36,32,512]{3,0,1,2:T(1,128)}), f32[1,36,32,512]{3,0,1,2:T(1,128)S(1)}, u32[]{:S(2)}, u32[]{:S(2)}) async-start(f32[1,36,32,512]{3,0,1,2:T(1,128)} %copy.17), calls=%async_computation | async-start | bytes 4718592 | tf_op jit(solution)/shard_map/all_to_all | solution.py:258
  27.3 0.7 dynamic-slice_multiply_fusion
  28.0 0.1 multiply_multiply_fusion
  28.1 1.9 %subtract_cosine_fusion = f32[36,8,512]{2,1,0:T(8,128)S(1)} fusion(f32[8,512]{1,0:T(8,128)S(1)} %get-tuple-element.33, f32[36]{0:T(128)S(1)} %add_multiply_fusion), kind=kLoop, calls=%fused_computation.57 | loop fusion | flops 147456 | bytes 606352 | tf_op jit(solution)/shard_map/cos | solution.py:287
  30.1 26.8 %all-to-all-done = f32[1,36,32,512]{3,0,1,2:T(1,128)S(1)} async-done(((f32[1,36,32,512]{3,0,1,2:T(1,128)}), f32[1,36,32,512]{3,0,1,2:T(1,128)S(1)}, u32[]{:S(2)}, u32[]{:S(2)}) %all-to-all-start) | async-done | bytes 2359328 | tf_op jit(solution)/shard_map/all_to_all | solution.py:258
  56.9 0.8 multiply_reduce_fusion
  57.7 6.6 %collective-permute-start.2 = (f32[3,8,512]{2,1,0:T(8,128)S(1)}, f32[3,8,512]{2,1,0:T(8,128)S(1)}, u32[]{:S(2)}, u32[]{:S(2)}) collective-permute-start(f32[3,8,512]{2,1,0:T(8,128)S(1)} %pad_maximum_fusion.6), channel_id=1, source_target_pairs={{0,16},{4,20},{8,24},{12,28},{16,0},{20,4},{24,8},{28,12},{1,17},{... | collective-permute-start | bytes 147464 | tf_op jit(solution)/shard_map/ppermute | solution.py:274
  64.3 2.5 %collective-permute-done.2 = f32[3,8,512]{2,1,0:T(8,128)S(1)} collective-permute-done((f32[3,8,512]{2,1,0:T(8,128)S(1)}, f32[3,8,512]{2,1,0:T(8,128)S(1)}, u32[]{:S(2)}, u32[]{:S(2)}) %collective-permute-start.2) | collective-permute-done | bytes 49184 | tf_op jit(solution)/shard_map/ppermute | solution.py:274
  66.8 2.9 %collective-permute-start.3 = (f32[3,8,512]{2,1,0:T(8,128)S(1)}, f32[3,8,512]{2,1,0:T(8,128)S(1)}, u32[]{:S(2)}, u32[]{:S(2)}) collective-permute-start(f32[3,8,512]{2,1,0:T(8,128)S(1)} %fusion.42), channel_id=1, source_target_pairs={{0,8},{4,12},{8,0},{12,4},{16,24},{20,28},{24,16},{28,20},{1,9},{5... | collective-permute-start | bytes 147464 | tf_op jit(solution)/shard_map/ppermute | solution.py:274
  69.7 2.1 %copy_bitcast_fusion.1.point_ref = f32[4,36,8,512]{3,2,1,0:T(8,128)} fusion(f32[1,36,32,512]{3,0,1,2:T(1,128)S(1)} %all-to-all-done), kind=kLoop, calls=%fused_computation.51 | loop fusion | bytes 4718592 | tf_op jit(solution)/shard_map/all_to_all | solution.py:258
  71.8 32.0 %shard_map.64 = f32[8,36,8,512]{3,2,1,0:T(8,128)} custom-call(f32[4,36,8,512]{3,2,1,0:T(8,128)} %copy_bitcast_fusion.1.point_ref), custom_call_target="tpu_custom_call" | custom-call | tf_op jit(solution)/shard_map/pallas_call | solution.py:214
  103.8 0.0 copy-start
  103.8 2.4 %slice.163 = f32[6,33,8,512]{3,2,1,0:T(8,128)S(1)} slice(f32[8,36,8,512]{3,2,1,0:T(8,128)} %shard_map.64), slice={[0:6], [0:33], [0:8], [0:512]} | slice | bytes 6488064 | tf_op jit(solution)/shard_map/jit(_roll_static)/slice | solution.py:278
  106.2 0.9 copy-done
  107.1 0.5 slice.160
  107.7 0.0 collective-permute-done.3
  107.7 0.1 collective-permute-start.4
  107.8 1.4 multiply_subtract_fusion
  109.2 0.3 slice.192
  109.5 0.3 slice.193
  109.8 2.1 %collective-permute-done.4 = f32[3,8,512]{2,1,0:T(8,128)S(1)} collective-permute-done((f32[3,8,512]{2,1,0:T(8,128)S(1)}, f32[3,8,512]{2,1,0:T(8,128)S(1)}, u32[]{:S(2)}, u32[]{:S(2)}) %collective-permute-start.4) | collective-permute-done | bytes 49184 | tf_op jit(solution)/shard_map/ppermute | solution.py:274
  111.9 0.1 fusion.30
  112.0 2.1 %fusion.21 = f32[4,36,8,512]{3,2,1,0:T(8,128)S(1)} fusion(f32[6,36,8,512]{3,2,1,0:T(8,128)S(1)} %multiply_subtract_fusion, f32[4,35,8,512]{3,2,1,0:T(8,128)S(1)} %slice.192, f32[4,1,8,512]{3,2,1,0:T(8,128)S(1)} %slice.191, f32[4,3,8,512]{3,2,1,0:T(8,128)S(1)} %slice.194, f32[4,33,8,512]{3,2,1,0:T(8,128)S(1)} %slice.193, ...), kind=kLoop, calls=%fused_computation.40 | loop fusion | flops 8847360 | bytes 12550160 | tf_op jit(solution)/shard_map/mul | solution.py:288
  114.1 29.9 %all_to_all.36 = f32[4,36,8,512]{3,2,1,0:T(8,128)S(1)} all-to-all(f32[4,36,8,512]{3,2,1,0:T(8,128)S(1)} %fusion.21), channel_id=1, replica_groups=mesh['geo'=8,'z'=8,'y'=4] {'y'}, dimensions={0} | all-to-all | bytes 4718592 | tf_op jit(solution)/shard_map/all_to_all | solution.py:301
  144.1 1.7 %copy_bitcast_fusion = f32[1,36,32,512]{3,2,1,0:T(8,128)} fusion(f32[4,36,8,512]{3,2,1,0:T(8,128)S(1)} %all_to_all.36), kind=kLoop, calls=%fused_computation.50 | loop fusion | bytes 4718592 | tf_op jit(solution)/shard_map/all_to_all | solution.py:301
  (20 shorter events, 0.4 us)
Async XLA Ops:
  3.0 4.7 %collective-permute-start.1 = (f32[1,36,2,512]{3,2,1,0:T(2,128)S(1)}, f32[1,36,2,512]{3,2,1,0:T(2,128)S(1)}, u32[]{:S(2)}, u32[]{:S(2)}) collective-permute-start(f32[1,36,2,512]{3,2,1,0:T(2,128)S(1)} %get-tuple-element.13), channel_id=1, source_target_pairs={{32,0},{64,32},{96,64},{128,96},{160,128},{192,160},{224,192},{33,... | collective-permute-start | bytes 442376 | tf_op jit(solution)/shard_map/ppermute | solution.py:35
  4.3 4.0 %collective-permute-start = (f32[1,36,2,512]{3,2,1,0:T(2,128)S(1)}, f32[1,36,2,512]{3,2,1,0:T(2,128)S(1)}, u32[]{:S(2)}, u32[]{:S(2)}) collective-permute-start(f32[1,36,2,512]{3,2,1,0:T(2,128)S(1)} %get-tuple-element.12), channel_id=1, source_target_pairs={{0,32},{32,64},{64,96},{96,128},{128,160},{160,192},{192,224},{1,3... | collective-permute-start | bytes 442376 | tf_op jit(solution)/shard_map/ppermute | solution.py:33
  8.3 2.5 %copy-start.1 = (f32[1,36,32,512]{3,2,1,0:T(8,128)S(1)}, f32[1,36,32,512]{3,2,1,0:T(8,128)}, u32[]{:S(2)}) copy-start(f32[1,36,32,512]{3,2,1,0:T(8,128)} %param.8) | copy-start | bytes 7077892
  14.4 0.8 copy-start.2
  14.4 0.9 copy-start.3
  22.8 34.1 %all-to-all-start = ((f32[1,36,32,512]{3,0,1,2:T(1,128)}), f32[1,36,32,512]{3,0,1,2:T(1,128)S(1)}, u32[]{:S(2)}, u32[]{:S(2)}) async-start(f32[1,36,32,512]{3,0,1,2:T(1,128)} %copy.17), calls=%async_computation | async-start | bytes 4718592 | tf_op jit(solution)/shard_map/all_to_all | solution.py:258
  57.7 9.1 %collective-permute-start.2 = (f32[3,8,512]{2,1,0:T(8,128)S(1)}, f32[3,8,512]{2,1,0:T(8,128)S(1)}, u32[]{:S(2)}, u32[]{:S(2)}) collective-permute-start(f32[3,8,512]{2,1,0:T(8,128)S(1)} %pad_maximum_fusion.6), channel_id=1, source_target_pairs={{0,16},{4,20},{8,24},{12,28},{16,0},{20,4},{24,8},{28,12},{1,17},{... | collective-permute-start | bytes 147464 | tf_op jit(solution)/shard_map/ppermute | solution.py:274
  66.8 40.9 %collective-permute-start.3 = (f32[3,8,512]{2,1,0:T(8,128)S(1)}, f32[3,8,512]{2,1,0:T(8,128)S(1)}, u32[]{:S(2)}, u32[]{:S(2)}) collective-permute-start(f32[3,8,512]{2,1,0:T(8,128)S(1)} %fusion.42), channel_id=1, source_target_pairs={{0,8},{4,12},{8,0},{12,4},{16,24},{20,28},{24,16},{28,20},{1,9},{5... | collective-permute-start | bytes 147464 | tf_op jit(solution)/shard_map/ppermute | solution.py:274
  103.8 3.3 %copy-start = (f32[8,36,8,512]{3,2,1,0:T(8,128)S(1)}, f32[8,36,8,512]{3,2,1,0:T(8,128)}, u32[]{:S(2)}) copy-start(f32[8,36,8,512]{3,2,1,0:T(8,128)} %shard_map.64) | copy-start | bytes 14155780
  107.7 4.2 %collective-permute-start.4 = (f32[3,8,512]{2,1,0:T(8,128)S(1)}, f32[3,8,512]{2,1,0:T(8,128)S(1)}, u32[]{:S(2)}, u32[]{:S(2)}) collective-permute-start(f32[3,8,512]{2,1,0:T(8,128)S(1)} %fusion.46), channel_id=1, source_target_pairs={{0,4},{4,0},{8,12},{12,8},{16,20},{20,16},{24,28},{28,24},{1,5},{5... | collective-permute-start | bytes 147464 | tf_op jit(solution)/shard_map/ppermute | solution.py:274

commit v23 on v21

--- a/solution.py
+++ b/solution.py
@@ -513,7 +513,8 @@
         )
         + extra
     ) * wet_block
-    return lax.all_to_all(updated, "y", split_axis=0, concat_axis=2, tiled=True)
+    by_quarter = lax.all_to_all(updated, "y", split_axis=0, concat_axis=0, tiled=True)
+    return jnp.transpose(by_quarter, (1, 0, 2, 3)).reshape(1, dir_count, row_count, col_count)
 
 
 def solution(mesh):

time: 140 us -> 140 us (level)
    all_to_all x1 -> x0, local copies, waits for them, and re-layouts: 1.66 us -> none  [shards(): return lax.all_to_all(updated, 'y', split_axis=0, concat_axis=2, tiled=True)]
    reshape x0 -> x1, local copies, waits for them, and re-layouts: none -> 1.66 us  [shards(): jnp.transpose(by_quarter, (1, 0, 2, 3))]
where the time goes in v23:
time: 140 us; the launch traced here: 138 us
  waiting for transfers between devices  34.1 us (24%)
  Pallas kernels  28.2 us (20%)
  blocking collectives  27.4 us (20%)
  other arithmetic  23 us (16%)
  starting transfers between devices  16.9 us (12%)
  local copies, waits for them, and re-layouts  8.39 us (6%)
    pallas_call x1, Pallas kernels, z_halo(): pl.pallas_call(functools.partial(_z_halo_kernel, z_count), out_shape=(hal...  28.2 us
    all_to_all x1, blocking collectives, shards(): lax.all_to_all(updated, 'y', split_axis=0, concat_axis=0, tiled=True)  27.4 us
    all_to_all x1, waiting for transfers between devices, shards(): lax.all_to_all(floored, 'y', split_axis=2, concat_axis=0, tiled=True)  25.6 us
    ppermute x3, starting transfers between devices, shards(): lax.ppermute(sums, 'z', [(i, i ^ step) for i in range(z_count)])  8.78 us
    mul x3, other arithmetic, quick_flux(): return courant * face_value  8.41 us
    ppermute x1, waiting for transfers between devices, extended(): lax.ppermute(tail, axis, [(i, (i + 1) % count) for i in range(ends)])  4.37 us
    ppermute x3, waiting for transfers between devices, shards(): lax.ppermute(sums, 'z', [(i, i ^ step) for i in range(z_count)])  4.09 us
    max x1, local copies, waits for them, and re-layouts, shards(): floored = jnp.maximum(advect(padded, turning, 1), 0.0)  3.83 us
  transfers between devices with their start and end apart: 6, of which 4 were waited for; matrix products, arithmetic and copies ran while one was open for 7% of the time, Pallas kernels for 20%

profile of v23, /device:TPU:2, one launch (start us, length us, event | category | flops | bytes accessed | tf_op | source)
XLA Modules:
  0.0 138.3 jit_solution(4792576416295670157)
XLA Ops:
  0.0 0.8 convert_element_type.84
  0.8 2.0 %broadcast_multiply_fusion = f32[1,36,32,512]{3,2,1,0:T(8,128)S(1)} fusion(f32[1,36,32,512]{3,2,1,0:T(8,128)} %param.8, f32[32,512]{1,0:T(8,128)S(1)} %convert_element_type.84), kind=kLoop, calls=%fused_computation.64 | loop fusion | flops 589824 | bytes 4784128 | tf_op jit(solution)/shard_map/mul | solution.py:455
  2.9 0.1 fusion.48
  3.0 1.9 %collective-permute-start.1 = (f32[1,36,2,512]{3,2,1,0:T(2,128)S(1)}, f32[1,36,2,512]{3,2,1,0:T(2,128)S(1)}, u32[]{:S(2)}, u32[]{:S(2)}) collective-permute-start(f32[1,36,2,512]{3,2,1,0:T(2,128)S(1)} %get-tuple-element.17), channel_id=1, source_target_pairs={{32,0},{64,32},{96,64},{128,96},{160,128},{192,160},{224,192},{33,... | collective-permute-start | bytes 442376 | tf_op jit(solution)/shard_map/ppermute | solution.py:233
  4.9 2.4 %collective-permute-start = (f32[1,36,2,512]{3,2,1,0:T(2,128)S(1)}, f32[1,36,2,512]{3,2,1,0:T(2,128)S(1)}, u32[]{:S(2)}, u32[]{:S(2)}) collective-permute-start(f32[1,36,2,512]{3,2,1,0:T(2,128)S(1)} %get-tuple-element.16), channel_id=1, source_target_pairs={{0,32},{32,64},{64,96},{96,128},{128,160},{160,192},{192,224},{1,3... | collective-permute-start | bytes 442376 | tf_op jit(solution)/shard_map/ppermute | solution.py:231
  7.6 0.0 collective-permute-done.1
  7.6 4.4 %collective-permute-done = f32[1,36,2,512]{3,2,1,0:T(2,128)S(1)} collective-permute-done((f32[1,36,2,512]{3,2,1,0:T(2,128)S(1)}, f32[1,36,2,512]{3,2,1,0:T(2,128)S(1)}, u32[]{:S(2)}, u32[]{:S(2)}) %collective-permute-start) | collective-permute-done | bytes 147488 | tf_op jit(solution)/shard_map/ppermute | solution.py:231
  12.0 0.0 copy-start.1
  12.0 2.5 %fusion.12 = f32[1,36,33,512]{3,2,1,0:T(8,128)S(1)} fusion(f32[1,36,2,512]{3,2,1,0:T(2,128)S(1)} %collective-permute-done.1, f32[1,36,32,512]{3,2,1,0:T(8,128)S(1)} %broadcast_multiply_fusion, f32[1,36,2,512]{3,2,1,0:T(2,128)S(1)} %collective-permute-done, f32[36]{0:T(128)S(1)} %get-tuple-element.29, f32[36]{0:T(128)S(1)} %get-tuple-element.30, ...), kind=kLoop, calls=%fused_computation.25 | loop fusion | flops 10948608 | bytes 5087700 | tf_op jit(solution)/shard_map/mul | solution.py:263
  14.6 0.0 copy-done.1
  14.6 0.7 fusion.30
  15.3 2.8 %fusion.7 = f32[1,36,32,513]{3,2,1,0:T(8,128)S(1)} fusion(f32[1,36,32,512]{3,2,1,0:T(8,128)S(1)} %fusion.30, f32[36]{0:T(128)S(1)} %get-tuple-element.26, f32[36]{0:T(128)S(1)} %get-tuple-element.27, f32[36]{0:T(128)S(1)} %get-tuple-element.28, pred[36]{0:T(512)(128)(4,1)S(1)} %get-tuple-element.32), kind=kLoop, calls=%fused_computation.19 | loop fusion | flops 8273664 | bytes 4723668 | tf_op jit(solution)/shard_map/mul | solution.py:263
  18.1 0.0 copy-start.4
  18.1 0.0 copy-start.5
  18.1 0.7 fusion.28
  18.8 0.1 copy-done.4
  18.9 0.0 copy-done.5
  19.0 3.1 %fusion.19 = f32[1,37,32,512]{3,2,1,0:T(8,128)S(1)} fusion(f32[1,2,32,512]{3,2,1,0:T(8,128)S(1)} %get-tuple-element.15, f32[1,36,32,512]{3,2,1,0:T(8,128)S(1)} %fusion.28, f32[1,2,32,512]{3,2,1,0:T(8,128)S(1)} %get-tuple-element.14, f32[32,512]{1,0:T(8,128)S(1)} %copy-done.4, f32[37]{0:T(128)S(1)} %get-tuple-element.34, f32[32,512]{1,0:T(8,128)S(1)} %copy-done.5, ...), kind=kLoop, calls=%fused_computation.40 | loop fusion | flops 16973824 | bytes 5177644 | tf_op jit(solution)/shard_map/mul | solution.py:263
  22.1 0.6 fusion.26
  22.7 3.8 %copy.17 = f32[1,36,32,512]{3,0,1,2:T(1,128)} copy(f32[1,36,32,512]{3,2,1,0:T(8,128)S(1)} %fusion.26) | data formatting | bytes 4718592 | tf_op jit(solution)/shard_map/max | solution.py:471
  26.5 3.8 %all-to-all-start = ((f32[1,36,32,512]{3,0,1,2:T(1,128)}), f32[1,36,32,512]{3,0,1,2:T(1,128)S(1)}, u32[]{:S(2)}, u32[]{:S(2)}) async-start(f32[1,36,32,512]{3,0,1,2:T(1,128)} %copy.17), calls=%async_computation | async-start | bytes 4718592 | tf_op jit(solution)/shard_map/all_to_all | solution.py:472
  30.4 0.7 dynamic-slice_multiply_fusion
  31.1 0.1 multiply_multiply_fusion
  31.2 1.9 %subtract_cosine_fusion = f32[36,8,512]{2,1,0:T(8,128)S(1)} fusion(f32[8,512]{1,0:T(8,128)S(1)} %get-tuple-element.37, f32[36]{0:T(128)S(1)} %add_multiply_fusion), kind=kLoop, calls=%fused_computation.65 | loop fusion | flops 147456 | bytes 606352 | tf_op jit(solution)/shard_map/cos | solution.py:502
  33.2 25.6 %all-to-all-done = f32[1,36,32,512]{3,0,1,2:T(1,128)S(1)} async-done(((f32[1,36,32,512]{3,0,1,2:T(1,128)}), f32[1,36,32,512]{3,0,1,2:T(1,128)S(1)}, u32[]{:S(2)}, u32[]{:S(2)}) %all-to-all-start) | async-done | bytes 2359328 | tf_op jit(solution)/shard_map/all_to_all | solution.py:472
  58.8 0.8 multiply_reduce_fusion
  59.6 7.5 %collective-permute-start.2 = (f32[3,8,512]{2,1,0:T(8,128)S(1)}, f32[3,8,512]{2,1,0:T(8,128)S(1)}, u32[]{:S(2)}, u32[]{:S(2)}) collective-permute-start(f32[3,8,512]{2,1,0:T(8,128)S(1)} %pad_maximum_fusion.9), channel_id=1, source_target_pairs={{0,16},{4,20},{8,24},{12,28},{16,0},{20,4},{24,8},{28,12},{1,17},{... | collective-permute-start | bytes 147464 | tf_op jit(solution)/shard_map/ppermute | solution.py:488
  67.0 2.1 %copy_bitcast_fusion.1.point_ref = f32[4,36,8,512]{3,2,1,0:T(8,128)} fusion(f32[1,36,32,512]{3,0,1,2:T(1,128)S(1)} %all-to-all-done), kind=kLoop, calls=%fused_computation.59 | loop fusion | bytes 4718592 | tf_op jit(solution)/shard_map/all_to_all | solution.py:472
  69.2 28.2 %shard_map.64 = (f32[2,36,8,512]{3,2,1,0:T(8,128)}, f32[2,36,8,512]{3,2,1,0:T(8,128)}) custom-call(f32[4,36,8,512]{3,2,1,0:T(8,128)} %copy_bitcast_fusion.1.point_ref), custom_call_target="tpu_custom_call" | custom-call | tf_op jit(solution)/shard_map/pallas_call | solution.py:210
  97.4 0.0 collective-permute-done.2
  97.4 1.1 collective-permute-start.3
  98.6 0.0 copy-start
  98.6 0.0 copy-start.2
  98.6 0.0 copy-start.3
  98.6 2.4 %fusion.2 = f32[6,35,8,512]{3,2,1,0:T(8,128)S(1)} fusion(f32[4,36,8,512]{3,2,1,0:T(8,128)} %copy_bitcast_fusion.1.point_ref, f32[2,36,8,512]{3,2,1,0:T(8,128)} %get-tuple-element.8), kind=kLoop, calls=%fused_computation.10 | loop fusion | flops 860160 | bytes 6979584 | tf_op jit(solution)/shard_map/concatenate | solution.py:492
  101.0 2.0 %collective-permute-done.3 = f32[3,8,512]{2,1,0:T(8,128)S(1)} collective-permute-done((f32[3,8,512]{2,1,0:T(8,128)S(1)}, f32[3,8,512]{2,1,0:T(8,128)S(1)}, u32[]{:S(2)}, u32[]{:S(2)}) %collective-permute-start.3) | collective-permute-done | bytes 49184 | tf_op jit(solution)/shard_map/ppermute | solution.py:488
  103.0 0.2 collective-permute-start.4
  103.2 0.0 copy-done
  103.2 0.0 copy-done.2
  103.2 0.0 copy-done.3
  103.2 1.4 %multiply_subtract_fusion = f32[6,36,8,512]{3,2,1,0:T(8,128)S(1)} fusion(f32[2,36,8,512]{3,2,1,0:T(8,128)S(1)} %copy-done.2, f32[4,36,8,512]{3,2,1,0:T(8,128)S(1)} %copy-done, f32[6,35,8,512]{3,2,1,0:T(8,128)S(1)} %fusion.2, f32[2,36,8,512]{3,2,1,0:T(8,128)S(1)} %copy-done.3), kind=kLoop, calls=%fused_computation.9 | loop fusion | flops 12386304 | bytes 11698176 | tf_op jit(solution)/shard_map/sub | solution.py:494
  104.6 0.2 slice.194
  104.9 0.2 slice.195
  105.1 2.1 %collective-permute-done.4 = f32[3,8,512]{2,1,0:T(8,128)S(1)} collective-permute-done((f32[3,8,512]{2,1,0:T(8,128)S(1)}, f32[3,8,512]{2,1,0:T(8,128)S(1)}, u32[]{:S(2)}, u32[]{:S(2)}) %collective-permute-start.4) | collective-permute-done | bytes 49184 | tf_op jit(solution)/shard_map/ppermute | solution.py:488
  107.3 0.1 fusion.33
  107.4 1.9 %fusion.24 = f32[4,36,8,512]{3,2,1,0:T(8,128)S(1)} fusion(f32[6,36,8,512]{3,2,1,0:T(8,128)S(1)} %multiply_subtract_fusion, f32[4,35,8,512]{3,2,1,0:T(8,128)S(1)} %slice.194, f32[4,1,8,512]{3,2,1,0:T(8,128)S(1)} %slice.193, f32[4,3,8,512]{3,2,1,0:T(8,128)S(1)} %slice.196, f32[4,33,8,512]{3,2,1,0:T(8,128)S(1)} %slice.195, ...), kind=kLoop, calls=%fused_computation.48 | loop fusion | flops 8847360 | bytes 12550160 | tf_op jit(solution)/shard_map/mul | solution.py:503
  109.3 27.4 %all_to_all.23 = f32[4,36,8,512]{3,2,1,0:T(8,128)S(1)} all-to-all(f32[4,36,8,512]{3,2,1,0:T(8,128)S(1)} %fusion.24), channel_id=1, replica_groups=mesh['geo'=8,'z'=8,'y'=4] {'y'}, dimensions={0} | all-to-all | bytes 4718592 | tf_op jit(solution)/shard_map/all_to_all | solution.py:516
  136.7 1.7 %copy_bitcast_fusion = f32[1,36,32,512]{3,2,1,0:T(8,128)} fusion(f32[4,36,8,512]{3,2,1,0:T(8,128)S(1)} %all_to_all.23), kind=kLoop, calls=%fused_computation.58 | loop fusion | bytes 4718592 | tf_op jit(solution)/shard_map/reshape | solution.py:517
  (18 shorter events, 0.4 us)
Async XLA Ops:
  3.0 4.6 %collective-permute-start.1 = (f32[1,36,2,512]{3,2,1,0:T(2,128)S(1)}, f32[1,36,2,512]{3,2,1,0:T(2,128)S(1)}, u32[]{:S(2)}, u32[]{:S(2)}) collective-permute-start(f32[1,36,2,512]{3,2,1,0:T(2,128)S(1)} %get-tuple-element.17), channel_id=1, source_target_pairs={{32,0},{64,32},{96,64},{128,96},{160,128},{192,160},{224,192},{33,... | collective-permute-start | bytes 442376 | tf_op jit(solution)/shard_map/ppermute | solution.py:233
  4.9 7.1 %collective-permute-start = (f32[1,36,2,512]{3,2,1,0:T(2,128)S(1)}, f32[1,36,2,512]{3,2,1,0:T(2,128)S(1)}, u32[]{:S(2)}, u32[]{:S(2)}) collective-permute-start(f32[1,36,2,512]{3,2,1,0:T(2,128)S(1)} %get-tuple-element.16), channel_id=1, source_target_pairs={{0,32},{32,64},{64,96},{96,128},{128,160},{160,192},{192,224},{1,3... | collective-permute-start | bytes 442376 | tf_op jit(solution)/shard_map/ppermute | solution.py:231
  12.0 2.5 %copy-start.1 = (f32[1,36,32,512]{3,2,1,0:T(8,128)S(1)}, f32[1,36,32,512]{3,2,1,0:T(8,128)}, u32[]{:S(2)}) copy-start(f32[1,36,32,512]{3,2,1,0:T(8,128)} %param.8) | copy-start | bytes 7077892
  18.1 0.8 copy-start.4
  18.1 0.9 copy-start.5
  26.5 32.3 %all-to-all-start = ((f32[1,36,32,512]{3,0,1,2:T(1,128)}), f32[1,36,32,512]{3,0,1,2:T(1,128)S(1)}, u32[]{:S(2)}, u32[]{:S(2)}) async-start(f32[1,36,32,512]{3,0,1,2:T(1,128)} %copy.17), calls=%async_computation | async-start | bytes 4718592 | tf_op jit(solution)/shard_map/all_to_all | solution.py:472
  59.6 37.8 %collective-permute-start.2 = (f32[3,8,512]{2,1,0:T(8,128)S(1)}, f32[3,8,512]{2,1,0:T(8,128)S(1)}, u32[]{:S(2)}, u32[]{:S(2)}) collective-permute-start(f32[3,8,512]{2,1,0:T(8,128)S(1)} %pad_maximum_fusion.9), channel_id=1, source_target_pairs={{0,16},{4,20},{8,24},{12,28},{16,0},{20,4},{24,8},{28,12},{1,17},{... | collective-permute-start | bytes 147464 | tf_op jit(solution)/shard_map/ppermute | solution.py:488
  97.4 5.6 %collective-permute-start.3 = (f32[3,8,512]{2,1,0:T(8,128)S(1)}, f32[3,8,512]{2,1,0:T(8,128)S(1)}, u32[]{:S(2)}, u32[]{:S(2)}) collective-permute-start(f32[3,8,512]{2,1,0:T(8,128)S(1)} %fusion.45), channel_id=1, source_target_pairs={{0,8},{4,12},{8,0},{12,4},{16,24},{20,28},{24,16},{28,20},{1,9},{5... | collective-permute-start | bytes 147464 | tf_op jit(solution)/shard_map/ppermute | solution.py:488
  98.6 4.6 %copy-start = (f32[4,36,8,512]{3,2,1,0:T(8,128)S(1)}, f32[4,36,8,512]{3,2,1,0:T(8,128)}, u32[]{:S(2)}) copy-start(f32[4,36,8,512]{3,2,1,0:T(8,128)} %copy_bitcast_fusion.1.point_ref) | copy-start | bytes 7077892
  98.6 4.6 %copy-start.2 = (f32[2,36,8,512]{3,2,1,0:T(8,128)S(1)}, f32[2,36,8,512]{3,2,1,0:T(8,128)}, u32[]{:S(2)}) copy-start(f32[2,36,8,512]{3,2,1,0:T(8,128)} %get-tuple-element.8) | copy-start | bytes 3538948
  98.6 4.6 %copy-start.3 = (f32[2,36,8,512]{3,2,1,0:T(8,128)S(1)}, f32[2,36,8,512]{3,2,1,0:T(8,128)}, u32[]{:S(2)}) copy-start(f32[2,36,8,512]{3,2,1,0:T(8,128)} %get-tuple-element.7) | copy-start | bytes 3538948
  103.0 4.2 %collective-permute-start.4 = (f32[3,8,512]{2,1,0:T(8,128)S(1)}, f32[3,8,512]{2,1,0:T(8,128)S(1)}, u32[]{:S(2)}, u32[]{:S(2)}) collective-permute-start(f32[3,8,512]{2,1,0:T(8,128)S(1)} %fusion.49), channel_id=1, source_target_pairs={{0,4},{4,0},{8,12},{12,8},{16,20},{20,16},{24,28},{28,24},{1,5},{5... | collective-permute-start | bytes 147464 | tf_op jit(solution)/shard_map/ppermute | solution.py:488
